TPU v7x, 256 devices: a whole 4x4x8 slice. The times are simulated.
256 devices in a mesh: tm: 8 (over z), gx: 8 (over y, core), gy: 4 (over x).
Axes of the slice: x: 4, y: 4, z: 8, core: 2. Of those that a mesh axis runs over, the one named last changes fastest.
Arguments:
- segment_opening_values: float32 [8, 4, 96, 64, 128], P('tm', None, 'gx', 'gy'), may hold values from -6 to 6
- cell_material_label: int32 [96, 64, 128], P('gx', 'gy'), may hold values from 0 to 5
- material_rigidity: float32 [6], replicated, may hold values from 0.3 to 3
- dilation_mismatch: float32 [6], replicated, may hold values from -1 to 1
- heat_swings_array: float32 [8, 2], P('tm'), may hold values from 0.5 to 4
- prony_coefficients: float32 [3], replicated, may hold values from 0.2 to 2
- prony_decay_times: float32 [3], replicated, may hold values from 0.7 to 48
Outputs:
- end_state: float32 [8, 4, 96, 64, 128], P('tm', None, 'gx', 'gy')
All inputs are finite; a program needn't handle non-finite values.
Results may differ from a plain program's by a relative error of at most 0.0001.
Values sent between devices are 32-bit elements; how exact they have to be, the bound alone decides.
No kernel may reach another device: no remote copies, remote signals or barrier semaphores. Data moves between devices by JAX's collectives and lax.ppermute only.
A program may use at most 64 MiB of HBM per device.

v0:
```python
import jax
import jax.numpy as jnp
from jax import lax
from jax.sharding import PartitionSpec as P

PARTITION_PACES = 2
SHARP_SOLVER_ITER = 3
LOOSE_SOLVER_ITER = 2


corners = [
    (near_one, near_two, near_three)
    for near_one in (0, 1)
    for near_two in (0, 1)
    for near_three in (0, 1)
]
diagonal_weights = [1.0 / 3.0] * 8
thermal_weights = [0.25 * (2 * near_three - 1) for near_one, near_two, near_three in corners]


def padded_2(block, sides, width):
    for axis, dim in sides:
        count = lax.axis_size(axis)
        forward = [(i, i + 1) for i in range(count - 1)]
        backward = [(target, source) for source, target in forward]
        low = lax.ppermute(
            lax.slice_in_dim(block, block.shape[dim] - width, None, axis=dim), axis, forward
        )
        high = lax.ppermute(lax.slice_in_dim(block, 0, width, axis=dim), axis, backward)
        block = jnp.concatenate([low, block, high], axis=dim)
    return block


def sent_to_all(shard, axis):
    length = lax.axis_size(axis)
    return lax.all_to_all(
        jnp.broadcast_to(shard[None], (length, *shard.shape)), axis, 0, 0, tiled=True
    )


def over_copies(shard, axis):
    everything = sent_to_all(shard, axis)
    return jnp.sum(everything, axis=0)


def together(arrays, axis):
    flat, at, done = (jnp.concatenate([a.reshape(-1) for a in arrays]), 0, [])
    subtotal = over_copies(flat, axis)
    for a in arrays:
        done.append(subtotal[at : at + a.size].reshape(a.shape))
        at += a.size
    return tuple(done)


def from_behind(value, axis, steps):
    count = lax.axis_size(axis)
    initial, last = (max(0, -steps), min(count, count - steps))
    return lax.ppermute(value, axis, [(source, source + steps) for source in range(initial, last)])


def region_lookup(cell_material_label, region_table):
    looked_up = jnp.zeros(cell_material_label.shape, region_table.dtype)
    for region in range(region_table.shape[0]):
        looked_up = looked_up + jnp.where(
            cell_material_label == region, region_table[region], jnp.zeros((), region_table.dtype)
        )
    return looked_up


def stencil_apply(padded, cell_rigidity):
    extent_one, extent_two, extent_three = cell_rigidity.shape
    values = [
        padded[
            near_one : near_one + extent_one,
            near_two : near_two + extent_two,
            near_three : near_three + extent_three,
        ]
        for near_one, near_two, near_three in corners
    ]
    corner_total = values[0]
    for corner_value in values[1:]:
        corner_total = corner_total + corner_value
    result = None
    for corner_index, (near_one, near_two, near_three) in enumerate(corners):
        face_sum = values[corner_index ^ 4] + values[corner_index ^ 2] + values[corner_index ^ 1]
        element_part = cell_rigidity * (
            5.0 / 12.0 * values[corner_index] + (face_sum - corner_total) / 12.0
        )
        node_part = element_part[
            1 - near_one : extent_one - near_one,
            1 - near_two : extent_two - near_two,
            1 - near_three : extent_three - near_three,
        ]
        result = node_part if result is None else result + node_part
    return result


def nodal_sum(element_field, weights):
    extent_one, extent_two, extent_three = element_field.shape
    result = None
    for corner_index, (near_one, near_two, near_three) in enumerate(corners):
        node_part = (
            weights[corner_index]
            * element_field[
                1 - near_one : extent_one - near_one,
                1 - near_two : extent_two - near_two,
                1 - near_three : extent_three - near_three,
            ]
        )
        result = node_part if result is None else result + node_part
    return result


def on_device(
    segment_opening_values,
    cell_material_label,
    material_rigidity,
    dilation_mismatch,
    heat_swings_array,
    prony_coefficients,
    prony_decay_times,
):
    extent_one, extent_two, extent_three = cell_material_label.shape
    margin = SHARP_SOLVER_ITER + 2
    depth_rim = margin - 1
    grid_one = extent_one * lax.axis_size("gx")
    grid_two = extent_two * lax.axis_size("gy")
    anchor_one = lax.axis_index("gx") * extent_one
    anchor_two = lax.axis_index("gy") * extent_two
    ids_wide = padded_2(cell_material_label, (("gx", 0), ("gy", 1)), margin)[:-1, :-1]
    element_one = anchor_one - margin + lax.iota(jnp.int32, extent_one + 2 * margin - 1)
    element_two = anchor_two - margin + lax.iota(jnp.int32, extent_two + 2 * margin - 1)
    element_inside = ((element_one >= 0) & (element_one < grid_one))[:, None, None] & (
        (element_two >= 0) & (element_two < grid_two)
    )[None, :, None]
    coefficient = jnp.where(
        element_inside,
        region_lookup(ids_wide, material_rigidity),
        jnp.zeros((), material_rigidity.dtype),
    )
    loaded = coefficient * region_lookup(ids_wide, dilation_mismatch)
    cell_rigidity = jnp.pad(coefficient, ((0, 0), (0, 0), (1, 0)))
    element_load = jnp.pad(loaded, ((0, 0), (0, 0), (1, 0)))
    thermal_wide = nodal_sum(element_load, thermal_weights)
    rigidity_main_terms = nodal_sum(cell_rigidity, diagonal_weights)
    node_one = anchor_one - depth_rim + lax.iota(jnp.int32, extent_one + 2 * depth_rim)
    node_two = anchor_two - depth_rim + lax.iota(jnp.int32, extent_two + 2 * depth_rim)
    node_inside = ((node_one >= 0) & (node_one < grid_one))[:, None, None] & (
        (node_two >= 0) & (node_two < grid_two)
    )[None, :, None]

    def owned(field):
        return field[depth_rim : depth_rim + extent_one, depth_rim : depth_rim + extent_two]

    dilation_deformation = owned(thermal_wide)

    def inner_sum(left, right):
        return jnp.sum(owned(left) * owned(right))

    def apply_operator(field, shift_value):
        padded = jnp.pad(field, 1)
        return shift_value * field + stencil_apply(padded, cell_rigidity)

    def pair_sum(remainder, scaled, image):
        return together((inner_sum(remainder, scaled), inner_sum(image, scaled)), ("gx", "gy"))

    def conjugate_solve(rhs_field, initial, shift_value, iterations):
        diagonal = shift_value + rigidity_main_terms
        widened = padded_2(jnp.stack([initial, rhs_field]), (("gx", 1), ("gy", 2)), depth_rim)
        initial = widened[0]
        rhs_field = widened[1]
        solution = initial
        remainder = rhs_field - apply_operator(solution, shift_value)
        scaled = jnp.where(node_inside, remainder / diagonal, 0.0)
        image = apply_operator(scaled, shift_value)
        gamma_now, curvature_sum = pair_sum(remainder, scaled, image)
        step_size = gamma_now / curvature_sum
        search = scaled
        along = image
        blend = 0.0
        for iteration in range(iterations):
            if iteration > 0:
                search = scaled + blend * search
                along = image + blend * along
            solution = solution + step_size * search
            if iteration + 1 < iterations:
                remainder = remainder - step_size * along
                scaled = jnp.where(node_inside, remainder / diagonal, 0.0)
                image = apply_operator(scaled, shift_value)
                gamma_next, curvature_sum = pair_sum(remainder, scaled, image)
                blend = gamma_next / gamma_now
                step_size = gamma_next / (curvature_sum - blend * gamma_next / step_size)
                gamma_now = gamma_next
        return owned(solution)

    def moment_forward(present_displacements, heat_level, step_length, iterations):
        decay_rate = jnp.exp(-step_length / prony_decay_times)
        factors = prony_coefficients * decay_rate
        shift_value = 1.0 / step_length + jnp.sum(factors)
        history = present_displacements[1:]
        rhs_field = (
            present_displacements[0] / step_length
            + heat_level * dilation_deformation
            + jnp.sum(factors[:, None, None, None] * history, axis=0)
        )
        displaced = conjugate_solve(rhs_field, present_displacements[0], shift_value, iterations)
        history = (
            decay_rate[:, None, None, None] * history
            + (1.0 - decay_rate)[:, None, None, None] * displaced[None]
        )
        return jnp.concatenate([displaced[None], history], axis=0)

    segment_number = lax.axis_index("tm")
    launch_moment = segment_opening_values[0]
    heat_trajectory = heat_swings_array[0]
    loose_interval_span = 1.0 * PARTITION_PACES
    sharp_result = launch_moment
    for sharp_interval_span in range(PARTITION_PACES):
        sharp_result = moment_forward(
            sharp_result, heat_trajectory[sharp_interval_span], 1.0, SHARP_SOLVER_ITER
        )
    coarse_old = moment_forward(
        launch_moment, heat_trajectory[PARTITION_PACES - 1], loose_interval_span, LOOSE_SOLVER_ITER
    )
    correction = sharp_result - coarse_old
    finished = coarse_old + correction

    def next_turn(turn_index, carried):
        received = from_behind(carried, "tm", 1)
        ongoing_approx = jnp.where(segment_number == 0, launch_moment, received)
        return (
            moment_forward(
                ongoing_approx,
                heat_trajectory[PARTITION_PACES - 1],
                loose_interval_span,
                LOOSE_SOLVER_ITER,
            )
            + correction
        )

    finished = lax.fori_loop(0, lax.axis_size("tm") - 1, next_turn, finished)
    return finished[None]


def solution(mesh):
    placed = (
        P("tm", None, "gx", "gy", None),
        P("gx", "gy", None),
        P(),
        P(),
        P("tm", None),
        P(),
        P(),
    )
    return jax.shard_map(
        on_device,
        mesh=mesh,
        in_specs=placed,
        out_specs=P("tm", None, "gx", "gy", None),
        check_vma=False,
    )
```

profile of v0, /device:TPU:129, one launch (start us, length us, event | category | flops | bytes accessed | tf_op | source)
XLA Modules:
  0.0 823.1 jit_solution(14822192614299697354)
XLA Ops:
  22.4 4.3 add_select_fusion
  26.6 8.0 add_multiply_fusion
  35.7 5.1 collective-permute-start.13
  64.8 12.9 %all_to_all.70 = f32[32,1,2]{2,1,0:T(1,128)S(1)} all-to-all(f32[32,1,2]{2,1,0:T(1,128)S(1)} %broadcast_in_dim.242), channel_id=1, replica_groups=mesh['tm'=8,'gx'=8,'gy'=4] {'gx','gy'}, dimensions={0} | all-to-all | bytes 512 | tf_op jit(solution)/shard_map/all_to_all | solution.py:36
  87.1 4.4 all-to-all-start.5
  91.5 7.0 all-to-all-done.5
  112.4 4.1 all-to-all-start.6
  117.4 6.2 all-to-all-done.6
  170.2 13.0 %all-to-all-start.2 = ((f32[32,1,2]{2,1,0:T(1,128)}), f32[32,1,2]{2,1,0:T(1,128)S(1)}, u32[]{:S(2)}, u32[]{:S(2)}) async-start(f32[32,1,2]{2,1,0:T(1,128)} %broadcast_in_dim.239), calls=%async_computation.2 | async-start | bytes 32768 | tf_op jit(solution)/shard_map/all_to_all | solution.py:36
  184.4 5.8 all-to-all-done.2
  190.8 5.3 all-to-all-start.7
  196.7 6.3 all-to-all-done.7
  212.4 4.1 all-to-all-start.8
  217.7 5.8 all-to-all-done.8
  242.8 4.2 all-to-all-start.3
  248.3 5.7 all-to-all-done.3
  259.8 4.2 all-to-all-start.9
  265.0 6.0 all-to-all-done.9
  277.5 544.4 %while.13 = (s32[]{:T(128)}, f32[4,12,16,128]{3,2,1,0:T(8,128)S(1)}, pred[]{:T(512)}, f32[4,12,16,128]{3,2,1,0:T(8,128)S(1)}, f32[2]{0:T(128)S(1)}, /*index=5*/f...) while((s32[]{:T(128)}, ...), condition=%wide.region_38.39_spmd.clone, body=%wide.region_29.38_spmd.clone.sunk | while | flops 14445726 | bytes 58459560 | solution.py:241
  281.6 9.2 %collective-permute-done = f32[4,12,16,128]{3,2,1,0:T(8,128)S(1)} collective-permute-done((f32[4,12,16,128]{3,2,1,0:T(8,128)S(1)}, f32[4,12,16,128]{3,2,1,0:T(8,128)S(1)}, u32[]{:S(2)}, u32[]{:S(2)}) %collective-permute-start) | collective-permute-done | bytes 393248 | tf_op jit(solution)/shard_map/while/body/eval_jaxpr/ppermute | solution.py:58
  315.3 14.9 %all_to_all.71 = f32[32,1,2]{2,1,0:T(1,128)S(1)} all-to-all(f32[32,1,2]{2,1,0:T(1,128)S(1)} %broadcast_in_dim.318), channel_id=1, replica_groups=mesh['tm'=8,'gx'=8,'gy'=4] {'gx','gy'}, dimensions={0} | all-to-all | bytes 512 | tf_op jit(solution)/shard_map/while/body/eval_jaxpr/all_to_all | solution.py:36
  339.2 4.1 all-to-all-start.1
  343.3 6.9 all-to-all-done.1
  358.7 9.9 %collective-permute-done = f32[4,12,16,128]{3,2,1,0:T(8,128)S(1)} collective-permute-done((f32[4,12,16,128]{3,2,1,0:T(8,128)S(1)}, f32[4,12,16,128]{3,2,1,0:T(8,128)S(1)}, u32[]{:S(2)}, u32[]{:S(2)}) %collective-permute-start) | collective-permute-done | bytes 393248 | tf_op jit(solution)/shard_map/while/body/eval_jaxpr/ppermute | solution.py:58
  377.6 4.0 collective-permute-start.4
  393.1 14.9 %all_to_all.71 = f32[32,1,2]{2,1,0:T(1,128)S(1)} all-to-all(f32[32,1,2]{2,1,0:T(1,128)S(1)} %broadcast_in_dim.318), channel_id=1, replica_groups=mesh['tm'=8,'gx'=8,'gy'=4] {'gx','gy'}, dimensions={0} | all-to-all | bytes 512 | tf_op jit(solution)/shard_map/while/body/eval_jaxpr/all_to_all | solution.py:36
  416.9 4.1 all-to-all-start.1
  421.1 6.9 all-to-all-done.1
  436.4 9.9 %collective-permute-done = f32[4,12,16,128]{3,2,1,0:T(8,128)S(1)} collective-permute-done((f32[4,12,16,128]{3,2,1,0:T(8,128)S(1)}, f32[4,12,16,128]{3,2,1,0:T(8,128)S(1)}, u32[]{:S(2)}, u32[]{:S(2)}) %collective-permute-start) | collective-permute-done | bytes 393248 | tf_op jit(solution)/shard_map/while/body/eval_jaxpr/ppermute | solution.py:58
  470.8 14.9 %all_to_all.71 = f32[32,1,2]{2,1,0:T(1,128)S(1)} all-to-all(f32[32,1,2]{2,1,0:T(1,128)S(1)} %broadcast_in_dim.318), channel_id=1, replica_groups=mesh['tm'=8,'gx'=8,'gy'=4] {'gx','gy'}, dimensions={0} | all-to-all | bytes 512 | tf_op jit(solution)/shard_map/while/body/eval_jaxpr/all_to_all | solution.py:36
  494.7 4.1 all-to-all-start.1
  498.8 6.9 all-to-all-done.1
  514.1 9.9 %collective-permute-done = f32[4,12,16,128]{3,2,1,0:T(8,128)S(1)} collective-permute-done((f32[4,12,16,128]{3,2,1,0:T(8,128)S(1)}, f32[4,12,16,128]{3,2,1,0:T(8,128)S(1)}, u32[]{:S(2)}, u32[]{:S(2)}) %collective-permute-start) | collective-permute-done | bytes 393248 | tf_op jit(solution)/shard_map/while/body/eval_jaxpr/ppermute | solution.py:58
  548.6 14.9 %all_to_all.71 = f32[32,1,2]{2,1,0:T(1,128)S(1)} all-to-all(f32[32,1,2]{2,1,0:T(1,128)S(1)} %broadcast_in_dim.318), channel_id=1, replica_groups=mesh['tm'=8,'gx'=8,'gy'=4] {'gx','gy'}, dimensions={0} | all-to-all | bytes 512 | tf_op jit(solution)/shard_map/while/body/eval_jaxpr/all_to_all | solution.py:36
  572.4 4.1 all-to-all-start.1
  576.6 6.9 all-to-all-done.1
  591.9 9.9 %collective-permute-done = f32[4,12,16,128]{3,2,1,0:T(8,128)S(1)} collective-permute-done((f32[4,12,16,128]{3,2,1,0:T(8,128)S(1)}, f32[4,12,16,128]{3,2,1,0:T(8,128)S(1)}, u32[]{:S(2)}, u32[]{:S(2)}) %collective-permute-start) | collective-permute-done | bytes 393248 | tf_op jit(solution)/shard_map/while/body/eval_jaxpr/ppermute | solution.py:58
  626.3 14.9 %all_to_all.71 = f32[32,1,2]{2,1,0:T(1,128)S(1)} all-to-all(f32[32,1,2]{2,1,0:T(1,128)S(1)} %broadcast_in_dim.318), channel_id=1, replica_groups=mesh['tm'=8,'gx'=8,'gy'=4] {'gx','gy'}, dimensions={0} | all-to-all | bytes 512 | tf_op jit(solution)/shard_map/while/body/eval_jaxpr/all_to_all | solution.py:36
  650.1 4.1 all-to-all-start.1
  654.3 6.9 all-to-all-done.1
  669.6 9.9 %collective-permute-done = f32[4,12,16,128]{3,2,1,0:T(8,128)S(1)} collective-permute-done((f32[4,12,16,128]{3,2,1,0:T(8,128)S(1)}, f32[4,12,16,128]{3,2,1,0:T(8,128)S(1)}, u32[]{:S(2)}, u32[]{:S(2)}) %collective-permute-start) | collective-permute-done | bytes 393248 | tf_op jit(solution)/shard_map/while/body/eval_jaxpr/ppermute | solution.py:58
  704.0 14.9 %all_to_all.71 = f32[32,1,2]{2,1,0:T(1,128)S(1)} all-to-all(f32[32,1,2]{2,1,0:T(1,128)S(1)} %broadcast_in_dim.318), channel_id=1, replica_groups=mesh['tm'=8,'gx'=8,'gy'=4] {'gx','gy'}, dimensions={0} | all-to-all | bytes 512 | tf_op jit(solution)/shard_map/while/body/eval_jaxpr/all_to_all | solution.py:36
  727.9 4.1 all-to-all-start.1
  732.0 6.9 all-to-all-done.1
  747.4 9.9 %collective-permute-done = f32[4,12,16,128]{3,2,1,0:T(8,128)S(1)} collective-permute-done((f32[4,12,16,128]{3,2,1,0:T(8,128)S(1)}, f32[4,12,16,128]{3,2,1,0:T(8,128)S(1)}, u32[]{:S(2)}, u32[]{:S(2)}) %collective-permute-start) | collective-permute-done | bytes 393248 | tf_op jit(solution)/shard_map/while/body/eval_jaxpr/ppermute | solution.py:58
  781.8 14.9 %all_to_all.71 = f32[32,1,2]{2,1,0:T(1,128)S(1)} all-to-all(f32[32,1,2]{2,1,0:T(1,128)S(1)} %broadcast_in_dim.318), channel_id=1, replica_groups=mesh['tm'=8,'gx'=8,'gy'=4] {'gx','gy'}, dimensions={0} | all-to-all | bytes 512 | tf_op jit(solution)/shard_map/while/body/eval_jaxpr/all_to_all | solution.py:36
  805.6 4.1 all-to-all-start.1
  809.8 6.9 all-to-all-done.1
  (506 shorter events, 382.7 us)
Async XLA Ops:
  0.9 13.0 %collective-permute-start.5 = (s32[5,16,128]{2,1,0:T(8,128)S(1)}, s32[5,16,128]{2,1,0:T(8,128)S(1)}, u32[]{:S(2)}, u32[]{:S(2)}) collective-permute-start(s32[5,16,128]{2,1,0:T(8,128)S(1)} %get-tuple-element.552), channel_id=1, source_target_pairs={{0,4},{4,8},{8,12},{12,16},{16,20},{20,24},{24,28},{1,5},{5,9},{9,... | collective-permute-start | bytes 122888 | tf_op jit(solution)/shard_map/ppermute | solution.py:26
  4.6 9.3 %collective-permute-start.6 = (s32[5,16,128]{2,1,0:T(8,128)S(1)}, s32[5,16,128]{2,1,0:T(8,128)S(1)}, u32[]{:S(2)}, u32[]{:S(2)}) collective-permute-start(s32[5,16,128]{2,1,0:T(8,128)S(1)} %get-tuple-element.551), channel_id=1, source_target_pairs={{4,0},{8,4},{12,8},{16,12},{20,16},{24,20},{28,24},{5,1},{9,5},{13... | collective-permute-start | bytes 122888 | tf_op jit(solution)/shard_map/ppermute | solution.py:29
  35.7 7.0 collective-permute-start.13
  40.8 5.6 collective-permute-start.14
  87.1 11.4 %all-to-all-start.5 = ((f32[32,1,2]{2,1,0:T(1,128)}), f32[32,1,2]{2,1,0:T(1,128)S(1)}, u32[]{:S(2)}, u32[]{:S(2)}) async-start(f32[32,1,2]{2,1,0:T(1,128)} %broadcast_in_dim.243), calls=%async_computation.5 | async-start | bytes 32768 | tf_op jit(solution)/shard_map/all_to_all | solution.py:36
  112.4 11.2 %all-to-all-start.6 = ((f32[32,1,2]{2,1,0:T(1,128)}), f32[32,1,2]{2,1,0:T(1,128)S(1)}, u32[]{:S(2)}, u32[]{:S(2)}) async-start(f32[32,1,2]{2,1,0:T(1,128)} %broadcast_in_dim.244), calls=%async_computation.6 | async-start | bytes 32768 | tf_op jit(solution)/shard_map/all_to_all | solution.py:36
  130.2 9.9 %collective-permute-start.10 = (f32[2,4,16,128]{3,2,1,0:T(8,128)S(1)}, f32[2,4,16,128]{3,2,1,0:T(8,128)S(1)}, u32[]{:S(2)}, u32[]{:S(2)}) collective-permute-start(f32[2,4,16,128]{3,2,1,0:T(8,128)S(1)} %get-tuple-element.544), channel_id=1, source_target_pairs={{4,0},{8,4},{12,8},{16,12},{20,16},{24,20},{28,24},{5,1},{9,5},{13... | collective-permute-start | bytes 196616 | tf_op jit(solution)/shard_map/ppermute | solution.py:29
  132.8 7.4 collective-permute-start.9
  135.8 7.9 collective-permute-start.17
  137.7 6.0 collective-permute-start.18
  140.2 8.9 %collective-permute-start.11 = (f32[2,20,4,128]{3,2,1,0:T(4,128)S(1)}, f32[2,20,4,128]{3,2,1,0:T(4,128)S(1)}, u32[]{:S(2)}, u32[]{:S(2)}) collective-permute-start(f32[2,20,4,128]{3,2,1,0:T(4,128)S(1)} %get-tuple-element.392), channel_id=1, source_target_pairs={{0,1},{1,2},{2,3},{4,5},{5,6},{6,7},{8,9},{9,10},{10,11},{12,13},{... | collective-permute-start | bytes 245768 | tf_op jit(solution)/shard_map/ppermute | solution.py:26
  142.4 6.7 collective-permute-start.12
  143.8 12.1 %collective-permute-start.19 = (f32[2,20,4,128]{3,2,1,0:T(4,128)S(1)}, f32[2,20,4,128]{3,2,1,0:T(4,128)S(1)}, u32[]{:S(2)}, u32[]{:S(2)}) collective-permute-start(f32[2,20,4,128]{3,2,1,0:T(4,128)S(1)} %get-tuple-element.390), channel_id=1, source_target_pairs={{0,1},{1,2},{2,3},{4,5},{5,6},{6,7},{8,9},{9,10},{10,11},{12,13},{... | collective-permute-start | bytes 245768 | tf_op jit(solution)/shard_map/ppermute | solution.py:26
  147.8 8.1 collective-permute-start.20
  170.2 20.0 %all-to-all-start.2 = ((f32[32,1,2]{2,1,0:T(1,128)}), f32[32,1,2]{2,1,0:T(1,128)S(1)}, u32[]{:S(2)}, u32[]{:S(2)}) async-start(f32[32,1,2]{2,1,0:T(1,128)} %broadcast_in_dim.239), calls=%async_computation.2 | async-start | bytes 32768 | tf_op jit(solution)/shard_map/all_to_all | solution.py:36
  190.8 12.2 %all-to-all-start.7 = ((f32[32,1,2]{2,1,0:T(1,128)}), f32[32,1,2]{2,1,0:T(1,128)S(1)}, u32[]{:S(2)}, u32[]{:S(2)}) async-start(f32[32,1,2]{2,1,0:T(1,128)} %broadcast_in_dim.246), calls=%async_computation.7 | async-start | bytes 32768 | tf_op jit(solution)/shard_map/all_to_all | solution.py:36
  212.4 11.1 %all-to-all-start.8 = ((f32[32,1,2]{2,1,0:T(1,128)}), f32[32,1,2]{2,1,0:T(1,128)S(1)}, u32[]{:S(2)}, u32[]{:S(2)}) async-start(f32[32,1,2]{2,1,0:T(1,128)} %broadcast_in_dim.247), calls=%async_computation.8 | async-start | bytes 32768 | tf_op jit(solution)/shard_map/all_to_all | solution.py:36
  242.8 11.2 %all-to-all-start.3 = ((f32[32,1,2]{2,1,0:T(1,128)}), f32[32,1,2]{2,1,0:T(1,128)S(1)}, u32[]{:S(2)}, u32[]{:S(2)}) async-start(f32[32,1,2]{2,1,0:T(1,128)} %broadcast_in_dim.240), calls=%async_computation.3 | async-start | bytes 32768 | tf_op jit(solution)/shard_map/all_to_all | solution.py:36
  259.8 11.2 %all-to-all-start.9 = ((f32[32,1,2]{2,1,0:T(1,128)}), f32[32,1,2]{2,1,0:T(1,128)S(1)}, u32[]{:S(2)}, u32[]{:S(2)}) async-start(f32[32,1,2]{2,1,0:T(1,128)} %broadcast_in_dim.248), calls=%async_computation.9 | async-start | bytes 32768 | tf_op jit(solution)/shard_map/all_to_all | solution.py:36
  277.7 13.1 %collective-permute-start = (f32[4,12,16,128]{3,2,1,0:T(8,128)S(1)}, f32[4,12,16,128]{3,2,1,0:T(8,128)S(1)}, u32[]{:S(2)}, u32[]{:S(2)}) collective-permute-start(f32[4,12,16,128]{3,2,1,0:T(8,128)S(1)} %get-tuple-element.834), channel_id=1, source_target_pairs={{0,32},{32,64},{64,96},{96,128},{128,160},{160,192},{192,224},{1,3... | collective-permute-start | bytes 1179656 | tf_op jit(solution)/shard_map/while/body/eval_jaxpr/ppermute | solution.py:58
  291.7 5.6 collective-permute-start.1
  298.6 6.1 collective-permute-start.3
  299.9 5.7 collective-permute-start.4
  339.2 11.1 %all-to-all-start.1 = ((f32[32,1,2]{2,1,0:T(1,128)}), f32[32,1,2]{2,1,0:T(1,128)S(1)}, u32[]{:S(2)}, u32[]{:S(2)}) async-start(f32[32,1,2]{2,1,0:T(1,128)} %broadcast_in_dim.319), calls=%async_computation.1 | async-start | bytes 32768 | tf_op jit(solution)/shard_map/while/body/eval_jaxpr/all_to_all | solution.py:36
  355.5 13.1 %collective-permute-start = (f32[4,12,16,128]{3,2,1,0:T(8,128)S(1)}, f32[4,12,16,128]{3,2,1,0:T(8,128)S(1)}, u32[]{:S(2)}, u32[]{:S(2)}) collective-permute-start(f32[4,12,16,128]{3,2,1,0:T(8,128)S(1)} %get-tuple-element.834), channel_id=1, source_target_pairs={{0,32},{32,64},{64,96},{96,128},{128,160},{160,192},{192,224},{1,3... | collective-permute-start | bytes 1179656 | tf_op jit(solution)/shard_map/while/body/eval_jaxpr/ppermute | solution.py:58
  376.3 6.1 collective-permute-start.3
  377.6 5.7 collective-permute-start.4
  416.9 11.1 %all-to-all-start.1 = ((f32[32,1,2]{2,1,0:T(1,128)}), f32[32,1,2]{2,1,0:T(1,128)S(1)}, u32[]{:S(2)}, u32[]{:S(2)}) async-start(f32[32,1,2]{2,1,0:T(1,128)} %broadcast_in_dim.319), calls=%async_computation.1 | async-start | bytes 32768 | tf_op jit(solution)/shard_map/while/body/eval_jaxpr/all_to_all | solution.py:36
  433.2 13.1 %collective-permute-start = (f32[4,12,16,128]{3,2,1,0:T(8,128)S(1)}, f32[4,12,16,128]{3,2,1,0:T(8,128)S(1)}, u32[]{:S(2)}, u32[]{:S(2)}) collective-permute-start(f32[4,12,16,128]{3,2,1,0:T(8,128)S(1)} %get-tuple-element.834), channel_id=1, source_target_pairs={{0,32},{32,64},{64,96},{96,128},{128,160},{160,192},{192,224},{1,3... | collective-permute-start | bytes 1179656 | tf_op jit(solution)/shard_map/while/body/eval_jaxpr/ppermute | solution.py:58
  454.1 6.1 collective-permute-start.3
  455.4 5.7 collective-permute-start.4
  494.7 11.1 %all-to-all-start.1 = ((f32[32,1,2]{2,1,0:T(1,128)}), f32[32,1,2]{2,1,0:T(1,128)S(1)}, u32[]{:S(2)}, u32[]{:S(2)}) async-start(f32[32,1,2]{2,1,0:T(1,128)} %broadcast_in_dim.319), calls=%async_computation.1 | async-start | bytes 32768 | tf_op jit(solution)/shard_map/while/body/eval_jaxpr/all_to_all | solution.py:36
  511.0 13.1 %collective-permute-start = (f32[4,12,16,128]{3,2,1,0:T(8,128)S(1)}, f32[4,12,16,128]{3,2,1,0:T(8,128)S(1)}, u32[]{:S(2)}, u32[]{:S(2)}) collective-permute-start(f32[4,12,16,128]{3,2,1,0:T(8,128)S(1)} %get-tuple-element.834), channel_id=1, source_target_pairs={{0,32},{32,64},{64,96},{96,128},{128,160},{160,192},{192,224},{1,3... | collective-permute-start | bytes 1179656 | tf_op jit(solution)/shard_map/while/body/eval_jaxpr/ppermute | solution.py:58
  531.8 6.1 collective-permute-start.3
  533.1 5.7 collective-permute-start.4
  572.4 11.1 %all-to-all-start.1 = ((f32[32,1,2]{2,1,0:T(1,128)}), f32[32,1,2]{2,1,0:T(1,128)S(1)}, u32[]{:S(2)}, u32[]{:S(2)}) async-start(f32[32,1,2]{2,1,0:T(1,128)} %broadcast_in_dim.319), calls=%async_computation.1 | async-start | bytes 32768 | tf_op jit(solution)/shard_map/while/body/eval_jaxpr/all_to_all | solution.py:36
  588.7 13.1 %collective-permute-start = (f32[4,12,16,128]{3,2,1,0:T(8,128)S(1)}, f32[4,12,16,128]{3,2,1,0:T(8,128)S(1)}, u32[]{:S(2)}, u32[]{:S(2)}) collective-permute-start(f32[4,12,16,128]{3,2,1,0:T(8,128)S(1)} %get-tuple-element.834), channel_id=1, source_target_pairs={{0,32},{32,64},{64,96},{96,128},{128,160},{160,192},{192,224},{1,3... | collective-permute-start | bytes 1179656 | tf_op jit(solution)/shard_map/while/body/eval_jaxpr/ppermute | solution.py:58
  609.6 6.1 collective-permute-start.3
  610.9 5.7 collective-permute-start.4
  650.1 11.1 %all-to-all-start.1 = ((f32[32,1,2]{2,1,0:T(1,128)}), f32[32,1,2]{2,1,0:T(1,128)S(1)}, u32[]{:S(2)}, u32[]{:S(2)}) async-start(f32[32,1,2]{2,1,0:T(1,128)} %broadcast_in_dim.319), calls=%async_computation.1 | async-start | bytes 32768 | tf_op jit(solution)/shard_map/while/body/eval_jaxpr/all_to_all | solution.py:36
  666.5 13.1 %collective-permute-start = (f32[4,12,16,128]{3,2,1,0:T(8,128)S(1)}, f32[4,12,16,128]{3,2,1,0:T(8,128)S(1)}, u32[]{:S(2)}, u32[]{:S(2)}) collective-permute-start(f32[4,12,16,128]{3,2,1,0:T(8,128)S(1)} %get-tuple-element.834), channel_id=1, source_target_pairs={{0,32},{32,64},{64,96},{96,128},{128,160},{160,192},{192,224},{1,3... | collective-permute-start | bytes 1179656 | tf_op jit(solution)/shard_map/while/body/eval_jaxpr/ppermute | solution.py:58
  687.3 6.1 collective-permute-start.3
  688.6 5.7 collective-permute-start.4
  727.9 11.1 %all-to-all-start.1 = ((f32[32,1,2]{2,1,0:T(1,128)}), f32[32,1,2]{2,1,0:T(1,128)S(1)}, u32[]{:S(2)}, u32[]{:S(2)}) async-start(f32[32,1,2]{2,1,0:T(1,128)} %broadcast_in_dim.319), calls=%async_computation.1 | async-start | bytes 32768 | tf_op jit(solution)/shard_map/while/body/eval_jaxpr/all_to_all | solution.py:36
  744.2 13.1 %collective-permute-start = (f32[4,12,16,128]{3,2,1,0:T(8,128)S(1)}, f32[4,12,16,128]{3,2,1,0:T(8,128)S(1)}, u32[]{:S(2)}, u32[]{:S(2)}) collective-permute-start(f32[4,12,16,128]{3,2,1,0:T(8,128)S(1)} %get-tuple-element.834), channel_id=1, source_target_pairs={{0,32},{32,64},{64,96},{96,128},{128,160},{160,192},{192,224},{1,3... | collective-permute-start | bytes 1179656 | tf_op jit(solution)/shard_map/while/body/eval_jaxpr/ppermute | solution.py:58
  765.1 6.1 collective-permute-start.3
  766.4 5.7 collective-permute-start.4
  805.6 11.1 %all-to-all-start.1 = ((f32[32,1,2]{2,1,0:T(1,128)}), f32[32,1,2]{2,1,0:T(1,128)S(1)}, u32[]{:S(2)}, u32[]{:S(2)}) async-start(f32[32,1,2]{2,1,0:T(1,128)} %broadcast_in_dim.319), calls=%async_computation.1 | async-start | bytes 32768 | tf_op jit(solution)/shard_map/while/body/eval_jaxpr/all_to_all | solution.py:36
  (50 other events, 247.2 us)
where the time goes:
time: 836 us; the launch traced here: 823 us
  other arithmetic  212 us (25%)
  starting transfers between devices  199 us (24%)
  waiting for transfers between devices  187 us (22%)
  blocking collectives  117 us (14%)
  loops' own time  45.6 us (5%)
  local copies, waits for them, and re-layouts  35.5 us (4%)
  between operations  27.7 us (3%)
    all_to_all x8, blocking collectives, sent_to_all(): lax.all_to_all(jnp.broadcast_to(shard[None], (length, *shard.shape)), axi...  117 us
    all_to_all x14, waiting for transfers between devices, sent_to_all(): lax.all_to_all(jnp.broadcast_to(shard[None], (length, *shard.shape)), axi...  91.4 us
    slice x32, other arithmetic, stencil_apply(): padded[near_one:near_one + extent_one, near_two:near_two + extent_two, ne...  73.5 us
    ppermute x22, starting transfers between devices, padded_2(): lax.ppermute(lax.slice_in_dim(block, block.shape[dim] - width, None, axis...  69.1 us
    ppermute x7, waiting for transfers between devices, from_behind(): lax.ppermute(value, axis, [(source, source + steps) for source in range(i...  68.9 us
    all_to_all x14, starting transfers between devices, sent_to_all(): lax.all_to_all(jnp.broadcast_to(shard[None], (length, *shard.shape)), axi...  68.3 us
    ppermute x22, starting transfers between devices, padded_2(): lax.ppermute(lax.slice_in_dim(block, 0, width, axis=dim), axis, backward)  46.9 us
    another operation x1, loops' own time, on_device(): finished = lax.fori_loop(0, lax.axis_size('tm') - 1, next_turn, finished)  45.6 us
  transfers between devices with their start and end apart: 65, of which 39 were waited for; matrix products, arithmetic and copies ran while one was open for 3% of the time, Pallas kernels for 0%

commit v1 on v0

v1 whole, which is shorter than its diff:
```python
import functools

import jax
import jax.numpy as jnp
from jax import lax
from jax.experimental import pallas as pl
from jax.experimental.pallas import tpu as pltpu
from jax.sharding import PartitionSpec as P

PACES = 2
SHARP = 3
LOOSE = 2
PRONY = 3
L = 3
LINE = ("gx", "gy")
LIMIT = 48 << 20


def masks(ny, nz):
    row = lax.broadcasted_iota(jnp.int32, (ny, nz), 0)
    lane = lax.broadcasted_iota(jnp.int32, (ny, nz), 1)
    return row == 0, row == ny - 1, lane == 0, lane == nz - 1


class Shifts:
    def __init__(self, ny, nz):
        self.ny, self.nz = ny, nz
        self.row_first, self.row_last, self.lane_first, self.lane_last = masks(ny, nz)

    def zup(self, v):
        return jnp.where(self.lane_last, 0.0, pltpu.roll(v, self.nz - 1, 1))

    def zdn(self, v):
        return jnp.where(self.lane_first, 0.0, pltpu.roll(v, 1, 1))

    def yup(self, v):
        return jnp.where(self.row_last, 0.0, pltpu.roll(v, self.ny - 1, 0))

    def ydn(self, v):
        return jnp.where(self.row_first, 0.0, pltpu.roll(v, 1, 0))


def off_diagonal(sh, v, k, low, high, put):
    def spread(plane):
        up = sh.zup(plane)
        side, side_up = sh.yup(plane), sh.yup(up)
        return plane, up, side, side_up, plane + up, side + side_up

    near = spread(v(low - 1))
    carry = None
    for e in range(low - 1, high + 1):
        far = spread(v(e + 1))
        a, a_up, b, b_up, a_sum, b_sum = near
        c, c_up, d, d_up, c_sum, d_sum = far
        one_up, two_up = b_up + c_up, a_up + d_up
        one, two = b + c, a + d
        kk = k(e)
        if e >= low:
            e00, f00 = kk * (d_sum + one_up), kk * (d_sum + one)
            e01, f01 = kk * (c_sum + two_up), kk * (c_sum + two)
            e10, e11, f10, f11 = carry
            put(e, (e00 + e10) + sh.ydn(e01 + e11) + sh.zdn((f00 + f10) + sh.ydn(f01 + f11)))
        if e < high:
            carry = (
                kk * (b_sum + two_up),
                kk * (a_sum + one_up),
                kk * (b_sum + two),
                kk * (a_sum + one),
            )
        near = far


def prony(dt, coef_ref, time_ref):
    decay = [jnp.exp(-dt / jnp.full((1, 128), time_ref[p], jnp.float32)) for p in range(PRONY)]
    rest = [1.0 - d for d in decay]
    f = [coef_ref[p] * decay[p] for p in range(PRONY)]
    return decay, rest, f, 1.0 / dt + (f[0] + f[1] + f[2])


def moments_out(values, red_ref):
    lane = lax.broadcasted_iota(jnp.int32, (1, 128), 1)
    packed = jnp.zeros((1, 128), jnp.float32)
    for at, field in enumerate(values):
        total = jnp.sum(jnp.sum(field, axis=0, keepdims=True), axis=1, keepdims=True)
        packed = jnp.where(lane == at, total, packed)
    red_ref[...] = jnp.broadcast_to(packed[None], red_ref.shape)


def moments_in(red_ref, first, count):
    total = jnp.sum(red_ref[...], axis=0)
    lane = lax.broadcasted_iota(jnp.int32, (1, 128), 1)
    return [
        jnp.broadcast_to(
            jnp.sum(jnp.where(lane == first + i, total, 0.0), axis=1, keepdims=True), (1, 128)
        )
        for i in range(count)
    ]


def galerkin(nu):
    m = len(nu) // 2
    mu = [nu[i] + nu[i + 1] for i in range(2 * m - 1)]
    rows = [[mu[i + j] for j in range(m)] + [nu[i]] for i in range(m)]
    for i in range(m):
        for r in range(i + 1, m):
            factor = rows[r][i] / rows[i][i]
            for j in range(i + 1, m + 1):
                rows[r][j] = rows[r][j] - factor * rows[i][j]
    c = [None] * m
    for i in reversed(range(m)):
        acc = rows[i][m]
        for j in range(i + 1, m):
            acc = acc - rows[i][j] * c[j]
        c[i] = acc / rows[i][i]
    return c


def start_kernel(
    rigid_ref, dilate_ref, heat_ref, coef_ref, time_ref,
    own_ref, lo_ref, hi_ref, lo2_ref, hi2_ref,
    kel_ref, theta_ref, inv_f_ref, inv_c_ref, state_ref,
    zf_ref, ozf_ref, oozf_ref, zc_ref, ozc_ref,
    lo1_out, hi1_out, lo2_out, hi2_out, red_ref,
    kal_ref, au_ref, w_ref,
):
    ny, nz = kel_ref.shape[1:]
    sh = Shifts(ny, nz)
    chunks = own_ref.shape[0]

    def raw(field, i):
        if i == -L - 1:
            parts = [lo2_ref[c, field, 0] for c in range(chunks)]
        elif i < 0:
            parts = [lo_ref[c, field, i + L] for c in range(chunks)]
        elif i < L:
            parts = [own_ref[c, field, i] for c in range(chunks)]
        elif i < 2 * L:
            parts = [hi_ref[c, field, i - L] for c in range(chunks)]
        else:
            parts = [hi2_ref[c, field, 0] for c in range(chunks)]
        return jnp.concatenate(parts, axis=0)

    for e in range(-4, 6):
        label = raw(0, e)
        stiff = jnp.zeros((ny, nz), jnp.float32)
        load = jnp.zeros((ny, nz), jnp.float32)
        for region in range(rigid_ref.shape[0]):
            here = label == (region + 1.0)
            stiff = jnp.where(here, rigid_ref[region], stiff)
            load = jnp.where(here, dilate_ref[region], load)
        kel_ref[e + 4] = stiff * (-1.0 / 12.0)
        kal_ref[e + 4] = 0.25 * (stiff * load)

    decay_f, rest_f, ff, shift_f = prony(1.0, coef_ref, time_ref)
    decay_c, rest_c, fc, shift_c = prony(1.0 * PACES, coef_ref, time_ref)

    for i in range(-3, 6):
        ksum = kel_ref[i + 3] + kel_ref[i + 4]
        ksum = ksum + sh.ydn(ksum)
        ksum = ksum + sh.zdn(ksum)
        diag = -4.0 * ksum
        asum = kal_ref[i + 3] + kal_ref[i + 4]
        asum = asum + sh.ydn(asum)
        theta_ref[i + 3] = sh.zdn(asum) - asum
        inside = raw(0, i) > 0.5
        inv_f_ref[i + 3] = jnp.where(inside, 1.0 / (diag + shift_f), 0.0)
        inv_c_ref[i + 3] = jnp.where(inside, 1.0 / (diag + shift_c), 0.0)

    for i in range(-4, 7):
        state_ref[i + 4] = raw(1, i)

    def u(i):
        return state_ref[i + 4]

    def k(e):
        return kel_ref[e + 4]

    def put_au(i, plane):
        au_ref[i + 3] = plane

    off_diagonal(sh, u, k, -3, 5, put_au)

    zeros = jnp.zeros((ny, nz), jnp.float32)
    acc = [zeros] * 10
    for i in range(-3, 6):
        h = [raw(2 + p, i) for p in range(PRONY)]
        fh = [ff[p] * h[p] for p in range(PRONY)]
        state_ref[11 + i + 3] = decay_f[0] * fh[0] + decay_f[1] * fh[1] + decay_f[2] * fh[2]
        ui = u(i)
        load = heat_ref[0, 0] * theta_ref[i + 3] + (fh[0] + fh[1] + fh[2])
        s = load + ui - au_ref[i + 3]
        z = inv_f_ref[i + 3] * s - ui
        zf_ref[i + 3] = z
        if 0 <= i < L:
            acc[0] = acc[0] + z * (s - ui * (1.0 / inv_f_ref[i + 3]))
        if -2 <= i < 5:
            load = heat_ref[0, 1] * theta_ref[i + 3]
            load = load + (fc[0] * h[0] + fc[1] * h[1] + fc[2] * h[2])
            s = load + ui * (1.0 / PACES) - au_ref[i + 3]
            z = inv_c_ref[i + 3] * s - ui
            w_ref[i + 2] = z
            if 0 <= i < L:
                zc_ref[i] = z
                acc[6] = acc[6] + z * (s - ui * (1.0 / inv_c_ref[i + 3]))

    def put_oz(i, plane):
        oz = inv_f_ref[i + 3] * plane
        ozf_ref[i + 2] = oz
        if 0 <= i < L:
            acc[1] = acc[1] + zf_ref[i + 3] * plane
            acc[2] = acc[2] + oz * plane

    off_diagonal(sh, lambda i: zf_ref[i + 3], k, -2, 4, put_oz)

    def put_ooz(i, plane):
        ooz = inv_f_ref[i + 3] * plane
        oozf_ref[i + 1] = ooz
        if 0 <= i < L:
            acc[3] = acc[3] + ozf_ref[i + 2] * plane
            acc[4] = acc[4] + ooz * plane

    off_diagonal(sh, lambda i: ozf_ref[i + 2], k, -1, 3, put_ooz)

    def put_last(i, plane):
        acc[5] = acc[5] + oozf_ref[i + 1] * plane

    off_diagonal(sh, lambda i: oozf_ref[i + 1], k, 0, 2, put_last)

    def put_ozc(i, plane):
        oz = inv_c_ref[i + 3] * plane
        au_ref[i + 3] = oz
        if 0 <= i < L:
            ozc_ref[i] = oz
            acc[7] = acc[7] + w_ref[i + 2] * plane
            acc[8] = acc[8] + oz * plane

    off_diagonal(sh, lambda i: w_ref[i + 2], k, -1, 3, put_ozc)

    def put_lastc(i, plane):
        acc[9] = acc[9] + au_ref[i + 3] * plane

    off_diagonal(sh, lambda i: au_ref[i + 3], k, 0, 2, put_lastc)

    moments_out(acc, red_ref)

    lo1_out[0], lo1_out[1], lo1_out[2] = ozf_ref[2 + 2], oozf_ref[1 + 1], oozf_ref[2 + 1]
    hi1_out[0], hi1_out[1], hi1_out[2] = ozf_ref[0 + 2], oozf_ref[0 + 1], oozf_ref[1 + 1]
    lo2_out[0], lo2_out[1], lo2_out[2] = zf_ref[0 + 3], ozf_ref[0 + 2], oozf_ref[0 + 1]
    hi2_out[0], hi2_out[1], hi2_out[2] = zf_ref[2 + 3], ozf_ref[2 + 2], oozf_ref[2 + 1]


def second_kernel(
    heat_ref, coef_ref, time_ref, place_ref,
    red_in, kel_ref, theta_ref, inv_f_ref, state_ref, own_ref,
    zf_ref, ozf_ref, oozf_ref, zc_ref, ozc_ref,
    lo1_ref, hi1_ref, lo2_ref, hi2_ref,
    base_ref, z_out, oz_out, ooz_out, red_ref,
    u_ref, z_ref, oz_ref, ooz_ref, au_ref,
):
    ny, nz = kel_ref.shape[1:]
    sh = Shifts(ny, nz)
    chunks = own_ref.shape[0]
    decay_f, rest_f, ff, shift_f = prony(1.0, coef_ref, time_ref)
    decay_c, rest_c, fc, shift_c = prony(1.0 * PACES, coef_ref, time_ref)
    c = galerkin(moments_in(red_in, 0, 6))
    b = galerkin(moments_in(red_in, 6, 4))

    def zf(i):
        return lo_hi(i, -3, 5, zf_ref, 3, None, None, 0)

    def lo_hi(i, low, high, ref, shift, near, off, far_at):
        if i == -4:
            return hi_lo2(True, far_at)
        if i == 6:
            return hi_lo2(False, far_at)
        if low <= i <= high:
            return ref[i + shift]
        return near[i][0][near[i][1]]

    def hi_lo2(low, at):
        return lo2_ref[at] if low else hi2_ref[at]

    near_oz = {-3: (lo1_ref, 0), 5: (hi1_ref, 0)}
    near_ooz = {-3: (lo1_ref, 1), -2: (lo1_ref, 2), 4: (hi1_ref, 1), 5: (hi1_ref, 2)}
    for i in range(-4, 7):
        z = zf(i)
        oz = lo_hi(i, -2, 4, ozf_ref, 2, near_oz, None, 1)
        ooz = lo_hi(i, -1, 3, oozf_ref, 1, near_ooz, None, 2)
        u_ref[i + 4] = state_ref[i + 4] + c[0] * z + c[1] * oz + c[2] * ooz

    def k(e):
        return kel_ref[e + 4]

    def put_au(i, plane):
        au_ref[i + 3] = plane

    off_diagonal(sh, lambda i: u_ref[i + 4], k, -3, 5, put_au)

    grow = ff[0] * rest_f[0] + ff[1] * rest_f[1] + ff[2] * rest_f[2]
    zeros = jnp.zeros((ny, nz), jnp.float32)
    acc = [zeros] * 6
    weight = jnp.where(place_ref[0] == 0, 0.0, 1.0)
    for i in range(-3, 6):
        ui = u_ref[i + 4]
        s = heat_ref[0, 1] * theta_ref[i + 3] + state_ref[11 + i + 3] + (grow + 1.0) * ui
        s = s - au_ref[i + 3]
        z = inv_f_ref[i + 3] * s - ui
        z_ref[i + 3] = z
        if 0 <= i < L:
            z_out[i] = z
            acc[0] = acc[0] + z * (s - ui * (1.0 / inv_f_ref[i + 3]))

    for i in range(L):
        u1 = u_ref[i + 4]
        g = state_ref[i + 4] + b[0] * zc_ref[i] + b[1] * ozc_ref[i]
        base_ref[i] = u1 - weight * g
        for p in range(PRONY):
            h = jnp.concatenate([own_ref[q, 2 + p, i] for q in range(chunks)], axis=0)
            h1 = decay_f[p] * h + rest_f[p] * u1
            gh = decay_c[p] * h + rest_c[p] * g
            base_ref[L * (1 + p) + i] = decay_f[p] * h1 + rest_f[p] * u1 - weight * gh

    def put_oz(i, plane):
        oz = inv_f_ref[i + 3] * plane
        oz_ref[i + 2] = oz
        if 0 <= i < L:
            oz_out[i] = oz
            acc[1] = acc[1] + z_ref[i + 3] * plane
            acc[2] = acc[2] + oz * plane

    off_diagonal(sh, lambda i: z_ref[i + 3], k, -2, 4, put_oz)

    def put_ooz(i, plane):
        ooz = inv_f_ref[i + 3] * plane
        ooz_ref[i + 1] = ooz
        if 0 <= i < L:
            ooz_out[i] = ooz
            acc[3] = acc[3] + oz_ref[i + 2] * plane
            acc[4] = acc[4] + ooz * plane

    off_diagonal(sh, lambda i: oz_ref[i + 2], k, -1, 3, put_ooz)

    def put_last(i, plane):
        acc[5] = acc[5] + ooz_ref[i + 1] * plane

    off_diagonal(sh, lambda i: ooz_ref[i + 1], k, 0, 2, put_last)
    moments_out(acc, red_ref)


def block_kernel(coef_ref, time_ref, red_in, base_ref, z_ref, oz_ref, ooz_ref, blk_ref):
    decay_f, rest_f, ff, shift_f = prony(1.0, coef_ref, time_ref)
    c = galerkin(moments_in(red_in, 0, 6))
    for i in range(L):
        delta = c[0] * z_ref[i] + c[1] * oz_ref[i] + c[2] * ooz_ref[i]
        blk_ref[i] = base_ref[i] + delta
        for p in range(PRONY):
            blk_ref[L * (1 + p) + i] = base_ref[L * (1 + p) + i] + rest_f[p] * delta


def opening_kernel(coef_ref, time_ref, blk_ref, lo_out, hi_out):
    decay, rest, f, shift = prony(1.0 * PACES, coef_ref, time_ref)

    def total(i):
        return f[0] * blk_ref[L + i] + f[1] * blk_ref[2 * L + i] + f[2] * blk_ref[3 * L + i]

    for i in range(L):
        lo_out[i] = blk_ref[i]
        hi_out[i] = blk_ref[i]
    sums = [total(i) for i in range(L)]
    lo_out[3], lo_out[4] = sums[0], sums[1]
    hi_out[3], hi_out[4] = sums[1], sums[2]


def chain_kernel(turn, count, opened, *refs):
    refs = list(refs)
    heat_ref, coef_ref, time_ref, place_ref = refs[:4]
    refs = refs[4:]
    if opened:
        base_in, lo_ref, hi_ref = refs[:3]
        refs = refs[3:]
    else:
        red_in, base_in, z_in, oz_in, lo_ref, hi_ref = refs[:6]
        refs = refs[6:]
    kel_ref, theta_ref, inv_ref, blk_ref = refs[:4]
    base_ref, z_ref, oz_ref, lo_out, hi_out, red_ref, u_ref, au_ref = refs[4:]
    ny, nz = kel_ref.shape[1:]
    sh = Shifts(ny, nz)
    decay, rest, f, shift = prony(1.0 * PACES, coef_ref, time_ref)
    grow = f[0] * rest[0] + f[1] * rest[1] + f[2] * rest[2]
    step = lax.rem(place_ref[0] + turn, count)
    heat = heat_ref[step, PACES - 1]
    opening = step == 0
    fresh = step == 1

    if not opened:
        c = galerkin(moments_in(red_in, 0, 4))

    def delta(i):
        if i == -3:
            z, oz = lo_ref[5], lo_ref[6]
        elif i == 5:
            z, oz = hi_ref[5], hi_ref[6]
        else:
            z = z_in[i + 2]
            oz = oz_in[i + 1] if -1 <= i <= 3 else (lo_ref[7] if i == -2 else hi_ref[7])
        return jnp.where(fresh, 0.0, c[0] * z + c[1] * oz)

    for i in range(-3, 6):
        base = lo_ref[i + 3] if i < 0 else hi_ref[i - L] if i >= L else base_in[i]
        if opened:
            u_ref[i + 3] = base
            d = None
        else:
            d = delta(i)
            u_ref[i + 3] = base + d
        if 0 <= i < L:
            h = [base_in[L * (1 + p) + i] for p in range(PRONY)]
            if d is not None:
                h = [h[p] + rest[p] * d for p in range(PRONY)]
            total = f[0] * h[0] + f[1] * h[1] + f[2] * h[2]
            ui = u_ref[i + 3]
            base_ref[i] = jnp.where(opening, 0.0, ui) + blk_ref[i]
            for p in range(PRONY):
                ahead = jnp.where(opening, 0.0, decay[p] * h[p] + rest[p] * ui)
                base_ref[L * (1 + p) + i] = ahead + blk_ref[L * (1 + p) + i]
        elif -2 <= i < 5:
            total = lo_ref[3 + i + 2] if i < 0 else hi_ref[3 + i - L]
            if d is not None:
                total = total + grow * d
        if -2 <= i < 5:
            au_ref[i + 2] = heat * theta_ref[i + 3] + total

    zeros = jnp.zeros((ny, nz), jnp.float32)
    acc = [zeros] * 4

    def k(e):
        return kel_ref[e + 4]

    def put_z(i, plane):
        ui = u_ref[i + 3]
        s = au_ref[i + 2] + ui * (1.0 / PACES) - plane
        inv = inv_ref[i + 3]
        z = inv * s - ui
        z_ref[i + 2] = z
        if 0 <= i < L:
            acc[0] = acc[0] + z * (s - ui * (1.0 / inv))

    off_diagonal(sh, lambda i: u_ref[i + 3], k, -2, 4, put_z)

    def put_oz(i, plane):
        oz = inv_ref[i + 3] * plane
        oz_ref[i + 1] = oz
        if 0 <= i < L:
            acc[1] = acc[1] + z_ref[i + 2] * plane
            acc[2] = acc[2] + oz * plane

    off_diagonal(sh, lambda i: z_ref[i + 2], k, -1, 3, put_oz)

    def put_last(i, plane):
        acc[3] = acc[3] + oz_ref[i + 1] * plane

    off_diagonal(sh, lambda i: oz_ref[i + 1], k, 0, 2, put_last)
    moments_out(acc, red_ref)

    def total(i):
        return f[0] * base_ref[L + i] + f[1] * base_ref[2 * L + i] + f[2] * base_ref[3 * L + i]

    sums = [total(i) for i in range(L)]
    for i in range(L):
        lo_out[i] = base_ref[i]
        hi_out[i] = base_ref[i]
    lo_out[3], lo_out[4] = sums[0], sums[1]
    hi_out[3], hi_out[4] = sums[1], sums[2]
    lo_out[5], lo_out[6], lo_out[7] = z_ref[2 + 2], oz_ref[2 + 1], oz_ref[1 + 1]
    hi_out[5], hi_out[6], hi_out[7] = z_ref[0 + 2], oz_ref[0 + 1], oz_ref[1 + 1]


def closing_kernel(coef_ref, time_ref, place_ref, red_in, base_ref, z_ref, oz_ref, out_ref):
    decay, rest, f, shift = prony(1.0 * PACES, coef_ref, time_ref)
    c = galerkin(moments_in(red_in, 0, 4))
    first = place_ref[0] == 0
    chunks, _, _, rows, _ = out_ref.shape
    for i in range(L):
        delta = jnp.where(first, 0.0, c[0] * z_ref[i + 2] + c[1] * oz_ref[i + 1])
        fields = [base_ref[i] + delta]
        for p in range(PRONY):
            fields.append(base_ref[L * (1 + p) + i] + rest[p] * delta)
        for at, field in enumerate(fields):
            for q in range(chunks):
                out_ref[q, at, i] = field[q * rows : (q + 1) * rows]


SMEM = pl.BlockSpec(memory_space=pltpu.SMEM)
VMEM = pl.BlockSpec(memory_space=pltpu.VMEM)


def call(kernel, name, small, large, outs, scratch=()):
    f32 = jnp.float32
    return pl.pallas_call(
        kernel,
        name=name,
        out_shape=[jax.ShapeDtypeStruct(s, f32) for s in outs],
        in_specs=[SMEM] * len(small) + [VMEM] * len(large),
        out_specs=[VMEM] * len(outs),
        scratch_shapes=[pltpu.VMEM(s, f32) for s in scratch],
        compiler_params=pltpu.CompilerParams(vmem_limit_bytes=LIMIT),
    )(*small, *large)


def on_device(
    segment_opening_values,
    cell_material_label,
    material_rigidity,
    dilation_mismatch,
    heat_swings_array,
    prony_coefficients,
    prony_decay_times,
):
    n_tm, n_gy = lax.axis_size("tm"), lax.axis_size("gy")
    line = lax.axis_size("gx") * n_gy
    nx, ny_part, nz = cell_material_label.shape
    ny = ny_part * n_gy
    assert nx == L * n_gy
    plane = (ny, nz)

    def up(value, by):
        return lax.ppermute(value, LINE, [(s, s + by) for s in range(line - by)])

    def down(value, by):
        return lax.ppermute(value, LINE, [(s + by, s) for s in range(line - by)])

    def exchanged(red):
        return lax.all_to_all(red, LINE, 0, 0, tiled=True)

    def ring(block):
        return lax.ppermute(block, "tm", [(s, (s - 1) % n_tm) for s in range(n_tm)])

    place = lax.axis_index("tm").astype(jnp.int32)[None]
    heats = lax.all_gather(heat_swings_array[0], "tm")
    prony_args = (prony_coefficients, prony_decay_times)

    label = cell_material_label.astype(jnp.float32)[None] + 1.0
    raw = jnp.concatenate([label, segment_opening_values[0]], axis=0)
    raw = raw.reshape(2 + PRONY, n_gy, L, ny_part, nz).transpose(1, 0, 2, 3, 4)
    own = lax.all_to_all(raw, "gy", 0, 0, tiled=True)
    lo, hi = up(own, 1), down(own, 1)
    lo2, hi2 = up(own[:, :2, L - 1 :], 2), down(own[:, :2, :1], 2)

    red_shape = (line, 1, 128)
    (kel, theta, inv_f, inv_c, state, zf, ozf, oozf, zc, ozc, lo1, hi1, lo2, hi2, red) = call(
        start_kernel,
        "start",
        (material_rigidity, dilation_mismatch, heat_swings_array, *prony_args),
        (own, lo, hi, lo2, hi2),
        [
            (10, *plane), (9, *plane), (9, *plane), (9, *plane), (20, *plane),
            (9, *plane), (7, *plane), (5, *plane), (L, *plane), (L, *plane),
            (3, *plane), (3, *plane), (3, *plane), (3, *plane), red_shape,
        ],
        [(10, *plane), (9, *plane), (7, *plane)],
    )
    red = exchanged(red)
    hi1, lo1 = down(lo1, 1), up(hi1, 1)
    hi2, lo2 = down(lo2, 2), up(hi2, 2)
    base, z, oz, ooz, red = call(
        second_kernel,
        "second",
        (heat_swings_array, *prony_args, place),
        (red, kel, theta, inv_f, state, own, zf, ozf, oozf, zc, ozc, lo1, hi1, lo2, hi2),
        [(4 * L, *plane), (L, *plane), (L, *plane), (L, *plane), red_shape],
        [(11, *plane), (9, *plane), (7, *plane), (5, *plane), (9, *plane)],
    )
    red = exchanged(red)
    (block,) = call(
        block_kernel, "block", prony_args, (red, base, z, oz, ooz), [(4 * L, *plane)]
    )
    mine = block
    block = ring(block)
    lo, hi = call(opening_kernel, "opening", prony_args, (block,), [(5, *plane)] * 2)
    hi, lo = down(lo, 1), up(hi, 1)
    base = block
    red = z = oz = None
    for turn in range(2, n_tm + 1):
        block = ring(block) if turn < n_tm else mine
        opened = turn == 2
        past = (base, lo, hi) if opened else (red, base, z, oz, lo, hi)
        base, z, oz, lo, hi, red = call(
            functools.partial(chain_kernel, turn, n_tm, opened),
            f"chain{turn}",
            (heats, *prony_args, place),
            (*past, kel, theta, inv_c, block),
            [(4 * L, *plane), (7, *plane), (5, *plane), (8, *plane), (8, *plane), red_shape],
            [(9, *plane), (7, *plane)],
        )
        red = exchanged(red)
        if turn < n_tm:
            hi, lo = down(lo, 1), up(hi, 1)
    (out,) = call(
        closing_kernel,
        "closing",
        (*prony_args, place),
        (red, base, z, oz),
        [(n_gy, 1 + PRONY, L, ny_part, nz)],
    )
    out = lax.all_to_all(out, "gy", 0, 0, tiled=True)
    return out.transpose(1, 0, 2, 3, 4).reshape(1, 1 + PRONY, nx, ny_part, nz)


def solution(mesh):
    placed = (
        P("tm", None, "gx", "gy", None),
        P("gx", "gy", None),
        P(),
        P(),
        P("tm", None),
        P(),
        P(),
    )
    return jax.shard_map(
        on_device,
        mesh=mesh,
        in_specs=placed,
        out_specs=P("tm", None, "gx", "gy", None),
        check_vma=False,
    )
```

time: 836 us -> 291 us (0.35)
  the two profiles are of different devices: /device:TPU:129 before, /device:TPU:1 now
where the time goes in v1:
time: 291 us; the launch traced here: 290 us
  blocking collectives  120 us (41%)
  starting transfers between devices  109 us (37%)
  waiting for transfers between devices  32.8 us (11%)
  Pallas kernels  24.5 us (8%)
    all_to_all x8, blocking collectives, exchanged(): return lax.all_to_all(red, LINE, 0, 0, tiled=True)  88.3 us
    ppermute x11, starting transfers between devices, down(): return lax.ppermute(value, LINE, [(s + by, s) for s in range(line - by)])  51.8 us
    ppermute x11, starting transfers between devices, up(): return lax.ppermute(value, LINE, [(s, s + by) for s in range(line - by)])  29.7 us
    pallas_call x12, Pallas kernels, call(): pl.pallas_call(kernel, name=name, out_shape=[jax.ShapeDtypeStruct(s, f32)...  24.5 us
    ppermute x7, waiting for transfers between devices, ring(): return lax.ppermute(block, 'tm', [(s, (s - 1) % n_tm) for s in range(n_tm)])  20.7 us
    ppermute x7, starting transfers between devices, ring(): return lax.ppermute(block, 'tm', [(s, (s - 1) % n_tm) for s in range(n_tm)])  19.4 us
    all_to_all x1, blocking collectives, on_device(): own = lax.all_to_all(raw, 'gy', 0, 0, tiled=True)  12.8 us
    all_gather x1, blocking collectives, on_device(): heats = lax.all_gather(heat_swings_array[0], 'tm')  9.71 us
  transfers between devices with their start and end apart: 30, of which 6 were waited for; matrix products, arithmetic and copies ran while one was open for 0% of the time, Pallas kernels for 4%

profile of v1, /device:TPU:1, one launch (start us, length us, event | category | flops | bytes accessed | tf_op | source)
XLA Modules:
  0.0 290.2 jit_solution(15599977836385264777)
XLA Ops:
  1.9 12.8 %all_to_all.55.own_ref = f32[4,5,3,16,128]{4,3,2,1,0:T(8,128)S(1)} all-to-all(f32[4,5,3,16,128]{4,3,2,1,0:T(8,128)S(1)} %maximum_bitcast_fusion), channel_id=1, replica_groups=mesh['tm'=8,'gx'=8,'gy'=4] {'gy'}, dimensions={0} | all-to-all | bytes 983040 | tf_op jit(solution)/shard_map/all_to_all | solution.py:545
  14.8 2.2 collective-permute-start
  17.0 4.6 %collective-permute-start.1 = (f32[4,5,3,16,128]{4,3,2,1,0:T(8,128)S(1)}, f32[4,5,3,16,128]{4,3,2,1,0:T(8,128)S(1)}, u32[]{:S(2)}, u32[]{:S(2)}) collective-permute-start(f32[4,5,3,16,128]{4,3,2,1,0:T(8,128)S(1)} %all_to_all.55.own_ref), channel_id=1, source_target_pairs={{1,0},{2,1},{3,2},{4,3},{5,4},{6,5},{7,6},{8,7},{9,8},{10,9},{11,1... | collective-permute-start | bytes 1474568 | tf_op jit(solution)/shard_map/ppermute | solution.py:530
  21.6 2.1 collective-permute-start.2
  23.7 5.1 %collective-permute-start.3 = (f32[4,2,1,16,128]{4,3,2,1,0:T(8,128)S(1)}, f32[4,2,1,16,128]{4,3,2,1,0:T(8,128)S(1)}, u32[]{:S(2)}, u32[]{:S(2)}) collective-permute-start(f32[4,2,1,16,128]{4,3,2,1,0:T(8,128)S(1)} %get-tuple-element.129), channel_id=1, source_target_pairs={{2,0},{3,1},{4,2},{5,3},{6,4},{7,5},{8,6},{9,7},{10,8},{11,9},{12,... | collective-permute-start | bytes 196616 | tf_op jit(solution)/shard_map/ppermute | solution.py:530
  28.8 2.2 collective-permute-done.2.lo2_ref
  31.0 2.9 collective-permute-done.3.hi2_ref
  33.9 4.8 %start.1 = (f32[10,64,128]{2,1,0:T(8,128)S(1)}, f32[9,64,128]{2,1,0:T(8,128)S(1)}, f32[9,64,128]{2,1,0:T(8,128)S(1)}, f32[9,64,128]{2,1,0:T(8,128)S(1)}, f32[20,...) custom-call(f32[6]{0:T(128)S(1)} %copy-done.4, ...), custom_call_target="tpu_custom_call" | custom-call | tf_op jit(solution)/shard_map/start/pallas_call | solution.py:499
  39.3 6.4 %collective-permute-start.4 = (f32[3,64,128]{2,1,0:T(8,128)}, f32[3,64,128]{2,1,0:T(8,128)S(1)}, u32[]{:S(2)}, u32[]{:S(2)}) collective-permute-start(f32[3,64,128]{2,1,0:T(8,128)} %get-tuple-element.77), channel_id=1, source_target_pairs={{0,1},{1,2},{2,3},{3,4},{4,5},{5,6},{6,7},{7,8},{8,9},{9,10},{10,1... | collective-permute-start | bytes 294920 | tf_op jit(solution)/shard_map/ppermute | solution.py:527
  47.7 4.2 %collective-permute-start.6 = (f32[3,64,128]{2,1,0:T(8,128)}, f32[3,64,128]{2,1,0:T(8,128)S(1)}, u32[]{:S(2)}, u32[]{:S(2)}) collective-permute-start(f32[3,64,128]{2,1,0:T(8,128)} %get-tuple-element.79), channel_id=1, source_target_pairs={{0,2},{1,3},{2,4},{3,5},{4,6},{5,7},{6,8},{7,9},{8,10},{9,11},{10,... | collective-permute-start | bytes 294920 | tf_op jit(solution)/shard_map/ppermute | solution.py:527
  51.9 2.9 collective-permute-start.7
  54.8 7.8 %all-to-all-start.1 = ((f32[32,1,128]{2,1,0:T(1,128)}), f32[32,1,128]{2,1,0:T(1,128)}, u32[]{:S(2)}, u32[]{:S(2)}) async-start(f32[32,1,128]{2,1,0:T(1,128)} %copy-done.2), calls=%async_computation.1 | async-start | bytes 32768 | tf_op jit(solution)/shard_map/all_to_all | solution.py:533
  62.6 7.0 %all-to-all-done.1.red_in = f32[32,1,128]{2,1,0:T(1,128)} async-done(((f32[32,1,128]{2,1,0:T(1,128)}), f32[32,1,128]{2,1,0:T(1,128)}, u32[]{:S(2)}, u32[]{:S(2)}) %all-to-all-start.1) | async-done | bytes 16416 | tf_op jit(solution)/shard_map/all_to_all | solution.py:533
  69.6 2.9 %second.1 = (f32[12,64,128]{2,1,0:T(8,128)S(1)}, f32[3,64,128]{2,1,0:T(8,128)S(1)}, f32[3,64,128]{2,1,0:T(8,128)S(1)}, f32[3,64,128]{2,1,0:T(8,128)S(1)}, f32[32,1,128]{2,1,0:T(1,128)S(1)}) custom-call(f32[1,2]{1,0:T(1,128)S(1)} %copy-done.3, f32[3]{0:T(128)S(1)} %copy-done, f32[3]{0:T(128)S(1)} %copy-done.1, s32[1]{0:T(128)} %bitcast.place_ref.refs_3_, ...), custom_call_target="tpu_custom_call" | custom-call | tf_op jit(solution)/shard_map/second/pallas_call | solution.py:499
  72.5 10.7 %all_to_all.56.red_in = f32[32,1,128]{2,1,0:T(1,128)S(1)} all-to-all(f32[32,1,128]{2,1,0:T(1,128)S(1)} %get-tuple-element.81), channel_id=1, replica_groups=mesh['tm'=8,'gx'=8,'gy'=4] {'gx','gy'}, dimensions={0} | all-to-all | bytes 32768 | tf_op jit(solution)/shard_map/all_to_all | solution.py:533
  84.0 5.7 %collective-permute-start.8 = (f32[12,64,128]{2,1,0:T(8,128)S(1)}, f32[12,64,128]{2,1,0:T(8,128)S(1)}, u32[]{:S(2)}, u32[]{:S(2)}) collective-permute-start(f32[12,64,128]{2,1,0:T(8,128)S(1)} %block.1.refs_13_), channel_id=1, source_target_pairs={{0,224},{32,0},{64,32},{96,64},{128,96},{160,128},{192,160},{224,1... | collective-permute-start | bytes 1179656 | tf_op jit(solution)/shard_map/ppermute | solution.py:536
  89.6 7.8 %collective-permute-done.8.blk_ref.refs_4_ = f32[12,64,128]{2,1,0:T(8,128)S(1)} collective-permute-done((f32[12,64,128]{2,1,0:T(8,128)S(1)}, f32[12,64,128]{2,1,0:T(8,128)S(1)}, u32[]{:S(2)}, u32[]{:S(2)}) %collective-permute-start.8) | collective-permute-done | bytes 393248 | tf_op jit(solution)/shard_map/ppermute | solution.py:536
  97.4 3.4 %collective-permute-start.11 = (f32[12,64,128]{2,1,0:T(8,128)S(1)}, f32[12,64,128]{2,1,0:T(8,128)S(1)}, u32[]{:S(2)}, u32[]{:S(2)}) collective-permute-start(f32[12,64,128]{2,1,0:T(8,128)S(1)} %collective-permute-done.8.blk_ref.refs_4_), channel_id=1, source_target_pairs={{0,224},{32,0},{64,32},{96,64},{128,96},{160,128},{192,160},{224,1... | collective-permute-start | bytes 1179656 | tf_op jit(solution)/shard_map/ppermute | solution.py:536
  100.8 6.9 %collective-permute-done.11.refs_10_ = f32[12,64,128]{2,1,0:T(8,128)S(1)} collective-permute-done((f32[12,64,128]{2,1,0:T(8,128)S(1)}, f32[12,64,128]{2,1,0:T(8,128)S(1)}, u32[]{:S(2)}, u32[]{:S(2)}) %collective-permute-start.11) | collective-permute-done | bytes 393248 | tf_op jit(solution)/shard_map/ppermute | solution.py:536
  107.7 3.4 %collective-permute-start.14 = (f32[12,64,128]{2,1,0:T(8,128)S(1)}, f32[12,64,128]{2,1,0:T(8,128)S(1)}, u32[]{:S(2)}, u32[]{:S(2)}) collective-permute-start(f32[12,64,128]{2,1,0:T(8,128)S(1)} %collective-permute-done.11.refs_10_), channel_id=1, source_target_pairs={{0,224},{32,0},{64,32},{96,64},{128,96},{160,128},{192,160},{224,1... | collective-permute-start | bytes 1179656 | tf_op jit(solution)/shard_map/ppermute | solution.py:536
  111.1 6.0 %collective-permute-done.14.refs_13_ = f32[12,64,128]{2,1,0:T(8,128)S(1)} collective-permute-done((f32[12,64,128]{2,1,0:T(8,128)S(1)}, f32[12,64,128]{2,1,0:T(8,128)S(1)}, u32[]{:S(2)}, u32[]{:S(2)}) %collective-permute-start.14) | collective-permute-done | bytes 393248 | tf_op jit(solution)/shard_map/ppermute | solution.py:536
  117.1 3.4 %collective-permute-start.17 = (f32[12,64,128]{2,1,0:T(8,128)S(1)}, f32[12,64,128]{2,1,0:T(8,128)S(1)}, u32[]{:S(2)}, u32[]{:S(2)}) collective-permute-start(f32[12,64,128]{2,1,0:T(8,128)S(1)} %collective-permute-done.14.refs_13_), channel_id=1, source_target_pairs={{0,224},{32,0},{64,32},{96,64},{128,96},{160,128},{192,160},{224,1... | collective-permute-start | bytes 1179656 | tf_op jit(solution)/shard_map/ppermute | solution.py:536
  121.1 6.1 %collective-permute-start.10 = (f32[5,64,128]{2,1,0:T(8,128)S(1)}, f32[5,64,128]{2,1,0:T(8,128)S(1)}, u32[]{:S(2)}, u32[]{:S(2)}) collective-permute-start(f32[5,64,128]{2,1,0:T(8,128)S(1)} %get-tuple-element.87), channel_id=1, source_target_pairs={{1,0},{2,1},{3,2},{4,3},{5,4},{6,5},{7,6},{8,7},{9,8},{10,9},{11,1... | collective-permute-start | bytes 491528 | tf_op jit(solution)/shard_map/ppermute | solution.py:530
  129.1 9.7 %all-gather = f32[8,1,2]{2,1,0:T(1,128)S(1)} all-gather(f32[1,1,2]{2,1,0:T(1,128)S(1)} %bitcast.16), channel_id=1, replica_groups=mesh['tm'=8,'gx'=8,'gy'=4] {'tm'}, dimensions={0}, use_global_device_ids=true | all-gather | bytes 72 | tf_op jit(solution)/shard_map/all_gather | solution.py:539
  142.7 8.3 %collective-permute-start.13 = (f32[8,64,128]{2,1,0:T(8,128)S(1)}, f32[8,64,128]{2,1,0:T(8,128)S(1)}, u32[]{:S(2)}, u32[]{:S(2)}) collective-permute-start(f32[8,64,128]{2,1,0:T(8,128)S(1)} %get-tuple-element.94), channel_id=1, source_target_pairs={{1,0},{2,1},{3,2},{4,3},{5,4},{6,5},{7,6},{8,7},{9,8},{10,9},{11,1... | collective-permute-start | bytes 786440 | tf_op jit(solution)/shard_map/ppermute | solution.py:530
  153.0 12.0 %all_to_all.57.refs_4_ = f32[32,1,128]{2,1,0:T(1,128)S(1)} all-to-all(f32[32,1,128]{2,1,0:T(1,128)S(1)} %get-tuple-element.89), channel_id=1, replica_groups=mesh['tm'=8,'gx'=8,'gy'=4] {'gx','gy'}, dimensions={0} | all-to-all | bytes 32768 | tf_op jit(solution)/shard_map/all_to_all | solution.py:533
  165.0 2.0 chain3.1
  167.1 2.2 collective-permute-start.15
  169.3 4.6 %collective-permute-start.16 = (f32[8,64,128]{2,1,0:T(8,128)S(1)}, f32[8,64,128]{2,1,0:T(8,128)S(1)}, u32[]{:S(2)}, u32[]{:S(2)}) collective-permute-start(f32[8,64,128]{2,1,0:T(8,128)S(1)} %get-tuple-element.100), channel_id=1, source_target_pairs={{1,0},{2,1},{3,2},{4,3},{5,4},{6,5},{7,6},{8,7},{9,8},{10,9},{11,1... | collective-permute-start | bytes 786440 | tf_op jit(solution)/shard_map/ppermute | solution.py:530
  173.9 10.9 %all_to_all.58.refs_4_ = f32[32,1,128]{2,1,0:T(1,128)S(1)} all-to-all(f32[32,1,128]{2,1,0:T(1,128)S(1)} %get-tuple-element.95), channel_id=1, replica_groups=mesh['tm'=8,'gx'=8,'gy'=4] {'gx','gy'}, dimensions={0} | all-to-all | bytes 32768 | tf_op jit(solution)/shard_map/all_to_all | solution.py:533
  186.9 2.2 collective-permute-start.18
  189.1 4.6 %collective-permute-start.19 = (f32[8,64,128]{2,1,0:T(8,128)S(1)}, f32[8,64,128]{2,1,0:T(8,128)S(1)}, u32[]{:S(2)}, u32[]{:S(2)}) collective-permute-start(f32[8,64,128]{2,1,0:T(8,128)S(1)} %get-tuple-element.106), channel_id=1, source_target_pairs={{1,0},{2,1},{3,2},{4,3},{5,4},{6,5},{7,6},{8,7},{9,8},{10,9},{11,1... | collective-permute-start | bytes 786440 | tf_op jit(solution)/shard_map/ppermute | solution.py:530
  193.8 10.9 %all_to_all.59.refs_4_ = f32[32,1,128]{2,1,0:T(1,128)S(1)} all-to-all(f32[32,1,128]{2,1,0:T(1,128)S(1)} %get-tuple-element.101), channel_id=1, replica_groups=mesh['tm'=8,'gx'=8,'gy'=4] {'gx','gy'}, dimensions={0} | all-to-all | bytes 32768 | tf_op jit(solution)/shard_map/all_to_all | solution.py:533
  204.7 2.0 chain5.1
  206.7 2.2 collective-permute-start.21
  208.9 4.6 %collective-permute-start.22 = (f32[8,64,128]{2,1,0:T(8,128)S(1)}, f32[8,64,128]{2,1,0:T(8,128)S(1)}, u32[]{:S(2)}, u32[]{:S(2)}) collective-permute-start(f32[8,64,128]{2,1,0:T(8,128)S(1)} %get-tuple-element.112), channel_id=1, source_target_pairs={{1,0},{2,1},{3,2},{4,3},{5,4},{6,5},{7,6},{8,7},{9,8},{10,9},{11,1... | collective-permute-start | bytes 786440 | tf_op jit(solution)/shard_map/ppermute | solution.py:530
  215.0 11.2 %all_to_all.60.refs_4_ = f32[32,1,128]{2,1,0:T(1,128)S(1)} all-to-all(f32[32,1,128]{2,1,0:T(1,128)S(1)} %get-tuple-element.107), channel_id=1, replica_groups=mesh['tm'=8,'gx'=8,'gy'=4] {'gx','gy'}, dimensions={0} | all-to-all | bytes 32768 | tf_op jit(solution)/shard_map/all_to_all | solution.py:533
  226.2 2.0 chain6.1
  228.3 2.2 collective-permute-start.24
  230.5 4.6 %collective-permute-start.25 = (f32[8,64,128]{2,1,0:T(8,128)S(1)}, f32[8,64,128]{2,1,0:T(8,128)S(1)}, u32[]{:S(2)}, u32[]{:S(2)}) collective-permute-start(f32[8,64,128]{2,1,0:T(8,128)S(1)} %get-tuple-element.118), channel_id=1, source_target_pairs={{1,0},{2,1},{3,2},{4,3},{5,4},{6,5},{7,6},{8,7},{9,8},{10,9},{11,1... | collective-permute-start | bytes 786440 | tf_op jit(solution)/shard_map/ppermute | solution.py:530
  235.0 10.9 %all_to_all.61.refs_4_ = f32[32,1,128]{2,1,0:T(1,128)S(1)} all-to-all(f32[32,1,128]{2,1,0:T(1,128)S(1)} %get-tuple-element.113), channel_id=1, replica_groups=mesh['tm'=8,'gx'=8,'gy'=4] {'gx','gy'}, dimensions={0} | all-to-all | bytes 32768 | tf_op jit(solution)/shard_map/all_to_all | solution.py:533
  246.0 2.0 chain7.1
  248.0 2.2 collective-permute-start.27
  250.2 4.6 %collective-permute-start.28 = (f32[8,64,128]{2,1,0:T(8,128)S(1)}, f32[8,64,128]{2,1,0:T(8,128)S(1)}, u32[]{:S(2)}, u32[]{:S(2)}) collective-permute-start(f32[8,64,128]{2,1,0:T(8,128)S(1)} %get-tuple-element.124), channel_id=1, source_target_pairs={{1,0},{2,1},{3,2},{4,3},{5,4},{6,5},{7,6},{8,7},{9,8},{10,9},{11,1... | collective-permute-start | bytes 786440 | tf_op jit(solution)/shard_map/ppermute | solution.py:530
  254.8 10.9 %all_to_all.62.refs_4_ = f32[32,1,128]{2,1,0:T(1,128)S(1)} all-to-all(f32[32,1,128]{2,1,0:T(1,128)S(1)} %get-tuple-element.119), channel_id=1, replica_groups=mesh['tm'=8,'gx'=8,'gy'=4] {'gx','gy'}, dimensions={0} | all-to-all | bytes 32768 | tf_op jit(solution)/shard_map/all_to_all | solution.py:533
  265.8 2.6 chain8.1
  268.4 10.7 %all_to_all.63.red_in = f32[32,1,128]{2,1,0:T(1,128)S(1)} all-to-all(f32[32,1,128]{2,1,0:T(1,128)S(1)} %get-tuple-element.125), channel_id=1, replica_groups=mesh['tm'=8,'gx'=8,'gy'=4] {'gx','gy'}, dimensions={0} | all-to-all | bytes 32768 | tf_op jit(solution)/shard_map/all_to_all | solution.py:533
  279.8 9.6 %all_to_all.64 = f32[4,4,3,16,128]{4,3,2,1,0:T(8,128)S(1)} all-to-all(f32[4,4,3,16,128]{4,3,2,1,0:T(8,128)S(1)} %closing.1), channel_id=1, replica_groups=mesh['tm'=8,'gx'=8,'gy'=4] {'gy'}, dimensions={0} | all-to-all | bytes 786432 | tf_op jit(solution)/shard_map/all_to_all | solution.py:605
  (51 shorter events, 18.6 us)
Async XLA Ops:
  14.8 19.1 %collective-permute-start = (f32[4,5,3,16,128]{4,3,2,1,0:T(8,128)S(1)}, f32[4,5,3,16,128]{4,3,2,1,0:T(8,128)S(1)}, u32[]{:S(2)}, u32[]{:S(2)}) collective-permute-start(f32[4,5,3,16,128]{4,3,2,1,0:T(8,128)S(1)} %all_to_all.55.own_ref), channel_id=1, source_target_pairs={{0,1},{1,2},{2,3},{3,4},{4,5},{5,6},{6,7},{7,8},{8,9},{9,10},{10,1... | collective-permute-start | bytes 1474568 | tf_op jit(solution)/shard_map/ppermute | solution.py:527
  17.0 16.9 %collective-permute-start.1 = (f32[4,5,3,16,128]{4,3,2,1,0:T(8,128)S(1)}, f32[4,5,3,16,128]{4,3,2,1,0:T(8,128)S(1)}, u32[]{:S(2)}, u32[]{:S(2)}) collective-permute-start(f32[4,5,3,16,128]{4,3,2,1,0:T(8,128)S(1)} %all_to_all.55.own_ref), channel_id=1, source_target_pairs={{1,0},{2,1},{3,2},{4,3},{5,4},{6,5},{7,6},{8,7},{9,8},{10,9},{11,1... | collective-permute-start | bytes 1474568 | tf_op jit(solution)/shard_map/ppermute | solution.py:530
  21.6 12.3 %copy-start.4 = (f32[6]{0:T(128)S(1)}, f32[6]{0:T(128)}, u32[]{:S(2)}) copy-start(f32[6]{0:T(128)} %rigid_ref.1) | copy-start | bytes 76
  21.6 12.3 %copy-start.5 = (f32[6]{0:T(128)S(1)}, f32[6]{0:T(128)}, u32[]{:S(2)}) copy-start(f32[6]{0:T(128)} %dilate_ref.1) | copy-start | bytes 76
  21.6 12.3 %copy-start = (f32[3]{0:T(128)S(1)}, f32[3]{0:T(128)}, u32[]{:S(2)}) copy-start(f32[3]{0:T(128)} %coef_ref.9) | copy-start | bytes 40
  21.6 12.3 %copy-start.1 = (f32[3]{0:T(128)S(1)}, f32[3]{0:T(128)}, u32[]{:S(2)}) copy-start(f32[3]{0:T(128)} %time_ref.9) | copy-start | bytes 40
  21.6 12.3 %copy-start.3 = (f32[1,2]{1,0:T(1,128)S(1)}, f32[1,2]{1,0:T(1,128)}, u32[]{:S(2)}) copy-start(f32[1,2]{1,0:T(1,128)} %heat_ref.3) | copy-start | bytes 28
  21.6 9.4 %collective-permute-start.2 = (f32[4,2,1,16,128]{4,3,2,1,0:T(8,128)S(1)}, f32[4,2,1,16,128]{4,3,2,1,0:T(8,128)S(1)}, u32[]{:S(2)}, u32[]{:S(2)}) collective-permute-start(f32[4,2,1,16,128]{4,3,2,1,0:T(8,128)S(1)} %get-tuple-element.130), channel_id=1, source_target_pairs={{0,2},{1,3},{2,4},{3,5},{4,6},{5,7},{6,8},{7,9},{8,10},{9,11},{10,... | collective-permute-start | bytes 196616 | tf_op jit(solution)/shard_map/ppermute | solution.py:527
  23.7 10.2 %collective-permute-start.3 = (f32[4,2,1,16,128]{4,3,2,1,0:T(8,128)S(1)}, f32[4,2,1,16,128]{4,3,2,1,0:T(8,128)S(1)}, u32[]{:S(2)}, u32[]{:S(2)}) collective-permute-start(f32[4,2,1,16,128]{4,3,2,1,0:T(8,128)S(1)} %get-tuple-element.129), channel_id=1, source_target_pairs={{2,0},{3,1},{4,2},{5,3},{6,4},{7,5},{8,6},{9,7},{10,8},{11,9},{12,... | collective-permute-start | bytes 196616 | tf_op jit(solution)/shard_map/ppermute | solution.py:530
  38.7 0.6 copy-start.2
  39.3 30.2 %collective-permute-start.4 = (f32[3,64,128]{2,1,0:T(8,128)}, f32[3,64,128]{2,1,0:T(8,128)S(1)}, u32[]{:S(2)}, u32[]{:S(2)}) collective-permute-start(f32[3,64,128]{2,1,0:T(8,128)} %get-tuple-element.77), channel_id=1, source_target_pairs={{0,1},{1,2},{2,3},{3,4},{4,5},{5,6},{6,7},{7,8},{8,9},{9,10},{10,1... | collective-permute-start | bytes 294920 | tf_op jit(solution)/shard_map/ppermute | solution.py:527
  45.8 23.8 %collective-permute-start.5 = (f32[3,64,128]{2,1,0:T(8,128)}, f32[3,64,128]{2,1,0:T(8,128)S(1)}, u32[]{:S(2)}, u32[]{:S(2)}) collective-permute-start(f32[3,64,128]{2,1,0:T(8,128)} %get-tuple-element.78), channel_id=1, source_target_pairs={{1,0},{2,1},{3,2},{4,3},{5,4},{6,5},{7,6},{8,7},{9,8},{10,9},{11,1... | collective-permute-start | bytes 294920 | tf_op jit(solution)/shard_map/ppermute | solution.py:530
  47.7 21.9 %collective-permute-start.6 = (f32[3,64,128]{2,1,0:T(8,128)}, f32[3,64,128]{2,1,0:T(8,128)S(1)}, u32[]{:S(2)}, u32[]{:S(2)}) collective-permute-start(f32[3,64,128]{2,1,0:T(8,128)} %get-tuple-element.79), channel_id=1, source_target_pairs={{0,2},{1,3},{2,4},{3,5},{4,6},{5,7},{6,8},{7,9},{8,10},{9,11},{10,... | collective-permute-start | bytes 294920 | tf_op jit(solution)/shard_map/ppermute | solution.py:527
  51.9 17.7 %collective-permute-start.7 = (f32[3,64,128]{2,1,0:T(8,128)}, f32[3,64,128]{2,1,0:T(8,128)}, u32[]{:S(2)}, u32[]{:S(2)}) collective-permute-start(f32[3,64,128]{2,1,0:T(8,128)} %get-tuple-element.80), channel_id=1, source_target_pairs={{2,0},{3,1},{4,2},{5,3},{6,4},{7,5},{8,6},{9,7},{10,8},{11,9},{12,... | collective-permute-start | bytes 294920 | tf_op jit(solution)/shard_map/ppermute | solution.py:530
  54.8 14.8 %all-to-all-start.1 = ((f32[32,1,128]{2,1,0:T(1,128)}), f32[32,1,128]{2,1,0:T(1,128)}, u32[]{:S(2)}, u32[]{:S(2)}) async-start(f32[32,1,128]{2,1,0:T(1,128)} %copy-done.2), calls=%async_computation.1 | async-start | bytes 32768 | tf_op jit(solution)/shard_map/all_to_all | solution.py:533
  84.0 13.5 %collective-permute-start.8 = (f32[12,64,128]{2,1,0:T(8,128)S(1)}, f32[12,64,128]{2,1,0:T(8,128)S(1)}, u32[]{:S(2)}, u32[]{:S(2)}) collective-permute-start(f32[12,64,128]{2,1,0:T(8,128)S(1)} %block.1.refs_13_), channel_id=1, source_target_pairs={{0,224},{32,0},{64,32},{96,64},{128,96},{160,128},{192,160},{224,1... | collective-permute-start | bytes 1179656 | tf_op jit(solution)/shard_map/ppermute | solution.py:536
  97.4 10.3 %collective-permute-start.11 = (f32[12,64,128]{2,1,0:T(8,128)S(1)}, f32[12,64,128]{2,1,0:T(8,128)S(1)}, u32[]{:S(2)}, u32[]{:S(2)}) collective-permute-start(f32[12,64,128]{2,1,0:T(8,128)S(1)} %collective-permute-done.8.blk_ref.refs_4_), channel_id=1, source_target_pairs={{0,224},{32,0},{64,32},{96,64},{128,96},{160,128},{192,160},{224,1... | collective-permute-start | bytes 1179656 | tf_op jit(solution)/shard_map/ppermute | solution.py:536
  107.7 9.4 %collective-permute-start.14 = (f32[12,64,128]{2,1,0:T(8,128)S(1)}, f32[12,64,128]{2,1,0:T(8,128)S(1)}, u32[]{:S(2)}, u32[]{:S(2)}) collective-permute-start(f32[12,64,128]{2,1,0:T(8,128)S(1)} %collective-permute-done.11.refs_10_), channel_id=1, source_target_pairs={{0,224},{32,0},{64,32},{96,64},{128,96},{160,128},{192,160},{224,1... | collective-permute-start | bytes 1179656 | tf_op jit(solution)/shard_map/ppermute | solution.py:536
  117.1 33.9 %collective-permute-start.17 = (f32[12,64,128]{2,1,0:T(8,128)S(1)}, f32[12,64,128]{2,1,0:T(8,128)S(1)}, u32[]{:S(2)}, u32[]{:S(2)}) collective-permute-start(f32[12,64,128]{2,1,0:T(8,128)S(1)} %collective-permute-done.14.refs_13_), channel_id=1, source_target_pairs={{0,224},{32,0},{64,32},{96,64},{128,96},{160,128},{192,160},{224,1... | collective-permute-start | bytes 1179656 | tf_op jit(solution)/shard_map/ppermute | solution.py:536
  121.1 17.7 %collective-permute-start.10 = (f32[5,64,128]{2,1,0:T(8,128)S(1)}, f32[5,64,128]{2,1,0:T(8,128)S(1)}, u32[]{:S(2)}, u32[]{:S(2)}) collective-permute-start(f32[5,64,128]{2,1,0:T(8,128)S(1)} %get-tuple-element.87), channel_id=1, source_target_pairs={{1,0},{2,1},{3,2},{4,3},{5,4},{6,5},{7,6},{8,7},{9,8},{10,9},{11,1... | collective-permute-start | bytes 491528 | tf_op jit(solution)/shard_map/ppermute | solution.py:530
  127.2 11.6 %collective-permute-start.9 = (f32[5,64,128]{2,1,0:T(8,128)S(1)}, f32[5,64,128]{2,1,0:T(8,128)S(1)}, u32[]{:S(2)}, u32[]{:S(2)}) collective-permute-start(f32[5,64,128]{2,1,0:T(8,128)S(1)} %get-tuple-element.86), channel_id=1, source_target_pairs={{0,1},{1,2},{2,3},{3,4},{4,5},{5,6},{6,7},{7,8},{8,9},{9,10},{10,1... | collective-permute-start | bytes 491528 | tf_op jit(solution)/shard_map/ppermute | solution.py:527
  140.7 24.3 %collective-permute-start.12 = (f32[8,64,128]{2,1,0:T(8,128)S(1)}, f32[8,64,128]{2,1,0:T(8,128)S(1)}, u32[]{:S(2)}, u32[]{:S(2)}) collective-permute-start(f32[8,64,128]{2,1,0:T(8,128)S(1)} %get-tuple-element.93), channel_id=1, source_target_pairs={{0,1},{1,2},{2,3},{3,4},{4,5},{5,6},{6,7},{7,8},{8,9},{9,10},{10,1... | collective-permute-start | bytes 786440 | tf_op jit(solution)/shard_map/ppermute | solution.py:527
  142.7 22.4 %collective-permute-start.13 = (f32[8,64,128]{2,1,0:T(8,128)S(1)}, f32[8,64,128]{2,1,0:T(8,128)S(1)}, u32[]{:S(2)}, u32[]{:S(2)}) collective-permute-start(f32[8,64,128]{2,1,0:T(8,128)S(1)} %get-tuple-element.94), channel_id=1, source_target_pairs={{1,0},{2,1},{3,2},{4,3},{5,4},{6,5},{7,6},{8,7},{9,8},{10,9},{11,1... | collective-permute-start | bytes 786440 | tf_op jit(solution)/shard_map/ppermute | solution.py:530
  151.0 42.6 %collective-permute-start.20 = (f32[12,64,128]{2,1,0:T(8,128)S(1)}, f32[12,64,128]{2,1,0:T(8,128)S(1)}, u32[]{:S(2)}, u32[]{:S(2)}) collective-permute-start(f32[12,64,128]{2,1,0:T(8,128)S(1)} %collective-permute-done.17.refs_13_), channel_id=1, source_target_pairs={{0,224},{32,0},{64,32},{96,64},{128,96},{160,128},{192,160},{224,1... | collective-permute-start | bytes 1179656 | tf_op jit(solution)/shard_map/ppermute | solution.py:536
  167.1 17.7 %collective-permute-start.15 = (f32[8,64,128]{2,1,0:T(8,128)S(1)}, f32[8,64,128]{2,1,0:T(8,128)S(1)}, u32[]{:S(2)}, u32[]{:S(2)}) collective-permute-start(f32[8,64,128]{2,1,0:T(8,128)S(1)} %get-tuple-element.99), channel_id=1, source_target_pairs={{0,1},{1,2},{2,3},{3,4},{4,5},{5,6},{6,7},{7,8},{8,9},{9,10},{10,1... | collective-permute-start | bytes 786440 | tf_op jit(solution)/shard_map/ppermute | solution.py:527
  169.3 15.5 %collective-permute-start.16 = (f32[8,64,128]{2,1,0:T(8,128)S(1)}, f32[8,64,128]{2,1,0:T(8,128)S(1)}, u32[]{:S(2)}, u32[]{:S(2)}) collective-permute-start(f32[8,64,128]{2,1,0:T(8,128)S(1)} %get-tuple-element.100), channel_id=1, source_target_pairs={{1,0},{2,1},{3,2},{4,3},{5,4},{6,5},{7,6},{8,7},{9,8},{10,9},{11,1... | collective-permute-start | bytes 786440 | tf_op jit(solution)/shard_map/ppermute | solution.py:530
  186.9 17.8 %collective-permute-start.18 = (f32[8,64,128]{2,1,0:T(8,128)S(1)}, f32[8,64,128]{2,1,0:T(8,128)S(1)}, u32[]{:S(2)}, u32[]{:S(2)}) collective-permute-start(f32[8,64,128]{2,1,0:T(8,128)S(1)} %get-tuple-element.105), channel_id=1, source_target_pairs={{0,1},{1,2},{2,3},{3,4},{4,5},{5,6},{6,7},{7,8},{8,9},{9,10},{10,1... | collective-permute-start | bytes 786440 | tf_op jit(solution)/shard_map/ppermute | solution.py:527
  189.1 15.6 %collective-permute-start.19 = (f32[8,64,128]{2,1,0:T(8,128)S(1)}, f32[8,64,128]{2,1,0:T(8,128)S(1)}, u32[]{:S(2)}, u32[]{:S(2)}) collective-permute-start(f32[8,64,128]{2,1,0:T(8,128)S(1)} %get-tuple-element.106), channel_id=1, source_target_pairs={{1,0},{2,1},{3,2},{4,3},{5,4},{6,5},{7,6},{8,7},{9,8},{10,9},{11,1... | collective-permute-start | bytes 786440 | tf_op jit(solution)/shard_map/ppermute | solution.py:530
  193.7 19.9 %collective-permute-start.23 = (f32[12,64,128]{2,1,0:T(8,128)S(1)}, f32[12,64,128]{2,1,0:T(8,128)S(1)}, u32[]{:S(2)}, u32[]{:S(2)}) collective-permute-start(f32[12,64,128]{2,1,0:T(8,128)S(1)} %collective-permute-done.20.refs_13_), channel_id=1, source_target_pairs={{0,224},{32,0},{64,32},{96,64},{128,96},{160,128},{192,160},{224,1... | collective-permute-start | bytes 1179656 | tf_op jit(solution)/shard_map/ppermute | solution.py:536
  206.7 19.5 %collective-permute-start.21 = (f32[8,64,128]{2,1,0:T(8,128)S(1)}, f32[8,64,128]{2,1,0:T(8,128)S(1)}, u32[]{:S(2)}, u32[]{:S(2)}) collective-permute-start(f32[8,64,128]{2,1,0:T(8,128)S(1)} %get-tuple-element.111), channel_id=1, source_target_pairs={{0,1},{1,2},{2,3},{3,4},{4,5},{5,6},{6,7},{7,8},{8,9},{9,10},{10,1... | collective-permute-start | bytes 786440 | tf_op jit(solution)/shard_map/ppermute | solution.py:527
  208.9 17.3 %collective-permute-start.22 = (f32[8,64,128]{2,1,0:T(8,128)S(1)}, f32[8,64,128]{2,1,0:T(8,128)S(1)}, u32[]{:S(2)}, u32[]{:S(2)}) collective-permute-start(f32[8,64,128]{2,1,0:T(8,128)S(1)} %get-tuple-element.112), channel_id=1, source_target_pairs={{1,0},{2,1},{3,2},{4,3},{5,4},{6,5},{7,6},{8,7},{9,8},{10,9},{11,1... | collective-permute-start | bytes 786440 | tf_op jit(solution)/shard_map/ppermute | solution.py:530
  213.5 32.4 %collective-permute-start.26 = (f32[12,64,128]{2,1,0:T(8,128)S(1)}, f32[12,64,128]{2,1,0:T(8,128)S(1)}, u32[]{:S(2)}, u32[]{:S(2)}) collective-permute-start(f32[12,64,128]{2,1,0:T(8,128)S(1)} %collective-permute-done.23.refs_13_), channel_id=1, source_target_pairs={{0,224},{32,0},{64,32},{96,64},{128,96},{160,128},{192,160},{224,1... | collective-permute-start | bytes 1179656 | tf_op jit(solution)/shard_map/ppermute | solution.py:536
  228.3 17.7 %collective-permute-start.24 = (f32[8,64,128]{2,1,0:T(8,128)S(1)}, f32[8,64,128]{2,1,0:T(8,128)S(1)}, u32[]{:S(2)}, u32[]{:S(2)}) collective-permute-start(f32[8,64,128]{2,1,0:T(8,128)S(1)} %get-tuple-element.117), channel_id=1, source_target_pairs={{0,1},{1,2},{2,3},{3,4},{4,5},{5,6},{6,7},{7,8},{8,9},{9,10},{10,1... | collective-permute-start | bytes 786440 | tf_op jit(solution)/shard_map/ppermute | solution.py:527
  230.5 15.5 %collective-permute-start.25 = (f32[8,64,128]{2,1,0:T(8,128)S(1)}, f32[8,64,128]{2,1,0:T(8,128)S(1)}, u32[]{:S(2)}, u32[]{:S(2)}) collective-permute-start(f32[8,64,128]{2,1,0:T(8,128)S(1)} %get-tuple-element.118), channel_id=1, source_target_pairs={{1,0},{2,1},{3,2},{4,3},{5,4},{6,5},{7,6},{8,7},{9,8},{10,9},{11,1... | collective-permute-start | bytes 786440 | tf_op jit(solution)/shard_map/ppermute | solution.py:530
  248.0 17.7 %collective-permute-start.27 = (f32[8,64,128]{2,1,0:T(8,128)S(1)}, f32[8,64,128]{2,1,0:T(8,128)S(1)}, u32[]{:S(2)}, u32[]{:S(2)}) collective-permute-start(f32[8,64,128]{2,1,0:T(8,128)S(1)} %get-tuple-element.123), channel_id=1, source_target_pairs={{0,1},{1,2},{2,3},{3,4},{4,5},{5,6},{6,7},{7,8},{8,9},{9,10},{10,1... | collective-permute-start | bytes 786440 | tf_op jit(solution)/shard_map/ppermute | solution.py:527
  250.2 15.5 %collective-permute-start.28 = (f32[8,64,128]{2,1,0:T(8,128)S(1)}, f32[8,64,128]{2,1,0:T(8,128)S(1)}, u32[]{:S(2)}, u32[]{:S(2)}) collective-permute-start(f32[8,64,128]{2,1,0:T(8,128)S(1)} %get-tuple-element.124), channel_id=1, source_target_pairs={{1,0},{2,1},{3,2},{4,3},{5,4},{6,5},{7,6},{8,7},{9,8},{10,9},{11,1... | collective-permute-start | bytes 786440 | tf_op jit(solution)/shard_map/ppermute | solution.py:530

commit v2 on v1

--- a/solution.py
+++ b/solution.py
@@ -13,7 +13,7 @@
 PRONY = 3
 L = 3
 LINE = ("gx", "gy")
-LIMIT = 48 << 20
+LIMIT = 14 << 20
 
 
 def masks(ny, nz):
@@ -115,12 +115,26 @@
     return c
 
 
+def send(odd_side, lo, hi, even_out, odd_out):
+    for at, (low, high) in enumerate(zip(lo, hi)):
+        even_out[at] = jnp.where(odd_side == 0, high, low)
+        odd_out[at] = jnp.where(odd_side == 0, low, high)
+
+
+def below(odd_side, even_ref, odd_ref, at):
+    return jnp.where(odd_side == 0, odd_ref[at], even_ref[at])
+
+
+def above(odd_side, even_ref, odd_ref, at):
+    return jnp.where(odd_side == 0, even_ref[at], odd_ref[at])
+
+
 def start_kernel(
-    rigid_ref, dilate_ref, heat_ref, coef_ref, time_ref,
-    own_ref, lo_ref, hi_ref, lo2_ref, hi2_ref,
+    rigid_ref, dilate_ref, heat_ref, coef_ref, time_ref, place_ref,
+    own_ref, even_ref, odd_ref, even2_ref, odd2_ref,
     kel_ref, theta_ref, inv_f_ref, inv_c_ref, state_ref,
     zf_ref, ozf_ref, oozf_ref, zc_ref, ozc_ref,
-    lo1_out, hi1_out, lo2_out, hi2_out, red_ref,
+    even_out, odd_out, even2_out, odd2_out, red_ref,
     kal_ref, au_ref, w_ref,
 ):
     ny, nz = kel_ref.shape[1:]
@@ -129,15 +143,15 @@
 
     def raw(field, i):
         if i == -L - 1:
-            parts = [lo2_ref[c, field, 0] for c in range(chunks)]
+            parts = [below(place_ref[2], even2_ref, odd2_ref, (c, field, 0)) for c in range(chunks)]
         elif i < 0:
-            parts = [lo_ref[c, field, i + L] for c in range(chunks)]
+            parts = [below(place_ref[1], even_ref, odd_ref, (c, field, i + L)) for c in range(chunks)]
         elif i < L:
             parts = [own_ref[c, field, i] for c in range(chunks)]
         elif i < 2 * L:
-            parts = [hi_ref[c, field, i - L] for c in range(chunks)]
+            parts = [above(place_ref[1], even_ref, odd_ref, (c, field, i - L)) for c in range(chunks)]
         else:
-            parts = [hi2_ref[c, field, 0] for c in range(chunks)]
+            parts = [above(place_ref[2], even2_ref, odd2_ref, (c, field, 0)) for c in range(chunks)]
         return jnp.concatenate(parts, axis=0)
 
     for e in range(-4, 6):
@@ -243,17 +257,19 @@
 
     moments_out(acc, red_ref)
 
-    lo1_out[0], lo1_out[1], lo1_out[2] = ozf_ref[2 + 2], oozf_ref[1 + 1], oozf_ref[2 + 1]
-    hi1_out[0], hi1_out[1], hi1_out[2] = ozf_ref[0 + 2], oozf_ref[0 + 1], oozf_ref[1 + 1]
-    lo2_out[0], lo2_out[1], lo2_out[2] = zf_ref[0 + 3], ozf_ref[0 + 2], oozf_ref[0 + 1]
-    hi2_out[0], hi2_out[1], hi2_out[2] = zf_ref[2 + 3], ozf_ref[2 + 2], oozf_ref[2 + 1]
+    lo1 = [ozf_ref[2 + 2], oozf_ref[1 + 1], oozf_ref[2 + 1]]
+    hi1 = [ozf_ref[0 + 2], oozf_ref[0 + 1], oozf_ref[1 + 1]]
+    lo2 = [zf_ref[0 + 3], ozf_ref[0 + 2], oozf_ref[0 + 1]]
+    hi2 = [zf_ref[2 + 3], ozf_ref[2 + 2], oozf_ref[2 + 1]]
+    send(place_ref[1], lo1, hi1, even_out, odd_out)
+    send(place_ref[2], lo2, hi2, even2_out, odd2_out)
 
 
 def second_kernel(
     heat_ref, coef_ref, time_ref, place_ref,
     red_in, kel_ref, theta_ref, inv_f_ref, state_ref, own_ref,
     zf_ref, ozf_ref, oozf_ref, zc_ref, ozc_ref,
-    lo1_ref, hi1_ref, lo2_ref, hi2_ref,
+    even_ref, odd_ref, even2_ref, odd2_ref,
     base_ref, z_out, oz_out, ooz_out, red_ref,
     u_ref, z_ref, oz_ref, ooz_ref, au_ref,
 ):
@@ -265,27 +281,23 @@
     c = galerkin(moments_in(red_in, 0, 6))
     b = galerkin(moments_in(red_in, 6, 4))
 
-    def zf(i):
-        return lo_hi(i, -3, 5, zf_ref, 3, None, None, 0)
-
-    def lo_hi(i, low, high, ref, shift, near, off, far_at):
+    near, far = place_ref[1], place_ref[2]
+
+    def basis(i, at, ref, reach):
         if i == -4:
-            return hi_lo2(True, far_at)
+            return below(far, even2_ref, odd2_ref, at)
         if i == 6:
-            return hi_lo2(False, far_at)
-        if low <= i <= high:
-            return ref[i + shift]
-        return near[i][0][near[i][1]]
-
-    def hi_lo2(low, at):
-        return lo2_ref[at] if low else hi2_ref[at]
-
-    near_oz = {-3: (lo1_ref, 0), 5: (hi1_ref, 0)}
-    near_ooz = {-3: (lo1_ref, 1), -2: (lo1_ref, 2), 4: (hi1_ref, 1), 5: (hi1_ref, 2)}
+            return above(far, even2_ref, odd2_ref, at)
+        if -reach <= i <= L - 1 + reach:
+            return ref[i + reach]
+        if at == 1:
+            return (below if i < 0 else above)(near, even_ref, odd_ref, 0)
+        if i < 0:
+            return below(near, even_ref, odd_ref, i + 4)
+        return above(near, even_ref, odd_ref, i - 3)
+
     for i in range(-4, 7):
-        z = zf(i)
-        oz = lo_hi(i, -2, 4, ozf_ref, 2, near_oz, None, 1)
-        ooz = lo_hi(i, -1, 3, oozf_ref, 1, near_ooz, None, 2)
+        z, oz, ooz = basis(i, 0, zf_ref, 3), basis(i, 1, ozf_ref, 2), basis(i, 2, oozf_ref, 1)
         u_ref[i + 4] = state_ref[i + 4] + c[0] * z + c[1] * oz + c[2] * ooz
 
     def k(e):
@@ -347,85 +359,94 @@
     moments_out(acc, red_ref)
 
 
-def block_kernel(coef_ref, time_ref, red_in, base_ref, z_ref, oz_ref, ooz_ref, blk_ref):
+def block_kernel(heat_ref, coef_ref, time_ref, red_in, base_ref, z_ref, oz_ref, ooz_ref, blk_ref):
     decay_f, rest_f, ff, shift_f = prony(1.0, coef_ref, time_ref)
     c = galerkin(moments_in(red_in, 0, 6))
+    ny = z_ref.shape[1]
     for i in range(L):
         delta = c[0] * z_ref[i] + c[1] * oz_ref[i] + c[2] * ooz_ref[i]
-        blk_ref[i] = base_ref[i] + delta
+        blk_ref[i * ny : (i + 1) * ny] = base_ref[i] + delta
         for p in range(PRONY):
-            blk_ref[L * (1 + p) + i] = base_ref[L * (1 + p) + i] + rest_f[p] * delta
-
-
-def opening_kernel(coef_ref, time_ref, blk_ref, lo_out, hi_out):
+            at = L * (1 + p) + i
+            blk_ref[at * ny : (at + 1) * ny] = base_ref[at] + rest_f[p] * delta
+    blk_ref[4 * L * ny :] = jnp.full((8, blk_ref.shape[1]), heat_ref[0, PACES - 1], jnp.float32)
+
+
+def halo_base(f, base_ref):
+    sums = [
+        f[0] * base_ref[L + i] + f[1] * base_ref[2 * L + i] + f[2] * base_ref[3 * L + i]
+        for i in range(L)
+    ]
+    u = [base_ref[i] for i in range(L)]
+    return u + [sums[0], sums[1]], u + [sums[1], sums[2]]
+
+
+def opening_kernel(coef_ref, time_ref, place_ref, blk_ref, base_ref, even_out, odd_out):
     decay, rest, f, shift = prony(1.0 * PACES, coef_ref, time_ref)
-
-    def total(i):
-        return f[0] * blk_ref[L + i] + f[1] * blk_ref[2 * L + i] + f[2] * blk_ref[3 * L + i]
-
-    for i in range(L):
-        lo_out[i] = blk_ref[i]
-        hi_out[i] = blk_ref[i]
-    sums = [total(i) for i in range(L)]
-    lo_out[3], lo_out[4] = sums[0], sums[1]
-    hi_out[3], hi_out[4] = sums[1], sums[2]
+    ny = even_out.shape[1]
+    for at in range(4 * L):
+        base_ref[at] = blk_ref[at * ny : (at + 1) * ny]
+    lo, hi = halo_base(f, base_ref)
+    send(place_ref[1], lo, hi, even_out, odd_out)
 
 
 def chain_kernel(turn, count, opened, *refs):
     refs = list(refs)
-    heat_ref, coef_ref, time_ref, place_ref = refs[:4]
-    refs = refs[4:]
+    coef_ref, time_ref, place_ref = refs[:3]
+    refs = refs[3:]
     if opened:
-        base_in, lo_ref, hi_ref = refs[:3]
+        base_in, even_ref, odd_ref = refs[:3]
         refs = refs[3:]
     else:
-        red_in, base_in, z_in, oz_in, lo_ref, hi_ref = refs[:6]
+        red_in, base_in, z_in, oz_in, even_ref, odd_ref = refs[:6]
         refs = refs[6:]
     kel_ref, theta_ref, inv_ref, blk_ref = refs[:4]
-    base_ref, z_ref, oz_ref, lo_out, hi_out, red_ref, u_ref, au_ref = refs[4:]
+    base_ref, z_ref, oz_ref, even_out, odd_out, red_ref, u_ref, au_ref = refs[4:]
     ny, nz = kel_ref.shape[1:]
     sh = Shifts(ny, nz)
     decay, rest, f, shift = prony(1.0 * PACES, coef_ref, time_ref)
     grow = f[0] * rest[0] + f[1] * rest[1] + f[2] * rest[2]
     step = lax.rem(place_ref[0] + turn, count)
-    heat = heat_ref[step, PACES - 1]
+    heat = blk_ref[4 * L * ny : 4 * L * ny + 1]
     opening = step == 0
     fresh = step == 1
+    side = place_ref[1]
 
     if not opened:
         c = galerkin(moments_in(red_in, 0, 4))
 
+    def near(i, low_at, high_at):
+        if i < 0:
+            return below(side, even_ref, odd_ref, low_at)
+        return above(side, even_ref, odd_ref, high_at)
+
     def delta(i):
-        if i == -3:
-            z, oz = lo_ref[5], lo_ref[6]
-        elif i == 5:
-            z, oz = hi_ref[5], hi_ref[6]
+        z = z_in[i + 2] if -2 <= i <= 4 else near(i, 5, 5)
+        if -1 <= i <= 3:
+            oz = oz_in[i + 1]
         else:
-            z = z_in[i + 2]
-            oz = oz_in[i + 1] if -1 <= i <= 3 else (lo_ref[7] if i == -2 else hi_ref[7])
+            at = 6 if i in (-3, 5) else 7
+            oz = near(i, at, at)
         return jnp.where(fresh, 0.0, c[0] * z + c[1] * oz)
 
     for i in range(-3, 6):
-        base = lo_ref[i + 3] if i < 0 else hi_ref[i - L] if i >= L else base_in[i]
-        if opened:
-            u_ref[i + 3] = base
-            d = None
-        else:
-            d = delta(i)
-            u_ref[i + 3] = base + d
+        base = base_in[i] if 0 <= i < L else near(i, i + 3, i - L)
+        d = None if opened else delta(i)
+        u_ref[i + 3] = base if opened else base + d
         if 0 <= i < L:
             h = [base_in[L * (1 + p) + i] for p in range(PRONY)]
-            if d is not None:
+            if not opened:
                 h = [h[p] + rest[p] * d for p in range(PRONY)]
             total = f[0] * h[0] + f[1] * h[1] + f[2] * h[2]
             ui = u_ref[i + 3]
-            base_ref[i] = jnp.where(opening, 0.0, ui) + blk_ref[i]
+            base_ref[i] = jnp.where(opening, 0.0, ui) + blk_ref[i * ny : (i + 1) * ny]
             for p in range(PRONY):
+                at = L * (1 + p) + i
                 ahead = jnp.where(opening, 0.0, decay[p] * h[p] + rest[p] * ui)
-                base_ref[L * (1 + p) + i] = ahead + blk_ref[L * (1 + p) + i]
+                base_ref[at] = ahead + blk_ref[at * ny : (at + 1) * ny]
         elif -2 <= i < 5:
-            total = lo_ref[3 + i + 2] if i < 0 else hi_ref[3 + i - L]
-            if d is not None:
+            total = near(i, 3 + i + 2, 3 + i - L)
+            if not opened:
                 total = total + grow * d
         if -2 <= i < 5:
             au_ref[i + 2] = heat * theta_ref[i + 3] + total
@@ -462,17 +483,10 @@
     off_diagonal(sh, lambda i: oz_ref[i + 1], k, 0, 2, put_last)
     moments_out(acc, red_ref)
 
-    def total(i):
-        return f[0] * base_ref[L + i] + f[1] * base_ref[2 * L + i] + f[2] * base_ref[3 * L + i]
-
-    sums = [total(i) for i in range(L)]
-    for i in range(L):
-        lo_out[i] = base_ref[i]
-        hi_out[i] = base_ref[i]
-    lo_out[3], lo_out[4] = sums[0], sums[1]
-    hi_out[3], hi_out[4] = sums[1], sums[2]
-    lo_out[5], lo_out[6], lo_out[7] = z_ref[2 + 2], oz_ref[2 + 1], oz_ref[1 + 1]
-    hi_out[5], hi_out[6], hi_out[7] = z_ref[0 + 2], oz_ref[0 + 1], oz_ref[1 + 1]
+    lo, hi = halo_base(f, base_ref)
+    lo = lo + [z_ref[2 + 2], oz_ref[2 + 1], oz_ref[1 + 1]]
+    hi = hi + [z_ref[0 + 2], oz_ref[0 + 1], oz_ref[1 + 1]]
+    send(side, lo, hi, even_out, odd_out)
 
 
 def closing_kernel(coef_ref, time_ref, place_ref, red_in, base_ref, z_ref, oz_ref, out_ref):
@@ -488,6 +502,29 @@
         for at, field in enumerate(fields):
             for q in range(chunks):
                 out_ref[q, at, i] = field[q * rows : (q + 1) * rows]
+
+
+def layers_of(place_ref, q, chunks):
+    return jnp.where(place_ref[3] == 0, q, chunks - 1 - q) * L
+
+
+def gather_kernel(place_ref, parts_ref, out_ref):
+    chunks = parts_ref.shape[0]
+    for q in range(chunks):
+        first = layers_of(place_ref, q, chunks)
+        for i in range(L):
+            for field in range(1 + PRONY):
+                out_ref[0, field, first + i] = parts_ref[q, field, i]
+
+
+def spread_kernel(place_ref, label_ref, values_ref, out_ref):
+    chunks = out_ref.shape[0]
+    for q in range(chunks):
+        first = layers_of(place_ref, q, chunks)
+        for i in range(L):
+            out_ref[q, 0, i] = label_ref[first + i].astype(jnp.float32) + 1.0
+            for field in range(1 + PRONY):
+                out_ref[q, 1 + field, i] = values_ref[0, field, first + i]
 
 
 SMEM = pl.BlockSpec(memory_space=pltpu.SMEM)
@@ -523,11 +560,18 @@
     assert nx == L * n_gy
     plane = (ny, nz)
 
-    def up(value, by):
-        return lax.ppermute(value, LINE, [(s, s + by) for s in range(line - by)])
-
-    def down(value, by):
-        return lax.ppermute(value, LINE, [(s + by, s) for s in range(line - by)])
+    def device(position):
+        row, column = divmod(position, n_gy)
+        return row * n_gy + (column if row % 2 == 0 else n_gy - 1 - column)
+
+    def trade(even, odd, by):
+        received = []
+        for side, value in enumerate((even, odd)):
+            pairs = [(p, p + by) for p in range(line - by) if p // by % 2 == side]
+            both = pairs + [(b, a) for a, b in pairs]
+            perm = sorted((device(a), device(b)) for a, b in both)
+            received.append(lax.ppermute(value, LINE, perm))
+        return received
 
     def exchanged(red):
         return lax.all_to_all(red, LINE, 0, 0, tiled=True)
@@ -535,23 +579,32 @@
     def ring(block):
         return lax.ppermute(block, "tm", [(s, (s - 1) % n_tm) for s in range(n_tm)])
 
-    place = lax.axis_index("tm").astype(jnp.int32)[None]
-    heats = lax.all_gather(heat_swings_array[0], "tm")
+    gx, gy = lax.axis_index("gx"), lax.axis_index("gy")
+    flip = gx % 2
+    position = gx * n_gy + jnp.where(flip == 0, gy, n_gy - 1 - gy)
+    place = jnp.stack([lax.axis_index("tm"), position % 2, position // 2 % 2, flip])
+    place = place.astype(jnp.int32)
     prony_args = (prony_coefficients, prony_decay_times)
 
-    label = cell_material_label.astype(jnp.float32)[None] + 1.0
-    raw = jnp.concatenate([label, segment_opening_values[0]], axis=0)
-    raw = raw.reshape(2 + PRONY, n_gy, L, ny_part, nz).transpose(1, 0, 2, 3, 4)
+    (raw,) = call(
+        spread_kernel,
+        "spread",
+        (place,),
+        (cell_material_label, segment_opening_values),
+        [(n_gy, 2 + PRONY, L, ny_part, nz)],
+    )
     own = lax.all_to_all(raw, "gy", 0, 0, tiled=True)
-    lo, hi = up(own, 1), down(own, 1)
-    lo2, hi2 = up(own[:, :2, L - 1 :], 2), down(own[:, :2, :1], 2)
+    near = trade(own, own, 1)
+    top, bottom = own[:, :2, L - 1 :], own[:, :2, :1]
+    upward = position // 2 % 2 == 0
+    far = trade(jnp.where(upward, top, bottom), jnp.where(upward, bottom, top), 2)
 
     red_shape = (line, 1, 128)
-    (kel, theta, inv_f, inv_c, state, zf, ozf, oozf, zc, ozc, lo1, hi1, lo2, hi2, red) = call(
+    (kel, theta, inv_f, inv_c, state, zf, ozf, oozf, zc, ozc, even, odd, even2, odd2, red) = call(
         start_kernel,
         "start",
-        (material_rigidity, dilation_mismatch, heat_swings_array, *prony_args),
-        (own, lo, hi, lo2, hi2),
+        (material_rigidity, dilation_mismatch, heat_swings_array, *prony_args, place),
+        (own, *near, *far),
         [
             (10, *plane), (9, *plane), (9, *plane), (9, *plane), (20, *plane),
             (9, *plane), (7, *plane), (5, *plane), (L, *plane), (L, *plane),
@@ -560,50 +613,61 @@
         [(10, *plane), (9, *plane), (7, *plane)],
     )
     red = exchanged(red)
-    hi1, lo1 = down(lo1, 1), up(hi1, 1)
-    hi2, lo2 = down(lo2, 2), up(hi2, 2)
+    near, far = trade(even, odd, 1), trade(even2, odd2, 2)
     base, z, oz, ooz, red = call(
         second_kernel,
         "second",
         (heat_swings_array, *prony_args, place),
-        (red, kel, theta, inv_f, state, own, zf, ozf, oozf, zc, ozc, lo1, hi1, lo2, hi2),
+        (red, kel, theta, inv_f, state, own, zf, ozf, oozf, zc, ozc, *near, *far),
         [(4 * L, *plane), (L, *plane), (L, *plane), (L, *plane), red_shape],
         [(11, *plane), (9, *plane), (7, *plane), (5, *plane), (9, *plane)],
     )
     red = exchanged(red)
     (block,) = call(
-        block_kernel, "block", prony_args, (red, base, z, oz, ooz), [(4 * L, *plane)]
+        block_kernel,
+        "block",
+        (heat_swings_array, *prony_args),
+        (red, base, z, oz, ooz),
+        [(4 * L * ny + 8, nz)],
     )
     mine = block
     block = ring(block)
-    lo, hi = call(opening_kernel, "opening", prony_args, (block,), [(5, *plane)] * 2)
-    hi, lo = down(lo, 1), up(hi, 1)
-    base = block
-    red = z = oz = None
+    base, even, odd = call(
+        opening_kernel,
+        "opening",
+        (*prony_args, place),
+        (block,),
+        [(4 * L, *plane), (5, *plane), (5, *plane)],
+    )
+    past = (base,)
     for turn in range(2, n_tm + 1):
-        block = ring(block) if turn < n_tm else mine
-        opened = turn == 2
-        past = (base, lo, hi) if opened else (red, base, z, oz, lo, hi)
-        base, z, oz, lo, hi, red = call(
-            functools.partial(chain_kernel, turn, n_tm, opened),
+        if turn < n_tm:
+            block, even = lax.optimization_barrier((block, even))
+            block = ring(block)
+        else:
+            block = mine
+        past = (*past, *trade(even, odd, 1))
+        base, z, oz, even, odd, red = call(
+            functools.partial(chain_kernel, turn, n_tm, turn == 2),
             f"chain{turn}",
-            (heats, *prony_args, place),
+            (*prony_args, place),
             (*past, kel, theta, inv_c, block),
             [(4 * L, *plane), (7, *plane), (5, *plane), (8, *plane), (8, *plane), red_shape],
             [(9, *plane), (7, *plane)],
         )
-        red = exchanged(red)
-        if turn < n_tm:
-            hi, lo = down(lo, 1), up(hi, 1)
-    (out,) = call(
+        past = (exchanged(red), base, z, oz)
+    (parts,) = call(
         closing_kernel,
         "closing",
         (*prony_args, place),
-        (red, base, z, oz),
+        past,
         [(n_gy, 1 + PRONY, L, ny_part, nz)],
     )
-    out = lax.all_to_all(out, "gy", 0, 0, tiled=True)
-    return out.transpose(1, 0, 2, 3, 4).reshape(1, 1 + PRONY, nx, ny_part, nz)
+    parts = lax.all_to_all(parts, "gy", 0, 0, tiled=True)
+    (out,) = call(
+        gather_kernel, "gather", (place,), (parts,), [(1, 1 + PRONY, nx, ny_part, nz)]
+    )
+    return out
 
 
 def solution(mesh):

time: 291 us -> 241 us (0.83)
  starting transfers between devices: 109 us -> 61.3 us
  waiting for transfers between devices: 32.8 us -> 21.1 us
  blocking collectives: 120 us -> 131 us
    ppermute x22, starting transfers between devices: 81.5 us -> 46.4 us  [trade(): received.append(lax.ppermute(value, LINE, perm))]
    all_to_all x8 -> x9, blocking collectives: 88.3 us -> 108 us  [exchanged(): return lax.all_to_all(red, LINE, 0, 0, tiled=True)]
    ppermute x7, waiting for transfers between devices: 20.7 us -> 7.92 us  [ring(): return lax.ppermute(block, 'tm', [(s, (s - 1) % n_tm) for s in range(n_tm)])]
    all_gather x1 -> x0, blocking collectives: 9.71 us -> none  [on_device(): heats = lax.all_gather(heat_swings_array[0], 'tm')]
    ppermute x22, waiting for transfers between devices: 5.11 us -> 13.2 us  [trade(): received.append(lax.ppermute(value, LINE, perm))]
    all_to_all x1 -> x0, starting transfers between devices: 7.81 us -> none  [exchanged(): return lax.all_to_all(red, LINE, 0, 0, tiled=True)]
    all_to_all x1 -> x0, waiting for transfers between devices: 6.98 us -> none  [exchanged(): return lax.all_to_all(red, LINE, 0, 0, tiled=True)]
    ppermute x7, starting transfers between devices: 19.4 us -> 14.9 us  [ring(): return lax.ppermute(block, 'tm', [(s, (s - 1) % n_tm) for s in range(n_tm)])]
  transfers between devices with their start and end apart: 30 -> 29, of which waited for: 6 -> 4; matrix products, arithmetic and copies ran while one was open for 0% -> 0% of each run, Pallas kernels for 4% -> 0%
where the time goes in v2:
time: 241 us
  blocking collectives  131 us (54%)
  starting transfers between devices  61.3 us (25%)
  Pallas kernels  25.2 us (10%)
  waiting for transfers between devices  21.1 us (9%)
    all_to_all x9, blocking collectives, exchanged(): return lax.all_to_all(red, LINE, 0, 0, tiled=True)  108 us
    ppermute x22, starting transfers between devices, trade(): received.append(lax.ppermute(value, LINE, perm))  46.4 us
    pallas_call x14, Pallas kernels, call(): pl.pallas_call(kernel, name=name, out_shape=[jax.ShapeDtypeStruct(s, f32)...  25.2 us
    ppermute x7, starting transfers between devices, ring(): return lax.ppermute(block, 'tm', [(s, (s - 1) % n_tm) for s in range(n_tm)])  14.9 us
    ppermute x22, waiting for transfers between devices, trade(): received.append(lax.ppermute(value, LINE, perm))  13.2 us
    all_to_all x1, blocking collectives, on_device(): own = lax.all_to_all(raw, 'gy', 0, 0, tiled=True)  12.8 us
    all_to_all x1, blocking collectives, on_device(): parts = lax.all_to_all(parts, 'gy', 0, 0, tiled=True)  9.62 us
    ppermute x7, waiting for transfers between devices, ring(): return lax.ppermute(block, 'tm', [(s, (s - 1) % n_tm) for s in range(n_tm)])  7.92 us
  transfers between devices with their start and end apart: 29, of which 4 were waited for; matrix products, arithmetic and copies ran while one was open for 0% of the time, Pallas kernels for 0%

profile of v2, /device:TPU:1, one launch (start us, length us, event | category | flops | bytes accessed | tf_op | source)
XLA Modules:
  0.0 240.6 jit_solution(16128469346175544556)
XLA Ops:
  0.1 0.8 copy-done.1
  0.9 1.0 copy-done
  1.9 0.6 spread.1
  2.5 12.8 %all_to_all.55.own_ref = f32[4,5,3,16,128]{4,3,2,1,0:T(8,128)S(1)} all-to-all(f32[4,5,3,16,128]{4,3,2,1,0:T(8,128)S(1)} %spread.1), channel_id=1, replica_groups=mesh['tm'=8,'gx'=8,'gy'=4] {'gy'}, dimensions={0} | all-to-all | bytes 983040 | tf_op jit(solution)/shard_map/all_to_all | solution.py:596
  15.3 5.0 %collective-permute-start.1 = (f32[4,5,3,16,128]{4,3,2,1,0:T(8,128)S(1)}, f32[4,5,3,16,128]{4,3,2,1,0:T(8,128)S(1)}, u32[]{:S(2)}, u32[]{:S(2)}) collective-permute-start(f32[4,5,3,16,128]{4,3,2,1,0:T(8,128)S(1)} %all_to_all.55.own_ref), channel_id=1, source_target_pairs={{1,2},{2,1},{3,7},{4,8},{5,6},{6,5},{7,3},{8,4},{9,10},{10,9},{11,... | collective-permute-start | bytes 1474568 | tf_op jit(solution)/shard_map/ppermute | solution.py:573
  20.5 3.5 %collective-permute-start.3 = (f32[4,2,1,16,128]{4,3,2,1,0:T(8,128)S(1)}, f32[4,2,1,16,128]{4,3,2,1,0:T(8,128)S(1)}, u32[]{:S(2)}, u32[]{:S(2)}) collective-permute-start(f32[4,2,1,16,128]{4,3,2,1,0:T(8,128)S(1)} %get-tuple-element.155), channel_id=1, source_target_pairs={{2,7},{3,6},{4,9},{5,8},{6,3},{7,2},{8,5},{9,4},{10,15},{11,14},{1... | collective-permute-start | bytes 196616 | tf_op jit(solution)/shard_map/ppermute | solution.py:573
  24.0 1.4 collective-permute-start.2
  25.4 9.0 %collective-permute-done.3.odd2_ref = f32[4,2,1,16,128]{4,3,2,1,0:T(8,128)S(1)} collective-permute-done((f32[4,2,1,16,128]{4,3,2,1,0:T(8,128)S(1)}, f32[4,2,1,16,128]{4,3,2,1,0:T(8,128)S(1)}, u32[]{:S(2)}, u32[]{:S(2)}) %collective-permute-start.3) | collective-permute-done | bytes 65568 | tf_op jit(solution)/shard_map/ppermute | solution.py:573
  34.4 1.1 collective-permute-done.2.even2_ref
  35.5 4.2 %start.1 = (f32[10,64,128]{2,1,0:T(8,128)S(1)}, f32[9,64,128]{2,1,0:T(8,128)S(1)}, f32[9,64,128]{2,1,0:T(8,128)S(1)}, f32[9,64,128]{2,1,0:T(8,128)S(1)}, f32[20,...) custom-call(f32[6]{0:T(128)S(1)} %copy-done.5, ...), custom_call_target="tpu_custom_call" | custom-call | tf_op jit(solution)/shard_map/start/pallas_call | solution.py:536
  39.8 3.9 %collective-permute-start.5 = (f32[3,64,128]{2,1,0:T(8,128)S(1)}, f32[3,64,128]{2,1,0:T(8,128)S(1)}, u32[]{:S(2)}, u32[]{:S(2)}) collective-permute-start(f32[3,64,128]{2,1,0:T(8,128)S(1)} %get-tuple-element.91), channel_id=1, source_target_pairs={{1,2},{2,1},{3,7},{4,8},{5,6},{6,5},{7,3},{8,4},{9,10},{10,9},{11,... | collective-permute-start | bytes 294920 | tf_op jit(solution)/shard_map/ppermute | solution.py:573
  43.7 1.3 collective-permute-start.6
  45.1 3.6 %collective-permute-start.7 = (f32[3,64,128]{2,1,0:T(8,128)S(1)}, f32[3,64,128]{2,1,0:T(8,128)S(1)}, u32[]{:S(2)}, u32[]{:S(2)}) collective-permute-start(f32[3,64,128]{2,1,0:T(8,128)S(1)} %get-tuple-element.93), channel_id=1, source_target_pairs={{2,7},{3,6},{4,9},{5,8},{6,3},{7,2},{8,5},{9,4},{10,15},{11,14},{1... | collective-permute-start | bytes 294920 | tf_op jit(solution)/shard_map/ppermute | solution.py:573
  48.6 14.1 %all_to_all.56.red_in = f32[32,1,128]{2,1,0:T(1,128)S(1)} all-to-all(f32[32,1,128]{2,1,0:T(1,128)S(1)} %get-tuple-element.80), channel_id=1, replica_groups=mesh['tm'=8,'gx'=8,'gy'=4] {'gx','gy'}, dimensions={0} | all-to-all | bytes 32768 | tf_op jit(solution)/shard_map/all_to_all | solution.py:577
  62.8 2.6 %second.1 = (f32[12,64,128]{2,1,0:T(8,128)S(1)}, f32[3,64,128]{2,1,0:T(8,128)S(1)}, f32[3,64,128]{2,1,0:T(8,128)S(1)}, f32[3,64,128]{2,1,0:T(8,128)S(1)}, f32[32,1,128]{2,1,0:T(1,128)S(1)}) custom-call(f32[1,2]{1,0:T(1,128)S(1)} %copy-done.4, f32[3]{0:T(128)S(1)} %copy-done.2, f32[3]{0:T(128)S(1)} %copy-done.3, s32[4]{0:T(128)S(1)} %pad_add_fusion.place_ref.refs_2_, ...), custom_call_target="tpu_custom_call" | custom-call | tf_op jit(solution)/shard_map/second/pallas_call | solution.py:536
  65.4 10.7 %all_to_all.57.red_in = f32[32,1,128]{2,1,0:T(1,128)S(1)} all-to-all(f32[32,1,128]{2,1,0:T(1,128)S(1)} %get-tuple-element.94), channel_id=1, replica_groups=mesh['tm'=8,'gx'=8,'gy'=4] {'gx','gy'}, dimensions={0} | all-to-all | bytes 32768 | tf_op jit(solution)/shard_map/all_to_all | solution.py:577
  76.1 0.7 block.1.refs_12_
  76.8 5.7 %collective-permute-start.8 = (f32[776,128]{1,0:T(8,128)S(1)}, f32[776,128]{1,0:T(8,128)S(1)}, u32[]{:S(2)}, u32[]{:S(2)}) collective-permute-start(f32[776,128]{1,0:T(8,128)S(1)} %block.1.refs_12_), channel_id=1, source_target_pairs={{0,224},{32,0},{64,32},{96,64},{128,96},{160,128},{192,160},{224,1... | collective-permute-start | bytes 1191944 | tf_op jit(solution)/shard_map/ppermute | solution.py:580
  82.5 7.9 %collective-permute-done.8.blk_ref = f32[776,128]{1,0:T(8,128)S(1)} collective-permute-done((f32[776,128]{1,0:T(8,128)S(1)}, f32[776,128]{1,0:T(8,128)S(1)}, u32[]{:S(2)}, u32[]{:S(2)}) %collective-permute-start.8) | collective-permute-done | bytes 397344 | tf_op jit(solution)/shard_map/ppermute | solution.py:580
  90.4 0.6 opening.1
  91.0 3.5 %collective-permute-start.11 = (f32[776,128]{1,0:T(8,128)S(1)}, f32[776,128]{1,0:T(8,128)S(1)}, u32[]{:S(2)}, u32[]{:S(2)}) collective-permute-start(f32[776,128]{1,0:T(8,128)S(1)} %collective-permute-done.8.blk_ref), channel_id=1, source_target_pairs={{0,224},{32,0},{64,32},{96,64},{128,96},{160,128},{192,160},{224,1... | collective-permute-start | bytes 1191944 | tf_op jit(solution)/shard_map/ppermute | solution.py:580
  94.8 4.4 %collective-permute-start.10 = (f32[5,64,128]{2,1,0:T(8,128)S(1)}, f32[5,64,128]{2,1,0:T(8,128)S(1)}, u32[]{:S(2)}, u32[]{:S(2)}) collective-permute-start(f32[5,64,128]{2,1,0:T(8,128)S(1)} %get-tuple-element.102), channel_id=1, source_target_pairs={{1,2},{2,1},{3,7},{4,8},{5,6},{6,5},{7,3},{8,4},{9,10},{10,9},{11,... | collective-permute-start | bytes 491528 | tf_op jit(solution)/shard_map/ppermute | solution.py:573
  99.2 3.1 %collective-permute-done.10.refs_5_ = f32[5,64,128]{2,1,0:T(8,128)S(1)} collective-permute-done((f32[5,64,128]{2,1,0:T(8,128)S(1)}, f32[5,64,128]{2,1,0:T(8,128)S(1)}, u32[]{:S(2)}, u32[]{:S(2)}) %collective-permute-start.10) | collective-permute-done | bytes 163872 | tf_op jit(solution)/shard_map/ppermute | solution.py:573
  102.3 1.8 chain2.1
  104.1 2.7 %collective-permute-start.14 = (f32[776,128]{1,0:T(8,128)S(1)}, f32[776,128]{1,0:T(8,128)S(1)}, u32[]{:S(2)}, u32[]{:S(2)}) collective-permute-start(f32[776,128]{1,0:T(8,128)S(1)} %collective-permute-done.11.refs_9_), channel_id=1, source_target_pairs={{0,224},{32,0},{64,32},{96,64},{128,96},{160,128},{192,160},{224,1... | collective-permute-start | bytes 1191944 | tf_op jit(solution)/shard_map/ppermute | solution.py:580
  107.1 5.1 %collective-permute-start.13 = (f32[8,64,128]{2,1,0:T(8,128)S(1)}, f32[8,64,128]{2,1,0:T(8,128)S(1)}, u32[]{:S(2)}, u32[]{:S(2)}) collective-permute-start(f32[8,64,128]{2,1,0:T(8,128)S(1)} %get-tuple-element.111), channel_id=1, source_target_pairs={{1,2},{2,1},{3,7},{4,8},{5,6},{6,5},{7,3},{8,4},{9,10},{10,9},{11,... | collective-permute-start | bytes 786440 | tf_op jit(solution)/shard_map/ppermute | solution.py:573
  112.2 12.1 %all_to_all.58.refs_3_ = f32[32,1,128]{2,1,0:T(1,128)S(1)} all-to-all(f32[32,1,128]{2,1,0:T(1,128)S(1)} %get-tuple-element.105), channel_id=1, replica_groups=mesh['tm'=8,'gx'=8,'gy'=4] {'gx','gy'}, dimensions={0} | all-to-all | bytes 32768 | tf_op jit(solution)/shard_map/all_to_all | solution.py:577
  124.3 2.0 chain3.1
  126.8 3.0 %collective-permute-start.16 = (f32[8,64,128]{2,1,0:T(8,128)S(1)}, f32[8,64,128]{2,1,0:T(8,128)S(1)}, u32[]{:S(2)}, u32[]{:S(2)}) collective-permute-start(f32[8,64,128]{2,1,0:T(8,128)S(1)} %get-tuple-element.119), channel_id=1, source_target_pairs={{1,2},{2,1},{3,7},{4,8},{5,6},{6,5},{7,3},{8,4},{9,10},{10,9},{11,... | collective-permute-start | bytes 786440 | tf_op jit(solution)/shard_map/ppermute | solution.py:573
  129.8 12.1 %all_to_all.59.refs_3_ = f32[32,1,128]{2,1,0:T(1,128)S(1)} all-to-all(f32[32,1,128]{2,1,0:T(1,128)S(1)} %get-tuple-element.113), channel_id=1, replica_groups=mesh['tm'=8,'gx'=8,'gy'=4] {'gx','gy'}, dimensions={0} | all-to-all | bytes 32768 | tf_op jit(solution)/shard_map/all_to_all | solution.py:577
  142.0 2.0 chain4.1
  144.5 3.0 %collective-permute-start.19 = (f32[8,64,128]{2,1,0:T(8,128)S(1)}, f32[8,64,128]{2,1,0:T(8,128)S(1)}, u32[]{:S(2)}, u32[]{:S(2)}) collective-permute-start(f32[8,64,128]{2,1,0:T(8,128)S(1)} %get-tuple-element.127), channel_id=1, source_target_pairs={{1,2},{2,1},{3,7},{4,8},{5,6},{6,5},{7,3},{8,4},{9,10},{10,9},{11,... | collective-permute-start | bytes 786440 | tf_op jit(solution)/shard_map/ppermute | solution.py:573
  147.5 12.1 %all_to_all.60.refs_3_ = f32[32,1,128]{2,1,0:T(1,128)S(1)} all-to-all(f32[32,1,128]{2,1,0:T(1,128)S(1)} %get-tuple-element.121), channel_id=1, replica_groups=mesh['tm'=8,'gx'=8,'gy'=4] {'gx','gy'}, dimensions={0} | all-to-all | bytes 32768 | tf_op jit(solution)/shard_map/all_to_all | solution.py:577
  159.6 2.0 chain5.1
  162.1 3.3 %collective-permute-start.22 = (f32[8,64,128]{2,1,0:T(8,128)S(1)}, f32[8,64,128]{2,1,0:T(8,128)S(1)}, u32[]{:S(2)}, u32[]{:S(2)}) collective-permute-start(f32[8,64,128]{2,1,0:T(8,128)S(1)} %get-tuple-element.135), channel_id=1, source_target_pairs={{1,2},{2,1},{3,7},{4,8},{5,6},{6,5},{7,3},{8,4},{9,10},{10,9},{11,... | collective-permute-start | bytes 786440 | tf_op jit(solution)/shard_map/ppermute | solution.py:573
  165.5 12.1 %all_to_all.61.refs_3_ = f32[32,1,128]{2,1,0:T(1,128)S(1)} all-to-all(f32[32,1,128]{2,1,0:T(1,128)S(1)} %get-tuple-element.129), channel_id=1, replica_groups=mesh['tm'=8,'gx'=8,'gy'=4] {'gx','gy'}, dimensions={0} | all-to-all | bytes 32768 | tf_op jit(solution)/shard_map/all_to_all | solution.py:577
  177.6 2.0 chain6.1
  179.6 2.7 %collective-permute-start.26 = (f32[776,128]{1,0:T(8,128)S(1)}, f32[776,128]{1,0:T(8,128)S(1)}, u32[]{:S(2)}, u32[]{:S(2)}) collective-permute-start(f32[776,128]{1,0:T(8,128)S(1)} %collective-permute-done.23.refs_12_), channel_id=1, source_target_pairs={{0,224},{32,0},{64,32},{96,64},{128,96},{160,128},{192,160},{224,1... | collective-permute-start | bytes 1191944 | tf_op jit(solution)/shard_map/ppermute | solution.py:580
  182.6 3.3 %collective-permute-start.25 = (f32[8,64,128]{2,1,0:T(8,128)S(1)}, f32[8,64,128]{2,1,0:T(8,128)S(1)}, u32[]{:S(2)}, u32[]{:S(2)}) collective-permute-start(f32[8,64,128]{2,1,0:T(8,128)S(1)} %get-tuple-element.143), channel_id=1, source_target_pairs={{1,2},{2,1},{3,7},{4,8},{5,6},{6,5},{7,3},{8,4},{9,10},{10,9},{11,... | collective-permute-start | bytes 786440 | tf_op jit(solution)/shard_map/ppermute | solution.py:573
  185.9 12.1 %all_to_all.62.refs_3_ = f32[32,1,128]{2,1,0:T(1,128)S(1)} all-to-all(f32[32,1,128]{2,1,0:T(1,128)S(1)} %get-tuple-element.137), channel_id=1, replica_groups=mesh['tm'=8,'gx'=8,'gy'=4] {'gx','gy'}, dimensions={0} | all-to-all | bytes 32768 | tf_op jit(solution)/shard_map/all_to_all | solution.py:577
  198.1 2.0 chain7.1
  200.5 3.0 %collective-permute-start.28 = (f32[8,64,128]{2,1,0:T(8,128)S(1)}, f32[8,64,128]{2,1,0:T(8,128)S(1)}, u32[]{:S(2)}, u32[]{:S(2)}) collective-permute-start(f32[8,64,128]{2,1,0:T(8,128)S(1)} %get-tuple-element.150), channel_id=1, source_target_pairs={{1,2},{2,1},{3,7},{4,8},{5,6},{6,5},{7,3},{8,4},{9,10},{10,9},{11,... | collective-permute-start | bytes 786440 | tf_op jit(solution)/shard_map/ppermute | solution.py:573
  203.5 12.1 %all_to_all.63.refs_3_ = f32[32,1,128]{2,1,0:T(1,128)S(1)} all-to-all(f32[32,1,128]{2,1,0:T(1,128)S(1)} %get-tuple-element.145), channel_id=1, replica_groups=mesh['tm'=8,'gx'=8,'gy'=4] {'gx','gy'}, dimensions={0} | all-to-all | bytes 32768 | tf_op jit(solution)/shard_map/all_to_all | solution.py:577
  215.6 2.6 %chain8.1 = (f32[12,64,128]{2,1,0:T(8,128)S(1)}, f32[7,64,128]{2,1,0:T(8,128)S(1)}, f32[5,64,128]{2,1,0:T(8,128)S(1)}, f32[8,64,128]{2,1,0:T(8,128)}, f32[8,64,128]{2,1,0:T(8,128)}, /*index=5*/f32[32,1,128]{2,1,0:T(1,128)S(1)}) custom-call(f32[3]{0:T(128)S(1)} %copy-done.2, f32[3]{0:T(128)S(1)} %copy-done.3, s32[4]{0:T(128)S(1)} %pad_add_fusion.place_ref.refs_2_, ...), custom_call_target="tpu_custom_call" | custom-call | tf_op jit(solution)/shard_map/chain8/pallas_call | solution.py:536
  218.2 10.7 %all_to_all.64.red_in = f32[32,1,128]{2,1,0:T(1,128)S(1)} all-to-all(f32[32,1,128]{2,1,0:T(1,128)S(1)} %get-tuple-element.151), channel_id=1, replica_groups=mesh['tm'=8,'gx'=8,'gy'=4] {'gx','gy'}, dimensions={0} | all-to-all | bytes 32768 | tf_op jit(solution)/shard_map/all_to_all | solution.py:577
  228.9 0.7 closing.1
  229.6 9.6 %all_to_all.65.parts_ref = f32[4,4,3,16,128]{4,3,2,1,0:T(8,128)S(1)} all-to-all(f32[4,4,3,16,128]{4,3,2,1,0:T(8,128)S(1)} %closing.1), channel_id=1, replica_groups=mesh['tm'=8,'gx'=8,'gy'=4] {'gy'}, dimensions={0} | all-to-all | bytes 786432 | tf_op jit(solution)/shard_map/all_to_all | solution.py:666
  239.3 1.3 gather.1
  (51 shorter events, 3.0 us)
Async XLA Ops:
  0.0 0.9 copy-start.1
  0.9 1.0 copy-start
  15.3 20.2 %collective-permute-start.1 = (f32[4,5,3,16,128]{4,3,2,1,0:T(8,128)S(1)}, f32[4,5,3,16,128]{4,3,2,1,0:T(8,128)S(1)}, u32[]{:S(2)}, u32[]{:S(2)}) collective-permute-start(f32[4,5,3,16,128]{4,3,2,1,0:T(8,128)S(1)} %all_to_all.55.own_ref), channel_id=1, source_target_pairs={{1,2},{2,1},{3,7},{4,8},{5,6},{6,5},{7,3},{8,4},{9,10},{10,9},{11,... | collective-permute-start | bytes 1474568 | tf_op jit(solution)/shard_map/ppermute | solution.py:573
  20.3 15.2 %collective-permute-start = (f32[4,5,3,16,128]{4,3,2,1,0:T(8,128)S(1)}, f32[4,5,3,16,128]{4,3,2,1,0:T(8,128)S(1)}, u32[]{:S(2)}, u32[]{:S(2)}) collective-permute-start(f32[4,5,3,16,128]{4,3,2,1,0:T(8,128)S(1)} %all_to_all.55.own_ref), channel_id=1, source_target_pairs={{0,1},{1,0},{2,3},{3,2},{4,5},{5,4},{6,7},{7,6},{8,9},{9,8},{10,11... | collective-permute-start | bytes 1474568 | tf_op jit(solution)/shard_map/ppermute | solution.py:573
  20.4 15.0 %copy-start.5 = (f32[6]{0:T(128)S(1)}, f32[6]{0:T(128)}, u32[]{:S(2)}) copy-start(f32[6]{0:T(128)} %rigid_ref.1) | copy-start | bytes 76
  20.4 15.0 %copy-start.6 = (f32[6]{0:T(128)S(1)}, f32[6]{0:T(128)}, u32[]{:S(2)}) copy-start(f32[6]{0:T(128)} %dilate_ref.1) | copy-start | bytes 76
  20.4 15.0 %copy-start.2 = (f32[3]{0:T(128)S(1)}, f32[3]{0:T(128)}, u32[]{:S(2)}) copy-start(f32[3]{0:T(128)} %coef_ref.9) | copy-start | bytes 40
  20.5 15.0 %copy-start.3 = (f32[3]{0:T(128)S(1)}, f32[3]{0:T(128)}, u32[]{:S(2)}) copy-start(f32[3]{0:T(128)} %time_ref.9) | copy-start | bytes 40
  20.5 15.0 %copy-start.4 = (f32[1,2]{1,0:T(1,128)S(1)}, f32[1,2]{1,0:T(1,128)}, u32[]{:S(2)}) copy-start(f32[1,2]{1,0:T(1,128)} %heat_ref.5) | copy-start | bytes 28
  20.5 13.9 %collective-permute-start.3 = (f32[4,2,1,16,128]{4,3,2,1,0:T(8,128)S(1)}, f32[4,2,1,16,128]{4,3,2,1,0:T(8,128)S(1)}, u32[]{:S(2)}, u32[]{:S(2)}) collective-permute-start(f32[4,2,1,16,128]{4,3,2,1,0:T(8,128)S(1)} %get-tuple-element.155), channel_id=1, source_target_pairs={{2,7},{3,6},{4,9},{5,8},{6,3},{7,2},{8,5},{9,4},{10,15},{11,14},{1... | collective-permute-start | bytes 196616 | tf_op jit(solution)/shard_map/ppermute | solution.py:573
  24.0 11.5 %collective-permute-start.2 = (f32[4,2,1,16,128]{4,3,2,1,0:T(8,128)S(1)}, f32[4,2,1,16,128]{4,3,2,1,0:T(8,128)S(1)}, u32[]{:S(2)}, u32[]{:S(2)}) collective-permute-start(f32[4,2,1,16,128]{4,3,2,1,0:T(8,128)S(1)} %get-tuple-element.156), channel_id=1, source_target_pairs={{0,2},{1,3},{2,0},{3,1},{4,6},{5,7},{6,4},{7,5},{8,10},{9,11},{10,... | collective-permute-start | bytes 196616 | tf_op jit(solution)/shard_map/ppermute | solution.py:573
  39.7 23.1 %collective-permute-start.4 = (f32[3,64,128]{2,1,0:T(8,128)S(1)}, f32[3,64,128]{2,1,0:T(8,128)S(1)}, u32[]{:S(2)}, u32[]{:S(2)}) collective-permute-start(f32[3,64,128]{2,1,0:T(8,128)S(1)} %get-tuple-element.90), channel_id=1, source_target_pairs={{0,1},{1,0},{2,3},{3,2},{4,5},{5,4},{6,7},{7,6},{8,9},{9,8},{10,11... | collective-permute-start | bytes 294920 | tf_op jit(solution)/shard_map/ppermute | solution.py:573
  39.8 22.9 %collective-permute-start.5 = (f32[3,64,128]{2,1,0:T(8,128)S(1)}, f32[3,64,128]{2,1,0:T(8,128)S(1)}, u32[]{:S(2)}, u32[]{:S(2)}) collective-permute-start(f32[3,64,128]{2,1,0:T(8,128)S(1)} %get-tuple-element.91), channel_id=1, source_target_pairs={{1,2},{2,1},{3,7},{4,8},{5,6},{6,5},{7,3},{8,4},{9,10},{10,9},{11,... | collective-permute-start | bytes 294920 | tf_op jit(solution)/shard_map/ppermute | solution.py:573
  43.7 19.1 %collective-permute-start.6 = (f32[3,64,128]{2,1,0:T(8,128)S(1)}, f32[3,64,128]{2,1,0:T(8,128)S(1)}, u32[]{:S(2)}, u32[]{:S(2)}) collective-permute-start(f32[3,64,128]{2,1,0:T(8,128)S(1)} %get-tuple-element.92), channel_id=1, source_target_pairs={{0,2},{1,3},{2,0},{3,1},{4,6},{5,7},{6,4},{7,5},{8,10},{9,11},{10,... | collective-permute-start | bytes 294920 | tf_op jit(solution)/shard_map/ppermute | solution.py:573
  45.1 17.7 %collective-permute-start.7 = (f32[3,64,128]{2,1,0:T(8,128)S(1)}, f32[3,64,128]{2,1,0:T(8,128)S(1)}, u32[]{:S(2)}, u32[]{:S(2)}) collective-permute-start(f32[3,64,128]{2,1,0:T(8,128)S(1)} %get-tuple-element.93), channel_id=1, source_target_pairs={{2,7},{3,6},{4,9},{5,8},{6,3},{7,2},{8,5},{9,4},{10,15},{11,14},{1... | collective-permute-start | bytes 294920 | tf_op jit(solution)/shard_map/ppermute | solution.py:573
  76.8 13.6 %collective-permute-start.8 = (f32[776,128]{1,0:T(8,128)S(1)}, f32[776,128]{1,0:T(8,128)S(1)}, u32[]{:S(2)}, u32[]{:S(2)}) collective-permute-start(f32[776,128]{1,0:T(8,128)S(1)} %block.1.refs_12_), channel_id=1, source_target_pairs={{0,224},{32,0},{64,32},{96,64},{128,96},{160,128},{192,160},{224,1... | collective-permute-start | bytes 1191944 | tf_op jit(solution)/shard_map/ppermute | solution.py:580
  91.0 11.3 %collective-permute-start.11 = (f32[776,128]{1,0:T(8,128)S(1)}, f32[776,128]{1,0:T(8,128)S(1)}, u32[]{:S(2)}, u32[]{:S(2)}) collective-permute-start(f32[776,128]{1,0:T(8,128)S(1)} %collective-permute-done.8.blk_ref), channel_id=1, source_target_pairs={{0,224},{32,0},{64,32},{96,64},{128,96},{160,128},{192,160},{224,1... | collective-permute-start | bytes 1191944 | tf_op jit(solution)/shard_map/ppermute | solution.py:580
  94.5 4.7 %collective-permute-start.9 = (f32[5,64,128]{2,1,0:T(8,128)S(1)}, f32[5,64,128]{2,1,0:T(8,128)S(1)}, u32[]{:S(2)}, u32[]{:S(2)}) collective-permute-start(f32[5,64,128]{2,1,0:T(8,128)S(1)} %get-tuple-element.101), channel_id=1, source_target_pairs={{0,1},{1,0},{2,3},{3,2},{4,5},{5,4},{6,7},{7,6},{8,9},{9,8},{10,11... | collective-permute-start | bytes 491528 | tf_op jit(solution)/shard_map/ppermute | solution.py:573
  94.8 7.5 %collective-permute-start.10 = (f32[5,64,128]{2,1,0:T(8,128)S(1)}, f32[5,64,128]{2,1,0:T(8,128)S(1)}, u32[]{:S(2)}, u32[]{:S(2)}) collective-permute-start(f32[5,64,128]{2,1,0:T(8,128)S(1)} %get-tuple-element.102), channel_id=1, source_target_pairs={{1,2},{2,1},{3,7},{4,8},{5,6},{6,5},{7,3},{8,4},{9,10},{10,9},{11,... | collective-permute-start | bytes 491528 | tf_op jit(solution)/shard_map/ppermute | solution.py:573
  104.1 20.2 %collective-permute-start.14 = (f32[776,128]{1,0:T(8,128)S(1)}, f32[776,128]{1,0:T(8,128)S(1)}, u32[]{:S(2)}, u32[]{:S(2)}) collective-permute-start(f32[776,128]{1,0:T(8,128)S(1)} %collective-permute-done.11.refs_9_), channel_id=1, source_target_pairs={{0,224},{32,0},{64,32},{96,64},{128,96},{160,128},{192,160},{224,1... | collective-permute-start | bytes 1191944 | tf_op jit(solution)/shard_map/ppermute | solution.py:580
  106.8 17.5 %collective-permute-start.12 = (f32[8,64,128]{2,1,0:T(8,128)S(1)}, f32[8,64,128]{2,1,0:T(8,128)S(1)}, u32[]{:S(2)}, u32[]{:S(2)}) collective-permute-start(f32[8,64,128]{2,1,0:T(8,128)S(1)} %get-tuple-element.110), channel_id=1, source_target_pairs={{0,1},{1,0},{2,3},{3,2},{4,5},{5,4},{6,7},{7,6},{8,9},{9,8},{10,11... | collective-permute-start | bytes 786440 | tf_op jit(solution)/shard_map/ppermute | solution.py:573
  107.1 17.3 %collective-permute-start.13 = (f32[8,64,128]{2,1,0:T(8,128)S(1)}, f32[8,64,128]{2,1,0:T(8,128)S(1)}, u32[]{:S(2)}, u32[]{:S(2)}) collective-permute-start(f32[8,64,128]{2,1,0:T(8,128)S(1)} %get-tuple-element.111), channel_id=1, source_target_pairs={{1,2},{2,1},{3,7},{4,8},{5,6},{6,5},{7,3},{8,4},{9,10},{10,9},{11,... | collective-permute-start | bytes 786440 | tf_op jit(solution)/shard_map/ppermute | solution.py:573
  126.3 15.7 %collective-permute-start.17 = (f32[776,128]{1,0:T(8,128)S(1)}, f32[776,128]{1,0:T(8,128)S(1)}, u32[]{:S(2)}, u32[]{:S(2)}) collective-permute-start(f32[776,128]{1,0:T(8,128)S(1)} %collective-permute-done.14.refs_12_), channel_id=1, source_target_pairs={{0,224},{32,0},{64,32},{96,64},{128,96},{160,128},{192,160},{224,1... | collective-permute-start | bytes 1191944 | tf_op jit(solution)/shard_map/ppermute | solution.py:580
  126.4 15.6 %collective-permute-start.15 = (f32[8,64,128]{2,1,0:T(8,128)S(1)}, f32[8,64,128]{2,1,0:T(8,128)S(1)}, u32[]{:S(2)}, u32[]{:S(2)}) collective-permute-start(f32[8,64,128]{2,1,0:T(8,128)S(1)} %get-tuple-element.118), channel_id=1, source_target_pairs={{0,1},{1,0},{2,3},{3,2},{4,5},{5,4},{6,7},{7,6},{8,9},{9,8},{10,11... | collective-permute-start | bytes 786440 | tf_op jit(solution)/shard_map/ppermute | solution.py:573
  126.8 15.2 %collective-permute-start.16 = (f32[8,64,128]{2,1,0:T(8,128)S(1)}, f32[8,64,128]{2,1,0:T(8,128)S(1)}, u32[]{:S(2)}, u32[]{:S(2)}) collective-permute-start(f32[8,64,128]{2,1,0:T(8,128)S(1)} %get-tuple-element.119), channel_id=1, source_target_pairs={{1,2},{2,1},{3,7},{4,8},{5,6},{6,5},{7,3},{8,4},{9,10},{10,9},{11,... | collective-permute-start | bytes 786440 | tf_op jit(solution)/shard_map/ppermute | solution.py:573
  144.0 15.7 %collective-permute-start.20 = (f32[776,128]{1,0:T(8,128)S(1)}, f32[776,128]{1,0:T(8,128)S(1)}, u32[]{:S(2)}, u32[]{:S(2)}) collective-permute-start(f32[776,128]{1,0:T(8,128)S(1)} %collective-permute-done.17.refs_12_), channel_id=1, source_target_pairs={{0,224},{32,0},{64,32},{96,64},{128,96},{160,128},{192,160},{224,1... | collective-permute-start | bytes 1191944 | tf_op jit(solution)/shard_map/ppermute | solution.py:580
  144.1 15.6 %collective-permute-start.18 = (f32[8,64,128]{2,1,0:T(8,128)S(1)}, f32[8,64,128]{2,1,0:T(8,128)S(1)}, u32[]{:S(2)}, u32[]{:S(2)}) collective-permute-start(f32[8,64,128]{2,1,0:T(8,128)S(1)} %get-tuple-element.126), channel_id=1, source_target_pairs={{0,1},{1,0},{2,3},{3,2},{4,5},{5,4},{6,7},{7,6},{8,9},{9,8},{10,11... | collective-permute-start | bytes 786440 | tf_op jit(solution)/shard_map/ppermute | solution.py:573
  144.5 15.2 %collective-permute-start.19 = (f32[8,64,128]{2,1,0:T(8,128)S(1)}, f32[8,64,128]{2,1,0:T(8,128)S(1)}, u32[]{:S(2)}, u32[]{:S(2)}) collective-permute-start(f32[8,64,128]{2,1,0:T(8,128)S(1)} %get-tuple-element.127), channel_id=1, source_target_pairs={{1,2},{2,1},{3,7},{4,8},{5,6},{6,5},{7,3},{8,4},{9,10},{10,9},{11,... | collective-permute-start | bytes 786440 | tf_op jit(solution)/shard_map/ppermute | solution.py:573
  161.7 16.0 %collective-permute-start.23 = (f32[776,128]{1,0:T(8,128)S(1)}, f32[776,128]{1,0:T(8,128)S(1)}, u32[]{:S(2)}, u32[]{:S(2)}) collective-permute-start(f32[776,128]{1,0:T(8,128)S(1)} %collective-permute-done.20.refs_12_), channel_id=1, source_target_pairs={{0,224},{32,0},{64,32},{96,64},{128,96},{160,128},{192,160},{224,1... | collective-permute-start | bytes 1191944 | tf_op jit(solution)/shard_map/ppermute | solution.py:580
  161.9 15.7 %collective-permute-start.21 = (f32[8,64,128]{2,1,0:T(8,128)S(1)}, f32[8,64,128]{2,1,0:T(8,128)S(1)}, u32[]{:S(2)}, u32[]{:S(2)}) collective-permute-start(f32[8,64,128]{2,1,0:T(8,128)S(1)} %get-tuple-element.134), channel_id=1, source_target_pairs={{0,1},{1,0},{2,3},{3,2},{4,5},{5,4},{6,7},{7,6},{8,9},{9,8},{10,11... | collective-permute-start | bytes 786440 | tf_op jit(solution)/shard_map/ppermute | solution.py:573
  162.1 15.5 %collective-permute-start.22 = (f32[8,64,128]{2,1,0:T(8,128)S(1)}, f32[8,64,128]{2,1,0:T(8,128)S(1)}, u32[]{:S(2)}, u32[]{:S(2)}) collective-permute-start(f32[8,64,128]{2,1,0:T(8,128)S(1)} %get-tuple-element.135), channel_id=1, source_target_pairs={{1,2},{2,1},{3,7},{4,8},{5,6},{6,5},{7,3},{8,4},{9,10},{10,9},{11,... | collective-permute-start | bytes 786440 | tf_op jit(solution)/shard_map/ppermute | solution.py:573
  179.6 18.5 %collective-permute-start.26 = (f32[776,128]{1,0:T(8,128)S(1)}, f32[776,128]{1,0:T(8,128)S(1)}, u32[]{:S(2)}, u32[]{:S(2)}) collective-permute-start(f32[776,128]{1,0:T(8,128)S(1)} %collective-permute-done.23.refs_12_), channel_id=1, source_target_pairs={{0,224},{32,0},{64,32},{96,64},{128,96},{160,128},{192,160},{224,1... | collective-permute-start | bytes 1191944 | tf_op jit(solution)/shard_map/ppermute | solution.py:580
  182.3 15.7 %collective-permute-start.24 = (f32[8,64,128]{2,1,0:T(8,128)S(1)}, f32[8,64,128]{2,1,0:T(8,128)S(1)}, u32[]{:S(2)}, u32[]{:S(2)}) collective-permute-start(f32[8,64,128]{2,1,0:T(8,128)S(1)} %get-tuple-element.142), channel_id=1, source_target_pairs={{0,1},{1,0},{2,3},{3,2},{4,5},{5,4},{6,7},{7,6},{8,9},{9,8},{10,11... | collective-permute-start | bytes 786440 | tf_op jit(solution)/shard_map/ppermute | solution.py:573
  182.6 15.5 %collective-permute-start.25 = (f32[8,64,128]{2,1,0:T(8,128)S(1)}, f32[8,64,128]{2,1,0:T(8,128)S(1)}, u32[]{:S(2)}, u32[]{:S(2)}) collective-permute-start(f32[8,64,128]{2,1,0:T(8,128)S(1)} %get-tuple-element.143), channel_id=1, source_target_pairs={{1,2},{2,1},{3,7},{4,8},{5,6},{6,5},{7,3},{8,4},{9,10},{10,9},{11,... | collective-permute-start | bytes 786440 | tf_op jit(solution)/shard_map/ppermute | solution.py:573
  200.1 15.6 %collective-permute-start.27 = (f32[8,64,128]{2,1,0:T(8,128)S(1)}, f32[8,64,128]{2,1,0:T(8,128)S(1)}, u32[]{:S(2)}, u32[]{:S(2)}) collective-permute-start(f32[8,64,128]{2,1,0:T(8,128)S(1)} %get-tuple-element.149), channel_id=1, source_target_pairs={{0,1},{1,0},{2,3},{3,2},{4,5},{5,4},{6,7},{7,6},{8,9},{9,8},{10,11... | collective-permute-start | bytes 786440 | tf_op jit(solution)/shard_map/ppermute | solution.py:573
  200.5 15.2 %collective-permute-start.28 = (f32[8,64,128]{2,1,0:T(8,128)S(1)}, f32[8,64,128]{2,1,0:T(8,128)S(1)}, u32[]{:S(2)}, u32[]{:S(2)}) collective-permute-start(f32[8,64,128]{2,1,0:T(8,128)S(1)} %get-tuple-element.150), channel_id=1, source_target_pairs={{1,2},{2,1},{3,7},{4,8},{5,6},{6,5},{7,3},{8,4},{9,10},{10,9},{11,... | collective-permute-start | bytes 786440 | tf_op jit(solution)/shard_map/ppermute | solution.py:573

commit v3 on v2

--- a/solution.py
+++ b/solution.py
@@ -504,27 +504,39 @@
                 out_ref[q, at, i] = field[q * rows : (q + 1) * rows]
 
 
-def layers_of(place_ref, q, chunks):
-    return jnp.where(place_ref[3] == 0, q, chunks - 1 - q) * L
-
-
-def gather_kernel(place_ref, parts_ref, out_ref):
-    chunks = parts_ref.shape[0]
-    for q in range(chunks):
-        first = layers_of(place_ref, q, chunks)
+def chip_of(place_ref, x, chips):
+    return jnp.where(place_ref[3] == 0, x, chips - 1 - x)
+
+
+def spread_kernel(place_ref, label_ref, values_ref, keep_out, send_out):
+    core = place_ref[1]
+    for j in range(keep_out.shape[0]):
+        for out_ref, first in ((keep_out, (2 * j + core) * L), (send_out, (2 * j + 1 - core) * L)):
+            for i in range(L):
+                out_ref[j, 0, i] = label_ref[first + i].astype(jnp.float32) + 1.0
+                for field in range(1 + PRONY):
+                    out_ref[j, 1 + field, i] = values_ref[0, field, first + i]
+
+
+def join_kernel(place_ref, keep_ref, got_ref, out_ref):
+    core, chips, half = place_ref[1], out_ref.shape[0], keep_ref.shape[0]
+    for j in range(half):
+        for ref, x in ((keep_ref, half * core + j), (got_ref, half * (1 - core) + j)):
+            to = chip_of(place_ref, x, chips)
+            for field in range(2 + PRONY):
+                for i in range(L):
+                    out_ref[to, field, i] = ref[j, field, i]
+
+
+def gather_kernel(place_ref, parts_ref, got_ref, out_ref):
+    core, chips, half = place_ref[1], parts_ref.shape[0], got_ref.shape[0]
+    for j in range(half):
+        own = chip_of(place_ref, half * core + j, chips)
+        other = jnp.where(place_ref[3] == 0, j, half - 1 - j)
         for i in range(L):
             for field in range(1 + PRONY):
-                out_ref[0, field, first + i] = parts_ref[q, field, i]
-
-
-def spread_kernel(place_ref, label_ref, values_ref, out_ref):
-    chunks = out_ref.shape[0]
-    for q in range(chunks):
-        first = layers_of(place_ref, q, chunks)
-        for i in range(L):
-            out_ref[q, 0, i] = label_ref[first + i].astype(jnp.float32) + 1.0
-            for field in range(1 + PRONY):
-                out_ref[q, 1 + field, i] = values_ref[0, field, first + i]
+                out_ref[0, field, (2 * j + core) * L + i] = parts_ref[own, field, i]
+                out_ref[0, field, (2 * j + 1 - core) * L + i] = got_ref[other, field, i]
 
 
 SMEM = pl.BlockSpec(memory_space=pltpu.SMEM)
@@ -561,8 +573,12 @@
     plane = (ny, nz)
 
     def device(position):
-        row, column = divmod(position, n_gy)
-        return row * n_gy + (column if row % 2 == 0 else n_gy - 1 - column)
+        row, rest = divmod(position, 2 * n_gy)
+        x, core = divmod(rest, 2)
+        return (2 * row + core) * n_gy + (x if row % 2 == 0 else n_gy - 1 - x)
+
+    def other_core(value):
+        return lax.ppermute(value, "gx", [(p, p ^ 1) for p in range(line // n_gy)])
 
     def trade(even, odd, by):
         received = []
@@ -580,23 +596,30 @@
         return lax.ppermute(block, "tm", [(s, (s - 1) % n_tm) for s in range(n_tm)])
 
     gx, gy = lax.axis_index("gx"), lax.axis_index("gy")
-    flip = gx % 2
-    position = gx * n_gy + jnp.where(flip == 0, gy, n_gy - 1 - gy)
-    place = jnp.stack([lax.axis_index("tm"), position % 2, position // 2 % 2, flip])
-    place = place.astype(jnp.int32)
+    core, flip = gx % 2, gx // 2 % 2
+    x = jnp.where(flip == 0, gy, n_gy - 1 - gy)
+    place = jnp.stack([lax.axis_index("tm"), core, x % 2, flip]).astype(jnp.int32)
     prony_args = (prony_coefficients, prony_decay_times)
 
-    (raw,) = call(
+    half = n_gy // 2
+    keep, give = call(
         spread_kernel,
         "spread",
         (place,),
         (cell_material_label, segment_opening_values),
+        [(half, 2 + PRONY, L, ny_part, nz)] * 2,
+    )
+    (raw,) = call(
+        join_kernel,
+        "join",
+        (place,),
+        (keep, other_core(give)),
         [(n_gy, 2 + PRONY, L, ny_part, nz)],
     )
     own = lax.all_to_all(raw, "gy", 0, 0, tiled=True)
     near = trade(own, own, 1)
     top, bottom = own[:, :2, L - 1 :], own[:, :2, :1]
-    upward = position // 2 % 2 == 0
+    upward = x % 2 == 0
     far = trade(jnp.where(upward, top, bottom), jnp.where(upward, bottom, top), 2)
 
     red_shape = (line, 1, 128)
@@ -664,8 +687,11 @@
         [(n_gy, 1 + PRONY, L, ny_part, nz)],
     )
     parts = lax.all_to_all(parts, "gy", 0, 0, tiled=True)
+    first = half * (1 - core)
+    first = jnp.where(flip == 0, first, n_gy - half - first)
+    got = other_core(lax.dynamic_slice_in_dim(parts, first, half, 0))
     (out,) = call(
-        gather_kernel, "gather", (place,), (parts,), [(1, 1 + PRONY, nx, ny_part, nz)]
+        gather_kernel, "gather", (place,), (parts, got), [(1, 1 + PRONY, nx, ny_part, nz)]
     )
     return out
 

time: 241 us -> 230 us (0.954)
  blocking collectives: 131 us -> 117 us
  waiting for transfers between devices: 21.1 us -> 25.5 us
  starting transfers between devices: 61.3 us -> 58.3 us
    ppermute x22, starting transfers between devices: 46.4 us -> 35.4 us  [trade(): received.append(lax.ppermute(value, LINE, perm))]
    all_to_all x1 -> x0, blocking collectives: 9.62 us -> none  [on_device(): parts = lax.all_to_all(parts, 'gy', 0, 0, tiled=True)]
    all_to_all x0 -> x1, waiting for transfers between devices: none -> 7.17 us  [on_device(): parts = lax.all_to_all(parts, 'gy', 0, 0, tiled=True)]
    ppermute x0 -> x2, starting transfers between devices: none -> 5.22 us  [other_core(): return lax.ppermute(value, 'gx', [(p, p ^ 1) for p in range(line // n_gy)])]
    ppermute x22, waiting for transfers between devices: 13.2 us -> 8.18 us  [trade(): received.append(lax.ppermute(value, LINE, perm))]
    all_to_all x0 -> x1, starting transfers between devices: none -> 3.46 us  [on_device(): parts = lax.all_to_all(parts, 'gy', 0, 0, tiled=True)]
    all_to_all x9, blocking collectives: 108 us -> 106 us  [exchanged(): return lax.all_to_all(red, LINE, 0, 0, tiled=True)]
    pallas_call x14 -> x15, Pallas kernels: 25.2 us -> 26.5 us  [call(): pl.pallas_call(kernel, name=name, out_shape=[jax.ShapeDtypeStruct(s, f32)...]
  transfers between devices with their start and end apart: 29 -> 32, of which waited for: 4 -> 7; matrix products, arithmetic and copies ran while one was open for 0% -> 0% of each run, Pallas kernels for 0% -> 0%
where the time goes in v3:
time: 230 us
  blocking collectives  117 us (51%)
  starting transfers between devices  58.3 us (25%)
  Pallas kernels  26.5 us (12%)
  waiting for transfers between devices  25.5 us (11%)
    all_to_all x9, blocking collectives, exchanged(): return lax.all_to_all(red, LINE, 0, 0, tiled=True)  106 us
    ppermute x22, starting transfers between devices, trade(): received.append(lax.ppermute(value, LINE, perm))  35.4 us
    pallas_call x15, Pallas kernels, call(): pl.pallas_call(kernel, name=name, out_shape=[jax.ShapeDtypeStruct(s, f32)...  26.5 us
    ppermute x7, starting transfers between devices, ring(): return lax.ppermute(block, 'tm', [(s, (s - 1) % n_tm) for s in range(n_tm)])  14.3 us
    all_to_all x1, blocking collectives, on_device(): own = lax.all_to_all(raw, 'gy', 0, 0, tiled=True)  11.3 us
    ppermute x22, waiting for transfers between devices, trade(): received.append(lax.ppermute(value, LINE, perm))  8.18 us
    ppermute x7, waiting for transfers between devices, ring(): return lax.ppermute(block, 'tm', [(s, (s - 1) % n_tm) for s in range(n_tm)])  7.92 us
    all_to_all x1, waiting for transfers between devices, on_device(): parts = lax.all_to_all(parts, 'gy', 0, 0, tiled=True)  7.17 us
  transfers between devices with their start and end apart: 32, of which 7 were waited for; matrix products, arithmetic and copies ran while one was open for 0% of the time, Pallas kernels for 0%

profile of v3, /device:TPU:1, one launch (start us, length us, event | category | flops | bytes accessed | tf_op | source)
XLA Modules:
  0.0 229.6 jit_solution(6699544280658755849)
XLA Ops:
  0.9 1.0 copy-done
  2.5 3.3 %collective-permute-start = (f32[2,5,3,16,128]{4,3,2,1,0:T(8,128)S(1)}, f32[2,5,3,16,128]{4,3,2,1,0:T(8,128)S(1)}, u32[]{:S(2)}, u32[]{:S(2)}) collective-permute-start(f32[2,5,3,16,128]{4,3,2,1,0:T(8,128)S(1)} %get-tuple-element.83), channel_id=1, source_target_pairs={{0,4},{4,0},{8,12},{12,8},{16,20},{20,16},{24,28},{28,24},{1,5},{5... | collective-permute-start | bytes 737288 | tf_op jit(solution)/shard_map/ppermute | solution.py:581
  5.8 1.1 collective-permute-done.got_ref
  7.5 11.3 %all_to_all.55.own_ref = f32[4,5,3,16,128]{4,3,2,1,0:T(8,128)S(1)} all-to-all(f32[4,5,3,16,128]{4,3,2,1,0:T(8,128)S(1)} %join.1), channel_id=1, replica_groups=mesh['tm'=8,'gx'=8,'gy'=4] {'gy'}, dimensions={0} | all-to-all | bytes 983040 | tf_op jit(solution)/shard_map/all_to_all | solution.py:619
  18.8 3.3 %collective-permute-start.2 = (f32[4,5,3,16,128]{4,3,2,1,0:T(8,128)S(1)}, f32[4,5,3,16,128]{4,3,2,1,0:T(8,128)S(1)}, u32[]{:S(2)}, u32[]{:S(2)}) collective-permute-start(f32[4,5,3,16,128]{4,3,2,1,0:T(8,128)S(1)} %all_to_all.55.own_ref), channel_id=1, source_target_pairs={{1,4},{2,5},{3,6},{4,1},{5,2},{6,3},{7,11},{8,13},{9,14},{10,15},{... | collective-permute-start | bytes 1474568 | tf_op jit(solution)/shard_map/ppermute | solution.py:589
  23.1 2.8 %collective-permute-start.3 = (f32[4,2,1,16,128]{4,3,2,1,0:T(8,128)S(1)}, f32[4,2,1,16,128]{4,3,2,1,0:T(8,128)S(1)}, u32[]{:S(2)}, u32[]{:S(2)}) collective-permute-start(f32[4,2,1,16,128]{4,3,2,1,0:T(8,128)S(1)} %get-tuple-element.160), channel_id=1, source_target_pairs={{0,1},{1,0},{2,3},{3,2},{4,5},{5,4},{6,7},{7,6},{8,9},{9,8},{10,11... | collective-permute-start | bytes 196616 | tf_op jit(solution)/shard_map/ppermute | solution.py:589
  25.9 3.4 %collective-permute-done.3.even2_ref = f32[4,2,1,16,128]{4,3,2,1,0:T(8,128)S(1)} collective-permute-done((f32[4,2,1,16,128]{4,3,2,1,0:T(8,128)S(1)}, f32[4,2,1,16,128]{4,3,2,1,0:T(8,128)S(1)}, u32[]{:S(2)}, u32[]{:S(2)}) %collective-permute-start.3) | collective-permute-done | bytes 65568 | tf_op jit(solution)/shard_map/ppermute | solution.py:589
  29.7 4.2 %start.1 = (f32[10,64,128]{2,1,0:T(8,128)S(1)}, f32[9,64,128]{2,1,0:T(8,128)S(1)}, f32[9,64,128]{2,1,0:T(8,128)S(1)}, f32[9,64,128]{2,1,0:T(8,128)S(1)}, f32[20,...) custom-call(f32[6]{0:T(128)S(1)} %copy-done.5, ...), custom_call_target="tpu_custom_call" | custom-call | tf_op jit(solution)/shard_map/start/pallas_call | solution.py:548
  33.9 1.5 collective-permute-start.5
  35.4 2.5 %collective-permute-start.6 = (f32[3,64,128]{2,1,0:T(8,128)S(1)}, f32[3,64,128]{2,1,0:T(8,128)S(1)}, u32[]{:S(2)}, u32[]{:S(2)}) collective-permute-start(f32[3,64,128]{2,1,0:T(8,128)S(1)} %get-tuple-element.95), channel_id=1, source_target_pairs={{1,4},{2,5},{3,6},{4,1},{5,2},{6,3},{7,11},{8,13},{9,14},{10,15},{... | collective-permute-start | bytes 294920 | tf_op jit(solution)/shard_map/ppermute | solution.py:589
  39.1 16.0 %all_to_all.56.red_in = f32[32,1,128]{2,1,0:T(1,128)S(1)} all-to-all(f32[32,1,128]{2,1,0:T(1,128)S(1)} %get-tuple-element.84), channel_id=1, replica_groups=mesh['tm'=8,'gx'=8,'gy'=4] {'gx','gy'}, dimensions={0} | all-to-all | bytes 32768 | tf_op jit(solution)/shard_map/all_to_all | solution.py:593
  55.1 2.6 %second.1 = (f32[12,64,128]{2,1,0:T(8,128)S(1)}, f32[3,64,128]{2,1,0:T(8,128)S(1)}, f32[3,64,128]{2,1,0:T(8,128)S(1)}, f32[3,64,128]{2,1,0:T(8,128)S(1)}, f32[32,1,128]{2,1,0:T(1,128)S(1)}) custom-call(f32[1,2]{1,0:T(1,128)S(1)} %copy-done.4, f32[3]{0:T(128)S(1)} %copy-done.2, f32[3]{0:T(128)S(1)} %copy-done.3, s32[4]{0:T(128)S(1)} %pad_add_fusion.place_ref.refs_2_, ...), custom_call_target="tpu_custom_call" | custom-call | tf_op jit(solution)/shard_map/second/pallas_call | solution.py:548
  57.7 10.7 %all_to_all.57.red_in = f32[32,1,128]{2,1,0:T(1,128)S(1)} all-to-all(f32[32,1,128]{2,1,0:T(1,128)S(1)} %get-tuple-element.98), channel_id=1, replica_groups=mesh['tm'=8,'gx'=8,'gy'=4] {'gx','gy'}, dimensions={0} | all-to-all | bytes 32768 | tf_op jit(solution)/shard_map/all_to_all | solution.py:593
  69.1 5.7 %collective-permute-start.9 = (f32[776,128]{1,0:T(8,128)S(1)}, f32[776,128]{1,0:T(8,128)S(1)}, u32[]{:S(2)}, u32[]{:S(2)}) collective-permute-start(f32[776,128]{1,0:T(8,128)S(1)} %block.1.refs_12_), channel_id=1, source_target_pairs={{0,224},{32,0},{64,32},{96,64},{128,96},{160,128},{192,160},{224,1... | collective-permute-start | bytes 1191944 | tf_op jit(solution)/shard_map/ppermute | solution.py:596
  74.8 7.9 %collective-permute-done.9.blk_ref = f32[776,128]{1,0:T(8,128)S(1)} collective-permute-done((f32[776,128]{1,0:T(8,128)S(1)}, f32[776,128]{1,0:T(8,128)S(1)}, u32[]{:S(2)}, u32[]{:S(2)}) %collective-permute-start.9) | collective-permute-done | bytes 397344 | tf_op jit(solution)/shard_map/ppermute | solution.py:596
  83.3 3.5 %collective-permute-start.12 = (f32[776,128]{1,0:T(8,128)S(1)}, f32[776,128]{1,0:T(8,128)S(1)}, u32[]{:S(2)}, u32[]{:S(2)}) collective-permute-start(f32[776,128]{1,0:T(8,128)S(1)} %collective-permute-done.9.blk_ref), channel_id=1, source_target_pairs={{0,224},{32,0},{64,32},{96,64},{128,96},{160,128},{192,160},{224,1... | collective-permute-start | bytes 1191944 | tf_op jit(solution)/shard_map/ppermute | solution.py:596
  86.8 1.8 collective-permute-start.10
  88.6 2.3 collective-permute-start.11
  90.9 4.4 %collective-permute-done.11.refs_5_ = f32[5,64,128]{2,1,0:T(8,128)S(1)} collective-permute-done((f32[5,64,128]{2,1,0:T(8,128)S(1)}, f32[5,64,128]{2,1,0:T(8,128)S(1)}, u32[]{:S(2)}, u32[]{:S(2)}) %collective-permute-start.11) | collective-permute-done | bytes 163872 | tf_op jit(solution)/shard_map/ppermute | solution.py:589
  95.2 1.8 chain2.1
  97.0 2.1 collective-permute-start.15
  99.1 2.7 %collective-permute-start.13 = (f32[8,64,128]{2,1,0:T(8,128)S(1)}, f32[8,64,128]{2,1,0:T(8,128)S(1)}, u32[]{:S(2)}, u32[]{:S(2)}) collective-permute-start(f32[8,64,128]{2,1,0:T(8,128)S(1)} %get-tuple-element.114), channel_id=1, source_target_pairs={{0,4},{1,5},{2,6},{3,7},{4,0},{5,1},{6,2},{7,3},{8,12},{9,13},{10,... | collective-permute-start | bytes 786440 | tf_op jit(solution)/shard_map/ppermute | solution.py:589
  101.8 2.1 collective-permute-start.14
  103.9 11.4 %all_to_all.58.refs_3_ = f32[32,1,128]{2,1,0:T(1,128)S(1)} all-to-all(f32[32,1,128]{2,1,0:T(1,128)S(1)} %get-tuple-element.109), channel_id=1, replica_groups=mesh['tm'=8,'gx'=8,'gy'=4] {'gx','gy'}, dimensions={0} | all-to-all | bytes 32768 | tf_op jit(solution)/shard_map/all_to_all | solution.py:593
  115.3 2.0 chain3.1
  118.1 2.1 collective-permute-start.17
  120.2 11.4 %all_to_all.59.refs_3_ = f32[32,1,128]{2,1,0:T(1,128)S(1)} all-to-all(f32[32,1,128]{2,1,0:T(1,128)S(1)} %get-tuple-element.117), channel_id=1, replica_groups=mesh['tm'=8,'gx'=8,'gy'=4] {'gx','gy'}, dimensions={0} | all-to-all | bytes 32768 | tf_op jit(solution)/shard_map/all_to_all | solution.py:593
  131.6 2.0 chain4.1
  134.4 2.1 collective-permute-start.20
  136.5 11.4 %all_to_all.60.refs_3_ = f32[32,1,128]{2,1,0:T(1,128)S(1)} all-to-all(f32[32,1,128]{2,1,0:T(1,128)S(1)} %get-tuple-element.125), channel_id=1, replica_groups=mesh['tm'=8,'gx'=8,'gy'=4] {'gx','gy'}, dimensions={0} | all-to-all | bytes 32768 | tf_op jit(solution)/shard_map/all_to_all | solution.py:593
  147.9 2.0 chain5.1
  151.1 2.1 collective-permute-start.23
  153.1 11.4 %all_to_all.61.refs_3_ = f32[32,1,128]{2,1,0:T(1,128)S(1)} all-to-all(f32[32,1,128]{2,1,0:T(1,128)S(1)} %get-tuple-element.133), channel_id=1, replica_groups=mesh['tm'=8,'gx'=8,'gy'=4] {'gx','gy'}, dimensions={0} | all-to-all | bytes 32768 | tf_op jit(solution)/shard_map/all_to_all | solution.py:593
  164.6 2.0 chain6.1
  166.6 2.7 %collective-permute-start.27 = (f32[776,128]{1,0:T(8,128)S(1)}, f32[776,128]{1,0:T(8,128)S(1)}, u32[]{:S(2)}, u32[]{:S(2)}) collective-permute-start(f32[776,128]{1,0:T(8,128)S(1)} %collective-permute-done.24.refs_12_), channel_id=1, source_target_pairs={{0,224},{32,0},{64,32},{96,64},{128,96},{160,128},{192,160},{224,1... | collective-permute-start | bytes 1191944 | tf_op jit(solution)/shard_map/ppermute | solution.py:596
  170.2 2.1 collective-permute-start.26
  172.3 11.4 %all_to_all.62.refs_3_ = f32[32,1,128]{2,1,0:T(1,128)S(1)} all-to-all(f32[32,1,128]{2,1,0:T(1,128)S(1)} %get-tuple-element.141), channel_id=1, replica_groups=mesh['tm'=8,'gx'=8,'gy'=4] {'gx','gy'}, dimensions={0} | all-to-all | bytes 32768 | tf_op jit(solution)/shard_map/all_to_all | solution.py:593
  183.7 2.0 chain7.1
  186.4 2.1 collective-permute-start.29
  188.5 11.4 %all_to_all.63.refs_3_ = f32[32,1,128]{2,1,0:T(1,128)S(1)} all-to-all(f32[32,1,128]{2,1,0:T(1,128)S(1)} %get-tuple-element.149), channel_id=1, replica_groups=mesh['tm'=8,'gx'=8,'gy'=4] {'gx','gy'}, dimensions={0} | all-to-all | bytes 32768 | tf_op jit(solution)/shard_map/all_to_all | solution.py:593
  199.9 2.6 %chain8.1 = (f32[12,64,128]{2,1,0:T(8,128)S(1)}, f32[7,64,128]{2,1,0:T(8,128)S(1)}, f32[5,64,128]{2,1,0:T(8,128)S(1)}, f32[8,64,128]{2,1,0:T(8,128)}, f32[8,64,128]{2,1,0:T(8,128)}, /*index=5*/f32[32,1,128]{2,1,0:T(1,128)S(1)}) custom-call(f32[3]{0:T(128)S(1)} %copy-done.2, f32[3]{0:T(128)S(1)} %copy-done.3, s32[4]{0:T(128)S(1)} %pad_add_fusion.place_ref.refs_2_, ...), custom_call_target="tpu_custom_call" | custom-call | tf_op jit(solution)/shard_map/chain8/pallas_call | solution.py:548
  202.5 10.7 %all_to_all.64.red_in = f32[32,1,128]{2,1,0:T(1,128)S(1)} all-to-all(f32[32,1,128]{2,1,0:T(1,128)S(1)} %get-tuple-element.155), channel_id=1, replica_groups=mesh['tm'=8,'gx'=8,'gy'=4] {'gx','gy'}, dimensions={0} | all-to-all | bytes 32768 | tf_op jit(solution)/shard_map/all_to_all | solution.py:593
  213.2 1.5 closing.1
  214.6 3.5 %all-to-all-start.10 = ((f32[4,4,3,16,128]{4,3,2,1,0:T(8,128)}), f32[4,4,3,16,128]{4,3,2,1,0:T(8,128)S(1)}, u32[]{:S(2)}, u32[]{:S(2)}) async-start(f32[4,4,3,16,128]{4,3,2,1,0:T(8,128)} %closing.1), calls=%async_computation.10 | async-start | bytes 786432 | tf_op jit(solution)/shard_map/all_to_all | solution.py:689
  218.1 7.2 %all-to-all-done.10.parts_ref = f32[4,4,3,16,128]{4,3,2,1,0:T(8,128)S(1)} async-done(((f32[4,4,3,16,128]{4,3,2,1,0:T(8,128)}), f32[4,4,3,16,128]{4,3,2,1,0:T(8,128)S(1)}, u32[]{:S(2)}, u32[]{:S(2)}) %all-to-all-start.10) | async-done | bytes 393248 | tf_op jit(solution)/shard_map/all_to_all | solution.py:689
  225.3 1.9 collective-permute-start.30
  227.2 1.1 collective-permute-done.30.got_ref
  228.3 1.3 gather.1
  (58 shorter events, 10.3 us)
Async XLA Ops:
  0.0 0.9 copy-start.1
  0.9 1.0 copy-start
  2.5 4.5 %collective-permute-start = (f32[2,5,3,16,128]{4,3,2,1,0:T(8,128)S(1)}, f32[2,5,3,16,128]{4,3,2,1,0:T(8,128)S(1)}, u32[]{:S(2)}, u32[]{:S(2)}) collective-permute-start(f32[2,5,3,16,128]{4,3,2,1,0:T(8,128)S(1)} %get-tuple-element.83), channel_id=1, source_target_pairs={{0,4},{4,0},{8,12},{12,8},{16,20},{20,16},{24,28},{28,24},{1,5},{5... | collective-permute-start | bytes 737288 | tf_op jit(solution)/shard_map/ppermute | solution.py:581
  18.8 10.8 %collective-permute-start.2 = (f32[4,5,3,16,128]{4,3,2,1,0:T(8,128)S(1)}, f32[4,5,3,16,128]{4,3,2,1,0:T(8,128)S(1)}, u32[]{:S(2)}, u32[]{:S(2)}) collective-permute-start(f32[4,5,3,16,128]{4,3,2,1,0:T(8,128)S(1)} %all_to_all.55.own_ref), channel_id=1, source_target_pairs={{1,4},{2,5},{3,6},{4,1},{5,2},{6,3},{7,11},{8,13},{9,14},{10,15},{... | collective-permute-start | bytes 1474568 | tf_op jit(solution)/shard_map/ppermute | solution.py:589
  22.1 7.6 %collective-permute-start.1 = (f32[4,5,3,16,128]{4,3,2,1,0:T(8,128)S(1)}, f32[4,5,3,16,128]{4,3,2,1,0:T(8,128)S(1)}, u32[]{:S(2)}, u32[]{:S(2)}) collective-permute-start(f32[4,5,3,16,128]{4,3,2,1,0:T(8,128)S(1)} %all_to_all.55.own_ref), channel_id=1, source_target_pairs={{0,4},{1,5},{2,6},{3,7},{4,0},{5,1},{6,2},{7,3},{8,12},{9,13},{10,... | collective-permute-start | bytes 1474568 | tf_op jit(solution)/shard_map/ppermute | solution.py:589
  22.2 7.4 %copy-start.5 = (f32[6]{0:T(128)S(1)}, f32[6]{0:T(128)}, u32[]{:S(2)}) copy-start(f32[6]{0:T(128)} %rigid_ref.1) | copy-start | bytes 76
  22.2 7.4 %copy-start.6 = (f32[6]{0:T(128)S(1)}, f32[6]{0:T(128)}, u32[]{:S(2)}) copy-start(f32[6]{0:T(128)} %dilate_ref.1) | copy-start | bytes 76
  22.2 7.4 %copy-start.2 = (f32[3]{0:T(128)S(1)}, f32[3]{0:T(128)}, u32[]{:S(2)}) copy-start(f32[3]{0:T(128)} %coef_ref.9) | copy-start | bytes 40
  22.2 7.4 %copy-start.3 = (f32[3]{0:T(128)S(1)}, f32[3]{0:T(128)}, u32[]{:S(2)}) copy-start(f32[3]{0:T(128)} %time_ref.9) | copy-start | bytes 40
  22.2 7.4 %copy-start.4 = (f32[1,2]{1,0:T(1,128)S(1)}, f32[1,2]{1,0:T(1,128)}, u32[]{:S(2)}) copy-start(f32[1,2]{1,0:T(1,128)} %heat_ref.5) | copy-start | bytes 28
  22.3 3.6 %collective-permute-start.4 = (f32[4,2,1,16,128]{4,3,2,1,0:T(8,128)S(1)}, f32[4,2,1,16,128]{4,3,2,1,0:T(8,128)S(1)}, u32[]{:S(2)}, u32[]{:S(2)}) collective-permute-start(f32[4,2,1,16,128]{4,3,2,1,0:T(8,128)S(1)} %get-tuple-element.159), channel_id=1, source_target_pairs={{1,2},{2,1},{3,11},{5,6},{6,5},{7,15},{8,16},{9,10},{10,9},{11,3},... | collective-permute-start | bytes 196616 | tf_op jit(solution)/shard_map/ppermute | solution.py:589
  23.1 6.2 %collective-permute-start.3 = (f32[4,2,1,16,128]{4,3,2,1,0:T(8,128)S(1)}, f32[4,2,1,16,128]{4,3,2,1,0:T(8,128)S(1)}, u32[]{:S(2)}, u32[]{:S(2)}) collective-permute-start(f32[4,2,1,16,128]{4,3,2,1,0:T(8,128)S(1)} %get-tuple-element.160), channel_id=1, source_target_pairs={{0,1},{1,0},{2,3},{3,2},{4,5},{5,4},{6,7},{7,6},{8,9},{9,8},{10,11... | collective-permute-start | bytes 196616 | tf_op jit(solution)/shard_map/ppermute | solution.py:589
  33.9 21.2 %collective-permute-start.5 = (f32[3,64,128]{2,1,0:T(8,128)S(1)}, f32[3,64,128]{2,1,0:T(8,128)S(1)}, u32[]{:S(2)}, u32[]{:S(2)}) collective-permute-start(f32[3,64,128]{2,1,0:T(8,128)S(1)} %get-tuple-element.94), channel_id=1, source_target_pairs={{0,4},{1,5},{2,6},{3,7},{4,0},{5,1},{6,2},{7,3},{8,12},{9,13},{10,... | collective-permute-start | bytes 294920 | tf_op jit(solution)/shard_map/ppermute | solution.py:589
  35.4 19.7 %collective-permute-start.6 = (f32[3,64,128]{2,1,0:T(8,128)S(1)}, f32[3,64,128]{2,1,0:T(8,128)S(1)}, u32[]{:S(2)}, u32[]{:S(2)}) collective-permute-start(f32[3,64,128]{2,1,0:T(8,128)S(1)} %get-tuple-element.95), channel_id=1, source_target_pairs={{1,4},{2,5},{3,6},{4,1},{5,2},{6,3},{7,11},{8,13},{9,14},{10,15},{... | collective-permute-start | bytes 294920 | tf_op jit(solution)/shard_map/ppermute | solution.py:589
  37.9 17.2 %collective-permute-start.7 = (f32[3,64,128]{2,1,0:T(8,128)S(1)}, f32[3,64,128]{2,1,0:T(8,128)S(1)}, u32[]{:S(2)}, u32[]{:S(2)}) collective-permute-start(f32[3,64,128]{2,1,0:T(8,128)S(1)} %get-tuple-element.96), channel_id=1, source_target_pairs={{0,1},{1,0},{2,3},{3,2},{4,5},{5,4},{6,7},{7,6},{8,9},{9,8},{10,11... | collective-permute-start | bytes 294920 | tf_op jit(solution)/shard_map/ppermute | solution.py:589
  38.4 16.7 %collective-permute-start.8 = (f32[3,64,128]{2,1,0:T(8,128)S(1)}, f32[3,64,128]{2,1,0:T(8,128)S(1)}, u32[]{:S(2)}, u32[]{:S(2)}) collective-permute-start(f32[3,64,128]{2,1,0:T(8,128)S(1)} %get-tuple-element.97), channel_id=1, source_target_pairs={{1,2},{2,1},{3,11},{5,6},{6,5},{7,15},{8,16},{9,10},{10,9},{11,3},... | collective-permute-start | bytes 294920 | tf_op jit(solution)/shard_map/ppermute | solution.py:589
  69.1 13.6 %collective-permute-start.9 = (f32[776,128]{1,0:T(8,128)S(1)}, f32[776,128]{1,0:T(8,128)S(1)}, u32[]{:S(2)}, u32[]{:S(2)}) collective-permute-start(f32[776,128]{1,0:T(8,128)S(1)} %block.1.refs_12_), channel_id=1, source_target_pairs={{0,224},{32,0},{64,32},{96,64},{128,96},{160,128},{192,160},{224,1... | collective-permute-start | bytes 1191944 | tf_op jit(solution)/shard_map/ppermute | solution.py:596
  83.3 11.9 %collective-permute-start.12 = (f32[776,128]{1,0:T(8,128)S(1)}, f32[776,128]{1,0:T(8,128)S(1)}, u32[]{:S(2)}, u32[]{:S(2)}) collective-permute-start(f32[776,128]{1,0:T(8,128)S(1)} %collective-permute-done.9.blk_ref), channel_id=1, source_target_pairs={{0,224},{32,0},{64,32},{96,64},{128,96},{160,128},{192,160},{224,1... | collective-permute-start | bytes 1191944 | tf_op jit(solution)/shard_map/ppermute | solution.py:596
  86.8 4.1 %collective-permute-start.10 = (f32[5,64,128]{2,1,0:T(8,128)S(1)}, f32[5,64,128]{2,1,0:T(8,128)S(1)}, u32[]{:S(2)}, u32[]{:S(2)}) collective-permute-start(f32[5,64,128]{2,1,0:T(8,128)S(1)} %get-tuple-element.105), channel_id=1, source_target_pairs={{0,4},{1,5},{2,6},{3,7},{4,0},{5,1},{6,2},{7,3},{8,12},{9,13},{10,... | collective-permute-start | bytes 491528 | tf_op jit(solution)/shard_map/ppermute | solution.py:589
  88.6 6.6 %collective-permute-start.11 = (f32[5,64,128]{2,1,0:T(8,128)S(1)}, f32[5,64,128]{2,1,0:T(8,128)S(1)}, u32[]{:S(2)}, u32[]{:S(2)}) collective-permute-start(f32[5,64,128]{2,1,0:T(8,128)S(1)} %get-tuple-element.106), channel_id=1, source_target_pairs={{1,4},{2,5},{3,6},{4,1},{5,2},{6,3},{7,11},{8,13},{9,14},{10,15},{... | collective-permute-start | bytes 491528 | tf_op jit(solution)/shard_map/ppermute | solution.py:589
  97.0 18.3 %collective-permute-start.15 = (f32[776,128]{1,0:T(8,128)S(1)}, f32[776,128]{1,0:T(8,128)S(1)}, u32[]{:S(2)}, u32[]{:S(2)}) collective-permute-start(f32[776,128]{1,0:T(8,128)S(1)} %collective-permute-done.12.refs_9_), channel_id=1, source_target_pairs={{0,224},{32,0},{64,32},{96,64},{128,96},{160,128},{192,160},{224,1... | collective-permute-start | bytes 1191944 | tf_op jit(solution)/shard_map/ppermute | solution.py:596
  99.1 16.2 %collective-permute-start.13 = (f32[8,64,128]{2,1,0:T(8,128)S(1)}, f32[8,64,128]{2,1,0:T(8,128)S(1)}, u32[]{:S(2)}, u32[]{:S(2)}) collective-permute-start(f32[8,64,128]{2,1,0:T(8,128)S(1)} %get-tuple-element.114), channel_id=1, source_target_pairs={{0,4},{1,5},{2,6},{3,7},{4,0},{5,1},{6,2},{7,3},{8,12},{9,13},{10,... | collective-permute-start | bytes 786440 | tf_op jit(solution)/shard_map/ppermute | solution.py:589
  101.8 13.5 %collective-permute-start.14 = (f32[8,64,128]{2,1,0:T(8,128)S(1)}, f32[8,64,128]{2,1,0:T(8,128)S(1)}, u32[]{:S(2)}, u32[]{:S(2)}) collective-permute-start(f32[8,64,128]{2,1,0:T(8,128)S(1)} %get-tuple-element.115), channel_id=1, source_target_pairs={{1,4},{2,5},{3,6},{4,1},{5,2},{6,3},{7,11},{8,13},{9,14},{10,15},{... | collective-permute-start | bytes 786440 | tf_op jit(solution)/shard_map/ppermute | solution.py:589
  117.3 14.3 %collective-permute-start.18 = (f32[776,128]{1,0:T(8,128)S(1)}, f32[776,128]{1,0:T(8,128)S(1)}, u32[]{:S(2)}, u32[]{:S(2)}) collective-permute-start(f32[776,128]{1,0:T(8,128)S(1)} %collective-permute-done.15.refs_12_), channel_id=1, source_target_pairs={{0,224},{32,0},{64,32},{96,64},{128,96},{160,128},{192,160},{224,1... | collective-permute-start | bytes 1191944 | tf_op jit(solution)/shard_map/ppermute | solution.py:596
  117.4 14.2 %collective-permute-start.16 = (f32[8,64,128]{2,1,0:T(8,128)S(1)}, f32[8,64,128]{2,1,0:T(8,128)S(1)}, u32[]{:S(2)}, u32[]{:S(2)}) collective-permute-start(f32[8,64,128]{2,1,0:T(8,128)S(1)} %get-tuple-element.122), channel_id=1, source_target_pairs={{0,4},{1,5},{2,6},{3,7},{4,0},{5,1},{6,2},{7,3},{8,12},{9,13},{10,... | collective-permute-start | bytes 786440 | tf_op jit(solution)/shard_map/ppermute | solution.py:589
  118.1 13.5 %collective-permute-start.17 = (f32[8,64,128]{2,1,0:T(8,128)S(1)}, f32[8,64,128]{2,1,0:T(8,128)S(1)}, u32[]{:S(2)}, u32[]{:S(2)}) collective-permute-start(f32[8,64,128]{2,1,0:T(8,128)S(1)} %get-tuple-element.123), channel_id=1, source_target_pairs={{1,4},{2,5},{3,6},{4,1},{5,2},{6,3},{7,11},{8,13},{9,14},{10,15},{... | collective-permute-start | bytes 786440 | tf_op jit(solution)/shard_map/ppermute | solution.py:589
  133.6 14.3 %collective-permute-start.21 = (f32[776,128]{1,0:T(8,128)S(1)}, f32[776,128]{1,0:T(8,128)S(1)}, u32[]{:S(2)}, u32[]{:S(2)}) collective-permute-start(f32[776,128]{1,0:T(8,128)S(1)} %collective-permute-done.18.refs_12_), channel_id=1, source_target_pairs={{0,224},{32,0},{64,32},{96,64},{128,96},{160,128},{192,160},{224,1... | collective-permute-start | bytes 1191944 | tf_op jit(solution)/shard_map/ppermute | solution.py:596
  133.7 14.2 %collective-permute-start.19 = (f32[8,64,128]{2,1,0:T(8,128)S(1)}, f32[8,64,128]{2,1,0:T(8,128)S(1)}, u32[]{:S(2)}, u32[]{:S(2)}) collective-permute-start(f32[8,64,128]{2,1,0:T(8,128)S(1)} %get-tuple-element.130), channel_id=1, source_target_pairs={{0,4},{1,5},{2,6},{3,7},{4,0},{5,1},{6,2},{7,3},{8,12},{9,13},{10,... | collective-permute-start | bytes 786440 | tf_op jit(solution)/shard_map/ppermute | solution.py:589
  134.4 13.5 %collective-permute-start.20 = (f32[8,64,128]{2,1,0:T(8,128)S(1)}, f32[8,64,128]{2,1,0:T(8,128)S(1)}, u32[]{:S(2)}, u32[]{:S(2)}) collective-permute-start(f32[8,64,128]{2,1,0:T(8,128)S(1)} %get-tuple-element.131), channel_id=1, source_target_pairs={{1,4},{2,5},{3,6},{4,1},{5,2},{6,3},{7,11},{8,13},{9,14},{10,15},{... | collective-permute-start | bytes 786440 | tf_op jit(solution)/shard_map/ppermute | solution.py:589
  149.9 14.6 %collective-permute-start.24 = (f32[776,128]{1,0:T(8,128)S(1)}, f32[776,128]{1,0:T(8,128)S(1)}, u32[]{:S(2)}, u32[]{:S(2)}) collective-permute-start(f32[776,128]{1,0:T(8,128)S(1)} %collective-permute-done.21.refs_12_), channel_id=1, source_target_pairs={{0,224},{32,0},{64,32},{96,64},{128,96},{160,128},{192,160},{224,1... | collective-permute-start | bytes 1191944 | tf_op jit(solution)/shard_map/ppermute | solution.py:596
  150.1 14.4 %collective-permute-start.22 = (f32[8,64,128]{2,1,0:T(8,128)S(1)}, f32[8,64,128]{2,1,0:T(8,128)S(1)}, u32[]{:S(2)}, u32[]{:S(2)}) collective-permute-start(f32[8,64,128]{2,1,0:T(8,128)S(1)} %get-tuple-element.138), channel_id=1, source_target_pairs={{0,4},{1,5},{2,6},{3,7},{4,0},{5,1},{6,2},{7,3},{8,12},{9,13},{10,... | collective-permute-start | bytes 786440 | tf_op jit(solution)/shard_map/ppermute | solution.py:589
  151.1 13.5 %collective-permute-start.23 = (f32[8,64,128]{2,1,0:T(8,128)S(1)}, f32[8,64,128]{2,1,0:T(8,128)S(1)}, u32[]{:S(2)}, u32[]{:S(2)}) collective-permute-start(f32[8,64,128]{2,1,0:T(8,128)S(1)} %get-tuple-element.139), channel_id=1, source_target_pairs={{1,4},{2,5},{3,6},{4,1},{5,2},{6,3},{7,11},{8,13},{9,14},{10,15},{... | collective-permute-start | bytes 786440 | tf_op jit(solution)/shard_map/ppermute | solution.py:589
  166.6 17.1 %collective-permute-start.27 = (f32[776,128]{1,0:T(8,128)S(1)}, f32[776,128]{1,0:T(8,128)S(1)}, u32[]{:S(2)}, u32[]{:S(2)}) collective-permute-start(f32[776,128]{1,0:T(8,128)S(1)} %collective-permute-done.24.refs_12_), channel_id=1, source_target_pairs={{0,224},{32,0},{64,32},{96,64},{128,96},{160,128},{192,160},{224,1... | collective-permute-start | bytes 1191944 | tf_op jit(solution)/shard_map/ppermute | solution.py:596
  169.3 14.4 %collective-permute-start.25 = (f32[8,64,128]{2,1,0:T(8,128)S(1)}, f32[8,64,128]{2,1,0:T(8,128)S(1)}, u32[]{:S(2)}, u32[]{:S(2)}) collective-permute-start(f32[8,64,128]{2,1,0:T(8,128)S(1)} %get-tuple-element.146), channel_id=1, source_target_pairs={{0,4},{1,5},{2,6},{3,7},{4,0},{5,1},{6,2},{7,3},{8,12},{9,13},{10,... | collective-permute-start | bytes 786440 | tf_op jit(solution)/shard_map/ppermute | solution.py:589
  170.2 13.5 %collective-permute-start.26 = (f32[8,64,128]{2,1,0:T(8,128)S(1)}, f32[8,64,128]{2,1,0:T(8,128)S(1)}, u32[]{:S(2)}, u32[]{:S(2)}) collective-permute-start(f32[8,64,128]{2,1,0:T(8,128)S(1)} %get-tuple-element.147), channel_id=1, source_target_pairs={{1,4},{2,5},{3,6},{4,1},{5,2},{6,3},{7,11},{8,13},{9,14},{10,15},{... | collective-permute-start | bytes 786440 | tf_op jit(solution)/shard_map/ppermute | solution.py:589
  185.7 14.2 %collective-permute-start.28 = (f32[8,64,128]{2,1,0:T(8,128)S(1)}, f32[8,64,128]{2,1,0:T(8,128)S(1)}, u32[]{:S(2)}, u32[]{:S(2)}) collective-permute-start(f32[8,64,128]{2,1,0:T(8,128)S(1)} %get-tuple-element.153), channel_id=1, source_target_pairs={{0,4},{1,5},{2,6},{3,7},{4,0},{5,1},{6,2},{7,3},{8,12},{9,13},{10,... | collective-permute-start | bytes 786440 | tf_op jit(solution)/shard_map/ppermute | solution.py:589
  186.4 13.5 %collective-permute-start.29 = (f32[8,64,128]{2,1,0:T(8,128)S(1)}, f32[8,64,128]{2,1,0:T(8,128)S(1)}, u32[]{:S(2)}, u32[]{:S(2)}) collective-permute-start(f32[8,64,128]{2,1,0:T(8,128)S(1)} %get-tuple-element.154), channel_id=1, source_target_pairs={{1,4},{2,5},{3,6},{4,1},{5,2},{6,3},{7,11},{8,13},{9,14},{10,15},{... | collective-permute-start | bytes 786440 | tf_op jit(solution)/shard_map/ppermute | solution.py:589
  214.6 10.7 %all-to-all-start.10 = ((f32[4,4,3,16,128]{4,3,2,1,0:T(8,128)}), f32[4,4,3,16,128]{4,3,2,1,0:T(8,128)S(1)}, u32[]{:S(2)}, u32[]{:S(2)}) async-start(f32[4,4,3,16,128]{4,3,2,1,0:T(8,128)} %closing.1), calls=%async_computation.10 | async-start | bytes 786432 | tf_op jit(solution)/shard_map/all_to_all | solution.py:689
  225.3 3.0 %collective-permute-start.30 = (f32[2,4,3,16,128]{4,3,2,1,0:T(8,128)S(1)}, f32[2,4,3,16,128]{4,3,2,1,0:T(8,128)S(1)}, u32[]{:S(2)}, u32[]{:S(2)}) collective-permute-start(f32[2,4,3,16,128]{4,3,2,1,0:T(8,128)S(1)} %constant_dynamic-slice_fusion), channel_id=1, source_target_pairs={{0,4},{4,0},{8,12},{12,8},{16,20},{20,16},{24,28},{28,24},{1,5},{5... | collective-permute-start | bytes 589832 | tf_op jit(solution)/shard_map/ppermute | solution.py:581

commit v4 on v2

v4 whole, which is shorter than its diff:
```python
import functools

import jax
import jax.numpy as jnp
from jax import lax
from jax.experimental import pallas as pl
from jax.experimental.pallas import tpu as pltpu
from jax.sharding import PartitionSpec as P

PACES = 2
SHARP = 3
LOOSE = 2
PRONY = 3
L = 3
LINE = ("gx", "gy")
LIMIT = 14 << 20


def masks(ny, nz):
    row = lax.broadcasted_iota(jnp.int32, (ny, nz), 0)
    lane = lax.broadcasted_iota(jnp.int32, (ny, nz), 1)
    return row == 0, row == ny - 1, lane == 0, lane == nz - 1


class Shifts:
    def __init__(self, ny, nz):
        self.ny, self.nz = ny, nz
        self.row_first, self.row_last, self.lane_first, self.lane_last = masks(ny, nz)

    def zup(self, v):
        return jnp.where(self.lane_last, 0.0, pltpu.roll(v, self.nz - 1, 1))

    def zdn(self, v):
        return jnp.where(self.lane_first, 0.0, pltpu.roll(v, 1, 1))

    def yup(self, v):
        return jnp.where(self.row_last, 0.0, pltpu.roll(v, self.ny - 1, 0))

    def ydn(self, v):
        return jnp.where(self.row_first, 0.0, pltpu.roll(v, 1, 0))


def off_diagonal(sh, v, k, low, high, put):
    def spread(plane):
        up = sh.zup(plane)
        side, side_up = sh.yup(plane), sh.yup(up)
        return plane, up, side, side_up, plane + up, side + side_up

    near = spread(v(low - 1))
    carry = None
    for e in range(low - 1, high + 1):
        far = spread(v(e + 1))
        a, a_up, b, b_up, a_sum, b_sum = near
        c, c_up, d, d_up, c_sum, d_sum = far
        one_up, two_up = b_up + c_up, a_up + d_up
        one, two = b + c, a + d
        kk = k(e)
        if e >= low:
            e00, f00 = kk * (d_sum + one_up), kk * (d_sum + one)
            e01, f01 = kk * (c_sum + two_up), kk * (c_sum + two)
            e10, e11, f10, f11 = carry
            put(e, (e00 + e10) + sh.ydn(e01 + e11) + sh.zdn((f00 + f10) + sh.ydn(f01 + f11)))
        if e < high:
            carry = (
                kk * (b_sum + two_up),
                kk * (a_sum + one_up),
                kk * (b_sum + two),
                kk * (a_sum + one),
            )
        near = far


def prony(dt, coef_ref, time_ref):
    decay = [jnp.exp(-dt / jnp.full((1, 128), time_ref[p], jnp.float32)) for p in range(PRONY)]
    rest = [1.0 - d for d in decay]
    f = [coef_ref[p] * decay[p] for p in range(PRONY)]
    return decay, rest, f, 1.0 / dt + (f[0] + f[1] + f[2])


def moments_out(values, red_ref):
    lane = lax.broadcasted_iota(jnp.int32, (1, 128), 1)
    packed = jnp.zeros((1, 128), jnp.float32)
    for at, field in enumerate(values):
        total = jnp.sum(jnp.sum(field, axis=0, keepdims=True), axis=1, keepdims=True)
        packed = jnp.where(lane == at, total, packed)
    red_ref[...] = jnp.broadcast_to(packed[None], red_ref.shape)


def moments_in(red_ref, first, count):
    total = jnp.sum(red_ref[...], axis=0)
    lane = lax.broadcasted_iota(jnp.int32, (1, 128), 1)
    return [
        jnp.broadcast_to(
            jnp.sum(jnp.where(lane == first + i, total, 0.0), axis=1, keepdims=True), (1, 128)
        )
        for i in range(count)
    ]


def galerkin(nu):
    m = len(nu) // 2
    mu = [nu[i] + nu[i + 1] for i in range(2 * m - 1)]
    rows = [[mu[i + j] for j in range(m)] + [nu[i]] for i in range(m)]
    for i in range(m):
        for r in range(i + 1, m):
            factor = rows[r][i] / rows[i][i]
            for j in range(i + 1, m + 1):
                rows[r][j] = rows[r][j] - factor * rows[i][j]
    c = [None] * m
    for i in reversed(range(m)):
        acc = rows[i][m]
        for j in range(i + 1, m):
            acc = acc - rows[i][j] * c[j]
        c[i] = acc / rows[i][i]
    return c


def send(odd_side, lo, hi, even_out, odd_out):
    for at, (low, high) in enumerate(zip(lo, hi)):
        even_out[at] = jnp.where(odd_side == 0, high, low)
        odd_out[at] = jnp.where(odd_side == 0, low, high)


def below(odd_side, even_ref, odd_ref, at):
    return jnp.where(odd_side == 0, odd_ref[at], even_ref[at])


def above(odd_side, even_ref, odd_ref, at):
    return jnp.where(odd_side == 0, even_ref[at], odd_ref[at])


def start_kernel(
    rigid_ref, dilate_ref, heat_ref, coef_ref, time_ref, place_ref,
    own_ref, even_ref, odd_ref, far_ref,
    kel_ref, theta_ref, inv_f_ref, inv_c_ref, state_ref,
    zf_ref, ozf_ref, oozf_ref, zc_ref, ozc_ref,
    even_out, odd_out, far_out, red_ref,
    kal_ref, au_ref, w_ref,
):
    ny, nz = kel_ref.shape[1:]
    sh = Shifts(ny, nz)
    chunks = own_ref.shape[0]
    side = place_ref[1]

    def raw(field, i):
        if i < 0:
            parts = [below(side, even_ref, odd_ref, (c, field, i + L)) for c in range(chunks)]
        elif i < L:
            parts = [own_ref[c, field, i] for c in range(chunks)]
        elif i < 2 * L:
            parts = [above(side, even_ref, odd_ref, (c, field, i - L)) for c in range(chunks)]
        else:
            parts = [far_ref[c, 0, 0] for c in range(chunks)]
        return jnp.concatenate(parts, axis=0)

    for e in range(-3, 6):
        label = raw(0, e)
        stiff = jnp.zeros((ny, nz), jnp.float32)
        load = jnp.zeros((ny, nz), jnp.float32)
        for region in range(rigid_ref.shape[0]):
            here = label == (region + 1.0)
            stiff = jnp.where(here, rigid_ref[region], stiff)
            load = jnp.where(here, dilate_ref[region], load)
        kel_ref[e + 3] = stiff * (-1.0 / 12.0)
        kal_ref[e + 3] = 0.25 * (stiff * load)

    decay_f, rest_f, ff, shift_f = prony(1.0, coef_ref, time_ref)
    decay_c, rest_c, fc, shift_c = prony(1.0 * PACES, coef_ref, time_ref)

    for i in range(-2, 6):
        ksum = kel_ref[i + 2] + kel_ref[i + 3]
        ksum = ksum + sh.ydn(ksum)
        ksum = ksum + sh.zdn(ksum)
        diag = -4.0 * ksum
        asum = kal_ref[i + 2] + kal_ref[i + 3]
        asum = asum + sh.ydn(asum)
        theta_ref[i + 2] = sh.zdn(asum) - asum
        inside = raw(0, i) > 0.5
        inv_f_ref[i + 2] = jnp.where(inside, 1.0 / (diag + shift_f), 0.0)
        inv_c_ref[i + 2] = jnp.where(inside, 1.0 / (diag + shift_c), 0.0)

    for i in range(-3, 7):
        state_ref[i + 3] = raw(1, i)

    def k(e):
        return kel_ref[e + 3]

    def put_au(i, plane):
        au_ref[i + 2] = plane

    off_diagonal(sh, lambda i: state_ref[i + 3], k, -2, 5, put_au)

    zeros = jnp.zeros((ny, nz), jnp.float32)
    acc = [zeros] * 10
    for i in range(-2, 6):
        h = [raw(2 + p, i) for p in range(PRONY)]
        fh = [ff[p] * h[p] for p in range(PRONY)]
        state_ref[10 + i + 2] = decay_f[0] * fh[0] + decay_f[1] * fh[1] + decay_f[2] * fh[2]
        ui = state_ref[i + 3]
        load = heat_ref[0, 0] * theta_ref[i + 2] + (fh[0] + fh[1] + fh[2])
        s = load + ui - au_ref[i + 2]
        z = inv_f_ref[i + 2] * s - ui
        zf_ref[i + 2] = z
        if 0 <= i < L:
            acc[0] = acc[0] + z * (s - ui * (1.0 / inv_f_ref[i + 2]))
        if i < 5:
            load = heat_ref[0, 1] * theta_ref[i + 2]
            load = load + (fc[0] * h[0] + fc[1] * h[1] + fc[2] * h[2])
            s = load + ui * (1.0 / PACES) - au_ref[i + 2]
            z = inv_c_ref[i + 2] * s - ui
            w_ref[i + 2] = z
            if 0 <= i < L:
                zc_ref[i] = z
                acc[6] = acc[6] + z * (s - ui * (1.0 / inv_c_ref[i + 2]))

    def put_oz(i, plane):
        oz = inv_f_ref[i + 2] * plane
        ozf_ref[i + 1] = oz
        if 0 <= i < L:
            acc[1] = acc[1] + zf_ref[i + 2] * plane
            acc[2] = acc[2] + oz * plane

    off_diagonal(sh, lambda i: zf_ref[i + 2], k, -1, 4, put_oz)

    def put_ooz(i, plane):
        ooz = inv_f_ref[i + 2] * plane
        oozf_ref[i] = ooz
        if i < L:
            acc[3] = acc[3] + ozf_ref[i + 1] * plane
            acc[4] = acc[4] + ooz * plane

    off_diagonal(sh, lambda i: ozf_ref[i + 1], k, 0, 3, put_ooz)

    def put_last(i, plane):
        acc[5] = acc[5] + oozf_ref[i] * plane

    by_elements(sh, lambda i: oozf_ref[i], k, put_last)

    def put_ozc(i, plane):
        oz = inv_c_ref[i + 2] * plane
        au_ref[i + 2] = oz
        if 0 <= i < L:
            ozc_ref[i] = oz
            acc[7] = acc[7] + w_ref[i + 2] * plane
            acc[8] = acc[8] + oz * plane

    off_diagonal(sh, lambda i: w_ref[i + 2], k, -1, 3, put_ozc)

    def put_lastc(i, plane):
        acc[9] = acc[9] + au_ref[i + 2] * plane

    off_diagonal(sh, lambda i: au_ref[i + 2], k, 0, 2, put_lastc)
    moments_out(acc, red_ref)

    hi = [zf_ref[2], ozf_ref[1], ozf_ref[2], oozf_ref[0], oozf_ref[1], oozf_ref[2]]
    lo = [ozf_ref[3], oozf_ref[1], oozf_ref[2]]
    send(side, lo + lo, hi, even_out, odd_out)
    far_out[0], far_out[1], far_out[2] = zf_ref[2], ozf_ref[1], oozf_ref[0]


def by_elements(sh, v, k, put):
    none = jnp.zeros((sh.ny, sh.nz), jnp.float32)

    def nodes(i):
        return v(i) if 0 <= i <= L else none

    def elements(e):
        return k(e) if 0 <= e < L else none

    off_diagonal(sh, nodes, elements, 0, L, put)


def second_kernel(
    heat_ref, coef_ref, time_ref, place_ref,
    red_in, kel_ref, theta_ref, inv_f_ref, state_ref, own_ref,
    zf_ref, ozf_ref, oozf_ref, zc_ref, ozc_ref,
    even_ref, odd_ref, far_ref,
    base_ref, z_out, oz_out, ooz_out, red_ref,
    u_ref, z_ref, oz_ref, ooz_ref, au_ref,
):
    ny, nz = kel_ref.shape[1:]
    sh = Shifts(ny, nz)
    chunks = own_ref.shape[0]
    decay_f, rest_f, ff, shift_f = prony(1.0, coef_ref, time_ref)
    decay_c, rest_c, fc, shift_c = prony(1.0 * PACES, coef_ref, time_ref)
    c = galerkin(moments_in(red_in, 0, 6))
    b = galerkin(moments_in(red_in, 6, 4))
    side = place_ref[1]

    def basis(i, at, ref, low, high, up, down):
        if i == 6:
            return far_ref[at]
        if i < low:
            return below(side, even_ref, odd_ref, up + i + L)
        if i > high:
            return above(side, even_ref, odd_ref, down + i - high - 1)
        return ref[i - low]

    for i in range(-3, 7):
        z = basis(i, 0, zf_ref, -2, 5, 0, None)
        oz = basis(i, 1, ozf_ref, -1, 4, 1, 0)
        ooz = basis(i, 2, oozf_ref, 0, 3, 3, 1)
        u_ref[i + 3] = state_ref[i + 3] + c[0] * z + c[1] * oz + c[2] * ooz

    def k(e):
        return kel_ref[e + 3]

    def put_au(i, plane):
        au_ref[i + 2] = plane

    off_diagonal(sh, lambda i: u_ref[i + 3], k, -2, 5, put_au)

    grow = ff[0] * rest_f[0] + ff[1] * rest_f[1] + ff[2] * rest_f[2]
    zeros = jnp.zeros((ny, nz), jnp.float32)
    acc = [zeros] * 6
    weight = jnp.where(place_ref[0] == 0, 0.0, 1.0)
    for i in range(-2, 6):
        ui = u_ref[i + 3]
        s = heat_ref[0, 1] * theta_ref[i + 2] + state_ref[10 + i + 2] + (grow + 1.0) * ui
        s = s - au_ref[i + 2]
        z = inv_f_ref[i + 2] * s - ui
        z_ref[i + 2] = z
        if 0 <= i < L:
            z_out[i] = z
            acc[0] = acc[0] + z * (s - ui * (1.0 / inv_f_ref[i + 2]))

    for i in range(L):
        u1 = u_ref[i + 3]
        g = state_ref[i + 3] + b[0] * zc_ref[i] + b[1] * ozc_ref[i]
        base_ref[i] = u1 - weight * g
        for p in range(PRONY):
            h = jnp.concatenate([own_ref[q, 2 + p, i] for q in range(chunks)], axis=0)
            h1 = decay_f[p] * h + rest_f[p] * u1
            gh = decay_c[p] * h + rest_c[p] * g
            base_ref[L * (1 + p) + i] = decay_f[p] * h1 + rest_f[p] * u1 - weight * gh

    def put_oz(i, plane):
        oz = inv_f_ref[i + 2] * plane
        oz_ref[i + 1] = oz
        if 0 <= i < L:
            oz_out[i] = oz
            acc[1] = acc[1] + z_ref[i + 2] * plane
            acc[2] = acc[2] + oz * plane

    off_diagonal(sh, lambda i: z_ref[i + 2], k, -1, 4, put_oz)

    def put_ooz(i, plane):
        ooz = inv_f_ref[i + 2] * plane
        ooz_ref[i] = ooz
        if i < L:
            ooz_out[i] = ooz
            acc[3] = acc[3] + oz_ref[i + 1] * plane
            acc[4] = acc[4] + ooz * plane

    off_diagonal(sh, lambda i: oz_ref[i + 1], k, 0, 3, put_ooz)

    def put_last(i, plane):
        acc[5] = acc[5] + ooz_ref[i] * plane

    by_elements(sh, lambda i: ooz_ref[i], k, put_last)
    moments_out(acc, red_ref)


def block_kernel(heat_ref, coef_ref, time_ref, red_in, base_ref, z_ref, oz_ref, ooz_ref, blk_ref):
    decay_f, rest_f, ff, shift_f = prony(1.0, coef_ref, time_ref)
    c = galerkin(moments_in(red_in, 0, 6))
    ny = z_ref.shape[1]
    for i in range(L):
        delta = c[0] * z_ref[i] + c[1] * oz_ref[i] + c[2] * ooz_ref[i]
        blk_ref[i * ny : (i + 1) * ny] = base_ref[i] + delta
        for p in range(PRONY):
            at = L * (1 + p) + i
            blk_ref[at * ny : (at + 1) * ny] = base_ref[at] + rest_f[p] * delta
    blk_ref[4 * L * ny :] = jnp.full((8, blk_ref.shape[1]), heat_ref[0, PACES - 1], jnp.float32)


def halo_base(f, base_ref):
    sums = [
        f[0] * base_ref[L + i] + f[1] * base_ref[2 * L + i] + f[2] * base_ref[3 * L + i]
        for i in range(L)
    ]
    u = [base_ref[i] for i in range(L)]
    return u + [sums[0], sums[1]], u + [sums[1], sums[2]]


def opening_kernel(coef_ref, time_ref, place_ref, blk_ref, base_ref, even_out, odd_out):
    decay, rest, f, shift = prony(1.0 * PACES, coef_ref, time_ref)
    ny = even_out.shape[1]
    for at in range(4 * L):
        base_ref[at] = blk_ref[at * ny : (at + 1) * ny]
    lo, hi = halo_base(f, base_ref)
    send(place_ref[1], lo, hi, even_out, odd_out)


def chain_kernel(turn, count, opened, rounds, *refs):
    refs = list(refs)
    coef_ref, time_ref, place_ref = refs[:3]
    refs = refs[3:]
    if opened:
        base_in, even_ref, odd_ref = refs[:3]
        refs = refs[3:]
    else:
        red_in, base_in, z_in, oz_in, even_ref, odd_ref = refs[:6]
        refs = refs[6:]
    kel_ref, theta_ref, inv_ref, blk_ref = refs[:4]
    if rounds:
        outs, (red_ref, u_ref, au_ref, base_ref, z_ref, oz_ref) = refs[4 : 4 + rounds], refs[4 + rounds :]
    else:
        base_ref, z_ref, oz_ref, even_out, odd_out, red_ref, u_ref, au_ref = refs[4:]
    ny, nz = kel_ref.shape[1:]
    sh = Shifts(ny, nz)
    decay, rest, f, shift = prony(1.0 * PACES, coef_ref, time_ref)
    grow = f[0] * rest[0] + f[1] * rest[1] + f[2] * rest[2]
    step = lax.rem(place_ref[0] + turn, count)
    heat = blk_ref[4 * L * ny : 4 * L * ny + 1]
    opening = step == 0
    fresh = step == 1
    side = place_ref[1]

    if not opened:
        c = galerkin(moments_in(red_in, 0, 4))

    def near(i, low_at, high_at):
        if i < 0:
            return below(side, even_ref, odd_ref, low_at)
        return above(side, even_ref, odd_ref, high_at)

    def delta(i):
        z = z_in[i + 2] if -2 <= i <= 4 else near(i, 5, 5)
        if -1 <= i <= 3:
            oz = oz_in[i + 1]
        else:
            at = 6 if i in (-3, 5) else 7
            oz = near(i, at, at)
        return jnp.where(fresh, 0.0, c[0] * z + c[1] * oz)

    for i in range(-3, 6):
        base = base_in[i] if 0 <= i < L else near(i, i + 3, i - L)
        d = None if opened else delta(i)
        u_ref[i + 3] = base if opened else base + d
        if 0 <= i < L:
            h = [base_in[L * (1 + p) + i] for p in range(PRONY)]
            if not opened:
                h = [h[p] + rest[p] * d for p in range(PRONY)]
            total = f[0] * h[0] + f[1] * h[1] + f[2] * h[2]
            ui = u_ref[i + 3]
            base_ref[i] = jnp.where(opening, 0.0, ui) + blk_ref[i * ny : (i + 1) * ny]
            for p in range(PRONY):
                at = L * (1 + p) + i
                ahead = jnp.where(opening, 0.0, decay[p] * h[p] + rest[p] * ui)
                base_ref[at] = ahead + blk_ref[at * ny : (at + 1) * ny]
        elif -2 <= i < 5:
            total = near(i, 3 + i + 2, 3 + i - L)
            if not opened:
                total = total + grow * d
        if -2 <= i < 5:
            au_ref[i + 2] = heat * theta_ref[i + 2] + total

    zeros = jnp.zeros((ny, nz), jnp.float32)
    acc = [zeros] * 4

    def k(e):
        return kel_ref[e + 3]

    def put_z(i, plane):
        ui = u_ref[i + 3]
        s = au_ref[i + 2] + ui * (1.0 / PACES) - plane
        inv = inv_ref[i + 2]
        z = inv * s - ui
        z_ref[i + 2] = z
        if 0 <= i < L:
            acc[0] = acc[0] + z * (s - ui * (1.0 / inv))

    off_diagonal(sh, lambda i: u_ref[i + 3], k, -2, 4, put_z)

    def put_oz(i, plane):
        oz = inv_ref[i + 2] * plane
        oz_ref[i + 1] = oz
        if 0 <= i < L:
            acc[1] = acc[1] + z_ref[i + 2] * plane
            acc[2] = acc[2] + oz * plane

    off_diagonal(sh, lambda i: z_ref[i + 2], k, -1, 3, put_oz)

    def put_last(i, plane):
        acc[3] = acc[3] + oz_ref[i + 1] * plane

    off_diagonal(sh, lambda i: oz_ref[i + 1], k, 0, 2, put_last)
    moments_out(acc, red_ref)

    if rounds:
        width = ny // rounds
        for r, out_ref in enumerate(outs):
            cut = lax.rem(2 * place_ref[2] + side + r, rounds) * width
            rows = pl.ds(pl.multiple_of(cut, width), width)
            for i in range(L):
                for field in range(1 + PRONY):
                    out_ref[field, i] = base_ref[L * field + i, rows]
                out_ref[4, i] = z_ref[i + 2, rows]
                out_ref[5, i] = oz_ref[i + 1, rows]
        return

    lo, hi = halo_base(f, base_ref)
    lo = lo + [z_ref[2 + 2], oz_ref[2 + 1], oz_ref[1 + 1]]
    hi = hi + [z_ref[0 + 2], oz_ref[0 + 1], oz_ref[1 + 1]]
    send(side, lo, hi, even_out, odd_out)


def closing_kernel(coef_ref, time_ref, place_ref, red_in, *refs):
    parts, out_ref = refs[:-1], refs[-1]
    decay, rest, f, shift = prony(1.0 * PACES, coef_ref, time_ref)
    c = galerkin(moments_in(red_in, 0, 4))
    first = place_ref[0] == 0
    count = len(parts)
    for r, part_ref in enumerate(parts):
        at = lax.rem(place_ref[4] + count - r, count) * L
        for i in range(L):
            delta = jnp.where(first, 0.0, c[0] * part_ref[4, i] + c[1] * part_ref[5, i])
            out_ref[0, 0, at + i] = part_ref[0, i] + delta
            for p in range(PRONY):
                out_ref[0, 1 + p, at + i] = part_ref[1 + p, i] + rest[p] * delta


def spread_kernel(place_ref, label_ref, values_ref, *out_refs):
    count = len(out_refs)
    for r, out_ref in enumerate(out_refs):
        first = lax.rem(place_ref[4] + count - r, count) * L
        for i in range(L):
            out_ref[0, i] = label_ref[first + i].astype(jnp.float32) + 1.0
            for field in range(1 + PRONY):
                out_ref[1 + field, i] = values_ref[0, field, first + i]


def join_kernel(place_ref, *refs):
    got_refs, out_ref = refs[:-1], refs[-1]
    count = len(got_refs)
    for r, got_ref in enumerate(got_refs):
        to = lax.rem(2 * place_ref[2] + place_ref[1] + r, count)
        for field in range(2 + PRONY):
            for i in range(L):
                out_ref[to, field, i] = got_ref[field, i]


SMEM = pl.BlockSpec(memory_space=pltpu.SMEM)
VMEM = pl.BlockSpec(memory_space=pltpu.VMEM)


def call(kernel, name, small, large, outs, scratch=()):
    f32 = jnp.float32
    return pl.pallas_call(
        kernel,
        name=name,
        out_shape=[jax.ShapeDtypeStruct(s, f32) for s in outs],
        in_specs=[SMEM] * len(small) + [VMEM] * len(large),
        out_specs=[VMEM] * len(outs),
        scratch_shapes=[pltpu.VMEM(s, f32) for s in scratch],
        compiler_params=pltpu.CompilerParams(vmem_limit_bytes=LIMIT),
    )(*small, *large)


def on_device(
    segment_opening_values,
    cell_material_label,
    material_rigidity,
    dilation_mismatch,
    heat_swings_array,
    prony_coefficients,
    prony_decay_times,
):
    n_tm, n_gy = lax.axis_size("tm"), lax.axis_size("gy")
    line = lax.axis_size("gx") * n_gy
    nx, ny_part, nz = cell_material_label.shape
    ny = ny_part * n_gy
    assert nx == L * n_gy and n_gy == 4
    plane = (ny, nz)

    def device(position):
        row, rest = divmod(position, 2 * n_gy)
        x, core = divmod(rest, 2)
        return (2 * row + core) * n_gy + (x if row % 2 == 0 else n_gy - 1 - x)

    def deal(values, back=False):
        received = []
        for r, value in enumerate(values):
            perm = []
            for position in range(line):
                row, rest = divmod(position, 2 * n_gy)
                x, core = divmod(rest, 2)
                to = (2 * row + x // 2) * n_gy + (2 * (x % 2) + core + r) % n_gy
                perm.append((to, device(position)) if back else (device(position), to))
            received.append(lax.ppermute(value, LINE, sorted(perm)))
        return received

    def trade(even, odd):
        received = []
        for side, value in enumerate((even, odd)):
            pairs = [(device(p), device(p + 1)) for p in range(side, line - 1, 2)]
            both = pairs + [(b, a) for a, b in pairs]
            received.append(lax.ppermute(value, LINE, sorted(both)))
        return received

    def from_next_but_one(value):
        perm = [(device(p + 2), device(p)) for p in range(line - 2)]
        return lax.ppermute(value, LINE, sorted(perm))

    def exchanged(red):
        return lax.all_to_all(red, LINE, 0, 0, tiled=True)

    def ring(block):
        return lax.ppermute(block, "tm", [(s, (s - 1) % n_tm) for s in range(n_tm)])

    gx, gy = lax.axis_index("gx"), lax.axis_index("gy")
    core, flip = gx % 2, gx // 2 % 2
    x = jnp.where(flip == 0, gy, n_gy - 1 - gy)
    place = jnp.stack([lax.axis_index("tm"), core, x % 2, flip, gy]).astype(jnp.int32)
    prony_args = (prony_coefficients, prony_decay_times)

    parts = call(
        spread_kernel,
        "spread",
        (place,),
        (cell_material_label, segment_opening_values),
        [(2 + PRONY, L, ny_part, nz)] * n_gy,
    )
    (own,) = call(
        join_kernel, "join", (place,), deal(parts, True), [(n_gy, 2 + PRONY, L, ny_part, nz)]
    )
    near, far = trade(own, own), from_next_but_one(own[:, 1:2, :1])

    red_shape = (line, 1, 128)
    (kel, theta, inv_f, inv_c, state, zf, ozf, oozf, zc, ozc, even, odd, far, red) = call(
        start_kernel,
        "start",
        (material_rigidity, dilation_mismatch, heat_swings_array, *prony_args, place),
        (own, *near, far),
        [
            (9, *plane), (8, *plane), (8, *plane), (8, *plane), (18, *plane),
            (8, *plane), (6, *plane), (4, *plane), (L, *plane), (L, *plane),
            (6, *plane), (6, *plane), (3, *plane), red_shape,
        ],
        [(9, *plane), (8, *plane), (7, *plane)],
    )
    red = exchanged(red)
    near, far = trade(even, odd), from_next_but_one(far)
    base, z, oz, ooz, red = call(
        second_kernel,
        "second",
        (heat_swings_array, *prony_args, place),
        (red, kel, theta, inv_f, state, own, zf, ozf, oozf, zc, ozc, *near, far),
        [(4 * L, *plane), (L, *plane), (L, *plane), (L, *plane), red_shape],
        [(10, *plane), (8, *plane), (6, *plane), (4, *plane), (8, *plane)],
    )
    red = exchanged(red)
    (block,) = call(
        block_kernel,
        "block",
        (heat_swings_array, *prony_args),
        (red, base, z, oz, ooz),
        [(4 * L * ny + 8, nz)],
    )
    mine = block
    block = ring(block)
    base, even, odd = call(
        opening_kernel,
        "opening",
        (*prony_args, place),
        (block,),
        [(4 * L, *plane), (5, *plane), (5, *plane)],
    )
    past = (base,)
    for turn in range(2, n_tm + 1):
        if turn < n_tm:
            block, even = lax.optimization_barrier((block, even))
            block = ring(block)
        else:
            block = mine
        past = (*past, *trade(even, odd))
        last = turn == n_tm
        state = [(4 * L, *plane), (7, *plane), (5, *plane)]
        work = [(9, *plane), (7, *plane)]
        *outs, red = call(
            functools.partial(chain_kernel, turn, n_tm, turn == 2, n_gy if last else 0),
            f"chain{turn}",
            (*prony_args, place),
            (*past, kel, theta, inv_c, block),
            [(3 + PRONY, L, ny_part, nz)] * n_gy + [red_shape]
            if last
            else [*state, (8, *plane), (8, *plane), red_shape],
            work + state if last else work,
        )
        if last:
            break
        base, z, oz, even, odd = outs
        past = (exchanged(red), base, z, oz)
    parts = deal(outs)
    (out,) = call(
        closing_kernel,
        "closing",
        (*prony_args, place),
        (exchanged(red), *parts),
        [(1, 1 + PRONY, nx, ny_part, nz)],
    )
    return out


def solution(mesh):
    placed = (
        P("tm", None, "gx", "gy", None),
        P("gx", "gy", None),
        P(),
        P(),
        P("tm", None),
        P(),
        P(),
    )
    return jax.shard_map(
        on_device,
        mesh=mesh,
        in_specs=placed,
        out_specs=P("tm", None, "gx", "gy", None),
        check_vma=False,
    )
```

time: 241 us -> 226 us (0.938)
  blocking collectives: 131 us -> 107 us
  starting transfers between devices: 61.3 us -> 69.9 us
    all_to_all x2 -> x0, blocking collectives: 22.4 us -> none  [the longest x1 12.8 us: on_device(): own = lax.all_to_all(raw, 'gy', 0, 0, tiled=True)]
    ppermute x22 -> x28, starting transfers between devices: 46.4 us -> 55.2 us  [the longest x18 29 us: trade(): received.append(lax.ppermute(value, LINE, sorted(both)))]
    ppermute x22 -> x28, waiting for transfers between devices: 13.2 us -> 13.9 us  [the longest x18 7.22 us: trade(): received.append(lax.ppermute(value, LINE, sorted(both)))]
  transfers between devices with their start and end apart: 29 -> 35, of which waited for: 4 -> 6; matrix products, arithmetic and copies ran while one was open for 0% -> 0% of each run, Pallas kernels for 0% -> 0%
where the time goes in v4:
time: 226 us; the launch traced here: 225 us
  blocking collectives  107 us (47%)
  starting transfers between devices  69.9 us (31%)
  Pallas kernels  24.1 us (11%)
  waiting for transfers between devices  21.8 us (10%)
    all_to_all x9, blocking collectives, exchanged(): return lax.all_to_all(red, LINE, 0, 0, tiled=True)  107 us
    ppermute x18, starting transfers between devices, trade(): received.append(lax.ppermute(value, LINE, sorted(both)))  29 us
    pallas_call x14, Pallas kernels, call(): pl.pallas_call(kernel, name=name, out_shape=[jax.ShapeDtypeStruct(s, f32)...  24.1 us
    ppermute x8, starting transfers between devices, deal(): received.append(lax.ppermute(value, LINE, sorted(perm)))  23.6 us
    ppermute x7, starting transfers between devices, ring(): return lax.ppermute(block, 'tm', [(s, (s - 1) % n_tm) for s in range(n_tm)])  14.7 us
    ppermute x7, waiting for transfers between devices, ring(): return lax.ppermute(block, 'tm', [(s, (s - 1) % n_tm) for s in range(n_tm)])  7.92 us
    ppermute x18, waiting for transfers between devices, trade(): received.append(lax.ppermute(value, LINE, sorted(both)))  7.22 us
  transfers between devices with their start and end apart: 35, of which 6 were waited for; matrix products, arithmetic and copies ran while one was open for 0% of the time, Pallas kernels for 0%

profile of v4, /device:TPU:1, one launch (start us, length us, event | category | flops | bytes accessed | tf_op | source)
XLA Modules:
  0.0 225.2 jit_solution(3716116799040733236)
XLA Ops:
  2.5 6.0 %collective-permute-start = (f32[5,3,16,128]{3,2,1,0:T(8,128)S(1)}, f32[5,3,16,128]{3,2,1,0:T(8,128)S(1)}, u32[]{:S(2)}, u32[]{:S(2)}) collective-permute-start(f32[5,3,16,128]{3,2,1,0:T(8,128)S(1)} %get-tuple-element.84), channel_id=1, source_target_pairs={{0,0},{1,4},{2,1},{3,5},{4,2},{5,6},{6,3},{7,7},{8,11},{9,15},{10,... | collective-permute-start | bytes 368648 | tf_op jit(solution)/shard_map/ppermute | solution.py:591
  8.5 1.9 collective-permute-start.1
  10.5 1.2 collective-permute-start.2
  11.7 4.1 %collective-permute-start.3 = (f32[5,3,16,128]{3,2,1,0:T(8,128)S(1)}, f32[5,3,16,128]{3,2,1,0:T(8,128)S(1)}, u32[]{:S(2)}, u32[]{:S(2)}) collective-permute-start(f32[5,3,16,128]{3,2,1,0:T(8,128)S(1)} %get-tuple-element.87), channel_id=1, source_target_pairs={{0,4},{1,1},{2,5},{3,0},{4,6},{5,3},{6,7},{7,2},{8,15},{9,10},{10,... | collective-permute-start | bytes 368648 | tf_op jit(solution)/shard_map/ppermute | solution.py:591
  16.3 2.4 %collective-permute-done.2.refs_2_ = f32[5,3,16,128]{3,2,1,0:T(8,128)S(1)} collective-permute-done((f32[5,3,16,128]{3,2,1,0:T(8,128)S(1)}, f32[5,3,16,128]{3,2,1,0:T(8,128)S(1)}, u32[]{:S(2)}, u32[]{:S(2)}) %collective-permute-start.2) | collective-permute-done | bytes 122912 | tf_op jit(solution)/shard_map/ppermute | solution.py:591
  19.3 2.1 collective-permute-start.5
  22.3 1.3 collective-permute-start.6
  23.6 3.8 %collective-permute-done.6.far_ref = f32[4,1,1,16,128]{4,3,2,1,0:T(8,128)S(1)} collective-permute-done((f32[4,1,1,16,128]{4,3,2,1,0:T(8,128)S(1)}, f32[4,1,1,16,128]{4,3,2,1,0:T(8,128)S(1)}, u32[]{:S(2)}, u32[]{:S(2)}) %collective-permute-start.6) | collective-permute-done | bytes 32800 | tf_op jit(solution)/shard_map/ppermute | solution.py:604
  27.3 2.6 %collective-permute-done.5.odd_ref = f32[4,5,3,16,128]{4,3,2,1,0:T(8,128)S(1)} collective-permute-done((f32[4,5,3,16,128]{4,3,2,1,0:T(8,128)S(1)}, f32[4,5,3,16,128]{4,3,2,1,0:T(8,128)S(1)}, u32[]{:S(2)}, u32[]{:S(2)}) %collective-permute-start.5) | collective-permute-done | bytes 491552 | tf_op jit(solution)/shard_map/ppermute | solution.py:599
  30.0 3.9 %start.1 = (f32[9,64,128]{2,1,0:T(8,128)S(1)}, f32[8,64,128]{2,1,0:T(8,128)S(1)}, f32[8,64,128]{2,1,0:T(8,128)S(1)}, f32[8,64,128]{2,1,0:T(8,128)S(1)}, f32[18,6...) custom-call(f32[6]{0:T(128)S(1)} %copy-done.5, ...), custom_call_target="tpu_custom_call" | custom-call | tf_op jit(solution)/shard_map/start/pallas_call | solution.py:550
  35.1 1.9 collective-permute-start.8
  37.0 1.3 collective-permute-start.9
  38.3 16.2 %all_to_all.45.red_in = f32[32,1,128]{2,1,0:T(1,128)S(1)} all-to-all(f32[32,1,128]{2,1,0:T(1,128)S(1)} %get-tuple-element.88), channel_id=1, replica_groups=mesh['tm'=8,'gx'=8,'gy'=4] {'gx','gy'}, dimensions={0} | all-to-all | bytes 32768 | tf_op jit(solution)/shard_map/all_to_all | solution.py:607
  54.5 2.4 %second.1 = (f32[12,64,128]{2,1,0:T(8,128)S(1)}, f32[3,64,128]{2,1,0:T(8,128)S(1)}, f32[3,64,128]{2,1,0:T(8,128)S(1)}, f32[3,64,128]{2,1,0:T(8,128)S(1)}, f32[32,1,128]{2,1,0:T(1,128)S(1)}) custom-call(f32[1,2]{1,0:T(1,128)S(1)} %copy-done.4, f32[3]{0:T(128)S(1)} %copy-done.2, f32[3]{0:T(128)S(1)} %copy-done.3, s32[5]{0:T(128)S(1)} %stack.23.place_ref.refs_2_, ...), custom_call_target="tpu_custom_call" | custom-call | tf_op jit(solution)/shard_map/second/pallas_call | solution.py:550
  56.9 10.7 %all_to_all.46.red_in = f32[32,1,128]{2,1,0:T(1,128)S(1)} all-to-all(f32[32,1,128]{2,1,0:T(1,128)S(1)} %get-tuple-element.101), channel_id=1, replica_groups=mesh['tm'=8,'gx'=8,'gy'=4] {'gx','gy'}, dimensions={0} | all-to-all | bytes 32768 | tf_op jit(solution)/shard_map/all_to_all | solution.py:607
  68.3 5.7 %collective-permute-start.10 = (f32[776,128]{1,0:T(8,128)S(1)}, f32[776,128]{1,0:T(8,128)S(1)}, u32[]{:S(2)}, u32[]{:S(2)}) collective-permute-start(f32[776,128]{1,0:T(8,128)S(1)} %block.1.refs_12_), channel_id=1, source_target_pairs={{0,224},{32,0},{64,32},{96,64},{128,96},{160,128},{192,160},{224,1... | collective-permute-start | bytes 1191944 | tf_op jit(solution)/shard_map/ppermute | solution.py:610
  74.0 7.9 %collective-permute-done.10.blk_ref = f32[776,128]{1,0:T(8,128)S(1)} collective-permute-done((f32[776,128]{1,0:T(8,128)S(1)}, f32[776,128]{1,0:T(8,128)S(1)}, u32[]{:S(2)}, u32[]{:S(2)}) %collective-permute-start.10) | collective-permute-done | bytes 397344 | tf_op jit(solution)/shard_map/ppermute | solution.py:610
  82.5 3.5 %collective-permute-start.13 = (f32[776,128]{1,0:T(8,128)S(1)}, f32[776,128]{1,0:T(8,128)S(1)}, u32[]{:S(2)}, u32[]{:S(2)}) collective-permute-start(f32[776,128]{1,0:T(8,128)S(1)} %collective-permute-done.10.blk_ref), channel_id=1, source_target_pairs={{0,224},{32,0},{64,32},{96,64},{128,96},{160,128},{192,160},{224,1... | collective-permute-start | bytes 1191944 | tf_op jit(solution)/shard_map/ppermute | solution.py:610
  86.0 1.8 collective-permute-start.11
  87.8 2.1 collective-permute-start.12
  89.9 4.5 %collective-permute-done.12.refs_5_ = f32[5,64,128]{2,1,0:T(8,128)S(1)} collective-permute-done((f32[5,64,128]{2,1,0:T(8,128)S(1)}, f32[5,64,128]{2,1,0:T(8,128)S(1)}, u32[]{:S(2)}, u32[]{:S(2)}) %collective-permute-start.12) | collective-permute-done | bytes 163872 | tf_op jit(solution)/shard_map/ppermute | solution.py:599
  94.4 1.8 chain2.1
  96.2 2.2 collective-permute-start.16
  98.5 2.7 %collective-permute-start.14 = (f32[8,64,128]{2,1,0:T(8,128)S(1)}, f32[8,64,128]{2,1,0:T(8,128)S(1)}, u32[]{:S(2)}, u32[]{:S(2)}) collective-permute-start(f32[8,64,128]{2,1,0:T(8,128)S(1)} %get-tuple-element.117), channel_id=1, source_target_pairs={{0,4},{1,5},{2,6},{3,7},{4,0},{5,1},{6,2},{7,3},{8,12},{9,13},{10,... | collective-permute-start | bytes 786440 | tf_op jit(solution)/shard_map/ppermute | solution.py:599
  101.2 2.1 collective-permute-start.15
  103.3 11.4 %all_to_all.47.refs_3_ = f32[32,1,128]{2,1,0:T(1,128)S(1)} all-to-all(f32[32,1,128]{2,1,0:T(1,128)S(1)} %get-tuple-element.112), channel_id=1, replica_groups=mesh['tm'=8,'gx'=8,'gy'=4] {'gx','gy'}, dimensions={0} | all-to-all | bytes 32768 | tf_op jit(solution)/shard_map/all_to_all | solution.py:607
  114.7 2.0 chain3.1
  117.5 2.1 collective-permute-start.18
  119.6 11.4 %all_to_all.48.refs_3_ = f32[32,1,128]{2,1,0:T(1,128)S(1)} all-to-all(f32[32,1,128]{2,1,0:T(1,128)S(1)} %get-tuple-element.120), channel_id=1, replica_groups=mesh['tm'=8,'gx'=8,'gy'=4] {'gx','gy'}, dimensions={0} | all-to-all | bytes 32768 | tf_op jit(solution)/shard_map/all_to_all | solution.py:607
  131.0 2.0 chain4.1
  133.8 2.1 collective-permute-start.21
  135.9 11.4 %all_to_all.49.refs_3_ = f32[32,1,128]{2,1,0:T(1,128)S(1)} all-to-all(f32[32,1,128]{2,1,0:T(1,128)S(1)} %get-tuple-element.128), channel_id=1, replica_groups=mesh['tm'=8,'gx'=8,'gy'=4] {'gx','gy'}, dimensions={0} | all-to-all | bytes 32768 | tf_op jit(solution)/shard_map/all_to_all | solution.py:607
  147.3 2.0 chain5.1
  150.5 2.1 collective-permute-start.24
  152.6 11.4 %all_to_all.50.refs_3_ = f32[32,1,128]{2,1,0:T(1,128)S(1)} all-to-all(f32[32,1,128]{2,1,0:T(1,128)S(1)} %get-tuple-element.136), channel_id=1, replica_groups=mesh['tm'=8,'gx'=8,'gy'=4] {'gx','gy'}, dimensions={0} | all-to-all | bytes 32768 | tf_op jit(solution)/shard_map/all_to_all | solution.py:607
  164.0 2.0 chain6.1
  166.0 2.9 %collective-permute-start.28 = (f32[776,128]{1,0:T(8,128)S(1)}, f32[776,128]{1,0:T(8,128)S(1)}, u32[]{:S(2)}, u32[]{:S(2)}) collective-permute-start(f32[776,128]{1,0:T(8,128)S(1)} %collective-permute-done.25.refs_12_), channel_id=1, source_target_pairs={{0,224},{32,0},{64,32},{96,64},{128,96},{160,128},{192,160},{224,1... | collective-permute-start | bytes 1191944 | tf_op jit(solution)/shard_map/ppermute | solution.py:610
  169.8 2.1 collective-permute-start.27
  171.9 11.4 %all_to_all.51.refs_3_ = f32[32,1,128]{2,1,0:T(1,128)S(1)} all-to-all(f32[32,1,128]{2,1,0:T(1,128)S(1)} %get-tuple-element.144), channel_id=1, replica_groups=mesh['tm'=8,'gx'=8,'gy'=4] {'gx','gy'}, dimensions={0} | all-to-all | bytes 32768 | tf_op jit(solution)/shard_map/all_to_all | solution.py:607
  183.3 2.0 chain7.1
  186.1 2.1 collective-permute-start.30
  188.2 11.4 %all_to_all.52.refs_3_ = f32[32,1,128]{2,1,0:T(1,128)S(1)} all-to-all(f32[32,1,128]{2,1,0:T(1,128)S(1)} %get-tuple-element.152), channel_id=1, replica_groups=mesh['tm'=8,'gx'=8,'gy'=4] {'gx','gy'}, dimensions={0} | all-to-all | bytes 32768 | tf_op jit(solution)/shard_map/all_to_all | solution.py:607
  199.6 2.0 chain8.1
  201.6 2.7 %collective-permute-start.31 = (f32[6,3,16,128]{3,2,1,0:T(8,128)S(1)}, f32[6,3,16,128]{3,2,1,0:T(8,128)S(1)}, u32[]{:S(2)}, u32[]{:S(2)}) collective-permute-start(f32[6,3,16,128]{3,2,1,0:T(8,128)S(1)} %get-tuple-element.159), channel_id=1, source_target_pairs={{0,0},{1,2},{2,4},{3,6},{4,1},{5,3},{6,5},{7,7},{8,14},{9,12},{10,... | collective-permute-start | bytes 442376 | tf_op jit(solution)/shard_map/ppermute | solution.py:591
  204.3 4.3 %collective-permute-start.32 = (f32[6,3,16,128]{3,2,1,0:T(8,128)S(1)}, f32[6,3,16,128]{3,2,1,0:T(8,128)S(1)}, u32[]{:S(2)}, u32[]{:S(2)}) collective-permute-start(f32[6,3,16,128]{3,2,1,0:T(8,128)S(1)} %get-tuple-element.160), channel_id=1, source_target_pairs={{0,1},{1,3},{2,5},{3,7},{4,2},{5,0},{6,6},{7,4},{8,15},{9,13},{10,... | collective-permute-start | bytes 442376 | tf_op jit(solution)/shard_map/ppermute | solution.py:591
  208.8 3.1 %collective-permute-start.34 = (f32[6,3,16,128]{3,2,1,0:T(8,128)S(1)}, f32[6,3,16,128]{3,2,1,0:T(8,128)S(1)}, u32[]{:S(2)}, u32[]{:S(2)}) collective-permute-start(f32[6,3,16,128]{3,2,1,0:T(8,128)S(1)} %get-tuple-element.162), channel_id=1, source_target_pairs={{0,3},{1,1},{2,7},{3,5},{4,0},{5,2},{6,4},{7,6},{8,13},{9,15},{10,... | collective-permute-start | bytes 442376 | tf_op jit(solution)/shard_map/ppermute | solution.py:591
  211.9 11.8 %all_to_all.53.red_in = f32[32,1,128]{2,1,0:T(1,128)S(1)} all-to-all(f32[32,1,128]{2,1,0:T(1,128)S(1)} %get-tuple-element.158), channel_id=1, replica_groups=mesh['tm'=8,'gx'=8,'gy'=4] {'gx','gy'}, dimensions={0} | all-to-all | bytes 32768 | tf_op jit(solution)/shard_map/all_to_all | solution.py:607
  223.7 1.5 closing.1
  (61 shorter events, 11.5 us)
Async XLA Ops:
  0.0 0.9 copy-start.1
  0.9 1.0 copy-start
  2.5 13.3 %collective-permute-start = (f32[5,3,16,128]{3,2,1,0:T(8,128)S(1)}, f32[5,3,16,128]{3,2,1,0:T(8,128)S(1)}, u32[]{:S(2)}, u32[]{:S(2)}) collective-permute-start(f32[5,3,16,128]{3,2,1,0:T(8,128)S(1)} %get-tuple-element.84), channel_id=1, source_target_pairs={{0,0},{1,4},{2,1},{3,5},{4,2},{5,6},{6,3},{7,7},{8,11},{9,15},{10,... | collective-permute-start | bytes 368648 | tf_op jit(solution)/shard_map/ppermute | solution.py:591
  8.5 7.8 %collective-permute-start.1 = (f32[5,3,16,128]{3,2,1,0:T(8,128)S(1)}, f32[5,3,16,128]{3,2,1,0:T(8,128)S(1)}, u32[]{:S(2)}, u32[]{:S(2)}) collective-permute-start(f32[5,3,16,128]{3,2,1,0:T(8,128)S(1)} %get-tuple-element.85), channel_id=1, source_target_pairs={{0,5},{1,0},{2,4},{3,1},{4,7},{5,2},{6,6},{7,3},{8,14},{9,11},{10,... | collective-permute-start | bytes 368648 | tf_op jit(solution)/shard_map/ppermute | solution.py:591
  10.5 8.2 %collective-permute-start.2 = (f32[5,3,16,128]{3,2,1,0:T(8,128)S(1)}, f32[5,3,16,128]{3,2,1,0:T(8,128)S(1)}, u32[]{:S(2)}, u32[]{:S(2)}) collective-permute-start(f32[5,3,16,128]{3,2,1,0:T(8,128)S(1)} %get-tuple-element.86), channel_id=1, source_target_pairs={{0,1},{1,5},{2,0},{3,4},{4,3},{5,7},{6,2},{7,6},{8,10},{9,14},{10,... | collective-permute-start | bytes 368648 | tf_op jit(solution)/shard_map/ppermute | solution.py:591
  11.7 7.0 %collective-permute-start.3 = (f32[5,3,16,128]{3,2,1,0:T(8,128)S(1)}, f32[5,3,16,128]{3,2,1,0:T(8,128)S(1)}, u32[]{:S(2)}, u32[]{:S(2)}) collective-permute-start(f32[5,3,16,128]{3,2,1,0:T(8,128)S(1)} %get-tuple-element.87), channel_id=1, source_target_pairs={{0,4},{1,1},{2,5},{3,0},{4,6},{5,3},{6,7},{7,2},{8,15},{9,10},{10,... | collective-permute-start | bytes 368648 | tf_op jit(solution)/shard_map/ppermute | solution.py:591
  19.3 10.7 %copy-start.2 = (f32[3]{0:T(128)S(1)}, f32[3]{0:T(128)}, u32[]{:S(2)}) copy-start(f32[3]{0:T(128)} %coef_ref.9) | copy-start | bytes 40
  19.3 10.7 %copy-start.3 = (f32[3]{0:T(128)S(1)}, f32[3]{0:T(128)}, u32[]{:S(2)}) copy-start(f32[3]{0:T(128)} %time_ref.9) | copy-start | bytes 40
  19.3 10.7 %copy-start.4 = (f32[1,2]{1,0:T(1,128)S(1)}, f32[1,2]{1,0:T(1,128)}, u32[]{:S(2)}) copy-start(f32[1,2]{1,0:T(1,128)} %heat_ref.5) | copy-start | bytes 28
  19.3 10.7 %copy-start.5 = (f32[6]{0:T(128)S(1)}, f32[6]{0:T(128)}, u32[]{:S(2)}) copy-start(f32[6]{0:T(128)} %rigid_ref.1) | copy-start | bytes 76
  19.3 10.7 %copy-start.6 = (f32[6]{0:T(128)S(1)}, f32[6]{0:T(128)}, u32[]{:S(2)}) copy-start(f32[6]{0:T(128)} %dilate_ref.1) | copy-start | bytes 76
  19.3 10.6 %collective-permute-start.5 = (f32[4,5,3,16,128]{4,3,2,1,0:T(8,128)S(1)}, f32[4,5,3,16,128]{4,3,2,1,0:T(8,128)S(1)}, u32[]{:S(2)}, u32[]{:S(2)}) collective-permute-start(f32[4,5,3,16,128]{4,3,2,1,0:T(8,128)S(1)} %join.1.own_ref), channel_id=1, source_target_pairs={{1,4},{2,5},{3,6},{4,1},{5,2},{6,3},{7,11},{8,13},{9,14},{10,15},{... | collective-permute-start | bytes 1474568 | tf_op jit(solution)/shard_map/ppermute | solution.py:599
  21.4 8.6 %collective-permute-start.4 = (f32[4,5,3,16,128]{4,3,2,1,0:T(8,128)S(1)}, f32[4,5,3,16,128]{4,3,2,1,0:T(8,128)S(1)}, u32[]{:S(2)}, u32[]{:S(2)}) collective-permute-start(f32[4,5,3,16,128]{4,3,2,1,0:T(8,128)S(1)} %join.1.own_ref), channel_id=1, source_target_pairs={{0,4},{1,5},{2,6},{3,7},{4,0},{5,1},{6,2},{7,3},{8,12},{9,13},{10,... | collective-permute-start | bytes 1474568 | tf_op jit(solution)/shard_map/ppermute | solution.py:599
  22.3 5.1 %collective-permute-start.6 = (f32[4,1,1,16,128]{4,3,2,1,0:T(8,128)S(1)}, f32[4,1,1,16,128]{4,3,2,1,0:T(8,128)S(1)}, u32[]{:S(2)}, u32[]{:S(2)}) collective-permute-start(f32[4,1,1,16,128]{4,3,2,1,0:T(8,128)S(1)} %slice.4), channel_id=1, source_target_pairs={{1,0},{2,1},{3,2},{5,4},{6,5},{7,6},{8,9},{9,10},{10,11},{11,3},{1... | collective-permute-start | bytes 98312 | tf_op jit(solution)/shard_map/ppermute | solution.py:604
  33.9 20.6 %collective-permute-start.7 = (f32[6,64,128]{2,1,0:T(8,128)S(1)}, f32[6,64,128]{2,1,0:T(8,128)S(1)}, u32[]{:S(2)}, u32[]{:S(2)}) collective-permute-start(f32[6,64,128]{2,1,0:T(8,128)S(1)} %get-tuple-element.98), channel_id=1, source_target_pairs={{0,4},{1,5},{2,6},{3,7},{4,0},{5,1},{6,2},{7,3},{8,12},{9,13},{10,... | collective-permute-start | bytes 589832 | tf_op jit(solution)/shard_map/ppermute | solution.py:599
  35.1 19.4 %collective-permute-start.8 = (f32[6,64,128]{2,1,0:T(8,128)S(1)}, f32[6,64,128]{2,1,0:T(8,128)S(1)}, u32[]{:S(2)}, u32[]{:S(2)}) collective-permute-start(f32[6,64,128]{2,1,0:T(8,128)S(1)} %get-tuple-element.99), channel_id=1, source_target_pairs={{1,4},{2,5},{3,6},{4,1},{5,2},{6,3},{7,11},{8,13},{9,14},{10,15},{... | collective-permute-start | bytes 589832 | tf_op jit(solution)/shard_map/ppermute | solution.py:599
  37.0 17.5 %collective-permute-start.9 = (f32[3,64,128]{2,1,0:T(8,128)S(1)}, f32[3,64,128]{2,1,0:T(8,128)S(1)}, u32[]{:S(2)}, u32[]{:S(2)}) collective-permute-start(f32[3,64,128]{2,1,0:T(8,128)S(1)} %get-tuple-element.100), channel_id=1, source_target_pairs={{1,0},{2,1},{3,2},{5,4},{6,5},{7,6},{8,9},{9,10},{10,11},{11,3},{1... | collective-permute-start | bytes 294920 | tf_op jit(solution)/shard_map/ppermute | solution.py:604
  68.3 13.6 %collective-permute-start.10 = (f32[776,128]{1,0:T(8,128)S(1)}, f32[776,128]{1,0:T(8,128)S(1)}, u32[]{:S(2)}, u32[]{:S(2)}) collective-permute-start(f32[776,128]{1,0:T(8,128)S(1)} %block.1.refs_12_), channel_id=1, source_target_pairs={{0,224},{32,0},{64,32},{96,64},{128,96},{160,128},{192,160},{224,1... | collective-permute-start | bytes 1191944 | tf_op jit(solution)/shard_map/ppermute | solution.py:610
  82.5 11.9 %collective-permute-start.13 = (f32[776,128]{1,0:T(8,128)S(1)}, f32[776,128]{1,0:T(8,128)S(1)}, u32[]{:S(2)}, u32[]{:S(2)}) collective-permute-start(f32[776,128]{1,0:T(8,128)S(1)} %collective-permute-done.10.blk_ref), channel_id=1, source_target_pairs={{0,224},{32,0},{64,32},{96,64},{128,96},{160,128},{192,160},{224,1... | collective-permute-start | bytes 1191944 | tf_op jit(solution)/shard_map/ppermute | solution.py:610
  86.0 3.9 %collective-permute-start.11 = (f32[5,64,128]{2,1,0:T(8,128)S(1)}, f32[5,64,128]{2,1,0:T(8,128)S(1)}, u32[]{:S(2)}, u32[]{:S(2)}) collective-permute-start(f32[5,64,128]{2,1,0:T(8,128)S(1)} %get-tuple-element.108), channel_id=1, source_target_pairs={{0,4},{1,5},{2,6},{3,7},{4,0},{5,1},{6,2},{7,3},{8,12},{9,13},{10,... | collective-permute-start | bytes 491528 | tf_op jit(solution)/shard_map/ppermute | solution.py:599
  87.8 6.6 %collective-permute-start.12 = (f32[5,64,128]{2,1,0:T(8,128)S(1)}, f32[5,64,128]{2,1,0:T(8,128)S(1)}, u32[]{:S(2)}, u32[]{:S(2)}) collective-permute-start(f32[5,64,128]{2,1,0:T(8,128)S(1)} %get-tuple-element.109), channel_id=1, source_target_pairs={{1,4},{2,5},{3,6},{4,1},{5,2},{6,3},{7,11},{8,13},{9,14},{10,15},{... | collective-permute-start | bytes 491528 | tf_op jit(solution)/shard_map/ppermute | solution.py:599
  96.2 18.4 %collective-permute-start.16 = (f32[776,128]{1,0:T(8,128)S(1)}, f32[776,128]{1,0:T(8,128)S(1)}, u32[]{:S(2)}, u32[]{:S(2)}) collective-permute-start(f32[776,128]{1,0:T(8,128)S(1)} %collective-permute-done.13.refs_9_), channel_id=1, source_target_pairs={{0,224},{32,0},{64,32},{96,64},{128,96},{160,128},{192,160},{224,1... | collective-permute-start | bytes 1191944 | tf_op jit(solution)/shard_map/ppermute | solution.py:610
  98.5 16.2 %collective-permute-start.14 = (f32[8,64,128]{2,1,0:T(8,128)S(1)}, f32[8,64,128]{2,1,0:T(8,128)S(1)}, u32[]{:S(2)}, u32[]{:S(2)}) collective-permute-start(f32[8,64,128]{2,1,0:T(8,128)S(1)} %get-tuple-element.117), channel_id=1, source_target_pairs={{0,4},{1,5},{2,6},{3,7},{4,0},{5,1},{6,2},{7,3},{8,12},{9,13},{10,... | collective-permute-start | bytes 786440 | tf_op jit(solution)/shard_map/ppermute | solution.py:599
  101.2 13.5 %collective-permute-start.15 = (f32[8,64,128]{2,1,0:T(8,128)S(1)}, f32[8,64,128]{2,1,0:T(8,128)S(1)}, u32[]{:S(2)}, u32[]{:S(2)}) collective-permute-start(f32[8,64,128]{2,1,0:T(8,128)S(1)} %get-tuple-element.118), channel_id=1, source_target_pairs={{1,4},{2,5},{3,6},{4,1},{5,2},{6,3},{7,11},{8,13},{9,14},{10,15},{... | collective-permute-start | bytes 786440 | tf_op jit(solution)/shard_map/ppermute | solution.py:599
  116.7 14.3 %collective-permute-start.19 = (f32[776,128]{1,0:T(8,128)S(1)}, f32[776,128]{1,0:T(8,128)S(1)}, u32[]{:S(2)}, u32[]{:S(2)}) collective-permute-start(f32[776,128]{1,0:T(8,128)S(1)} %collective-permute-done.16.refs_12_), channel_id=1, source_target_pairs={{0,224},{32,0},{64,32},{96,64},{128,96},{160,128},{192,160},{224,1... | collective-permute-start | bytes 1191944 | tf_op jit(solution)/shard_map/ppermute | solution.py:610
  116.8 14.2 %collective-permute-start.17 = (f32[8,64,128]{2,1,0:T(8,128)S(1)}, f32[8,64,128]{2,1,0:T(8,128)S(1)}, u32[]{:S(2)}, u32[]{:S(2)}) collective-permute-start(f32[8,64,128]{2,1,0:T(8,128)S(1)} %get-tuple-element.125), channel_id=1, source_target_pairs={{0,4},{1,5},{2,6},{3,7},{4,0},{5,1},{6,2},{7,3},{8,12},{9,13},{10,... | collective-permute-start | bytes 786440 | tf_op jit(solution)/shard_map/ppermute | solution.py:599
  117.5 13.5 %collective-permute-start.18 = (f32[8,64,128]{2,1,0:T(8,128)S(1)}, f32[8,64,128]{2,1,0:T(8,128)S(1)}, u32[]{:S(2)}, u32[]{:S(2)}) collective-permute-start(f32[8,64,128]{2,1,0:T(8,128)S(1)} %get-tuple-element.126), channel_id=1, source_target_pairs={{1,4},{2,5},{3,6},{4,1},{5,2},{6,3},{7,11},{8,13},{9,14},{10,15},{... | collective-permute-start | bytes 786440 | tf_op jit(solution)/shard_map/ppermute | solution.py:599
  133.0 14.3 %collective-permute-start.22 = (f32[776,128]{1,0:T(8,128)S(1)}, f32[776,128]{1,0:T(8,128)S(1)}, u32[]{:S(2)}, u32[]{:S(2)}) collective-permute-start(f32[776,128]{1,0:T(8,128)S(1)} %collective-permute-done.19.refs_12_), channel_id=1, source_target_pairs={{0,224},{32,0},{64,32},{96,64},{128,96},{160,128},{192,160},{224,1... | collective-permute-start | bytes 1191944 | tf_op jit(solution)/shard_map/ppermute | solution.py:610
  133.1 14.2 %collective-permute-start.20 = (f32[8,64,128]{2,1,0:T(8,128)S(1)}, f32[8,64,128]{2,1,0:T(8,128)S(1)}, u32[]{:S(2)}, u32[]{:S(2)}) collective-permute-start(f32[8,64,128]{2,1,0:T(8,128)S(1)} %get-tuple-element.133), channel_id=1, source_target_pairs={{0,4},{1,5},{2,6},{3,7},{4,0},{5,1},{6,2},{7,3},{8,12},{9,13},{10,... | collective-permute-start | bytes 786440 | tf_op jit(solution)/shard_map/ppermute | solution.py:599
  133.8 13.5 %collective-permute-start.21 = (f32[8,64,128]{2,1,0:T(8,128)S(1)}, f32[8,64,128]{2,1,0:T(8,128)S(1)}, u32[]{:S(2)}, u32[]{:S(2)}) collective-permute-start(f32[8,64,128]{2,1,0:T(8,128)S(1)} %get-tuple-element.134), channel_id=1, source_target_pairs={{1,4},{2,5},{3,6},{4,1},{5,2},{6,3},{7,11},{8,13},{9,14},{10,15},{... | collective-permute-start | bytes 786440 | tf_op jit(solution)/shard_map/ppermute | solution.py:599
  149.4 14.6 %collective-permute-start.25 = (f32[776,128]{1,0:T(8,128)S(1)}, f32[776,128]{1,0:T(8,128)S(1)}, u32[]{:S(2)}, u32[]{:S(2)}) collective-permute-start(f32[776,128]{1,0:T(8,128)S(1)} %collective-permute-done.22.refs_12_), channel_id=1, source_target_pairs={{0,224},{32,0},{64,32},{96,64},{128,96},{160,128},{192,160},{224,1... | collective-permute-start | bytes 1191944 | tf_op jit(solution)/shard_map/ppermute | solution.py:610
  149.6 14.4 %collective-permute-start.23 = (f32[8,64,128]{2,1,0:T(8,128)S(1)}, f32[8,64,128]{2,1,0:T(8,128)S(1)}, u32[]{:S(2)}, u32[]{:S(2)}) collective-permute-start(f32[8,64,128]{2,1,0:T(8,128)S(1)} %get-tuple-element.141), channel_id=1, source_target_pairs={{0,4},{1,5},{2,6},{3,7},{4,0},{5,1},{6,2},{7,3},{8,12},{9,13},{10,... | collective-permute-start | bytes 786440 | tf_op jit(solution)/shard_map/ppermute | solution.py:599
  150.5 13.5 %collective-permute-start.24 = (f32[8,64,128]{2,1,0:T(8,128)S(1)}, f32[8,64,128]{2,1,0:T(8,128)S(1)}, u32[]{:S(2)}, u32[]{:S(2)}) collective-permute-start(f32[8,64,128]{2,1,0:T(8,128)S(1)} %get-tuple-element.142), channel_id=1, source_target_pairs={{1,4},{2,5},{3,6},{4,1},{5,2},{6,3},{7,11},{8,13},{9,14},{10,15},{... | collective-permute-start | bytes 786440 | tf_op jit(solution)/shard_map/ppermute | solution.py:599
  166.0 17.3 %collective-permute-start.28 = (f32[776,128]{1,0:T(8,128)S(1)}, f32[776,128]{1,0:T(8,128)S(1)}, u32[]{:S(2)}, u32[]{:S(2)}) collective-permute-start(f32[776,128]{1,0:T(8,128)S(1)} %collective-permute-done.25.refs_12_), channel_id=1, source_target_pairs={{0,224},{32,0},{64,32},{96,64},{128,96},{160,128},{192,160},{224,1... | collective-permute-start | bytes 1191944 | tf_op jit(solution)/shard_map/ppermute | solution.py:610
  168.9 14.4 %collective-permute-start.26 = (f32[8,64,128]{2,1,0:T(8,128)S(1)}, f32[8,64,128]{2,1,0:T(8,128)S(1)}, u32[]{:S(2)}, u32[]{:S(2)}) collective-permute-start(f32[8,64,128]{2,1,0:T(8,128)S(1)} %get-tuple-element.149), channel_id=1, source_target_pairs={{0,4},{1,5},{2,6},{3,7},{4,0},{5,1},{6,2},{7,3},{8,12},{9,13},{10,... | collective-permute-start | bytes 786440 | tf_op jit(solution)/shard_map/ppermute | solution.py:599
  169.8 13.5 %collective-permute-start.27 = (f32[8,64,128]{2,1,0:T(8,128)S(1)}, f32[8,64,128]{2,1,0:T(8,128)S(1)}, u32[]{:S(2)}, u32[]{:S(2)}) collective-permute-start(f32[8,64,128]{2,1,0:T(8,128)S(1)} %get-tuple-element.150), channel_id=1, source_target_pairs={{1,4},{2,5},{3,6},{4,1},{5,2},{6,3},{7,11},{8,13},{9,14},{10,15},{... | collective-permute-start | bytes 786440 | tf_op jit(solution)/shard_map/ppermute | solution.py:599
  185.4 14.2 %collective-permute-start.29 = (f32[8,64,128]{2,1,0:T(8,128)S(1)}, f32[8,64,128]{2,1,0:T(8,128)S(1)}, u32[]{:S(2)}, u32[]{:S(2)}) collective-permute-start(f32[8,64,128]{2,1,0:T(8,128)S(1)} %get-tuple-element.156), channel_id=1, source_target_pairs={{0,4},{1,5},{2,6},{3,7},{4,0},{5,1},{6,2},{7,3},{8,12},{9,13},{10,... | collective-permute-start | bytes 786440 | tf_op jit(solution)/shard_map/ppermute | solution.py:599
  186.1 13.5 %collective-permute-start.30 = (f32[8,64,128]{2,1,0:T(8,128)S(1)}, f32[8,64,128]{2,1,0:T(8,128)S(1)}, u32[]{:S(2)}, u32[]{:S(2)}) collective-permute-start(f32[8,64,128]{2,1,0:T(8,128)S(1)} %get-tuple-element.157), channel_id=1, source_target_pairs={{1,4},{2,5},{3,6},{4,1},{5,2},{6,3},{7,11},{8,13},{9,14},{10,15},{... | collective-permute-start | bytes 786440 | tf_op jit(solution)/shard_map/ppermute | solution.py:599
  201.6 22.1 %collective-permute-start.31 = (f32[6,3,16,128]{3,2,1,0:T(8,128)S(1)}, f32[6,3,16,128]{3,2,1,0:T(8,128)S(1)}, u32[]{:S(2)}, u32[]{:S(2)}) collective-permute-start(f32[6,3,16,128]{3,2,1,0:T(8,128)S(1)} %get-tuple-element.159), channel_id=1, source_target_pairs={{0,0},{1,2},{2,4},{3,6},{4,1},{5,3},{6,5},{7,7},{8,14},{9,12},{10,... | collective-permute-start | bytes 442376 | tf_op jit(solution)/shard_map/ppermute | solution.py:591
  204.3 19.4 %collective-permute-start.32 = (f32[6,3,16,128]{3,2,1,0:T(8,128)S(1)}, f32[6,3,16,128]{3,2,1,0:T(8,128)S(1)}, u32[]{:S(2)}, u32[]{:S(2)}) collective-permute-start(f32[6,3,16,128]{3,2,1,0:T(8,128)S(1)} %get-tuple-element.160), channel_id=1, source_target_pairs={{0,1},{1,3},{2,5},{3,7},{4,2},{5,0},{6,6},{7,4},{8,15},{9,13},{10,... | collective-permute-start | bytes 442376 | tf_op jit(solution)/shard_map/ppermute | solution.py:591
  208.7 15.0 %collective-permute-start.33 = (f32[6,3,16,128]{3,2,1,0:T(8,128)S(1)}, f32[6,3,16,128]{3,2,1,0:T(8,128)S(1)}, u32[]{:S(2)}, u32[]{:S(2)}) collective-permute-start(f32[6,3,16,128]{3,2,1,0:T(8,128)S(1)} %get-tuple-element.161), channel_id=1, source_target_pairs={{0,2},{1,0},{2,6},{3,4},{4,3},{5,1},{6,7},{7,5},{8,12},{9,14},{10,... | collective-permute-start | bytes 442376 | tf_op jit(solution)/shard_map/ppermute | solution.py:591
  208.8 14.9 %collective-permute-start.34 = (f32[6,3,16,128]{3,2,1,0:T(8,128)S(1)}, f32[6,3,16,128]{3,2,1,0:T(8,128)S(1)}, u32[]{:S(2)}, u32[]{:S(2)}) collective-permute-start(f32[6,3,16,128]{3,2,1,0:T(8,128)S(1)} %get-tuple-element.162), channel_id=1, source_target_pairs={{0,3},{1,1},{2,7},{3,5},{4,0},{5,2},{6,4},{7,6},{8,13},{9,15},{10,... | collective-permute-start | bytes 442376 | tf_op jit(solution)/shard_map/ppermute | solution.py:591

commit v5 on v4

--- a/solution.py
+++ b/solution.py
@@ -16,16 +16,13 @@
 LIMIT = 14 << 20
 
 
-def masks(ny, nz):
-    row = lax.broadcasted_iota(jnp.int32, (ny, nz), 0)
-    lane = lax.broadcasted_iota(jnp.int32, (ny, nz), 1)
-    return row == 0, row == ny - 1, lane == 0, lane == nz - 1
-
-
 class Shifts:
     def __init__(self, ny, nz):
         self.ny, self.nz = ny, nz
-        self.row_first, self.row_last, self.lane_first, self.lane_last = masks(ny, nz)
+        lane = lax.broadcasted_iota(jnp.int32, (ny, nz), 1)
+        row = lax.broadcasted_iota(jnp.int32, (8, nz), 0)
+        self.lane_first, self.lane_last = lane == 0, lane == nz - 1
+        self.row_first, self.row_last = row == 0, row == 7
 
     def zup(self, v):
         return jnp.where(self.lane_last, 0.0, pltpu.roll(v, self.nz - 1, 1))
@@ -34,10 +31,13 @@
         return jnp.where(self.lane_first, 0.0, pltpu.roll(v, 1, 1))
 
     def yup(self, v):
-        return jnp.where(self.row_last, 0.0, pltpu.roll(v, self.ny - 1, 0))
+        v = pltpu.roll(v, self.ny - 1, 0)
+        end = jnp.where(self.row_last, 0.0, v[self.ny - 8 :])
+        return jnp.concatenate([v[: self.ny - 8], end], axis=0)
 
     def ydn(self, v):
-        return jnp.where(self.row_first, 0.0, pltpu.roll(v, 1, 0))
+        v = pltpu.roll(v, 1, 0)
+        return jnp.concatenate([jnp.where(self.row_first, 0.0, v[:8]), v[8:]], axis=0)
 
 
 def off_diagonal(sh, v, k, low, high, put):
@@ -70,11 +70,43 @@
         near = far
 
 
-def prony(dt, coef_ref, time_ref):
-    decay = [jnp.exp(-dt / jnp.full((1, 128), time_ref[p], jnp.float32)) for p in range(PRONY)]
-    rest = [1.0 - d for d in decay]
-    f = [coef_ref[p] * decay[p] for p in range(PRONY)]
-    return decay, rest, f, 1.0 / dt + (f[0] + f[1] + f[2])
+COARSE, HEAT, SLICE, SIDE, PART, CHIP, RIGID = 10, 20, 22, 23, 24, 25, 26
+
+
+def fill_constants(heat_ref, coef_ref, time_ref, rigid_ref, dilate_ref, place_ref, const_ref):
+    def put(at, value):
+        const_ref[at : at + 1] = jnp.broadcast_to(value, (1, 128))
+
+    def entry(ref, i):
+        return jnp.broadcast_to(ref[0:1, i : i + 1], (1, 128))
+
+    for first, dt in ((0, 1.0), (COARSE, 1.0 * PACES)):
+        total = jnp.full((1, 128), 1.0 / dt, jnp.float32)
+        for p in range(PRONY):
+            decay = jnp.exp(-dt / entry(time_ref, p))
+            f = entry(coef_ref, p) * decay
+            put(first + p, decay)
+            put(first + 3 + p, 1.0 - decay)
+            put(first + 6 + p, f)
+            total = total + f
+        put(first + 9, total)
+    put(HEAT, entry(heat_ref, 0))
+    put(HEAT + 1, entry(heat_ref, PACES - 1))
+    for i in range(4):
+        put(SLICE + i, entry(place_ref, i))
+    regions = rigid_ref.shape[1]
+    for i in range(regions):
+        put(RIGID + i, entry(rigid_ref, i))
+        put(RIGID + regions + i, entry(dilate_ref, i))
+
+
+def prony(const_ref, first):
+    rows = [const_ref[first + i : first + i + 1] for i in range(10)]
+    return rows[:3], rows[3:6], rows[6:9], rows[9]
+
+
+def holds(const_ref, row, value, shape):
+    return jnp.broadcast_to(const_ref[row : row + 1], shape) == float(value)
 
 
 def moments_out(values, red_ref):
@@ -115,23 +147,29 @@
     return c
 
 
-def send(odd_side, lo, hi, even_out, odd_out):
+def send(even_place, lo, hi, even_out, odd_out):
     for at, (low, high) in enumerate(zip(lo, hi)):
-        even_out[at] = jnp.where(odd_side == 0, high, low)
-        odd_out[at] = jnp.where(odd_side == 0, low, high)
-
-
-def below(odd_side, even_ref, odd_ref, at):
-    return jnp.where(odd_side == 0, odd_ref[at], even_ref[at])
-
-
-def above(odd_side, even_ref, odd_ref, at):
-    return jnp.where(odd_side == 0, even_ref[at], odd_ref[at])
+        even_out[at] = jnp.where(even_place, high, low)
+        odd_out[at] = jnp.where(even_place, low, high)
+
+
+def below(even_place, even_ref, odd_ref, at):
+    return jnp.where(even_place, odd_ref[at], even_ref[at])
+
+
+def above(even_place, even_ref, odd_ref, at):
+    return jnp.where(even_place, even_ref[at], odd_ref[at])
+
+
+def chosen(const_ref, row, values):
+    value = values[-1]
+    for v in range(len(values) - 1):
+        value = jnp.where(holds(const_ref, row, v, value.shape), values[v], value)
+    return value
 
 
 def start_kernel(
-    rigid_ref, dilate_ref, heat_ref, coef_ref, time_ref, place_ref,
-    own_ref, even_ref, odd_ref, far_ref,
+    own_ref, even_ref, odd_ref, far_ref, const_ref,
     kel_ref, theta_ref, inv_f_ref, inv_c_ref, state_ref,
     zf_ref, ozf_ref, oozf_ref, zc_ref, ozc_ref,
     even_out, odd_out, far_out, red_ref,
@@ -140,32 +178,37 @@
     ny, nz = kel_ref.shape[1:]
     sh = Shifts(ny, nz)
     chunks = own_ref.shape[0]
-    side = place_ref[1]
+    side = holds(const_ref, SIDE, 0, (ny, nz))
+    side_part = holds(const_ref, SIDE, 0, (ny // chunks, nz))
 
     def raw(field, i):
         if i < 0:
-            parts = [below(side, even_ref, odd_ref, (c, field, i + L)) for c in range(chunks)]
+            parts = [below(side_part, even_ref, odd_ref, (c, field, i + L)) for c in range(chunks)]
         elif i < L:
             parts = [own_ref[c, field, i] for c in range(chunks)]
         elif i < 2 * L:
-            parts = [above(side, even_ref, odd_ref, (c, field, i - L)) for c in range(chunks)]
+            parts = [above(side_part, even_ref, odd_ref, (c, field, i - L)) for c in range(chunks)]
         else:
             parts = [far_ref[c, 0, 0] for c in range(chunks)]
         return jnp.concatenate(parts, axis=0)
+
+    regions = (const_ref.shape[0] - RIGID) // 2
+    table = [const_ref[RIGID + i : RIGID + i + 1] for i in range(2 * regions)]
 
     for e in range(-3, 6):
         label = raw(0, e)
         stiff = jnp.zeros((ny, nz), jnp.float32)
         load = jnp.zeros((ny, nz), jnp.float32)
-        for region in range(rigid_ref.shape[0]):
+        for region in range(regions):
             here = label == (region + 1.0)
-            stiff = jnp.where(here, rigid_ref[region], stiff)
-            load = jnp.where(here, dilate_ref[region], load)
+            stiff = jnp.where(here, table[region], stiff)
+            load = jnp.where(here, table[regions + region], load)
         kel_ref[e + 3] = stiff * (-1.0 / 12.0)
         kal_ref[e + 3] = 0.25 * (stiff * load)
 
-    decay_f, rest_f, ff, shift_f = prony(1.0, coef_ref, time_ref)
-    decay_c, rest_c, fc, shift_c = prony(1.0 * PACES, coef_ref, time_ref)
+    heat = [const_ref[HEAT + i : HEAT + i + 1] for i in range(2)]
+    decay_f, rest_f, ff, shift_f = prony(const_ref, 0)
+    decay_c, rest_c, fc, shift_c = prony(const_ref, COARSE)
 
     for i in range(-2, 6):
         ksum = kel_ref[i + 2] + kel_ref[i + 3]
@@ -197,14 +240,14 @@
         fh = [ff[p] * h[p] for p in range(PRONY)]
         state_ref[10 + i + 2] = decay_f[0] * fh[0] + decay_f[1] * fh[1] + decay_f[2] * fh[2]
         ui = state_ref[i + 3]
-        load = heat_ref[0, 0] * theta_ref[i + 2] + (fh[0] + fh[1] + fh[2])
+        load = heat[0] * theta_ref[i + 2] + (fh[0] + fh[1] + fh[2])
         s = load + ui - au_ref[i + 2]
         z = inv_f_ref[i + 2] * s - ui
         zf_ref[i + 2] = z
         if 0 <= i < L:
             acc[0] = acc[0] + z * (s - ui * (1.0 / inv_f_ref[i + 2]))
         if i < 5:
-            load = heat_ref[0, 1] * theta_ref[i + 2]
+            load = heat[1] * theta_ref[i + 2]
             load = load + (fc[0] * h[0] + fc[1] * h[1] + fc[2] * h[2])
             s = load + ui * (1.0 / PACES) - au_ref[i + 2]
             z = inv_c_ref[i + 2] * s - ui
@@ -271,8 +314,7 @@
 
 
 def second_kernel(
-    heat_ref, coef_ref, time_ref, place_ref,
-    red_in, kel_ref, theta_ref, inv_f_ref, state_ref, own_ref,
+    const_ref, red_in, kel_ref, theta_ref, inv_f_ref, state_ref, own_ref,
     zf_ref, ozf_ref, oozf_ref, zc_ref, ozc_ref,
     even_ref, odd_ref, far_ref,
     base_ref, z_out, oz_out, ooz_out, red_ref,
@@ -281,11 +323,12 @@
     ny, nz = kel_ref.shape[1:]
     sh = Shifts(ny, nz)
     chunks = own_ref.shape[0]
-    decay_f, rest_f, ff, shift_f = prony(1.0, coef_ref, time_ref)
-    decay_c, rest_c, fc, shift_c = prony(1.0 * PACES, coef_ref, time_ref)
+    decay_f, rest_f, ff, shift_f = prony(const_ref, 0)
+    decay_c, rest_c, fc, shift_c = prony(const_ref, COARSE)
     c = galerkin(moments_in(red_in, 0, 6))
     b = galerkin(moments_in(red_in, 6, 4))
-    side = place_ref[1]
+    side = holds(const_ref, SIDE, 0, (ny, nz))
+    heat = const_ref[HEAT + 1 : HEAT + 2]
 
     def basis(i, at, ref, low, high, up, down):
         if i == 6:
@@ -313,10 +356,10 @@
     grow = ff[0] * rest_f[0] + ff[1] * rest_f[1] + ff[2] * rest_f[2]
     zeros = jnp.zeros((ny, nz), jnp.float32)
     acc = [zeros] * 6
-    weight = jnp.where(place_ref[0] == 0, 0.0, 1.0)
+    weight = jnp.where(holds(const_ref, SLICE, 0, (1, nz)), 0.0, 1.0)
     for i in range(-2, 6):
         ui = u_ref[i + 3]
-        s = heat_ref[0, 1] * theta_ref[i + 2] + state_ref[10 + i + 2] + (grow + 1.0) * ui
+        s = heat * theta_ref[i + 2] + state_ref[10 + i + 2] + (grow + 1.0) * ui
         s = s - au_ref[i + 2]
         z = inv_f_ref[i + 2] * s - ui
         z_ref[i + 2] = z
@@ -361,8 +404,8 @@
     moments_out(acc, red_ref)
 
 
-def block_kernel(heat_ref, coef_ref, time_ref, red_in, base_ref, z_ref, oz_ref, ooz_ref, blk_ref):
-    decay_f, rest_f, ff, shift_f = prony(1.0, coef_ref, time_ref)
+def block_kernel(const_ref, red_in, base_ref, z_ref, oz_ref, ooz_ref, blk_ref):
+    decay_f, rest_f, ff, shift_f = prony(const_ref, 0)
     c = galerkin(moments_in(red_in, 0, 6))
     ny = z_ref.shape[1]
     for i in range(L):
@@ -371,7 +414,7 @@
         for p in range(PRONY):
             at = L * (1 + p) + i
             blk_ref[at * ny : (at + 1) * ny] = base_ref[at] + rest_f[p] * delta
-    blk_ref[4 * L * ny :] = jnp.full((8, blk_ref.shape[1]), heat_ref[0, PACES - 1], jnp.float32)
+    blk_ref[4 * L * ny :] = jnp.broadcast_to(const_ref[HEAT + 1 : HEAT + 2], (8, blk_ref.shape[1]))
 
 
 def halo_base(f, base_ref):
@@ -383,19 +426,18 @@
     return u + [sums[0], sums[1]], u + [sums[1], sums[2]]
 
 
-def opening_kernel(coef_ref, time_ref, place_ref, blk_ref, base_ref, even_out, odd_out):
-    decay, rest, f, shift = prony(1.0 * PACES, coef_ref, time_ref)
+def opening_kernel(const_ref, blk_ref, base_ref, even_out, odd_out):
+    decay, rest, f, shift = prony(const_ref, COARSE)
     ny = even_out.shape[1]
     for at in range(4 * L):
         base_ref[at] = blk_ref[at * ny : (at + 1) * ny]
     lo, hi = halo_base(f, base_ref)
-    send(place_ref[1], lo, hi, even_out, odd_out)
+    send(holds(const_ref, SIDE, 0, even_out.shape[1:]), lo, hi, even_out, odd_out)
 
 
 def chain_kernel(turn, count, opened, rounds, *refs):
     refs = list(refs)
-    coef_ref, time_ref, place_ref = refs[:3]
-    refs = refs[3:]
+    const_ref = refs.pop(0)
     if opened:
         base_in, even_ref, odd_ref = refs[:3]
         refs = refs[3:]
@@ -409,13 +451,12 @@
         base_ref, z_ref, oz_ref, even_out, odd_out, red_ref, u_ref, au_ref = refs[4:]
     ny, nz = kel_ref.shape[1:]
     sh = Shifts(ny, nz)
-    decay, rest, f, shift = prony(1.0 * PACES, coef_ref, time_ref)
+    decay, rest, f, shift = prony(const_ref, COARSE)
     grow = f[0] * rest[0] + f[1] * rest[1] + f[2] * rest[2]
-    step = lax.rem(place_ref[0] + turn, count)
     heat = blk_ref[4 * L * ny : 4 * L * ny + 1]
-    opening = step == 0
-    fresh = step == 1
-    side = place_ref[1]
+    opening = holds(const_ref, SLICE, -turn % count, (ny, nz))
+    fresh = holds(const_ref, SLICE, (1 - turn) % count, (ny, nz))
+    side = holds(const_ref, SIDE, 0, (ny, nz))
 
     if not opened:
         c = galerkin(moments_in(red_in, 0, 4))
@@ -490,14 +531,13 @@
 
     if rounds:
         width = ny // rounds
-        for r, out_ref in enumerate(outs):
-            cut = lax.rem(2 * place_ref[2] + side + r, rounds) * width
-            rows = pl.ds(pl.multiple_of(cut, width), width)
-            for i in range(L):
-                for field in range(1 + PRONY):
-                    out_ref[field, i] = base_ref[L * field + i, rows]
-                out_ref[4, i] = z_ref[i + 2, rows]
-                out_ref[5, i] = oz_ref[i + 1, rows]
+        for i in range(L):
+            fields = [base_ref[L * field + i] for field in range(1 + PRONY)]
+            for at, field in enumerate(fields + [z_ref[i + 2], oz_ref[i + 1]]):
+                cuts = [field[q * width : (q + 1) * width] for q in range(rounds)]
+                for r, out_ref in enumerate(outs):
+                    ahead = [cuts[(v + r) % rounds] for v in range(rounds)]
+                    out_ref[at, i] = chosen(const_ref, PART, ahead)
         return
 
     lo, hi = halo_base(f, base_ref)
@@ -506,56 +546,65 @@
     send(side, lo, hi, even_out, odd_out)
 
 
-def closing_kernel(coef_ref, time_ref, place_ref, red_in, *refs):
+def closing_kernel(const_ref, red_in, *refs):
     parts, out_ref = refs[:-1], refs[-1]
-    decay, rest, f, shift = prony(1.0 * PACES, coef_ref, time_ref)
+    decay, rest, f, shift = prony(const_ref, COARSE)
     c = galerkin(moments_in(red_in, 0, 4))
-    first = place_ref[0] == 0
+    first = holds(const_ref, SLICE, 0, out_ref.shape[3:])
     count = len(parts)
-    for r, part_ref in enumerate(parts):
-        at = lax.rem(place_ref[4] + count - r, count) * L
+    for k in range(count):
         for i in range(L):
-            delta = jnp.where(first, 0.0, c[0] * part_ref[4, i] + c[1] * part_ref[5, i])
-            out_ref[0, 0, at + i] = part_ref[0, i] + delta
+            base_u, *base_h, z, oz = [
+                chosen(const_ref, CHIP, [parts[(v - k) % count][at, i] for v in range(count)])
+                for at in range(3 + PRONY)
+            ]
+            delta = jnp.where(first, 0.0, c[0] * z + c[1] * oz)
+            out_ref[0, 0, k * L + i] = base_u + delta
             for p in range(PRONY):
-                out_ref[0, 1 + p, at + i] = part_ref[1 + p, i] + rest[p] * delta
-
-
-def spread_kernel(place_ref, label_ref, values_ref, *out_refs):
+                out_ref[0, 1 + p, k * L + i] = base_h[p] + rest[p] * delta
+
+
+def spread_kernel(
+    heat_ref, coef_ref, time_ref, rigid_ref, dilate_ref, place_ref, label_ref, values_ref,
+    const_ref, *out_refs,
+):
+    fill_constants(heat_ref, coef_ref, time_ref, rigid_ref, dilate_ref, place_ref, const_ref)
     count = len(out_refs)
-    for r, out_ref in enumerate(out_refs):
-        first = lax.rem(place_ref[4] + count - r, count) * L
-        for i in range(L):
-            out_ref[0, i] = label_ref[first + i].astype(jnp.float32) + 1.0
-            for field in range(1 + PRONY):
-                out_ref[1 + field, i] = values_ref[0, field, first + i]
-
-
-def join_kernel(place_ref, *refs):
+    for i in range(L):
+        labels = [label_ref[k * L + i].astype(jnp.float32) + 1.0 for k in range(count)]
+        fields = [labels]
+        for field in range(1 + PRONY):
+            fields.append([values_ref[0, field, k * L + i] for k in range(count)])
+        for at, blocks in enumerate(fields):
+            for r, out_ref in enumerate(out_refs):
+                ahead = [blocks[(v - r) % count] for v in range(count)]
+                out_ref[at, i] = chosen(const_ref, CHIP, ahead)
+
+
+def join_kernel(const_ref, *refs):
     got_refs, out_ref = refs[:-1], refs[-1]
     count = len(got_refs)
-    for r, got_ref in enumerate(got_refs):
-        to = lax.rem(2 * place_ref[2] + place_ref[1] + r, count)
+    for q in range(count):
         for field in range(2 + PRONY):
             for i in range(L):
-                out_ref[to, field, i] = got_ref[field, i]
-
-
-SMEM = pl.BlockSpec(memory_space=pltpu.SMEM)
+                parts = [got_refs[(q - v) % count][field, i] for v in range(count)]
+                out_ref[q, field, i] = chosen(const_ref, PART, parts)
+
+
 VMEM = pl.BlockSpec(memory_space=pltpu.VMEM)
 
 
-def call(kernel, name, small, large, outs, scratch=()):
+def call(kernel, name, arrays, outs, scratch=()):
     f32 = jnp.float32
     return pl.pallas_call(
         kernel,
         name=name,
         out_shape=[jax.ShapeDtypeStruct(s, f32) for s in outs],
-        in_specs=[SMEM] * len(small) + [VMEM] * len(large),
+        in_specs=[VMEM] * len(arrays),
         out_specs=[VMEM] * len(outs),
         scratch_shapes=[pltpu.VMEM(s, f32) for s in scratch],
         compiler_params=pltpu.CompilerParams(vmem_limit_bytes=LIMIT),
-    )(*small, *large)
+    )(*arrays)
 
 
 def on_device(
@@ -612,18 +661,25 @@
     gx, gy = lax.axis_index("gx"), lax.axis_index("gy")
     core, flip = gx % 2, gx // 2 % 2
     x = jnp.where(flip == 0, gy, n_gy - 1 - gy)
-    place = jnp.stack([lax.axis_index("tm"), core, x % 2, flip, gy]).astype(jnp.int32)
-    prony_args = (prony_coefficients, prony_decay_times)
-
-    parts = call(
+    place = jnp.stack([lax.axis_index("tm"), core, 2 * (x % 2) + core, gy])
+    place = place.astype(jnp.float32)[None]
+    regions = material_rigidity.shape[0]
+    tables = (prony_coefficients, prony_decay_times, material_rigidity, dilation_mismatch)
+
+    const, *parts = call(
         spread_kernel,
         "spread",
-        (place,),
-        (cell_material_label, segment_opening_values),
-        [(2 + PRONY, L, ny_part, nz)] * n_gy,
+        (
+            heat_swings_array,
+            *[table[None] for table in tables],
+            place,
+            cell_material_label,
+            segment_opening_values,
+        ),
+        [(RIGID + 2 * regions, nz)] + [(2 + PRONY, L, ny_part, nz)] * n_gy,
     )
     (own,) = call(
-        join_kernel, "join", (place,), deal(parts, True), [(n_gy, 2 + PRONY, L, ny_part, nz)]
+        join_kernel, "join", (const, *deal(parts, True)), [(n_gy, 2 + PRONY, L, ny_part, nz)]
     )
     near, far = trade(own, own), from_next_but_one(own[:, 1:2, :1])
 
@@ -631,8 +687,7 @@
     (kel, theta, inv_f, inv_c, state, zf, ozf, oozf, zc, ozc, even, odd, far, red) = call(
         start_kernel,
         "start",
-        (material_rigidity, dilation_mismatch, heat_swings_array, *prony_args, place),
-        (own, *near, far),
+        (own, *near, far, const),
         [
             (9, *plane), (8, *plane), (8, *plane), (8, *plane), (18, *plane),
             (8, *plane), (6, *plane), (4, *plane), (L, *plane), (L, *plane),
@@ -645,8 +700,7 @@
     base, z, oz, ooz, red = call(
         second_kernel,
         "second",
-        (heat_swings_array, *prony_args, place),
-        (red, kel, theta, inv_f, state, own, zf, ozf, oozf, zc, ozc, *near, far),
+        (const, red, kel, theta, inv_f, state, own, zf, ozf, oozf, zc, ozc, *near, far),
         [(4 * L, *plane), (L, *plane), (L, *plane), (L, *plane), red_shape],
         [(10, *plane), (8, *plane), (6, *plane), (4, *plane), (8, *plane)],
     )
@@ -654,8 +708,7 @@
     (block,) = call(
         block_kernel,
         "block",
-        (heat_swings_array, *prony_args),
-        (red, base, z, oz, ooz),
+        (const, red, base, z, oz, ooz),
         [(4 * L * ny + 8, nz)],
     )
     mine = block
@@ -663,8 +716,7 @@
     base, even, odd = call(
         opening_kernel,
         "opening",
-        (*prony_args, place),
-        (block,),
+        (const, block),
         [(4 * L, *plane), (5, *plane), (5, *plane)],
     )
     past = (base,)
@@ -681,8 +733,7 @@
         *outs, red = call(
             functools.partial(chain_kernel, turn, n_tm, turn == 2, n_gy if last else 0),
             f"chain{turn}",
-            (*prony_args, place),
-            (*past, kel, theta, inv_c, block),
+            (const, *past, kel, theta, inv_c, block),
             [(3 + PRONY, L, ny_part, nz)] * n_gy + [red_shape]
             if last
             else [*state, (8, *plane), (8, *plane), red_shape],
@@ -696,8 +747,7 @@
     (out,) = call(
         closing_kernel,
         "closing",
-        (*prony_args, place),
-        (exchanged(red), *parts),
+        (const, exchanged(red), *parts),
         [(1, 1 + PRONY, nx, ny_part, nz)],
     )
     return out

time: 226 us -> 218 us (0.965)
  Pallas kernels: 24.1 us -> 16.4 us
    pallas_call x14, Pallas kernels: 24.1 us -> 16.4 us  [call(): pl.pallas_call(kernel, name=name, out_shape=[jax.ShapeDtypeStruct(s, f32)...]
where the time goes in v5:
time: 218 us; the launch traced here: 217 us
  blocking collectives  107 us (49%)
  starting transfers between devices  69.7 us (32%)
  waiting for transfers between devices  21.8 us (10%)
  Pallas kernels  16.4 us (8%)
    all_to_all x9, blocking collectives, exchanged(): return lax.all_to_all(red, LINE, 0, 0, tiled=True)  107 us
    ppermute x18, starting transfers between devices, trade(): received.append(lax.ppermute(value, LINE, sorted(both)))  28.9 us
    ppermute x8, starting transfers between devices, deal(): received.append(lax.ppermute(value, LINE, sorted(perm)))  23.6 us
    pallas_call x14, Pallas kernels, call(): pl.pallas_call(kernel, name=name, out_shape=[jax.ShapeDtypeStruct(s, f32)...  16.4 us
    ppermute x7, starting transfers between devices, ring(): return lax.ppermute(block, 'tm', [(s, (s - 1) % n_tm) for s in range(n_tm)])  14.7 us
    ppermute x7, waiting for transfers between devices, ring(): return lax.ppermute(block, 'tm', [(s, (s - 1) % n_tm) for s in range(n_tm)])  7.92 us
    ppermute x18, waiting for transfers between devices, trade(): received.append(lax.ppermute(value, LINE, sorted(both)))  7.22 us
  transfers between devices with their start and end apart: 35, of which 6 were waited for; matrix products, arithmetic and copies ran while one was open for 0% of the time, Pallas kernels for 0%

profile of v5, /device:TPU:1, one launch (start us, length us, event | category | flops | bytes accessed | tf_op | source)
XLA Modules:
  0.0 217.2 jit_solution(4688061126375018496)
XLA Ops:
  2.1 6.0 %collective-permute-start = (f32[5,3,16,128]{3,2,1,0:T(8,128)S(1)}, f32[5,3,16,128]{3,2,1,0:T(8,128)S(1)}, u32[]{:S(2)}, u32[]{:S(2)}) collective-permute-start(f32[5,3,16,128]{3,2,1,0:T(8,128)S(1)} %get-tuple-element.86), channel_id=1, source_target_pairs={{0,0},{1,4},{2,1},{3,5},{4,2},{5,6},{6,3},{7,7},{8,11},{9,15},{10,... | collective-permute-start | bytes 368648 | tf_op jit(solution)/shard_map/ppermute | solution.py:640
  8.1 1.9 collective-permute-start.1
  10.0 1.2 collective-permute-start.2
  11.3 4.1 %collective-permute-start.3 = (f32[5,3,16,128]{3,2,1,0:T(8,128)S(1)}, f32[5,3,16,128]{3,2,1,0:T(8,128)S(1)}, u32[]{:S(2)}, u32[]{:S(2)}) collective-permute-start(f32[5,3,16,128]{3,2,1,0:T(8,128)S(1)} %get-tuple-element.89), channel_id=1, source_target_pairs={{0,4},{1,1},{2,5},{3,0},{4,6},{5,3},{6,7},{7,2},{8,15},{9,10},{10,... | collective-permute-start | bytes 368648 | tf_op jit(solution)/shard_map/ppermute | solution.py:640
  15.9 2.4 %collective-permute-done.2.refs_2_ = f32[5,3,16,128]{3,2,1,0:T(8,128)S(1)} collective-permute-done((f32[5,3,16,128]{3,2,1,0:T(8,128)S(1)}, f32[5,3,16,128]{3,2,1,0:T(8,128)S(1)}, u32[]{:S(2)}, u32[]{:S(2)}) %collective-permute-start.2) | collective-permute-done | bytes 122912 | tf_op jit(solution)/shard_map/ppermute | solution.py:640
  18.4 1.9 collective-permute-start.5
  21.2 1.3 collective-permute-start.6
  22.4 3.8 %collective-permute-done.6.far_ref = f32[4,1,1,16,128]{4,3,2,1,0:T(8,128)S(1)} collective-permute-done((f32[4,1,1,16,128]{4,3,2,1,0:T(8,128)S(1)}, f32[4,1,1,16,128]{4,3,2,1,0:T(8,128)S(1)}, u32[]{:S(2)}, u32[]{:S(2)}) %collective-permute-start.6) | collective-permute-done | bytes 32800 | tf_op jit(solution)/shard_map/ppermute | solution.py:653
  26.2 2.6 %collective-permute-done.5.odd_ref = f32[4,5,3,16,128]{4,3,2,1,0:T(8,128)S(1)} collective-permute-done((f32[4,5,3,16,128]{4,3,2,1,0:T(8,128)S(1)}, f32[4,5,3,16,128]{4,3,2,1,0:T(8,128)S(1)}, u32[]{:S(2)}, u32[]{:S(2)}) %collective-permute-start.5) | collective-permute-done | bytes 491552 | tf_op jit(solution)/shard_map/ppermute | solution.py:648
  28.9 3.3 %start.1 = (f32[9,64,128]{2,1,0:T(8,128)S(1)}, f32[8,64,128]{2,1,0:T(8,128)S(1)}, f32[8,64,128]{2,1,0:T(8,128)S(1)}, f32[8,64,128]{2,1,0:T(8,128)S(1)}, f32[18,6...) custom-call(f32[4,5,3,16,128]{4,3,2,1,0:T(8,128)S(1)} %join.1.own_re, ...), custom_call_target="tpu_custom_call" | custom-call | tf_op jit(solution)/shard_map/start/pallas_call | solution.py:599
  32.2 1.1 collective-permute-start.7
  33.3 1.9 collective-permute-start.8
  35.2 1.3 collective-permute-start.9
  36.5 16.2 %all_to_all.45.red_in = f32[32,1,128]{2,1,0:T(1,128)S(1)} all-to-all(f32[32,1,128]{2,1,0:T(1,128)S(1)} %get-tuple-element.90), channel_id=1, replica_groups=mesh['tm'=8,'gx'=8,'gy'=4] {'gx','gy'}, dimensions={0} | all-to-all | bytes 32768 | tf_op jit(solution)/shard_map/all_to_all | solution.py:656
  52.7 1.8 second.1
  54.6 10.7 %all_to_all.46.red_in = f32[32,1,128]{2,1,0:T(1,128)S(1)} all-to-all(f32[32,1,128]{2,1,0:T(1,128)S(1)} %get-tuple-element.103), channel_id=1, replica_groups=mesh['tm'=8,'gx'=8,'gy'=4] {'gx','gy'}, dimensions={0} | all-to-all | bytes 32768 | tf_op jit(solution)/shard_map/all_to_all | solution.py:656
  65.4 5.7 %collective-permute-start.10 = (f32[776,128]{1,0:T(8,128)S(1)}, f32[776,128]{1,0:T(8,128)S(1)}, u32[]{:S(2)}, u32[]{:S(2)}) collective-permute-start(f32[776,128]{1,0:T(8,128)S(1)} %block.1.refs_10_), channel_id=1, source_target_pairs={{0,224},{32,0},{64,32},{96,64},{128,96},{160,128},{192,160},{224,1... | collective-permute-start | bytes 1191944 | tf_op jit(solution)/shard_map/ppermute | solution.py:659
  71.1 7.9 %collective-permute-done.10.blk_ref = f32[776,128]{1,0:T(8,128)S(1)} collective-permute-done((f32[776,128]{1,0:T(8,128)S(1)}, f32[776,128]{1,0:T(8,128)S(1)}, u32[]{:S(2)}, u32[]{:S(2)}) %collective-permute-start.10) | collective-permute-done | bytes 397344 | tf_op jit(solution)/shard_map/ppermute | solution.py:659
  79.1 3.5 %collective-permute-start.13 = (f32[776,128]{1,0:T(8,128)S(1)}, f32[776,128]{1,0:T(8,128)S(1)}, u32[]{:S(2)}, u32[]{:S(2)}) collective-permute-start(f32[776,128]{1,0:T(8,128)S(1)} %collective-permute-done.10.blk_ref), channel_id=1, source_target_pairs={{0,224},{32,0},{64,32},{96,64},{128,96},{160,128},{192,160},{224,1... | collective-permute-start | bytes 1191944 | tf_op jit(solution)/shard_map/ppermute | solution.py:659
  82.6 1.8 collective-permute-start.11
  84.3 2.1 collective-permute-start.12
  86.4 4.5 %collective-permute-done.12.refs_3_ = f32[5,64,128]{2,1,0:T(8,128)S(1)} collective-permute-done((f32[5,64,128]{2,1,0:T(8,128)S(1)}, f32[5,64,128]{2,1,0:T(8,128)S(1)}, u32[]{:S(2)}, u32[]{:S(2)}) %collective-permute-start.12) | collective-permute-done | bytes 163872 | tf_op jit(solution)/shard_map/ppermute | solution.py:648
  91.0 1.3 chain2.1
  92.3 2.2 %collective-permute-start.16 = (f32[776,128]{1,0:T(8,128)S(1)}, f32[776,128]{1,0:T(8,128)S(1)}, u32[]{:S(2)}, u32[]{:S(2)}) collective-permute-start(f32[776,128]{1,0:T(8,128)S(1)} %collective-permute-done.13.refs_7_), channel_id=1, source_target_pairs={{0,224},{32,0},{64,32},{96,64},{128,96},{160,128},{192,160},{224,1... | collective-permute-start | bytes 1191944 | tf_op jit(solution)/shard_map/ppermute | solution.py:659
  94.5 2.7 %collective-permute-start.14 = (f32[8,64,128]{2,1,0:T(8,128)S(1)}, f32[8,64,128]{2,1,0:T(8,128)S(1)}, u32[]{:S(2)}, u32[]{:S(2)}) collective-permute-start(f32[8,64,128]{2,1,0:T(8,128)S(1)} %get-tuple-element.119), channel_id=1, source_target_pairs={{0,4},{1,5},{2,6},{3,7},{4,0},{5,1},{6,2},{7,3},{8,12},{9,13},{10,... | collective-permute-start | bytes 786440 | tf_op jit(solution)/shard_map/ppermute | solution.py:648
  97.2 2.1 collective-permute-start.15
  99.3 11.4 %all_to_all.47.refs_1_ = f32[32,1,128]{2,1,0:T(1,128)S(1)} all-to-all(f32[32,1,128]{2,1,0:T(1,128)S(1)} %get-tuple-element.114), channel_id=1, replica_groups=mesh['tm'=8,'gx'=8,'gy'=4] {'gx','gy'}, dimensions={0} | all-to-all | bytes 32768 | tf_op jit(solution)/shard_map/all_to_all | solution.py:656
  110.7 1.4 chain3.1
  112.9 2.1 collective-permute-start.18
  115.0 11.4 %all_to_all.48.refs_1_ = f32[32,1,128]{2,1,0:T(1,128)S(1)} all-to-all(f32[32,1,128]{2,1,0:T(1,128)S(1)} %get-tuple-element.122), channel_id=1, replica_groups=mesh['tm'=8,'gx'=8,'gy'=4] {'gx','gy'}, dimensions={0} | all-to-all | bytes 32768 | tf_op jit(solution)/shard_map/all_to_all | solution.py:656
  126.4 1.4 chain4.1
  128.7 2.1 collective-permute-start.21
  130.8 11.4 %all_to_all.49.refs_1_ = f32[32,1,128]{2,1,0:T(1,128)S(1)} all-to-all(f32[32,1,128]{2,1,0:T(1,128)S(1)} %get-tuple-element.130), channel_id=1, replica_groups=mesh['tm'=8,'gx'=8,'gy'=4] {'gx','gy'}, dimensions={0} | all-to-all | bytes 32768 | tf_op jit(solution)/shard_map/all_to_all | solution.py:656
  142.2 1.4 chain5.1
  144.8 2.1 collective-permute-start.24
  146.8 11.4 %all_to_all.50.refs_1_ = f32[32,1,128]{2,1,0:T(1,128)S(1)} all-to-all(f32[32,1,128]{2,1,0:T(1,128)S(1)} %get-tuple-element.138), channel_id=1, replica_groups=mesh['tm'=8,'gx'=8,'gy'=4] {'gx','gy'}, dimensions={0} | all-to-all | bytes 32768 | tf_op jit(solution)/shard_map/all_to_all | solution.py:656
  158.3 1.4 chain6.1
  159.7 2.9 %collective-permute-start.28 = (f32[776,128]{1,0:T(8,128)S(1)}, f32[776,128]{1,0:T(8,128)S(1)}, u32[]{:S(2)}, u32[]{:S(2)}) collective-permute-start(f32[776,128]{1,0:T(8,128)S(1)} %collective-permute-done.25.refs_10_), channel_id=1, source_target_pairs={{0,224},{32,0},{64,32},{96,64},{128,96},{160,128},{192,160},{224,1... | collective-permute-start | bytes 1191944 | tf_op jit(solution)/shard_map/ppermute | solution.py:659
  163.6 2.1 collective-permute-start.27
  165.6 11.4 %all_to_all.51.refs_1_ = f32[32,1,128]{2,1,0:T(1,128)S(1)} all-to-all(f32[32,1,128]{2,1,0:T(1,128)S(1)} %get-tuple-element.146), channel_id=1, replica_groups=mesh['tm'=8,'gx'=8,'gy'=4] {'gx','gy'}, dimensions={0} | all-to-all | bytes 32768 | tf_op jit(solution)/shard_map/all_to_all | solution.py:656
  177.0 1.4 chain7.1
  179.2 2.1 collective-permute-start.30
  181.3 11.4 %all_to_all.52.refs_1_ = f32[32,1,128]{2,1,0:T(1,128)S(1)} all-to-all(f32[32,1,128]{2,1,0:T(1,128)S(1)} %get-tuple-element.154), channel_id=1, replica_groups=mesh['tm'=8,'gx'=8,'gy'=4] {'gx','gy'}, dimensions={0} | all-to-all | bytes 32768 | tf_op jit(solution)/shard_map/all_to_all | solution.py:656
  192.7 1.5 chain8.1
  194.2 2.7 %collective-permute-start.31 = (f32[6,3,16,128]{3,2,1,0:T(8,128)S(1)}, f32[6,3,16,128]{3,2,1,0:T(8,128)S(1)}, u32[]{:S(2)}, u32[]{:S(2)}) collective-permute-start(f32[6,3,16,128]{3,2,1,0:T(8,128)S(1)} %get-tuple-element.161), channel_id=1, source_target_pairs={{0,0},{1,2},{2,4},{3,6},{4,1},{5,3},{6,5},{7,7},{8,14},{9,12},{10,... | collective-permute-start | bytes 442376 | tf_op jit(solution)/shard_map/ppermute | solution.py:640
  196.9 4.3 %collective-permute-start.32 = (f32[6,3,16,128]{3,2,1,0:T(8,128)S(1)}, f32[6,3,16,128]{3,2,1,0:T(8,128)S(1)}, u32[]{:S(2)}, u32[]{:S(2)}) collective-permute-start(f32[6,3,16,128]{3,2,1,0:T(8,128)S(1)} %get-tuple-element.162), channel_id=1, source_target_pairs={{0,1},{1,3},{2,5},{3,7},{4,2},{5,0},{6,6},{7,4},{8,15},{9,13},{10,... | collective-permute-start | bytes 442376 | tf_op jit(solution)/shard_map/ppermute | solution.py:640
  201.4 3.1 %collective-permute-start.34 = (f32[6,3,16,128]{3,2,1,0:T(8,128)S(1)}, f32[6,3,16,128]{3,2,1,0:T(8,128)S(1)}, u32[]{:S(2)}, u32[]{:S(2)}) collective-permute-start(f32[6,3,16,128]{3,2,1,0:T(8,128)S(1)} %get-tuple-element.164), channel_id=1, source_target_pairs={{0,3},{1,1},{2,7},{3,5},{4,0},{5,2},{6,4},{7,6},{8,13},{9,15},{10,... | collective-permute-start | bytes 442376 | tf_op jit(solution)/shard_map/ppermute | solution.py:640
  204.5 11.8 %all_to_all.53.red_in = f32[32,1,128]{2,1,0:T(1,128)S(1)} all-to-all(f32[32,1,128]{2,1,0:T(1,128)S(1)} %get-tuple-element.160), channel_id=1, replica_groups=mesh['tm'=8,'gx'=8,'gy'=4] {'gx','gy'}, dimensions={0} | all-to-all | bytes 32768 | tf_op jit(solution)/shard_map/all_to_all | solution.py:656
  (61 shorter events, 9.2 us)
Async XLA Ops:
  0.0 0.9 copy-start.1
  0.1 0.8 copy-start.5
  0.1 0.8 copy-start.6
  0.1 0.8 copy-start.2
  0.1 0.8 copy-start.3
  0.1 0.8 copy-start.4
  0.9 1.0 copy-start
  2.1 13.3 %collective-permute-start = (f32[5,3,16,128]{3,2,1,0:T(8,128)S(1)}, f32[5,3,16,128]{3,2,1,0:T(8,128)S(1)}, u32[]{:S(2)}, u32[]{:S(2)}) collective-permute-start(f32[5,3,16,128]{3,2,1,0:T(8,128)S(1)} %get-tuple-element.86), channel_id=1, source_target_pairs={{0,0},{1,4},{2,1},{3,5},{4,2},{5,6},{6,3},{7,7},{8,11},{9,15},{10,... | collective-permute-start | bytes 368648 | tf_op jit(solution)/shard_map/ppermute | solution.py:640
  8.1 7.8 %collective-permute-start.1 = (f32[5,3,16,128]{3,2,1,0:T(8,128)S(1)}, f32[5,3,16,128]{3,2,1,0:T(8,128)S(1)}, u32[]{:S(2)}, u32[]{:S(2)}) collective-permute-start(f32[5,3,16,128]{3,2,1,0:T(8,128)S(1)} %get-tuple-element.87), channel_id=1, source_target_pairs={{0,5},{1,0},{2,4},{3,1},{4,7},{5,2},{6,6},{7,3},{8,14},{9,11},{10,... | collective-permute-start | bytes 368648 | tf_op jit(solution)/shard_map/ppermute | solution.py:640
  10.0 8.2 %collective-permute-start.2 = (f32[5,3,16,128]{3,2,1,0:T(8,128)S(1)}, f32[5,3,16,128]{3,2,1,0:T(8,128)S(1)}, u32[]{:S(2)}, u32[]{:S(2)}) collective-permute-start(f32[5,3,16,128]{3,2,1,0:T(8,128)S(1)} %get-tuple-element.88), channel_id=1, source_target_pairs={{0,1},{1,5},{2,0},{3,4},{4,3},{5,7},{6,2},{7,6},{8,10},{9,14},{10,... | collective-permute-start | bytes 368648 | tf_op jit(solution)/shard_map/ppermute | solution.py:640
  11.3 7.0 %collective-permute-start.3 = (f32[5,3,16,128]{3,2,1,0:T(8,128)S(1)}, f32[5,3,16,128]{3,2,1,0:T(8,128)S(1)}, u32[]{:S(2)}, u32[]{:S(2)}) collective-permute-start(f32[5,3,16,128]{3,2,1,0:T(8,128)S(1)} %get-tuple-element.89), channel_id=1, source_target_pairs={{0,4},{1,1},{2,5},{3,0},{4,6},{5,3},{6,7},{7,2},{8,15},{9,10},{10,... | collective-permute-start | bytes 368648 | tf_op jit(solution)/shard_map/ppermute | solution.py:640
  18.4 10.5 %collective-permute-start.5 = (f32[4,5,3,16,128]{4,3,2,1,0:T(8,128)S(1)}, f32[4,5,3,16,128]{4,3,2,1,0:T(8,128)S(1)}, u32[]{:S(2)}, u32[]{:S(2)}) collective-permute-start(f32[4,5,3,16,128]{4,3,2,1,0:T(8,128)S(1)} %join.1.own_ref), channel_id=1, source_target_pairs={{1,4},{2,5},{3,6},{4,1},{5,2},{6,3},{7,11},{8,13},{9,14},{10,15},{... | collective-permute-start | bytes 1474568 | tf_op jit(solution)/shard_map/ppermute | solution.py:648
  20.3 8.6 %collective-permute-start.4 = (f32[4,5,3,16,128]{4,3,2,1,0:T(8,128)S(1)}, f32[4,5,3,16,128]{4,3,2,1,0:T(8,128)S(1)}, u32[]{:S(2)}, u32[]{:S(2)}) collective-permute-start(f32[4,5,3,16,128]{4,3,2,1,0:T(8,128)S(1)} %join.1.own_ref), channel_id=1, source_target_pairs={{0,4},{1,5},{2,6},{3,7},{4,0},{5,1},{6,2},{7,3},{8,12},{9,13},{10,... | collective-permute-start | bytes 1474568 | tf_op jit(solution)/shard_map/ppermute | solution.py:648
  21.2 5.1 %collective-permute-start.6 = (f32[4,1,1,16,128]{4,3,2,1,0:T(8,128)S(1)}, f32[4,1,1,16,128]{4,3,2,1,0:T(8,128)S(1)}, u32[]{:S(2)}, u32[]{:S(2)}) collective-permute-start(f32[4,1,1,16,128]{4,3,2,1,0:T(8,128)S(1)} %slice.4), channel_id=1, source_target_pairs={{1,0},{2,1},{3,2},{5,4},{6,5},{7,6},{8,9},{9,10},{10,11},{11,3},{1... | collective-permute-start | bytes 98312 | tf_op jit(solution)/shard_map/ppermute | solution.py:653
  32.2 20.6 %collective-permute-start.7 = (f32[6,64,128]{2,1,0:T(8,128)S(1)}, f32[6,64,128]{2,1,0:T(8,128)S(1)}, u32[]{:S(2)}, u32[]{:S(2)}) collective-permute-start(f32[6,64,128]{2,1,0:T(8,128)S(1)} %get-tuple-element.100), channel_id=1, source_target_pairs={{0,4},{1,5},{2,6},{3,7},{4,0},{5,1},{6,2},{7,3},{8,12},{9,13},{10,... | collective-permute-start | bytes 589832 | tf_op jit(solution)/shard_map/ppermute | solution.py:648
  33.3 19.4 %collective-permute-start.8 = (f32[6,64,128]{2,1,0:T(8,128)S(1)}, f32[6,64,128]{2,1,0:T(8,128)S(1)}, u32[]{:S(2)}, u32[]{:S(2)}) collective-permute-start(f32[6,64,128]{2,1,0:T(8,128)S(1)} %get-tuple-element.101), channel_id=1, source_target_pairs={{1,4},{2,5},{3,6},{4,1},{5,2},{6,3},{7,11},{8,13},{9,14},{10,15},{... | collective-permute-start | bytes 589832 | tf_op jit(solution)/shard_map/ppermute | solution.py:648
  35.2 17.5 %collective-permute-start.9 = (f32[3,64,128]{2,1,0:T(8,128)S(1)}, f32[3,64,128]{2,1,0:T(8,128)S(1)}, u32[]{:S(2)}, u32[]{:S(2)}) collective-permute-start(f32[3,64,128]{2,1,0:T(8,128)S(1)} %get-tuple-element.102), channel_id=1, source_target_pairs={{1,0},{2,1},{3,2},{5,4},{6,5},{7,6},{8,9},{9,10},{10,11},{11,3},{1... | collective-permute-start | bytes 294920 | tf_op jit(solution)/shard_map/ppermute | solution.py:653
  65.4 13.6 %collective-permute-start.10 = (f32[776,128]{1,0:T(8,128)S(1)}, f32[776,128]{1,0:T(8,128)S(1)}, u32[]{:S(2)}, u32[]{:S(2)}) collective-permute-start(f32[776,128]{1,0:T(8,128)S(1)} %block.1.refs_10_), channel_id=1, source_target_pairs={{0,224},{32,0},{64,32},{96,64},{128,96},{160,128},{192,160},{224,1... | collective-permute-start | bytes 1191944 | tf_op jit(solution)/shard_map/ppermute | solution.py:659
  79.1 11.9 %collective-permute-start.13 = (f32[776,128]{1,0:T(8,128)S(1)}, f32[776,128]{1,0:T(8,128)S(1)}, u32[]{:S(2)}, u32[]{:S(2)}) collective-permute-start(f32[776,128]{1,0:T(8,128)S(1)} %collective-permute-done.10.blk_ref), channel_id=1, source_target_pairs={{0,224},{32,0},{64,32},{96,64},{128,96},{160,128},{192,160},{224,1... | collective-permute-start | bytes 1191944 | tf_op jit(solution)/shard_map/ppermute | solution.py:659
  82.6 3.9 %collective-permute-start.11 = (f32[5,64,128]{2,1,0:T(8,128)S(1)}, f32[5,64,128]{2,1,0:T(8,128)S(1)}, u32[]{:S(2)}, u32[]{:S(2)}) collective-permute-start(f32[5,64,128]{2,1,0:T(8,128)S(1)} %get-tuple-element.110), channel_id=1, source_target_pairs={{0,4},{1,5},{2,6},{3,7},{4,0},{5,1},{6,2},{7,3},{8,12},{9,13},{10,... | collective-permute-start | bytes 491528 | tf_op jit(solution)/shard_map/ppermute | solution.py:648
  84.3 6.6 %collective-permute-start.12 = (f32[5,64,128]{2,1,0:T(8,128)S(1)}, f32[5,64,128]{2,1,0:T(8,128)S(1)}, u32[]{:S(2)}, u32[]{:S(2)}) collective-permute-start(f32[5,64,128]{2,1,0:T(8,128)S(1)} %get-tuple-element.111), channel_id=1, source_target_pairs={{1,4},{2,5},{3,6},{4,1},{5,2},{6,3},{7,11},{8,13},{9,14},{10,15},{... | collective-permute-start | bytes 491528 | tf_op jit(solution)/shard_map/ppermute | solution.py:648
  92.3 18.4 %collective-permute-start.16 = (f32[776,128]{1,0:T(8,128)S(1)}, f32[776,128]{1,0:T(8,128)S(1)}, u32[]{:S(2)}, u32[]{:S(2)}) collective-permute-start(f32[776,128]{1,0:T(8,128)S(1)} %collective-permute-done.13.refs_7_), channel_id=1, source_target_pairs={{0,224},{32,0},{64,32},{96,64},{128,96},{160,128},{192,160},{224,1... | collective-permute-start | bytes 1191944 | tf_op jit(solution)/shard_map/ppermute | solution.py:659
  94.5 16.2 %collective-permute-start.14 = (f32[8,64,128]{2,1,0:T(8,128)S(1)}, f32[8,64,128]{2,1,0:T(8,128)S(1)}, u32[]{:S(2)}, u32[]{:S(2)}) collective-permute-start(f32[8,64,128]{2,1,0:T(8,128)S(1)} %get-tuple-element.119), channel_id=1, source_target_pairs={{0,4},{1,5},{2,6},{3,7},{4,0},{5,1},{6,2},{7,3},{8,12},{9,13},{10,... | collective-permute-start | bytes 786440 | tf_op jit(solution)/shard_map/ppermute | solution.py:648
  97.2 13.5 %collective-permute-start.15 = (f32[8,64,128]{2,1,0:T(8,128)S(1)}, f32[8,64,128]{2,1,0:T(8,128)S(1)}, u32[]{:S(2)}, u32[]{:S(2)}) collective-permute-start(f32[8,64,128]{2,1,0:T(8,128)S(1)} %get-tuple-element.120), channel_id=1, source_target_pairs={{1,4},{2,5},{3,6},{4,1},{5,2},{6,3},{7,11},{8,13},{9,14},{10,15},{... | collective-permute-start | bytes 786440 | tf_op jit(solution)/shard_map/ppermute | solution.py:648
  112.1 14.3 %collective-permute-start.19 = (f32[776,128]{1,0:T(8,128)S(1)}, f32[776,128]{1,0:T(8,128)S(1)}, u32[]{:S(2)}, u32[]{:S(2)}) collective-permute-start(f32[776,128]{1,0:T(8,128)S(1)} %collective-permute-done.16.refs_10_), channel_id=1, source_target_pairs={{0,224},{32,0},{64,32},{96,64},{128,96},{160,128},{192,160},{224,1... | collective-permute-start | bytes 1191944 | tf_op jit(solution)/shard_map/ppermute | solution.py:659
  112.2 14.2 %collective-permute-start.17 = (f32[8,64,128]{2,1,0:T(8,128)S(1)}, f32[8,64,128]{2,1,0:T(8,128)S(1)}, u32[]{:S(2)}, u32[]{:S(2)}) collective-permute-start(f32[8,64,128]{2,1,0:T(8,128)S(1)} %get-tuple-element.127), channel_id=1, source_target_pairs={{0,4},{1,5},{2,6},{3,7},{4,0},{5,1},{6,2},{7,3},{8,12},{9,13},{10,... | collective-permute-start | bytes 786440 | tf_op jit(solution)/shard_map/ppermute | solution.py:648
  112.9 13.5 %collective-permute-start.18 = (f32[8,64,128]{2,1,0:T(8,128)S(1)}, f32[8,64,128]{2,1,0:T(8,128)S(1)}, u32[]{:S(2)}, u32[]{:S(2)}) collective-permute-start(f32[8,64,128]{2,1,0:T(8,128)S(1)} %get-tuple-element.128), channel_id=1, source_target_pairs={{1,4},{2,5},{3,6},{4,1},{5,2},{6,3},{7,11},{8,13},{9,14},{10,15},{... | collective-permute-start | bytes 786440 | tf_op jit(solution)/shard_map/ppermute | solution.py:648
  127.9 14.3 %collective-permute-start.22 = (f32[776,128]{1,0:T(8,128)S(1)}, f32[776,128]{1,0:T(8,128)S(1)}, u32[]{:S(2)}, u32[]{:S(2)}) collective-permute-start(f32[776,128]{1,0:T(8,128)S(1)} %collective-permute-done.19.refs_10_), channel_id=1, source_target_pairs={{0,224},{32,0},{64,32},{96,64},{128,96},{160,128},{192,160},{224,1... | collective-permute-start | bytes 1191944 | tf_op jit(solution)/shard_map/ppermute | solution.py:659
  128.0 14.2 %collective-permute-start.20 = (f32[8,64,128]{2,1,0:T(8,128)S(1)}, f32[8,64,128]{2,1,0:T(8,128)S(1)}, u32[]{:S(2)}, u32[]{:S(2)}) collective-permute-start(f32[8,64,128]{2,1,0:T(8,128)S(1)} %get-tuple-element.135), channel_id=1, source_target_pairs={{0,4},{1,5},{2,6},{3,7},{4,0},{5,1},{6,2},{7,3},{8,12},{9,13},{10,... | collective-permute-start | bytes 786440 | tf_op jit(solution)/shard_map/ppermute | solution.py:648
  128.7 13.5 %collective-permute-start.21 = (f32[8,64,128]{2,1,0:T(8,128)S(1)}, f32[8,64,128]{2,1,0:T(8,128)S(1)}, u32[]{:S(2)}, u32[]{:S(2)}) collective-permute-start(f32[8,64,128]{2,1,0:T(8,128)S(1)} %get-tuple-element.136), channel_id=1, source_target_pairs={{1,4},{2,5},{3,6},{4,1},{5,2},{6,3},{7,11},{8,13},{9,14},{10,15},{... | collective-permute-start | bytes 786440 | tf_op jit(solution)/shard_map/ppermute | solution.py:648
  143.6 14.6 %collective-permute-start.25 = (f32[776,128]{1,0:T(8,128)S(1)}, f32[776,128]{1,0:T(8,128)S(1)}, u32[]{:S(2)}, u32[]{:S(2)}) collective-permute-start(f32[776,128]{1,0:T(8,128)S(1)} %collective-permute-done.22.refs_10_), channel_id=1, source_target_pairs={{0,224},{32,0},{64,32},{96,64},{128,96},{160,128},{192,160},{224,1... | collective-permute-start | bytes 1191944 | tf_op jit(solution)/shard_map/ppermute | solution.py:659
  143.8 14.4 %collective-permute-start.23 = (f32[8,64,128]{2,1,0:T(8,128)S(1)}, f32[8,64,128]{2,1,0:T(8,128)S(1)}, u32[]{:S(2)}, u32[]{:S(2)}) collective-permute-start(f32[8,64,128]{2,1,0:T(8,128)S(1)} %get-tuple-element.143), channel_id=1, source_target_pairs={{0,4},{1,5},{2,6},{3,7},{4,0},{5,1},{6,2},{7,3},{8,12},{9,13},{10,... | collective-permute-start | bytes 786440 | tf_op jit(solution)/shard_map/ppermute | solution.py:648
  144.8 13.5 %collective-permute-start.24 = (f32[8,64,128]{2,1,0:T(8,128)S(1)}, f32[8,64,128]{2,1,0:T(8,128)S(1)}, u32[]{:S(2)}, u32[]{:S(2)}) collective-permute-start(f32[8,64,128]{2,1,0:T(8,128)S(1)} %get-tuple-element.144), channel_id=1, source_target_pairs={{1,4},{2,5},{3,6},{4,1},{5,2},{6,3},{7,11},{8,13},{9,14},{10,15},{... | collective-permute-start | bytes 786440 | tf_op jit(solution)/shard_map/ppermute | solution.py:648
  159.7 17.3 %collective-permute-start.28 = (f32[776,128]{1,0:T(8,128)S(1)}, f32[776,128]{1,0:T(8,128)S(1)}, u32[]{:S(2)}, u32[]{:S(2)}) collective-permute-start(f32[776,128]{1,0:T(8,128)S(1)} %collective-permute-done.25.refs_10_), channel_id=1, source_target_pairs={{0,224},{32,0},{64,32},{96,64},{128,96},{160,128},{192,160},{224,1... | collective-permute-start | bytes 1191944 | tf_op jit(solution)/shard_map/ppermute | solution.py:659
  162.6 14.4 %collective-permute-start.26 = (f32[8,64,128]{2,1,0:T(8,128)S(1)}, f32[8,64,128]{2,1,0:T(8,128)S(1)}, u32[]{:S(2)}, u32[]{:S(2)}) collective-permute-start(f32[8,64,128]{2,1,0:T(8,128)S(1)} %get-tuple-element.151), channel_id=1, source_target_pairs={{0,4},{1,5},{2,6},{3,7},{4,0},{5,1},{6,2},{7,3},{8,12},{9,13},{10,... | collective-permute-start | bytes 786440 | tf_op jit(solution)/shard_map/ppermute | solution.py:648
  163.6 13.5 %collective-permute-start.27 = (f32[8,64,128]{2,1,0:T(8,128)S(1)}, f32[8,64,128]{2,1,0:T(8,128)S(1)}, u32[]{:S(2)}, u32[]{:S(2)}) collective-permute-start(f32[8,64,128]{2,1,0:T(8,128)S(1)} %get-tuple-element.152), channel_id=1, source_target_pairs={{1,4},{2,5},{3,6},{4,1},{5,2},{6,3},{7,11},{8,13},{9,14},{10,15},{... | collective-permute-start | bytes 786440 | tf_op jit(solution)/shard_map/ppermute | solution.py:648
  178.5 14.2 %collective-permute-start.29 = (f32[8,64,128]{2,1,0:T(8,128)S(1)}, f32[8,64,128]{2,1,0:T(8,128)S(1)}, u32[]{:S(2)}, u32[]{:S(2)}) collective-permute-start(f32[8,64,128]{2,1,0:T(8,128)S(1)} %get-tuple-element.158), channel_id=1, source_target_pairs={{0,4},{1,5},{2,6},{3,7},{4,0},{5,1},{6,2},{7,3},{8,12},{9,13},{10,... | collective-permute-start | bytes 786440 | tf_op jit(solution)/shard_map/ppermute | solution.py:648
  179.2 13.5 %collective-permute-start.30 = (f32[8,64,128]{2,1,0:T(8,128)S(1)}, f32[8,64,128]{2,1,0:T(8,128)S(1)}, u32[]{:S(2)}, u32[]{:S(2)}) collective-permute-start(f32[8,64,128]{2,1,0:T(8,128)S(1)} %get-tuple-element.159), channel_id=1, source_target_pairs={{1,4},{2,5},{3,6},{4,1},{5,2},{6,3},{7,11},{8,13},{9,14},{10,15},{... | collective-permute-start | bytes 786440 | tf_op jit(solution)/shard_map/ppermute | solution.py:648
  194.2 22.1 %collective-permute-start.31 = (f32[6,3,16,128]{3,2,1,0:T(8,128)S(1)}, f32[6,3,16,128]{3,2,1,0:T(8,128)S(1)}, u32[]{:S(2)}, u32[]{:S(2)}) collective-permute-start(f32[6,3,16,128]{3,2,1,0:T(8,128)S(1)} %get-tuple-element.161), channel_id=1, source_target_pairs={{0,0},{1,2},{2,4},{3,6},{4,1},{5,3},{6,5},{7,7},{8,14},{9,12},{10,... | collective-permute-start | bytes 442376 | tf_op jit(solution)/shard_map/ppermute | solution.py:640
  196.9 19.4 %collective-permute-start.32 = (f32[6,3,16,128]{3,2,1,0:T(8,128)S(1)}, f32[6,3,16,128]{3,2,1,0:T(8,128)S(1)}, u32[]{:S(2)}, u32[]{:S(2)}) collective-permute-start(f32[6,3,16,128]{3,2,1,0:T(8,128)S(1)} %get-tuple-element.162), channel_id=1, source_target_pairs={{0,1},{1,3},{2,5},{3,7},{4,2},{5,0},{6,6},{7,4},{8,15},{9,13},{10,... | collective-permute-start | bytes 442376 | tf_op jit(solution)/shard_map/ppermute | solution.py:640
  201.3 15.0 %collective-permute-start.33 = (f32[6,3,16,128]{3,2,1,0:T(8,128)S(1)}, f32[6,3,16,128]{3,2,1,0:T(8,128)S(1)}, u32[]{:S(2)}, u32[]{:S(2)}) collective-permute-start(f32[6,3,16,128]{3,2,1,0:T(8,128)S(1)} %get-tuple-element.163), channel_id=1, source_target_pairs={{0,2},{1,0},{2,6},{3,4},{4,3},{5,1},{6,7},{7,5},{8,12},{9,14},{10,... | collective-permute-start | bytes 442376 | tf_op jit(solution)/shard_map/ppermute | solution.py:640
  201.4 14.9 %collective-permute-start.34 = (f32[6,3,16,128]{3,2,1,0:T(8,128)S(1)}, f32[6,3,16,128]{3,2,1,0:T(8,128)S(1)}, u32[]{:S(2)}, u32[]{:S(2)}) collective-permute-start(f32[6,3,16,128]{3,2,1,0:T(8,128)S(1)} %get-tuple-element.164), channel_id=1, source_target_pairs={{0,3},{1,1},{2,7},{3,5},{4,0},{5,2},{6,4},{7,6},{8,13},{9,15},{10,... | collective-permute-start | bytes 442376 | tf_op jit(solution)/shard_map/ppermute | solution.py:640

commit v6 on v5

--- a/solution.py
+++ b/solution.py
@@ -207,8 +207,7 @@
         kal_ref[e + 3] = 0.25 * (stiff * load)
 
     heat = [const_ref[HEAT + i : HEAT + i + 1] for i in range(2)]
-    decay_f, rest_f, ff, shift_f = prony(const_ref, 0)
-    decay_c, rest_c, fc, shift_c = prony(const_ref, COARSE)
+    shift_f, shift_c = prony(const_ref, 0)[3], prony(const_ref, COARSE)[3]
 
     for i in range(-2, 6):
         ksum = kel_ref[i + 2] + kel_ref[i + 3]
@@ -236,19 +235,17 @@
     zeros = jnp.zeros((ny, nz), jnp.float32)
     acc = [zeros] * 10
     for i in range(-2, 6):
-        h = [raw(2 + p, i) for p in range(PRONY)]
-        fh = [ff[p] * h[p] for p in range(PRONY)]
-        state_ref[10 + i + 2] = decay_f[0] * fh[0] + decay_f[1] * fh[1] + decay_f[2] * fh[2]
+        later = raw(3, i)
+        state_ref[10 + i + 2] = later
         ui = state_ref[i + 3]
-        load = heat[0] * theta_ref[i + 2] + (fh[0] + fh[1] + fh[2])
+        load = heat[0] * theta_ref[i + 2] + raw(2, i)
         s = load + ui - au_ref[i + 2]
         z = inv_f_ref[i + 2] * s - ui
         zf_ref[i + 2] = z
         if 0 <= i < L:
             acc[0] = acc[0] + z * (s - ui * (1.0 / inv_f_ref[i + 2]))
         if i < 5:
-            load = heat[1] * theta_ref[i + 2]
-            load = load + (fc[0] * h[0] + fc[1] * h[1] + fc[2] * h[2])
+            load = heat[1] * theta_ref[i + 2] + later
             s = load + ui * (1.0 / PACES) - au_ref[i + 2]
             z = inv_c_ref[i + 2] * s - ui
             w_ref[i + 2] = z
@@ -372,7 +369,7 @@
         g = state_ref[i + 3] + b[0] * zc_ref[i] + b[1] * ozc_ref[i]
         base_ref[i] = u1 - weight * g
         for p in range(PRONY):
-            h = jnp.concatenate([own_ref[q, 2 + p, i] for q in range(chunks)], axis=0)
+            h = jnp.concatenate([own_ref[q, p, i] for q in range(chunks)], axis=0)
             h1 = decay_f[p] * h + rest_f[p] * u1
             gh = decay_c[p] * h + rest_c[p] * g
             base_ref[L * (1 + p) + i] = decay_f[p] * h1 + rest_f[p] * u1 - weight * gh
@@ -582,13 +579,21 @@
 
 
 def join_kernel(const_ref, *refs):
-    got_refs, out_ref = refs[:-1], refs[-1]
+    got_refs, (out_ref, past_ref) = refs[:-2], refs[-2:]
+    decay, rest, f, shift = prony(const_ref, 0)
     count = len(got_refs)
     for q in range(count):
-        for field in range(2 + PRONY):
-            for i in range(L):
-                parts = [got_refs[(q - v) % count][field, i] for v in range(count)]
-                out_ref[q, field, i] = chosen(const_ref, PART, parts)
+        for i in range(L):
+            label, u, *h = [
+                chosen(const_ref, PART, [got_refs[(q - v) % count][at, i] for v in range(count)])
+                for at in range(2 + PRONY)
+            ]
+            fh = [f[p] * h[p] for p in range(PRONY)]
+            out_ref[q, 0, i], out_ref[q, 1, i] = label, u
+            out_ref[q, 2, i] = fh[0] + fh[1] + fh[2]
+            out_ref[q, 3, i] = decay[0] * fh[0] + decay[1] * fh[1] + decay[2] * fh[2]
+            for p in range(PRONY):
+                past_ref[q, p, i] = h[p]
 
 
 VMEM = pl.BlockSpec(memory_space=pltpu.VMEM)
@@ -678,8 +683,11 @@
         ),
         [(RIGID + 2 * regions, nz)] + [(2 + PRONY, L, ny_part, nz)] * n_gy,
     )
-    (own,) = call(
-        join_kernel, "join", (const, *deal(parts, True)), [(n_gy, 2 + PRONY, L, ny_part, nz)]
+    own, past = call(
+        join_kernel,
+        "join",
+        (const, *deal(parts, True)),
+        [(n_gy, 4, L, ny_part, nz), (n_gy, PRONY, L, ny_part, nz)],
     )
     near, far = trade(own, own), from_next_but_one(own[:, 1:2, :1])
 
@@ -700,7 +708,7 @@
     base, z, oz, ooz, red = call(
         second_kernel,
         "second",
-        (const, red, kel, theta, inv_f, state, own, zf, ozf, oozf, zc, ozc, *near, far),
+        (const, red, kel, theta, inv_f, state, past, zf, ozf, oozf, zc, ozc, *near, far),
         [(4 * L, *plane), (L, *plane), (L, *plane), (L, *plane), red_shape],
         [(10, *plane), (8, *plane), (6, *plane), (4, *plane), (8, *plane)],
     )

time: 218 us -> 217 us (level)
  no operation moved by 1% of the time
where the time goes in v6:
time: 217 us; the launch traced here: 216 us
  blocking collectives  107 us (49%)
  starting transfers between devices  69.7 us (32%)
  waiting for transfers between devices  20.8 us (10%)
  Pallas kernels  16.5 us (8%)
    all_to_all x9, blocking collectives, exchanged(): return lax.all_to_all(red, LINE, 0, 0, tiled=True)  107 us
    ppermute x18, starting transfers between devices, trade(): received.append(lax.ppermute(value, LINE, sorted(both)))  28.9 us
    ppermute x8, starting transfers between devices, deal(): received.append(lax.ppermute(value, LINE, sorted(perm)))  23.6 us
    pallas_call x14, Pallas kernels, call(): pl.pallas_call(kernel, name=name, out_shape=[jax.ShapeDtypeStruct(s, f32)...  16.5 us
    ppermute x7, starting transfers between devices, ring(): return lax.ppermute(block, 'tm', [(s, (s - 1) % n_tm) for s in range(n_tm)])  14.7 us
    ppermute x7, waiting for transfers between devices, ring(): return lax.ppermute(block, 'tm', [(s, (s - 1) % n_tm) for s in range(n_tm)])  7.92 us
    ppermute x18, waiting for transfers between devices, trade(): received.append(lax.ppermute(value, LINE, sorted(both)))  6.17 us
  transfers between devices with their start and end apart: 35, of which 6 were waited for; matrix products, arithmetic and copies ran while one was open for 0% of the time, Pallas kernels for 0%

profile of v6, /device:TPU:1, one launch (start us, length us, event | category | flops | bytes accessed | tf_op | source)
XLA Modules:
  0.0 216.2 jit_solution(9293285609285716973)
XLA Ops:
  2.1 6.0 %collective-permute-start = (f32[5,3,16,128]{3,2,1,0:T(8,128)S(1)}, f32[5,3,16,128]{3,2,1,0:T(8,128)S(1)}, u32[]{:S(2)}, u32[]{:S(2)}) collective-permute-start(f32[5,3,16,128]{3,2,1,0:T(8,128)S(1)} %get-tuple-element.88), channel_id=1, source_target_pairs={{0,0},{1,4},{2,1},{3,5},{4,2},{5,6},{6,3},{7,7},{8,11},{9,15},{10,... | collective-permute-start | bytes 368648 | tf_op jit(solution)/shard_map/ppermute | solution.py:645
  8.1 1.9 collective-permute-start.1
  10.0 1.2 collective-permute-start.2
  11.3 4.1 %collective-permute-start.3 = (f32[5,3,16,128]{3,2,1,0:T(8,128)S(1)}, f32[5,3,16,128]{3,2,1,0:T(8,128)S(1)}, u32[]{:S(2)}, u32[]{:S(2)}) collective-permute-start(f32[5,3,16,128]{3,2,1,0:T(8,128)S(1)} %get-tuple-element.91), channel_id=1, source_target_pairs={{0,4},{1,1},{2,5},{3,0},{4,6},{5,3},{6,7},{7,2},{8,15},{9,10},{10,... | collective-permute-start | bytes 368648 | tf_op jit(solution)/shard_map/ppermute | solution.py:645
  15.9 2.4 %collective-permute-done.2.refs_2_ = f32[5,3,16,128]{3,2,1,0:T(8,128)S(1)} collective-permute-done((f32[5,3,16,128]{3,2,1,0:T(8,128)S(1)}, f32[5,3,16,128]{3,2,1,0:T(8,128)S(1)}, u32[]{:S(2)}, u32[]{:S(2)}) %collective-permute-start.2) | collective-permute-done | bytes 122912 | tf_op jit(solution)/shard_map/ppermute | solution.py:645
  18.4 1.9 collective-permute-start.5
  21.2 1.3 collective-permute-start.6
  22.5 3.8 %collective-permute-done.6.far_ref = f32[4,1,1,16,128]{4,3,2,1,0:T(8,128)S(1)} collective-permute-done((f32[4,1,1,16,128]{4,3,2,1,0:T(8,128)S(1)}, f32[4,1,1,16,128]{4,3,2,1,0:T(8,128)S(1)}, u32[]{:S(2)}, u32[]{:S(2)}) %collective-permute-start.6) | collective-permute-done | bytes 32800 | tf_op jit(solution)/shard_map/ppermute | solution.py:658
  26.3 1.6 collective-permute-done.5.odd_ref
  27.9 3.2 %start.1 = (f32[9,64,128]{2,1,0:T(8,128)S(1)}, f32[8,64,128]{2,1,0:T(8,128)S(1)}, f32[8,64,128]{2,1,0:T(8,128)S(1)}, f32[8,64,128]{2,1,0:T(8,128)S(1)}, f32[18,6...) custom-call(f32[4,4,3,16,128]{4,3,2,1,0:T(8,128)S(1)} %get-tuple-ele, ...), custom_call_target="tpu_custom_call" | custom-call | tf_op jit(solution)/shard_map/start/pallas_call | solution.py:604
  31.1 1.1 collective-permute-start.7
  32.2 1.9 collective-permute-start.8
  34.2 1.3 collective-permute-start.9
  35.5 16.2 %all_to_all.45.red_in = f32[32,1,128]{2,1,0:T(1,128)S(1)} all-to-all(f32[32,1,128]{2,1,0:T(1,128)S(1)} %get-tuple-element.93), channel_id=1, replica_groups=mesh['tm'=8,'gx'=8,'gy'=4] {'gx','gy'}, dimensions={0} | all-to-all | bytes 32768 | tf_op jit(solution)/shard_map/all_to_all | solution.py:661
  51.7 1.8 second.1
  53.5 10.7 %all_to_all.46.red_in = f32[32,1,128]{2,1,0:T(1,128)S(1)} all-to-all(f32[32,1,128]{2,1,0:T(1,128)S(1)} %get-tuple-element.107), channel_id=1, replica_groups=mesh['tm'=8,'gx'=8,'gy'=4] {'gx','gy'}, dimensions={0} | all-to-all | bytes 32768 | tf_op jit(solution)/shard_map/all_to_all | solution.py:661
  64.4 5.7 %collective-permute-start.10 = (f32[776,128]{1,0:T(8,128)S(1)}, f32[776,128]{1,0:T(8,128)S(1)}, u32[]{:S(2)}, u32[]{:S(2)}) collective-permute-start(f32[776,128]{1,0:T(8,128)S(1)} %block.1.refs_10_), channel_id=1, source_target_pairs={{0,224},{32,0},{64,32},{96,64},{128,96},{160,128},{192,160},{224,1... | collective-permute-start | bytes 1191944 | tf_op jit(solution)/shard_map/ppermute | solution.py:664
  70.0 7.9 %collective-permute-done.10.blk_ref = f32[776,128]{1,0:T(8,128)S(1)} collective-permute-done((f32[776,128]{1,0:T(8,128)S(1)}, f32[776,128]{1,0:T(8,128)S(1)}, u32[]{:S(2)}, u32[]{:S(2)}) %collective-permute-start.10) | collective-permute-done | bytes 397344 | tf_op jit(solution)/shard_map/ppermute | solution.py:664
  78.0 3.5 %collective-permute-start.13 = (f32[776,128]{1,0:T(8,128)S(1)}, f32[776,128]{1,0:T(8,128)S(1)}, u32[]{:S(2)}, u32[]{:S(2)}) collective-permute-start(f32[776,128]{1,0:T(8,128)S(1)} %collective-permute-done.10.blk_ref), channel_id=1, source_target_pairs={{0,224},{32,0},{64,32},{96,64},{128,96},{160,128},{192,160},{224,1... | collective-permute-start | bytes 1191944 | tf_op jit(solution)/shard_map/ppermute | solution.py:664
  81.5 1.8 collective-permute-start.11
  83.3 2.1 collective-permute-start.12
  85.4 4.5 %collective-permute-done.12.refs_3_ = f32[5,64,128]{2,1,0:T(8,128)S(1)} collective-permute-done((f32[5,64,128]{2,1,0:T(8,128)S(1)}, f32[5,64,128]{2,1,0:T(8,128)S(1)}, u32[]{:S(2)}, u32[]{:S(2)}) %collective-permute-start.12) | collective-permute-done | bytes 163872 | tf_op jit(solution)/shard_map/ppermute | solution.py:653
  89.9 1.3 chain2.1
  91.2 2.2 %collective-permute-start.16 = (f32[776,128]{1,0:T(8,128)S(1)}, f32[776,128]{1,0:T(8,128)S(1)}, u32[]{:S(2)}, u32[]{:S(2)}) collective-permute-start(f32[776,128]{1,0:T(8,128)S(1)} %collective-permute-done.13.refs_7_), channel_id=1, source_target_pairs={{0,224},{32,0},{64,32},{96,64},{128,96},{160,128},{192,160},{224,1... | collective-permute-start | bytes 1191944 | tf_op jit(solution)/shard_map/ppermute | solution.py:664
  93.4 2.7 %collective-permute-start.14 = (f32[8,64,128]{2,1,0:T(8,128)S(1)}, f32[8,64,128]{2,1,0:T(8,128)S(1)}, u32[]{:S(2)}, u32[]{:S(2)}) collective-permute-start(f32[8,64,128]{2,1,0:T(8,128)S(1)} %get-tuple-element.123), channel_id=1, source_target_pairs={{0,4},{1,5},{2,6},{3,7},{4,0},{5,1},{6,2},{7,3},{8,12},{9,13},{10,... | collective-permute-start | bytes 786440 | tf_op jit(solution)/shard_map/ppermute | solution.py:653
  96.2 2.1 collective-permute-start.15
  98.2 11.4 %all_to_all.47.refs_1_ = f32[32,1,128]{2,1,0:T(1,128)S(1)} all-to-all(f32[32,1,128]{2,1,0:T(1,128)S(1)} %get-tuple-element.118), channel_id=1, replica_groups=mesh['tm'=8,'gx'=8,'gy'=4] {'gx','gy'}, dimensions={0} | all-to-all | bytes 32768 | tf_op jit(solution)/shard_map/all_to_all | solution.py:661
  109.7 1.4 chain3.1
  111.9 2.1 collective-permute-start.18
  114.0 11.4 %all_to_all.48.refs_1_ = f32[32,1,128]{2,1,0:T(1,128)S(1)} all-to-all(f32[32,1,128]{2,1,0:T(1,128)S(1)} %get-tuple-element.126), channel_id=1, replica_groups=mesh['tm'=8,'gx'=8,'gy'=4] {'gx','gy'}, dimensions={0} | all-to-all | bytes 32768 | tf_op jit(solution)/shard_map/all_to_all | solution.py:661
  125.4 1.4 chain4.1
  127.7 2.1 collective-permute-start.21
  129.8 11.4 %all_to_all.49.refs_1_ = f32[32,1,128]{2,1,0:T(1,128)S(1)} all-to-all(f32[32,1,128]{2,1,0:T(1,128)S(1)} %get-tuple-element.134), channel_id=1, replica_groups=mesh['tm'=8,'gx'=8,'gy'=4] {'gx','gy'}, dimensions={0} | all-to-all | bytes 32768 | tf_op jit(solution)/shard_map/all_to_all | solution.py:661
  141.2 1.4 chain5.1
  143.7 2.1 collective-permute-start.24
  145.8 11.4 %all_to_all.50.refs_1_ = f32[32,1,128]{2,1,0:T(1,128)S(1)} all-to-all(f32[32,1,128]{2,1,0:T(1,128)S(1)} %get-tuple-element.142), channel_id=1, replica_groups=mesh['tm'=8,'gx'=8,'gy'=4] {'gx','gy'}, dimensions={0} | all-to-all | bytes 32768 | tf_op jit(solution)/shard_map/all_to_all | solution.py:661
  157.2 1.5 chain6.1
  158.7 2.9 %collective-permute-start.28 = (f32[776,128]{1,0:T(8,128)S(1)}, f32[776,128]{1,0:T(8,128)S(1)}, u32[]{:S(2)}, u32[]{:S(2)}) collective-permute-start(f32[776,128]{1,0:T(8,128)S(1)} %collective-permute-done.25.refs_10_), channel_id=1, source_target_pairs={{0,224},{32,0},{64,32},{96,64},{128,96},{160,128},{192,160},{224,1... | collective-permute-start | bytes 1191944 | tf_op jit(solution)/shard_map/ppermute | solution.py:664
  162.5 2.1 collective-permute-start.27
  164.6 11.4 %all_to_all.51.refs_1_ = f32[32,1,128]{2,1,0:T(1,128)S(1)} all-to-all(f32[32,1,128]{2,1,0:T(1,128)S(1)} %get-tuple-element.150), channel_id=1, replica_groups=mesh['tm'=8,'gx'=8,'gy'=4] {'gx','gy'}, dimensions={0} | all-to-all | bytes 32768 | tf_op jit(solution)/shard_map/all_to_all | solution.py:661
  176.0 1.4 chain7.1
  178.2 2.1 collective-permute-start.30
  180.3 11.4 %all_to_all.52.refs_1_ = f32[32,1,128]{2,1,0:T(1,128)S(1)} all-to-all(f32[32,1,128]{2,1,0:T(1,128)S(1)} %get-tuple-element.158), channel_id=1, replica_groups=mesh['tm'=8,'gx'=8,'gy'=4] {'gx','gy'}, dimensions={0} | all-to-all | bytes 32768 | tf_op jit(solution)/shard_map/all_to_all | solution.py:661
  191.7 1.5 chain8.1
  193.2 2.7 %collective-permute-start.31 = (f32[6,3,16,128]{3,2,1,0:T(8,128)S(1)}, f32[6,3,16,128]{3,2,1,0:T(8,128)S(1)}, u32[]{:S(2)}, u32[]{:S(2)}) collective-permute-start(f32[6,3,16,128]{3,2,1,0:T(8,128)S(1)} %get-tuple-element.165), channel_id=1, source_target_pairs={{0,0},{1,2},{2,4},{3,6},{4,1},{5,3},{6,5},{7,7},{8,14},{9,12},{10,... | collective-permute-start | bytes 442376 | tf_op jit(solution)/shard_map/ppermute | solution.py:645
  195.9 4.3 %collective-permute-start.32 = (f32[6,3,16,128]{3,2,1,0:T(8,128)S(1)}, f32[6,3,16,128]{3,2,1,0:T(8,128)S(1)}, u32[]{:S(2)}, u32[]{:S(2)}) collective-permute-start(f32[6,3,16,128]{3,2,1,0:T(8,128)S(1)} %get-tuple-element.166), channel_id=1, source_target_pairs={{0,1},{1,3},{2,5},{3,7},{4,2},{5,0},{6,6},{7,4},{8,15},{9,13},{10,... | collective-permute-start | bytes 442376 | tf_op jit(solution)/shard_map/ppermute | solution.py:645
  200.3 3.1 %collective-permute-start.34 = (f32[6,3,16,128]{3,2,1,0:T(8,128)S(1)}, f32[6,3,16,128]{3,2,1,0:T(8,128)S(1)}, u32[]{:S(2)}, u32[]{:S(2)}) collective-permute-start(f32[6,3,16,128]{3,2,1,0:T(8,128)S(1)} %get-tuple-element.168), channel_id=1, source_target_pairs={{0,3},{1,1},{2,7},{3,5},{4,0},{5,2},{6,4},{7,6},{8,13},{9,15},{10,... | collective-permute-start | bytes 442376 | tf_op jit(solution)/shard_map/ppermute | solution.py:645
  203.5 11.8 %all_to_all.53.red_in = f32[32,1,128]{2,1,0:T(1,128)S(1)} all-to-all(f32[32,1,128]{2,1,0:T(1,128)S(1)} %get-tuple-element.164), channel_id=1, replica_groups=mesh['tm'=8,'gx'=8,'gy'=4] {'gx','gy'}, dimensions={0} | all-to-all | bytes 32768 | tf_op jit(solution)/shard_map/all_to_all | solution.py:661
  (61 shorter events, 9.3 us)
Async XLA Ops:
  0.0 0.9 copy-start.1
  0.1 0.8 copy-start.5
  0.1 0.8 copy-start.6
  0.1 0.8 copy-start.2
  0.1 0.8 copy-start.3
  0.1 0.8 copy-start.4
  0.9 1.0 copy-start
  2.1 13.3 %collective-permute-start = (f32[5,3,16,128]{3,2,1,0:T(8,128)S(1)}, f32[5,3,16,128]{3,2,1,0:T(8,128)S(1)}, u32[]{:S(2)}, u32[]{:S(2)}) collective-permute-start(f32[5,3,16,128]{3,2,1,0:T(8,128)S(1)} %get-tuple-element.88), channel_id=1, source_target_pairs={{0,0},{1,4},{2,1},{3,5},{4,2},{5,6},{6,3},{7,7},{8,11},{9,15},{10,... | collective-permute-start | bytes 368648 | tf_op jit(solution)/shard_map/ppermute | solution.py:645
  8.1 7.8 %collective-permute-start.1 = (f32[5,3,16,128]{3,2,1,0:T(8,128)S(1)}, f32[5,3,16,128]{3,2,1,0:T(8,128)S(1)}, u32[]{:S(2)}, u32[]{:S(2)}) collective-permute-start(f32[5,3,16,128]{3,2,1,0:T(8,128)S(1)} %get-tuple-element.89), channel_id=1, source_target_pairs={{0,5},{1,0},{2,4},{3,1},{4,7},{5,2},{6,6},{7,3},{8,14},{9,11},{10,... | collective-permute-start | bytes 368648 | tf_op jit(solution)/shard_map/ppermute | solution.py:645
  10.0 8.2 %collective-permute-start.2 = (f32[5,3,16,128]{3,2,1,0:T(8,128)S(1)}, f32[5,3,16,128]{3,2,1,0:T(8,128)S(1)}, u32[]{:S(2)}, u32[]{:S(2)}) collective-permute-start(f32[5,3,16,128]{3,2,1,0:T(8,128)S(1)} %get-tuple-element.90), channel_id=1, source_target_pairs={{0,1},{1,5},{2,0},{3,4},{4,3},{5,7},{6,2},{7,6},{8,10},{9,14},{10,... | collective-permute-start | bytes 368648 | tf_op jit(solution)/shard_map/ppermute | solution.py:645
  11.3 7.0 %collective-permute-start.3 = (f32[5,3,16,128]{3,2,1,0:T(8,128)S(1)}, f32[5,3,16,128]{3,2,1,0:T(8,128)S(1)}, u32[]{:S(2)}, u32[]{:S(2)}) collective-permute-start(f32[5,3,16,128]{3,2,1,0:T(8,128)S(1)} %get-tuple-element.91), channel_id=1, source_target_pairs={{0,4},{1,1},{2,5},{3,0},{4,6},{5,3},{6,7},{7,2},{8,15},{9,10},{10,... | collective-permute-start | bytes 368648 | tf_op jit(solution)/shard_map/ppermute | solution.py:645
  18.4 9.4 %collective-permute-start.5 = (f32[4,4,3,16,128]{4,3,2,1,0:T(8,128)S(1)}, f32[4,4,3,16,128]{4,3,2,1,0:T(8,128)S(1)}, u32[]{:S(2)}, u32[]{:S(2)}) collective-permute-start(f32[4,4,3,16,128]{4,3,2,1,0:T(8,128)S(1)} %get-tuple-element.92.own_ref), channel_id=1, source_target_pairs={{1,4},{2,5},{3,6},{4,1},{5,2},{6,3},{7,11},{8,13},{9,14},{10,15},{... | collective-permute-start | bytes 1179656 | tf_op jit(solution)/shard_map/ppermute | solution.py:653
  20.3 7.5 %collective-permute-start.4 = (f32[4,4,3,16,128]{4,3,2,1,0:T(8,128)S(1)}, f32[4,4,3,16,128]{4,3,2,1,0:T(8,128)S(1)}, u32[]{:S(2)}, u32[]{:S(2)}) collective-permute-start(f32[4,4,3,16,128]{4,3,2,1,0:T(8,128)S(1)} %get-tuple-element.92.own_ref), channel_id=1, source_target_pairs={{0,4},{1,5},{2,6},{3,7},{4,0},{5,1},{6,2},{7,3},{8,12},{9,13},{10,... | collective-permute-start | bytes 1179656 | tf_op jit(solution)/shard_map/ppermute | solution.py:653
  21.2 5.1 %collective-permute-start.6 = (f32[4,1,1,16,128]{4,3,2,1,0:T(8,128)S(1)}, f32[4,1,1,16,128]{4,3,2,1,0:T(8,128)S(1)}, u32[]{:S(2)}, u32[]{:S(2)}) collective-permute-start(f32[4,1,1,16,128]{4,3,2,1,0:T(8,128)S(1)} %slice.3), channel_id=1, source_target_pairs={{1,0},{2,1},{3,2},{5,4},{6,5},{7,6},{8,9},{9,10},{10,11},{11,3},{1... | collective-permute-start | bytes 98312 | tf_op jit(solution)/shard_map/ppermute | solution.py:658
  31.1 20.6 %collective-permute-start.7 = (f32[6,64,128]{2,1,0:T(8,128)S(1)}, f32[6,64,128]{2,1,0:T(8,128)S(1)}, u32[]{:S(2)}, u32[]{:S(2)}) collective-permute-start(f32[6,64,128]{2,1,0:T(8,128)S(1)} %get-tuple-element.104), channel_id=1, source_target_pairs={{0,4},{1,5},{2,6},{3,7},{4,0},{5,1},{6,2},{7,3},{8,12},{9,13},{10,... | collective-permute-start | bytes 589832 | tf_op jit(solution)/shard_map/ppermute | solution.py:653
  32.2 19.4 %collective-permute-start.8 = (f32[6,64,128]{2,1,0:T(8,128)S(1)}, f32[6,64,128]{2,1,0:T(8,128)S(1)}, u32[]{:S(2)}, u32[]{:S(2)}) collective-permute-start(f32[6,64,128]{2,1,0:T(8,128)S(1)} %get-tuple-element.105), channel_id=1, source_target_pairs={{1,4},{2,5},{3,6},{4,1},{5,2},{6,3},{7,11},{8,13},{9,14},{10,15},{... | collective-permute-start | bytes 589832 | tf_op jit(solution)/shard_map/ppermute | solution.py:653
  34.2 17.5 %collective-permute-start.9 = (f32[3,64,128]{2,1,0:T(8,128)S(1)}, f32[3,64,128]{2,1,0:T(8,128)S(1)}, u32[]{:S(2)}, u32[]{:S(2)}) collective-permute-start(f32[3,64,128]{2,1,0:T(8,128)S(1)} %get-tuple-element.106), channel_id=1, source_target_pairs={{1,0},{2,1},{3,2},{5,4},{6,5},{7,6},{8,9},{9,10},{10,11},{11,3},{1... | collective-permute-start | bytes 294920 | tf_op jit(solution)/shard_map/ppermute | solution.py:658
  64.4 13.6 %collective-permute-start.10 = (f32[776,128]{1,0:T(8,128)S(1)}, f32[776,128]{1,0:T(8,128)S(1)}, u32[]{:S(2)}, u32[]{:S(2)}) collective-permute-start(f32[776,128]{1,0:T(8,128)S(1)} %block.1.refs_10_), channel_id=1, source_target_pairs={{0,224},{32,0},{64,32},{96,64},{128,96},{160,128},{192,160},{224,1... | collective-permute-start | bytes 1191944 | tf_op jit(solution)/shard_map/ppermute | solution.py:664
  78.0 11.9 %collective-permute-start.13 = (f32[776,128]{1,0:T(8,128)S(1)}, f32[776,128]{1,0:T(8,128)S(1)}, u32[]{:S(2)}, u32[]{:S(2)}) collective-permute-start(f32[776,128]{1,0:T(8,128)S(1)} %collective-permute-done.10.blk_ref), channel_id=1, source_target_pairs={{0,224},{32,0},{64,32},{96,64},{128,96},{160,128},{192,160},{224,1... | collective-permute-start | bytes 1191944 | tf_op jit(solution)/shard_map/ppermute | solution.py:664
  81.5 3.9 %collective-permute-start.11 = (f32[5,64,128]{2,1,0:T(8,128)S(1)}, f32[5,64,128]{2,1,0:T(8,128)S(1)}, u32[]{:S(2)}, u32[]{:S(2)}) collective-permute-start(f32[5,64,128]{2,1,0:T(8,128)S(1)} %get-tuple-element.114), channel_id=1, source_target_pairs={{0,4},{1,5},{2,6},{3,7},{4,0},{5,1},{6,2},{7,3},{8,12},{9,13},{10,... | collective-permute-start | bytes 491528 | tf_op jit(solution)/shard_map/ppermute | solution.py:653
  83.3 6.6 %collective-permute-start.12 = (f32[5,64,128]{2,1,0:T(8,128)S(1)}, f32[5,64,128]{2,1,0:T(8,128)S(1)}, u32[]{:S(2)}, u32[]{:S(2)}) collective-permute-start(f32[5,64,128]{2,1,0:T(8,128)S(1)} %get-tuple-element.115), channel_id=1, source_target_pairs={{1,4},{2,5},{3,6},{4,1},{5,2},{6,3},{7,11},{8,13},{9,14},{10,15},{... | collective-permute-start | bytes 491528 | tf_op jit(solution)/shard_map/ppermute | solution.py:653
  91.2 18.4 %collective-permute-start.16 = (f32[776,128]{1,0:T(8,128)S(1)}, f32[776,128]{1,0:T(8,128)S(1)}, u32[]{:S(2)}, u32[]{:S(2)}) collective-permute-start(f32[776,128]{1,0:T(8,128)S(1)} %collective-permute-done.13.refs_7_), channel_id=1, source_target_pairs={{0,224},{32,0},{64,32},{96,64},{128,96},{160,128},{192,160},{224,1... | collective-permute-start | bytes 1191944 | tf_op jit(solution)/shard_map/ppermute | solution.py:664
  93.4 16.2 %collective-permute-start.14 = (f32[8,64,128]{2,1,0:T(8,128)S(1)}, f32[8,64,128]{2,1,0:T(8,128)S(1)}, u32[]{:S(2)}, u32[]{:S(2)}) collective-permute-start(f32[8,64,128]{2,1,0:T(8,128)S(1)} %get-tuple-element.123), channel_id=1, source_target_pairs={{0,4},{1,5},{2,6},{3,7},{4,0},{5,1},{6,2},{7,3},{8,12},{9,13},{10,... | collective-permute-start | bytes 786440 | tf_op jit(solution)/shard_map/ppermute | solution.py:653
  96.2 13.5 %collective-permute-start.15 = (f32[8,64,128]{2,1,0:T(8,128)S(1)}, f32[8,64,128]{2,1,0:T(8,128)S(1)}, u32[]{:S(2)}, u32[]{:S(2)}) collective-permute-start(f32[8,64,128]{2,1,0:T(8,128)S(1)} %get-tuple-element.124), channel_id=1, source_target_pairs={{1,4},{2,5},{3,6},{4,1},{5,2},{6,3},{7,11},{8,13},{9,14},{10,15},{... | collective-permute-start | bytes 786440 | tf_op jit(solution)/shard_map/ppermute | solution.py:653
  111.1 14.3 %collective-permute-start.19 = (f32[776,128]{1,0:T(8,128)S(1)}, f32[776,128]{1,0:T(8,128)S(1)}, u32[]{:S(2)}, u32[]{:S(2)}) collective-permute-start(f32[776,128]{1,0:T(8,128)S(1)} %collective-permute-done.16.refs_10_), channel_id=1, source_target_pairs={{0,224},{32,0},{64,32},{96,64},{128,96},{160,128},{192,160},{224,1... | collective-permute-start | bytes 1191944 | tf_op jit(solution)/shard_map/ppermute | solution.py:664
  111.2 14.2 %collective-permute-start.17 = (f32[8,64,128]{2,1,0:T(8,128)S(1)}, f32[8,64,128]{2,1,0:T(8,128)S(1)}, u32[]{:S(2)}, u32[]{:S(2)}) collective-permute-start(f32[8,64,128]{2,1,0:T(8,128)S(1)} %get-tuple-element.131), channel_id=1, source_target_pairs={{0,4},{1,5},{2,6},{3,7},{4,0},{5,1},{6,2},{7,3},{8,12},{9,13},{10,... | collective-permute-start | bytes 786440 | tf_op jit(solution)/shard_map/ppermute | solution.py:653
  111.9 13.5 %collective-permute-start.18 = (f32[8,64,128]{2,1,0:T(8,128)S(1)}, f32[8,64,128]{2,1,0:T(8,128)S(1)}, u32[]{:S(2)}, u32[]{:S(2)}) collective-permute-start(f32[8,64,128]{2,1,0:T(8,128)S(1)} %get-tuple-element.132), channel_id=1, source_target_pairs={{1,4},{2,5},{3,6},{4,1},{5,2},{6,3},{7,11},{8,13},{9,14},{10,15},{... | collective-permute-start | bytes 786440 | tf_op jit(solution)/shard_map/ppermute | solution.py:653
  126.9 14.3 %collective-permute-start.22 = (f32[776,128]{1,0:T(8,128)S(1)}, f32[776,128]{1,0:T(8,128)S(1)}, u32[]{:S(2)}, u32[]{:S(2)}) collective-permute-start(f32[776,128]{1,0:T(8,128)S(1)} %collective-permute-done.19.refs_10_), channel_id=1, source_target_pairs={{0,224},{32,0},{64,32},{96,64},{128,96},{160,128},{192,160},{224,1... | collective-permute-start | bytes 1191944 | tf_op jit(solution)/shard_map/ppermute | solution.py:664
  126.9 14.2 %collective-permute-start.20 = (f32[8,64,128]{2,1,0:T(8,128)S(1)}, f32[8,64,128]{2,1,0:T(8,128)S(1)}, u32[]{:S(2)}, u32[]{:S(2)}) collective-permute-start(f32[8,64,128]{2,1,0:T(8,128)S(1)} %get-tuple-element.139), channel_id=1, source_target_pairs={{0,4},{1,5},{2,6},{3,7},{4,0},{5,1},{6,2},{7,3},{8,12},{9,13},{10,... | collective-permute-start | bytes 786440 | tf_op jit(solution)/shard_map/ppermute | solution.py:653
  127.7 13.5 %collective-permute-start.21 = (f32[8,64,128]{2,1,0:T(8,128)S(1)}, f32[8,64,128]{2,1,0:T(8,128)S(1)}, u32[]{:S(2)}, u32[]{:S(2)}) collective-permute-start(f32[8,64,128]{2,1,0:T(8,128)S(1)} %get-tuple-element.140), channel_id=1, source_target_pairs={{1,4},{2,5},{3,6},{4,1},{5,2},{6,3},{7,11},{8,13},{9,14},{10,15},{... | collective-permute-start | bytes 786440 | tf_op jit(solution)/shard_map/ppermute | solution.py:653
  142.6 14.6 %collective-permute-start.25 = (f32[776,128]{1,0:T(8,128)S(1)}, f32[776,128]{1,0:T(8,128)S(1)}, u32[]{:S(2)}, u32[]{:S(2)}) collective-permute-start(f32[776,128]{1,0:T(8,128)S(1)} %collective-permute-done.22.refs_10_), channel_id=1, source_target_pairs={{0,224},{32,0},{64,32},{96,64},{128,96},{160,128},{192,160},{224,1... | collective-permute-start | bytes 1191944 | tf_op jit(solution)/shard_map/ppermute | solution.py:664
  142.8 14.4 %collective-permute-start.23 = (f32[8,64,128]{2,1,0:T(8,128)S(1)}, f32[8,64,128]{2,1,0:T(8,128)S(1)}, u32[]{:S(2)}, u32[]{:S(2)}) collective-permute-start(f32[8,64,128]{2,1,0:T(8,128)S(1)} %get-tuple-element.147), channel_id=1, source_target_pairs={{0,4},{1,5},{2,6},{3,7},{4,0},{5,1},{6,2},{7,3},{8,12},{9,13},{10,... | collective-permute-start | bytes 786440 | tf_op jit(solution)/shard_map/ppermute | solution.py:653
  143.7 13.5 %collective-permute-start.24 = (f32[8,64,128]{2,1,0:T(8,128)S(1)}, f32[8,64,128]{2,1,0:T(8,128)S(1)}, u32[]{:S(2)}, u32[]{:S(2)}) collective-permute-start(f32[8,64,128]{2,1,0:T(8,128)S(1)} %get-tuple-element.148), channel_id=1, source_target_pairs={{1,4},{2,5},{3,6},{4,1},{5,2},{6,3},{7,11},{8,13},{9,14},{10,15},{... | collective-permute-start | bytes 786440 | tf_op jit(solution)/shard_map/ppermute | solution.py:653
  158.7 17.3 %collective-permute-start.28 = (f32[776,128]{1,0:T(8,128)S(1)}, f32[776,128]{1,0:T(8,128)S(1)}, u32[]{:S(2)}, u32[]{:S(2)}) collective-permute-start(f32[776,128]{1,0:T(8,128)S(1)} %collective-permute-done.25.refs_10_), channel_id=1, source_target_pairs={{0,224},{32,0},{64,32},{96,64},{128,96},{160,128},{192,160},{224,1... | collective-permute-start | bytes 1191944 | tf_op jit(solution)/shard_map/ppermute | solution.py:664
  161.6 14.4 %collective-permute-start.26 = (f32[8,64,128]{2,1,0:T(8,128)S(1)}, f32[8,64,128]{2,1,0:T(8,128)S(1)}, u32[]{:S(2)}, u32[]{:S(2)}) collective-permute-start(f32[8,64,128]{2,1,0:T(8,128)S(1)} %get-tuple-element.155), channel_id=1, source_target_pairs={{0,4},{1,5},{2,6},{3,7},{4,0},{5,1},{6,2},{7,3},{8,12},{9,13},{10,... | collective-permute-start | bytes 786440 | tf_op jit(solution)/shard_map/ppermute | solution.py:653
  162.5 13.5 %collective-permute-start.27 = (f32[8,64,128]{2,1,0:T(8,128)S(1)}, f32[8,64,128]{2,1,0:T(8,128)S(1)}, u32[]{:S(2)}, u32[]{:S(2)}) collective-permute-start(f32[8,64,128]{2,1,0:T(8,128)S(1)} %get-tuple-element.156), channel_id=1, source_target_pairs={{1,4},{2,5},{3,6},{4,1},{5,2},{6,3},{7,11},{8,13},{9,14},{10,15},{... | collective-permute-start | bytes 786440 | tf_op jit(solution)/shard_map/ppermute | solution.py:653
  177.5 14.2 %collective-permute-start.29 = (f32[8,64,128]{2,1,0:T(8,128)S(1)}, f32[8,64,128]{2,1,0:T(8,128)S(1)}, u32[]{:S(2)}, u32[]{:S(2)}) collective-permute-start(f32[8,64,128]{2,1,0:T(8,128)S(1)} %get-tuple-element.162), channel_id=1, source_target_pairs={{0,4},{1,5},{2,6},{3,7},{4,0},{5,1},{6,2},{7,3},{8,12},{9,13},{10,... | collective-permute-start | bytes 786440 | tf_op jit(solution)/shard_map/ppermute | solution.py:653
  178.2 13.5 %collective-permute-start.30 = (f32[8,64,128]{2,1,0:T(8,128)S(1)}, f32[8,64,128]{2,1,0:T(8,128)S(1)}, u32[]{:S(2)}, u32[]{:S(2)}) collective-permute-start(f32[8,64,128]{2,1,0:T(8,128)S(1)} %get-tuple-element.163), channel_id=1, source_target_pairs={{1,4},{2,5},{3,6},{4,1},{5,2},{6,3},{7,11},{8,13},{9,14},{10,15},{... | collective-permute-start | bytes 786440 | tf_op jit(solution)/shard_map/ppermute | solution.py:653
  193.2 22.1 %collective-permute-start.31 = (f32[6,3,16,128]{3,2,1,0:T(8,128)S(1)}, f32[6,3,16,128]{3,2,1,0:T(8,128)S(1)}, u32[]{:S(2)}, u32[]{:S(2)}) collective-permute-start(f32[6,3,16,128]{3,2,1,0:T(8,128)S(1)} %get-tuple-element.165), channel_id=1, source_target_pairs={{0,0},{1,2},{2,4},{3,6},{4,1},{5,3},{6,5},{7,7},{8,14},{9,12},{10,... | collective-permute-start | bytes 442376 | tf_op jit(solution)/shard_map/ppermute | solution.py:645
  195.9 19.4 %collective-permute-start.32 = (f32[6,3,16,128]{3,2,1,0:T(8,128)S(1)}, f32[6,3,16,128]{3,2,1,0:T(8,128)S(1)}, u32[]{:S(2)}, u32[]{:S(2)}) collective-permute-start(f32[6,3,16,128]{3,2,1,0:T(8,128)S(1)} %get-tuple-element.166), channel_id=1, source_target_pairs={{0,1},{1,3},{2,5},{3,7},{4,2},{5,0},{6,6},{7,4},{8,15},{9,13},{10,... | collective-permute-start | bytes 442376 | tf_op jit(solution)/shard_map/ppermute | solution.py:645
  200.2 15.0 %collective-permute-start.33 = (f32[6,3,16,128]{3,2,1,0:T(8,128)S(1)}, f32[6,3,16,128]{3,2,1,0:T(8,128)S(1)}, u32[]{:S(2)}, u32[]{:S(2)}) collective-permute-start(f32[6,3,16,128]{3,2,1,0:T(8,128)S(1)} %get-tuple-element.167), channel_id=1, source_target_pairs={{0,2},{1,0},{2,6},{3,4},{4,3},{5,1},{6,7},{7,5},{8,12},{9,14},{10,... | collective-permute-start | bytes 442376 | tf_op jit(solution)/shard_map/ppermute | solution.py:645
  200.3 14.9 %collective-permute-start.34 = (f32[6,3,16,128]{3,2,1,0:T(8,128)S(1)}, f32[6,3,16,128]{3,2,1,0:T(8,128)S(1)}, u32[]{:S(2)}, u32[]{:S(2)}) collective-permute-start(f32[6,3,16,128]{3,2,1,0:T(8,128)S(1)} %get-tuple-element.168), channel_id=1, source_target_pairs={{0,3},{1,1},{2,7},{3,5},{4,0},{5,2},{6,4},{7,6},{8,13},{9,15},{10,... | collective-permute-start | bytes 442376 | tf_op jit(solution)/shard_map/ppermute | solution.py:645

commit v7 on v6

--- a/solution.py
+++ b/solution.py
@@ -420,7 +420,7 @@
         for i in range(L)
     ]
     u = [base_ref[i] for i in range(L)]
-    return u + [sums[0], sums[1]], u + [sums[1], sums[2]]
+    return u + [sums[0], sums[1]], [u[1], u[2], sums[2]]
 
 
 def opening_kernel(const_ref, blk_ref, base_ref, even_out, odd_out):
@@ -429,6 +429,7 @@
     for at in range(4 * L):
         base_ref[at] = blk_ref[at * ny : (at + 1) * ny]
     lo, hi = halo_base(f, base_ref)
+    hi = hi + hi[:2]
     send(holds(const_ref, SIDE, 0, even_out.shape[1:]), lo, hi, even_out, odd_out)
 
 
@@ -464,35 +465,31 @@
         return above(side, even_ref, odd_ref, high_at)
 
     def delta(i):
-        z = z_in[i + 2] if -2 <= i <= 4 else near(i, 5, 5)
-        if -1 <= i <= 3:
-            oz = oz_in[i + 1]
-        else:
-            at = 6 if i in (-3, 5) else 7
-            oz = near(i, at, at)
+        z = z_in[i + 1] if -1 <= i <= 4 else near(i, 3, 5)
+        oz = oz_in[i] if 0 <= i <= 3 else near(i, i + 6, i + 2)
         return jnp.where(fresh, 0.0, c[0] * z + c[1] * oz)
 
-    for i in range(-3, 6):
-        base = base_in[i] if 0 <= i < L else near(i, i + 3, i - L)
+    for i in range(-2, 6):
+        base = base_in[i] if 0 <= i < L else near(i, i + 2, i - L)
         d = None if opened else delta(i)
-        u_ref[i + 3] = base if opened else base + d
+        u_ref[i + 2] = base if opened else base + d
         if 0 <= i < L:
             h = [base_in[L * (1 + p) + i] for p in range(PRONY)]
             if not opened:
                 h = [h[p] + rest[p] * d for p in range(PRONY)]
             total = f[0] * h[0] + f[1] * h[1] + f[2] * h[2]
-            ui = u_ref[i + 3]
+            ui = u_ref[i + 2]
             base_ref[i] = jnp.where(opening, 0.0, ui) + blk_ref[i * ny : (i + 1) * ny]
             for p in range(PRONY):
                 at = L * (1 + p) + i
                 ahead = jnp.where(opening, 0.0, decay[p] * h[p] + rest[p] * ui)
                 base_ref[at] = ahead + blk_ref[at * ny : (at + 1) * ny]
-        elif -2 <= i < 5:
-            total = near(i, 3 + i + 2, 3 + i - L)
+        elif -1 <= i < 5:
+            total = near(i, 2, 3 + i - L)
             if not opened:
                 total = total + grow * d
-        if -2 <= i < 5:
-            au_ref[i + 2] = heat * theta_ref[i + 2] + total
+        if -1 <= i < 5:
+            au_ref[i + 1] = heat * theta_ref[i + 2] + total
 
     zeros = jnp.zeros((ny, nz), jnp.float32)
     acc = [zeros] * 4
@@ -501,36 +498,36 @@
         return kel_ref[e + 3]
 
     def put_z(i, plane):
-        ui = u_ref[i + 3]
-        s = au_ref[i + 2] + ui * (1.0 / PACES) - plane
+        ui = u_ref[i + 2]
+        s = au_ref[i + 1] + ui * (1.0 / PACES) - plane
         inv = inv_ref[i + 2]
         z = inv * s - ui
-        z_ref[i + 2] = z
+        z_ref[i + 1] = z
         if 0 <= i < L:
             acc[0] = acc[0] + z * (s - ui * (1.0 / inv))
 
-    off_diagonal(sh, lambda i: u_ref[i + 3], k, -2, 4, put_z)
+    off_diagonal(sh, lambda i: u_ref[i + 2], k, -1, 4, put_z)
 
     def put_oz(i, plane):
         oz = inv_ref[i + 2] * plane
-        oz_ref[i + 1] = oz
+        oz_ref[i] = oz
         if 0 <= i < L:
-            acc[1] = acc[1] + z_ref[i + 2] * plane
+            acc[1] = acc[1] + z_ref[i + 1] * plane
             acc[2] = acc[2] + oz * plane
 
-    off_diagonal(sh, lambda i: z_ref[i + 2], k, -1, 3, put_oz)
+    off_diagonal(sh, lambda i: z_ref[i + 1], k, 0, 3, put_oz)
 
     def put_last(i, plane):
-        acc[3] = acc[3] + oz_ref[i + 1] * plane
-
-    off_diagonal(sh, lambda i: oz_ref[i + 1], k, 0, 2, put_last)
+        acc[3] = acc[3] + oz_ref[i] * plane
+
+    by_elements(sh, lambda i: oz_ref[i], k, put_last)
     moments_out(acc, red_ref)
 
     if rounds:
         width = ny // rounds
         for i in range(L):
             fields = [base_ref[L * field + i] for field in range(1 + PRONY)]
-            for at, field in enumerate(fields + [z_ref[i + 2], oz_ref[i + 1]]):
+            for at, field in enumerate(fields + [z_ref[i + 1], oz_ref[i]]):
                 cuts = [field[q * width : (q + 1) * width] for q in range(rounds)]
                 for r, out_ref in enumerate(outs):
                     ahead = [cuts[(v + r) % rounds] for v in range(rounds)]
@@ -538,8 +535,9 @@
         return
 
     lo, hi = halo_base(f, base_ref)
-    lo = lo + [z_ref[2 + 2], oz_ref[2 + 1], oz_ref[1 + 1]]
-    hi = hi + [z_ref[0 + 2], oz_ref[0 + 1], oz_ref[1 + 1]]
+    lo = lo + [z_ref[2 + 1], oz_ref[1], oz_ref[2]]
+    hi = hi + [z_ref[1 + 1], oz_ref[1], oz_ref[2]]
+    hi = hi + hi[:2]
     send(side, lo, hi, even_out, odd_out)
 
 
@@ -736,8 +734,8 @@
             block = mine
         past = (*past, *trade(even, odd))
         last = turn == n_tm
-        state = [(4 * L, *plane), (7, *plane), (5, *plane)]
-        work = [(9, *plane), (7, *plane)]
+        state = [(4 * L, *plane), (6, *plane), (4, *plane)]
+        work = [(8, *plane), (6, *plane)]
         *outs, red = call(
             functools.partial(chain_kernel, turn, n_tm, turn == 2, n_gy if last else 0),
             f"chain{turn}",

time: 217 us -> 216 us (level)
  no operation moved by 1% of the time
where the time goes in v7:
time: 216 us; the launch traced here: 215 us
  blocking collectives  107 us (50%)
  starting transfers between devices  69.5 us (32%)
  waiting for transfers between devices  20.8 us (10%)
  Pallas kernels  15.7 us (7%)
    all_to_all x9, blocking collectives, exchanged(): return lax.all_to_all(red, LINE, 0, 0, tiled=True)  107 us
    ppermute x18, starting transfers between devices, trade(): received.append(lax.ppermute(value, LINE, sorted(both)))  28.9 us
    ppermute x8, starting transfers between devices, deal(): received.append(lax.ppermute(value, LINE, sorted(perm)))  23.6 us
    pallas_call x14, Pallas kernels, call(): pl.pallas_call(kernel, name=name, out_shape=[jax.ShapeDtypeStruct(s, f32)...  15.7 us
    ppermute x7, starting transfers between devices, ring(): return lax.ppermute(block, 'tm', [(s, (s - 1) % n_tm) for s in range(n_tm)])  14.4 us
    ppermute x7, waiting for transfers between devices, ring(): return lax.ppermute(block, 'tm', [(s, (s - 1) % n_tm) for s in range(n_tm)])  7.92 us
    ppermute x18, waiting for transfers between devices, trade(): received.append(lax.ppermute(value, LINE, sorted(both)))  6.17 us
  transfers between devices with their start and end apart: 35, of which 6 were waited for; matrix products, arithmetic and copies ran while one was open for 0% of the time, Pallas kernels for 0%

profile of v7, /device:TPU:1, one launch (start us, length us, event | category | flops | bytes accessed | tf_op | source)
XLA Modules:
  0.0 215.2 jit_solution(16165625937626840503)
XLA Ops:
  2.1 6.0 %collective-permute-start = (f32[5,3,16,128]{3,2,1,0:T(8,128)S(1)}, f32[5,3,16,128]{3,2,1,0:T(8,128)S(1)}, u32[]{:S(2)}, u32[]{:S(2)}) collective-permute-start(f32[5,3,16,128]{3,2,1,0:T(8,128)S(1)} %get-tuple-element.88), channel_id=1, source_target_pairs={{0,0},{1,4},{2,1},{3,5},{4,2},{5,6},{6,3},{7,7},{8,11},{9,15},{10,... | collective-permute-start | bytes 368648 | tf_op jit(solution)/shard_map/ppermute | solution.py:643
  8.1 1.9 collective-permute-start.1
  10.0 1.2 collective-permute-start.2
  11.3 4.1 %collective-permute-start.3 = (f32[5,3,16,128]{3,2,1,0:T(8,128)S(1)}, f32[5,3,16,128]{3,2,1,0:T(8,128)S(1)}, u32[]{:S(2)}, u32[]{:S(2)}) collective-permute-start(f32[5,3,16,128]{3,2,1,0:T(8,128)S(1)} %get-tuple-element.91), channel_id=1, source_target_pairs={{0,4},{1,1},{2,5},{3,0},{4,6},{5,3},{6,7},{7,2},{8,15},{9,10},{10,... | collective-permute-start | bytes 368648 | tf_op jit(solution)/shard_map/ppermute | solution.py:643
  15.9 2.4 %collective-permute-done.2.refs_2_ = f32[5,3,16,128]{3,2,1,0:T(8,128)S(1)} collective-permute-done((f32[5,3,16,128]{3,2,1,0:T(8,128)S(1)}, f32[5,3,16,128]{3,2,1,0:T(8,128)S(1)}, u32[]{:S(2)}, u32[]{:S(2)}) %collective-permute-start.2) | collective-permute-done | bytes 122912 | tf_op jit(solution)/shard_map/ppermute | solution.py:643
  18.4 1.9 collective-permute-start.5
  21.2 1.3 collective-permute-start.6
  22.5 3.8 %collective-permute-done.6.far_ref = f32[4,1,1,16,128]{4,3,2,1,0:T(8,128)S(1)} collective-permute-done((f32[4,1,1,16,128]{4,3,2,1,0:T(8,128)S(1)}, f32[4,1,1,16,128]{4,3,2,1,0:T(8,128)S(1)}, u32[]{:S(2)}, u32[]{:S(2)}) %collective-permute-start.6) | collective-permute-done | bytes 32800 | tf_op jit(solution)/shard_map/ppermute | solution.py:656
  26.3 1.6 collective-permute-done.5.odd_ref
  27.9 3.2 %start.1 = (f32[9,64,128]{2,1,0:T(8,128)S(1)}, f32[8,64,128]{2,1,0:T(8,128)S(1)}, f32[8,64,128]{2,1,0:T(8,128)S(1)}, f32[8,64,128]{2,1,0:T(8,128)S(1)}, f32[18,6...) custom-call(f32[4,4,3,16,128]{4,3,2,1,0:T(8,128)S(1)} %get-tuple-ele, ...), custom_call_target="tpu_custom_call" | custom-call | tf_op jit(solution)/shard_map/start/pallas_call | solution.py:602
  31.1 1.1 collective-permute-start.7
  32.2 1.9 collective-permute-start.8
  34.2 1.3 collective-permute-start.9
  35.5 16.2 %all_to_all.45.red_in = f32[32,1,128]{2,1,0:T(1,128)S(1)} all-to-all(f32[32,1,128]{2,1,0:T(1,128)S(1)} %get-tuple-element.93), channel_id=1, replica_groups=mesh['tm'=8,'gx'=8,'gy'=4] {'gx','gy'}, dimensions={0} | all-to-all | bytes 32768 | tf_op jit(solution)/shard_map/all_to_all | solution.py:659
  51.7 1.8 second.1
  53.5 10.7 %all_to_all.46.red_in = f32[32,1,128]{2,1,0:T(1,128)S(1)} all-to-all(f32[32,1,128]{2,1,0:T(1,128)S(1)} %get-tuple-element.107), channel_id=1, replica_groups=mesh['tm'=8,'gx'=8,'gy'=4] {'gx','gy'}, dimensions={0} | all-to-all | bytes 32768 | tf_op jit(solution)/shard_map/all_to_all | solution.py:659
  64.4 5.7 %collective-permute-start.10 = (f32[776,128]{1,0:T(8,128)S(1)}, f32[776,128]{1,0:T(8,128)S(1)}, u32[]{:S(2)}, u32[]{:S(2)}) collective-permute-start(f32[776,128]{1,0:T(8,128)S(1)} %block.1.refs_10_), channel_id=1, source_target_pairs={{0,224},{32,0},{64,32},{96,64},{128,96},{160,128},{192,160},{224,1... | collective-permute-start | bytes 1191944 | tf_op jit(solution)/shard_map/ppermute | solution.py:662
  70.0 7.9 %collective-permute-done.10.blk_ref = f32[776,128]{1,0:T(8,128)S(1)} collective-permute-done((f32[776,128]{1,0:T(8,128)S(1)}, f32[776,128]{1,0:T(8,128)S(1)}, u32[]{:S(2)}, u32[]{:S(2)}) %collective-permute-start.10) | collective-permute-done | bytes 397344 | tf_op jit(solution)/shard_map/ppermute | solution.py:662
  78.0 3.5 %collective-permute-start.13 = (f32[776,128]{1,0:T(8,128)S(1)}, f32[776,128]{1,0:T(8,128)S(1)}, u32[]{:S(2)}, u32[]{:S(2)}) collective-permute-start(f32[776,128]{1,0:T(8,128)S(1)} %collective-permute-done.10.blk_ref), channel_id=1, source_target_pairs={{0,224},{32,0},{64,32},{96,64},{128,96},{160,128},{192,160},{224,1... | collective-permute-start | bytes 1191944 | tf_op jit(solution)/shard_map/ppermute | solution.py:662
  81.5 1.8 collective-permute-start.11
  83.3 2.1 collective-permute-start.12
  85.4 4.5 %collective-permute-done.12.refs_3_ = f32[5,64,128]{2,1,0:T(8,128)S(1)} collective-permute-done((f32[5,64,128]{2,1,0:T(8,128)S(1)}, f32[5,64,128]{2,1,0:T(8,128)S(1)}, u32[]{:S(2)}, u32[]{:S(2)}) %collective-permute-start.12) | collective-permute-done | bytes 163872 | tf_op jit(solution)/shard_map/ppermute | solution.py:651
  89.9 1.2 chain2.1
  91.1 2.2 %collective-permute-start.16 = (f32[776,128]{1,0:T(8,128)S(1)}, f32[776,128]{1,0:T(8,128)S(1)}, u32[]{:S(2)}, u32[]{:S(2)}) collective-permute-start(f32[776,128]{1,0:T(8,128)S(1)} %collective-permute-done.13.refs_7_), channel_id=1, source_target_pairs={{0,224},{32,0},{64,32},{96,64},{128,96},{160,128},{192,160},{224,1... | collective-permute-start | bytes 1191944 | tf_op jit(solution)/shard_map/ppermute | solution.py:662
  93.3 2.7 %collective-permute-start.14 = (f32[8,64,128]{2,1,0:T(8,128)S(1)}, f32[8,64,128]{2,1,0:T(8,128)S(1)}, u32[]{:S(2)}, u32[]{:S(2)}) collective-permute-start(f32[8,64,128]{2,1,0:T(8,128)S(1)} %get-tuple-element.123), channel_id=1, source_target_pairs={{0,4},{1,5},{2,6},{3,7},{4,0},{5,1},{6,2},{7,3},{8,12},{9,13},{10,... | collective-permute-start | bytes 786440 | tf_op jit(solution)/shard_map/ppermute | solution.py:651
  96.0 2.1 collective-permute-start.15
  98.1 11.4 %all_to_all.47.refs_1_ = f32[32,1,128]{2,1,0:T(1,128)S(1)} all-to-all(f32[32,1,128]{2,1,0:T(1,128)S(1)} %get-tuple-element.118), channel_id=1, replica_groups=mesh['tm'=8,'gx'=8,'gy'=4] {'gx','gy'}, dimensions={0} | all-to-all | bytes 32768 | tf_op jit(solution)/shard_map/all_to_all | solution.py:659
  109.5 1.3 chain3.1
  111.7 2.1 collective-permute-start.18
  113.8 11.4 %all_to_all.48.refs_1_ = f32[32,1,128]{2,1,0:T(1,128)S(1)} all-to-all(f32[32,1,128]{2,1,0:T(1,128)S(1)} %get-tuple-element.126), channel_id=1, replica_groups=mesh['tm'=8,'gx'=8,'gy'=4] {'gx','gy'}, dimensions={0} | all-to-all | bytes 32768 | tf_op jit(solution)/shard_map/all_to_all | solution.py:659
  125.2 1.3 chain4.1
  127.3 2.1 collective-permute-start.21
  129.4 11.4 %all_to_all.49.refs_1_ = f32[32,1,128]{2,1,0:T(1,128)S(1)} all-to-all(f32[32,1,128]{2,1,0:T(1,128)S(1)} %get-tuple-element.134), channel_id=1, replica_groups=mesh['tm'=8,'gx'=8,'gy'=4] {'gx','gy'}, dimensions={0} | all-to-all | bytes 32768 | tf_op jit(solution)/shard_map/all_to_all | solution.py:659
  140.8 1.3 chain5.1
  143.3 2.1 collective-permute-start.24
  145.3 11.4 %all_to_all.50.refs_1_ = f32[32,1,128]{2,1,0:T(1,128)S(1)} all-to-all(f32[32,1,128]{2,1,0:T(1,128)S(1)} %get-tuple-element.142), channel_id=1, replica_groups=mesh['tm'=8,'gx'=8,'gy'=4] {'gx','gy'}, dimensions={0} | all-to-all | bytes 32768 | tf_op jit(solution)/shard_map/all_to_all | solution.py:659
  156.8 1.3 chain6.1
  158.1 2.7 %collective-permute-start.28 = (f32[776,128]{1,0:T(8,128)S(1)}, f32[776,128]{1,0:T(8,128)S(1)}, u32[]{:S(2)}, u32[]{:S(2)}) collective-permute-start(f32[776,128]{1,0:T(8,128)S(1)} %collective-permute-done.25.refs_10_), channel_id=1, source_target_pairs={{0,224},{32,0},{64,32},{96,64},{128,96},{160,128},{192,160},{224,1... | collective-permute-start | bytes 1191944 | tf_op jit(solution)/shard_map/ppermute | solution.py:662
  161.7 2.1 collective-permute-start.27
  163.8 11.4 %all_to_all.51.refs_1_ = f32[32,1,128]{2,1,0:T(1,128)S(1)} all-to-all(f32[32,1,128]{2,1,0:T(1,128)S(1)} %get-tuple-element.150), channel_id=1, replica_groups=mesh['tm'=8,'gx'=8,'gy'=4] {'gx','gy'}, dimensions={0} | all-to-all | bytes 32768 | tf_op jit(solution)/shard_map/all_to_all | solution.py:659
  175.2 1.3 chain7.1
  177.3 2.1 collective-permute-start.30
  179.4 11.4 %all_to_all.52.refs_1_ = f32[32,1,128]{2,1,0:T(1,128)S(1)} all-to-all(f32[32,1,128]{2,1,0:T(1,128)S(1)} %get-tuple-element.158), channel_id=1, replica_groups=mesh['tm'=8,'gx'=8,'gy'=4] {'gx','gy'}, dimensions={0} | all-to-all | bytes 32768 | tf_op jit(solution)/shard_map/all_to_all | solution.py:659
  190.8 1.4 chain8.1
  192.1 2.7 %collective-permute-start.31 = (f32[6,3,16,128]{3,2,1,0:T(8,128)S(1)}, f32[6,3,16,128]{3,2,1,0:T(8,128)S(1)}, u32[]{:S(2)}, u32[]{:S(2)}) collective-permute-start(f32[6,3,16,128]{3,2,1,0:T(8,128)S(1)} %get-tuple-element.165), channel_id=1, source_target_pairs={{0,0},{1,2},{2,4},{3,6},{4,1},{5,3},{6,5},{7,7},{8,14},{9,12},{10,... | collective-permute-start | bytes 442376 | tf_op jit(solution)/shard_map/ppermute | solution.py:643
  194.9 4.3 %collective-permute-start.32 = (f32[6,3,16,128]{3,2,1,0:T(8,128)S(1)}, f32[6,3,16,128]{3,2,1,0:T(8,128)S(1)}, u32[]{:S(2)}, u32[]{:S(2)}) collective-permute-start(f32[6,3,16,128]{3,2,1,0:T(8,128)S(1)} %get-tuple-element.166), channel_id=1, source_target_pairs={{0,1},{1,3},{2,5},{3,7},{4,2},{5,0},{6,6},{7,4},{8,15},{9,13},{10,... | collective-permute-start | bytes 442376 | tf_op jit(solution)/shard_map/ppermute | solution.py:643
  199.3 3.1 %collective-permute-start.34 = (f32[6,3,16,128]{3,2,1,0:T(8,128)S(1)}, f32[6,3,16,128]{3,2,1,0:T(8,128)S(1)}, u32[]{:S(2)}, u32[]{:S(2)}) collective-permute-start(f32[6,3,16,128]{3,2,1,0:T(8,128)S(1)} %get-tuple-element.168), channel_id=1, source_target_pairs={{0,3},{1,1},{2,7},{3,5},{4,0},{5,2},{6,4},{7,6},{8,13},{9,15},{10,... | collective-permute-start | bytes 442376 | tf_op jit(solution)/shard_map/ppermute | solution.py:643
  202.5 11.8 %all_to_all.53.red_in = f32[32,1,128]{2,1,0:T(1,128)S(1)} all-to-all(f32[32,1,128]{2,1,0:T(1,128)S(1)} %get-tuple-element.164), channel_id=1, replica_groups=mesh['tm'=8,'gx'=8,'gy'=4] {'gx','gy'}, dimensions={0} | all-to-all | bytes 32768 | tf_op jit(solution)/shard_map/all_to_all | solution.py:659
  (61 shorter events, 9.3 us)
Async XLA Ops:
  0.0 0.9 copy-start.1
  0.1 0.8 copy-start.5
  0.1 0.8 copy-start.6
  0.1 0.8 copy-start.2
  0.1 0.8 copy-start.3
  0.1 0.8 copy-start.4
  0.9 1.0 copy-start
  2.1 13.3 %collective-permute-start = (f32[5,3,16,128]{3,2,1,0:T(8,128)S(1)}, f32[5,3,16,128]{3,2,1,0:T(8,128)S(1)}, u32[]{:S(2)}, u32[]{:S(2)}) collective-permute-start(f32[5,3,16,128]{3,2,1,0:T(8,128)S(1)} %get-tuple-element.88), channel_id=1, source_target_pairs={{0,0},{1,4},{2,1},{3,5},{4,2},{5,6},{6,3},{7,7},{8,11},{9,15},{10,... | collective-permute-start | bytes 368648 | tf_op jit(solution)/shard_map/ppermute | solution.py:643
  8.1 7.8 %collective-permute-start.1 = (f32[5,3,16,128]{3,2,1,0:T(8,128)S(1)}, f32[5,3,16,128]{3,2,1,0:T(8,128)S(1)}, u32[]{:S(2)}, u32[]{:S(2)}) collective-permute-start(f32[5,3,16,128]{3,2,1,0:T(8,128)S(1)} %get-tuple-element.89), channel_id=1, source_target_pairs={{0,5},{1,0},{2,4},{3,1},{4,7},{5,2},{6,6},{7,3},{8,14},{9,11},{10,... | collective-permute-start | bytes 368648 | tf_op jit(solution)/shard_map/ppermute | solution.py:643
  10.0 8.2 %collective-permute-start.2 = (f32[5,3,16,128]{3,2,1,0:T(8,128)S(1)}, f32[5,3,16,128]{3,2,1,0:T(8,128)S(1)}, u32[]{:S(2)}, u32[]{:S(2)}) collective-permute-start(f32[5,3,16,128]{3,2,1,0:T(8,128)S(1)} %get-tuple-element.90), channel_id=1, source_target_pairs={{0,1},{1,5},{2,0},{3,4},{4,3},{5,7},{6,2},{7,6},{8,10},{9,14},{10,... | collective-permute-start | bytes 368648 | tf_op jit(solution)/shard_map/ppermute | solution.py:643
  11.3 7.0 %collective-permute-start.3 = (f32[5,3,16,128]{3,2,1,0:T(8,128)S(1)}, f32[5,3,16,128]{3,2,1,0:T(8,128)S(1)}, u32[]{:S(2)}, u32[]{:S(2)}) collective-permute-start(f32[5,3,16,128]{3,2,1,0:T(8,128)S(1)} %get-tuple-element.91), channel_id=1, source_target_pairs={{0,4},{1,1},{2,5},{3,0},{4,6},{5,3},{6,7},{7,2},{8,15},{9,10},{10,... | collective-permute-start | bytes 368648 | tf_op jit(solution)/shard_map/ppermute | solution.py:643
  18.4 9.4 %collective-permute-start.5 = (f32[4,4,3,16,128]{4,3,2,1,0:T(8,128)S(1)}, f32[4,4,3,16,128]{4,3,2,1,0:T(8,128)S(1)}, u32[]{:S(2)}, u32[]{:S(2)}) collective-permute-start(f32[4,4,3,16,128]{4,3,2,1,0:T(8,128)S(1)} %get-tuple-element.92.own_ref), channel_id=1, source_target_pairs={{1,4},{2,5},{3,6},{4,1},{5,2},{6,3},{7,11},{8,13},{9,14},{10,15},{... | collective-permute-start | bytes 1179656 | tf_op jit(solution)/shard_map/ppermute | solution.py:651
  20.3 7.5 %collective-permute-start.4 = (f32[4,4,3,16,128]{4,3,2,1,0:T(8,128)S(1)}, f32[4,4,3,16,128]{4,3,2,1,0:T(8,128)S(1)}, u32[]{:S(2)}, u32[]{:S(2)}) collective-permute-start(f32[4,4,3,16,128]{4,3,2,1,0:T(8,128)S(1)} %get-tuple-element.92.own_ref), channel_id=1, source_target_pairs={{0,4},{1,5},{2,6},{3,7},{4,0},{5,1},{6,2},{7,3},{8,12},{9,13},{10,... | collective-permute-start | bytes 1179656 | tf_op jit(solution)/shard_map/ppermute | solution.py:651
  21.2 5.1 %collective-permute-start.6 = (f32[4,1,1,16,128]{4,3,2,1,0:T(8,128)S(1)}, f32[4,1,1,16,128]{4,3,2,1,0:T(8,128)S(1)}, u32[]{:S(2)}, u32[]{:S(2)}) collective-permute-start(f32[4,1,1,16,128]{4,3,2,1,0:T(8,128)S(1)} %slice.3), channel_id=1, source_target_pairs={{1,0},{2,1},{3,2},{5,4},{6,5},{7,6},{8,9},{9,10},{10,11},{11,3},{1... | collective-permute-start | bytes 98312 | tf_op jit(solution)/shard_map/ppermute | solution.py:656
  31.1 20.6 %collective-permute-start.7 = (f32[6,64,128]{2,1,0:T(8,128)S(1)}, f32[6,64,128]{2,1,0:T(8,128)S(1)}, u32[]{:S(2)}, u32[]{:S(2)}) collective-permute-start(f32[6,64,128]{2,1,0:T(8,128)S(1)} %get-tuple-element.104), channel_id=1, source_target_pairs={{0,4},{1,5},{2,6},{3,7},{4,0},{5,1},{6,2},{7,3},{8,12},{9,13},{10,... | collective-permute-start | bytes 589832 | tf_op jit(solution)/shard_map/ppermute | solution.py:651
  32.2 19.4 %collective-permute-start.8 = (f32[6,64,128]{2,1,0:T(8,128)S(1)}, f32[6,64,128]{2,1,0:T(8,128)S(1)}, u32[]{:S(2)}, u32[]{:S(2)}) collective-permute-start(f32[6,64,128]{2,1,0:T(8,128)S(1)} %get-tuple-element.105), channel_id=1, source_target_pairs={{1,4},{2,5},{3,6},{4,1},{5,2},{6,3},{7,11},{8,13},{9,14},{10,15},{... | collective-permute-start | bytes 589832 | tf_op jit(solution)/shard_map/ppermute | solution.py:651
  34.2 17.5 %collective-permute-start.9 = (f32[3,64,128]{2,1,0:T(8,128)S(1)}, f32[3,64,128]{2,1,0:T(8,128)S(1)}, u32[]{:S(2)}, u32[]{:S(2)}) collective-permute-start(f32[3,64,128]{2,1,0:T(8,128)S(1)} %get-tuple-element.106), channel_id=1, source_target_pairs={{1,0},{2,1},{3,2},{5,4},{6,5},{7,6},{8,9},{9,10},{10,11},{11,3},{1... | collective-permute-start | bytes 294920 | tf_op jit(solution)/shard_map/ppermute | solution.py:656
  64.4 13.6 %collective-permute-start.10 = (f32[776,128]{1,0:T(8,128)S(1)}, f32[776,128]{1,0:T(8,128)S(1)}, u32[]{:S(2)}, u32[]{:S(2)}) collective-permute-start(f32[776,128]{1,0:T(8,128)S(1)} %block.1.refs_10_), channel_id=1, source_target_pairs={{0,224},{32,0},{64,32},{96,64},{128,96},{160,128},{192,160},{224,1... | collective-permute-start | bytes 1191944 | tf_op jit(solution)/shard_map/ppermute | solution.py:662
  78.0 11.9 %collective-permute-start.13 = (f32[776,128]{1,0:T(8,128)S(1)}, f32[776,128]{1,0:T(8,128)S(1)}, u32[]{:S(2)}, u32[]{:S(2)}) collective-permute-start(f32[776,128]{1,0:T(8,128)S(1)} %collective-permute-done.10.blk_ref), channel_id=1, source_target_pairs={{0,224},{32,0},{64,32},{96,64},{128,96},{160,128},{192,160},{224,1... | collective-permute-start | bytes 1191944 | tf_op jit(solution)/shard_map/ppermute | solution.py:662
  81.5 3.9 %collective-permute-start.11 = (f32[5,64,128]{2,1,0:T(8,128)S(1)}, f32[5,64,128]{2,1,0:T(8,128)S(1)}, u32[]{:S(2)}, u32[]{:S(2)}) collective-permute-start(f32[5,64,128]{2,1,0:T(8,128)S(1)} %get-tuple-element.114), channel_id=1, source_target_pairs={{0,4},{1,5},{2,6},{3,7},{4,0},{5,1},{6,2},{7,3},{8,12},{9,13},{10,... | collective-permute-start | bytes 491528 | tf_op jit(solution)/shard_map/ppermute | solution.py:651
  83.3 6.6 %collective-permute-start.12 = (f32[5,64,128]{2,1,0:T(8,128)S(1)}, f32[5,64,128]{2,1,0:T(8,128)S(1)}, u32[]{:S(2)}, u32[]{:S(2)}) collective-permute-start(f32[5,64,128]{2,1,0:T(8,128)S(1)} %get-tuple-element.115), channel_id=1, source_target_pairs={{1,4},{2,5},{3,6},{4,1},{5,2},{6,3},{7,11},{8,13},{9,14},{10,15},{... | collective-permute-start | bytes 491528 | tf_op jit(solution)/shard_map/ppermute | solution.py:651
  91.1 18.4 %collective-permute-start.16 = (f32[776,128]{1,0:T(8,128)S(1)}, f32[776,128]{1,0:T(8,128)S(1)}, u32[]{:S(2)}, u32[]{:S(2)}) collective-permute-start(f32[776,128]{1,0:T(8,128)S(1)} %collective-permute-done.13.refs_7_), channel_id=1, source_target_pairs={{0,224},{32,0},{64,32},{96,64},{128,96},{160,128},{192,160},{224,1... | collective-permute-start | bytes 1191944 | tf_op jit(solution)/shard_map/ppermute | solution.py:662
  93.3 16.2 %collective-permute-start.14 = (f32[8,64,128]{2,1,0:T(8,128)S(1)}, f32[8,64,128]{2,1,0:T(8,128)S(1)}, u32[]{:S(2)}, u32[]{:S(2)}) collective-permute-start(f32[8,64,128]{2,1,0:T(8,128)S(1)} %get-tuple-element.123), channel_id=1, source_target_pairs={{0,4},{1,5},{2,6},{3,7},{4,0},{5,1},{6,2},{7,3},{8,12},{9,13},{10,... | collective-permute-start | bytes 786440 | tf_op jit(solution)/shard_map/ppermute | solution.py:651
  96.0 13.5 %collective-permute-start.15 = (f32[8,64,128]{2,1,0:T(8,128)S(1)}, f32[8,64,128]{2,1,0:T(8,128)S(1)}, u32[]{:S(2)}, u32[]{:S(2)}) collective-permute-start(f32[8,64,128]{2,1,0:T(8,128)S(1)} %get-tuple-element.124), channel_id=1, source_target_pairs={{1,4},{2,5},{3,6},{4,1},{5,2},{6,3},{7,11},{8,13},{9,14},{10,15},{... | collective-permute-start | bytes 786440 | tf_op jit(solution)/shard_map/ppermute | solution.py:651
  110.9 14.3 %collective-permute-start.19 = (f32[776,128]{1,0:T(8,128)S(1)}, f32[776,128]{1,0:T(8,128)S(1)}, u32[]{:S(2)}, u32[]{:S(2)}) collective-permute-start(f32[776,128]{1,0:T(8,128)S(1)} %collective-permute-done.16.refs_10_), channel_id=1, source_target_pairs={{0,224},{32,0},{64,32},{96,64},{128,96},{160,128},{192,160},{224,1... | collective-permute-start | bytes 1191944 | tf_op jit(solution)/shard_map/ppermute | solution.py:662
  110.9 14.2 %collective-permute-start.17 = (f32[8,64,128]{2,1,0:T(8,128)S(1)}, f32[8,64,128]{2,1,0:T(8,128)S(1)}, u32[]{:S(2)}, u32[]{:S(2)}) collective-permute-start(f32[8,64,128]{2,1,0:T(8,128)S(1)} %get-tuple-element.131), channel_id=1, source_target_pairs={{0,4},{1,5},{2,6},{3,7},{4,0},{5,1},{6,2},{7,3},{8,12},{9,13},{10,... | collective-permute-start | bytes 786440 | tf_op jit(solution)/shard_map/ppermute | solution.py:651
  111.7 13.5 %collective-permute-start.18 = (f32[8,64,128]{2,1,0:T(8,128)S(1)}, f32[8,64,128]{2,1,0:T(8,128)S(1)}, u32[]{:S(2)}, u32[]{:S(2)}) collective-permute-start(f32[8,64,128]{2,1,0:T(8,128)S(1)} %get-tuple-element.132), channel_id=1, source_target_pairs={{1,4},{2,5},{3,6},{4,1},{5,2},{6,3},{7,11},{8,13},{9,14},{10,15},{... | collective-permute-start | bytes 786440 | tf_op jit(solution)/shard_map/ppermute | solution.py:651
  126.5 14.3 %collective-permute-start.22 = (f32[776,128]{1,0:T(8,128)S(1)}, f32[776,128]{1,0:T(8,128)S(1)}, u32[]{:S(2)}, u32[]{:S(2)}) collective-permute-start(f32[776,128]{1,0:T(8,128)S(1)} %collective-permute-done.19.refs_10_), channel_id=1, source_target_pairs={{0,224},{32,0},{64,32},{96,64},{128,96},{160,128},{192,160},{224,1... | collective-permute-start | bytes 1191944 | tf_op jit(solution)/shard_map/ppermute | solution.py:662
  126.6 14.2 %collective-permute-start.20 = (f32[8,64,128]{2,1,0:T(8,128)S(1)}, f32[8,64,128]{2,1,0:T(8,128)S(1)}, u32[]{:S(2)}, u32[]{:S(2)}) collective-permute-start(f32[8,64,128]{2,1,0:T(8,128)S(1)} %get-tuple-element.139), channel_id=1, source_target_pairs={{0,4},{1,5},{2,6},{3,7},{4,0},{5,1},{6,2},{7,3},{8,12},{9,13},{10,... | collective-permute-start | bytes 786440 | tf_op jit(solution)/shard_map/ppermute | solution.py:651
  127.3 13.5 %collective-permute-start.21 = (f32[8,64,128]{2,1,0:T(8,128)S(1)}, f32[8,64,128]{2,1,0:T(8,128)S(1)}, u32[]{:S(2)}, u32[]{:S(2)}) collective-permute-start(f32[8,64,128]{2,1,0:T(8,128)S(1)} %get-tuple-element.140), channel_id=1, source_target_pairs={{1,4},{2,5},{3,6},{4,1},{5,2},{6,3},{7,11},{8,13},{9,14},{10,15},{... | collective-permute-start | bytes 786440 | tf_op jit(solution)/shard_map/ppermute | solution.py:651
  142.1 14.6 %collective-permute-start.25 = (f32[776,128]{1,0:T(8,128)S(1)}, f32[776,128]{1,0:T(8,128)S(1)}, u32[]{:S(2)}, u32[]{:S(2)}) collective-permute-start(f32[776,128]{1,0:T(8,128)S(1)} %collective-permute-done.22.refs_10_), channel_id=1, source_target_pairs={{0,224},{32,0},{64,32},{96,64},{128,96},{160,128},{192,160},{224,1... | collective-permute-start | bytes 1191944 | tf_op jit(solution)/shard_map/ppermute | solution.py:662
  142.3 14.4 %collective-permute-start.23 = (f32[8,64,128]{2,1,0:T(8,128)S(1)}, f32[8,64,128]{2,1,0:T(8,128)S(1)}, u32[]{:S(2)}, u32[]{:S(2)}) collective-permute-start(f32[8,64,128]{2,1,0:T(8,128)S(1)} %get-tuple-element.147), channel_id=1, source_target_pairs={{0,4},{1,5},{2,6},{3,7},{4,0},{5,1},{6,2},{7,3},{8,12},{9,13},{10,... | collective-permute-start | bytes 786440 | tf_op jit(solution)/shard_map/ppermute | solution.py:651
  143.3 13.5 %collective-permute-start.24 = (f32[8,64,128]{2,1,0:T(8,128)S(1)}, f32[8,64,128]{2,1,0:T(8,128)S(1)}, u32[]{:S(2)}, u32[]{:S(2)}) collective-permute-start(f32[8,64,128]{2,1,0:T(8,128)S(1)} %get-tuple-element.148), channel_id=1, source_target_pairs={{1,4},{2,5},{3,6},{4,1},{5,2},{6,3},{7,11},{8,13},{9,14},{10,15},{... | collective-permute-start | bytes 786440 | tf_op jit(solution)/shard_map/ppermute | solution.py:651
  158.1 17.1 %collective-permute-start.28 = (f32[776,128]{1,0:T(8,128)S(1)}, f32[776,128]{1,0:T(8,128)S(1)}, u32[]{:S(2)}, u32[]{:S(2)}) collective-permute-start(f32[776,128]{1,0:T(8,128)S(1)} %collective-permute-done.25.refs_10_), channel_id=1, source_target_pairs={{0,224},{32,0},{64,32},{96,64},{128,96},{160,128},{192,160},{224,1... | collective-permute-start | bytes 1191944 | tf_op jit(solution)/shard_map/ppermute | solution.py:662
  160.8 14.4 %collective-permute-start.26 = (f32[8,64,128]{2,1,0:T(8,128)S(1)}, f32[8,64,128]{2,1,0:T(8,128)S(1)}, u32[]{:S(2)}, u32[]{:S(2)}) collective-permute-start(f32[8,64,128]{2,1,0:T(8,128)S(1)} %get-tuple-element.155), channel_id=1, source_target_pairs={{0,4},{1,5},{2,6},{3,7},{4,0},{5,1},{6,2},{7,3},{8,12},{9,13},{10,... | collective-permute-start | bytes 786440 | tf_op jit(solution)/shard_map/ppermute | solution.py:651
  161.7 13.5 %collective-permute-start.27 = (f32[8,64,128]{2,1,0:T(8,128)S(1)}, f32[8,64,128]{2,1,0:T(8,128)S(1)}, u32[]{:S(2)}, u32[]{:S(2)}) collective-permute-start(f32[8,64,128]{2,1,0:T(8,128)S(1)} %get-tuple-element.156), channel_id=1, source_target_pairs={{1,4},{2,5},{3,6},{4,1},{5,2},{6,3},{7,11},{8,13},{9,14},{10,15},{... | collective-permute-start | bytes 786440 | tf_op jit(solution)/shard_map/ppermute | solution.py:651
  176.6 14.2 %collective-permute-start.29 = (f32[8,64,128]{2,1,0:T(8,128)S(1)}, f32[8,64,128]{2,1,0:T(8,128)S(1)}, u32[]{:S(2)}, u32[]{:S(2)}) collective-permute-start(f32[8,64,128]{2,1,0:T(8,128)S(1)} %get-tuple-element.162), channel_id=1, source_target_pairs={{0,4},{1,5},{2,6},{3,7},{4,0},{5,1},{6,2},{7,3},{8,12},{9,13},{10,... | collective-permute-start | bytes 786440 | tf_op jit(solution)/shard_map/ppermute | solution.py:651
  177.3 13.5 %collective-permute-start.30 = (f32[8,64,128]{2,1,0:T(8,128)S(1)}, f32[8,64,128]{2,1,0:T(8,128)S(1)}, u32[]{:S(2)}, u32[]{:S(2)}) collective-permute-start(f32[8,64,128]{2,1,0:T(8,128)S(1)} %get-tuple-element.163), channel_id=1, source_target_pairs={{1,4},{2,5},{3,6},{4,1},{5,2},{6,3},{7,11},{8,13},{9,14},{10,15},{... | collective-permute-start | bytes 786440 | tf_op jit(solution)/shard_map/ppermute | solution.py:651
  192.1 22.1 %collective-permute-start.31 = (f32[6,3,16,128]{3,2,1,0:T(8,128)S(1)}, f32[6,3,16,128]{3,2,1,0:T(8,128)S(1)}, u32[]{:S(2)}, u32[]{:S(2)}) collective-permute-start(f32[6,3,16,128]{3,2,1,0:T(8,128)S(1)} %get-tuple-element.165), channel_id=1, source_target_pairs={{0,0},{1,2},{2,4},{3,6},{4,1},{5,3},{6,5},{7,7},{8,14},{9,12},{10,... | collective-permute-start | bytes 442376 | tf_op jit(solution)/shard_map/ppermute | solution.py:643
  194.9 19.4 %collective-permute-start.32 = (f32[6,3,16,128]{3,2,1,0:T(8,128)S(1)}, f32[6,3,16,128]{3,2,1,0:T(8,128)S(1)}, u32[]{:S(2)}, u32[]{:S(2)}) collective-permute-start(f32[6,3,16,128]{3,2,1,0:T(8,128)S(1)} %get-tuple-element.166), channel_id=1, source_target_pairs={{0,1},{1,3},{2,5},{3,7},{4,2},{5,0},{6,6},{7,4},{8,15},{9,13},{10,... | collective-permute-start | bytes 442376 | tf_op jit(solution)/shard_map/ppermute | solution.py:643
  199.2 15.0 %collective-permute-start.33 = (f32[6,3,16,128]{3,2,1,0:T(8,128)S(1)}, f32[6,3,16,128]{3,2,1,0:T(8,128)S(1)}, u32[]{:S(2)}, u32[]{:S(2)}) collective-permute-start(f32[6,3,16,128]{3,2,1,0:T(8,128)S(1)} %get-tuple-element.167), channel_id=1, source_target_pairs={{0,2},{1,0},{2,6},{3,4},{4,3},{5,1},{6,7},{7,5},{8,12},{9,14},{10,... | collective-permute-start | bytes 442376 | tf_op jit(solution)/shard_map/ppermute | solution.py:643
  199.3 14.9 %collective-permute-start.34 = (f32[6,3,16,128]{3,2,1,0:T(8,128)S(1)}, f32[6,3,16,128]{3,2,1,0:T(8,128)S(1)}, u32[]{:S(2)}, u32[]{:S(2)}) collective-permute-start(f32[6,3,16,128]{3,2,1,0:T(8,128)S(1)} %get-tuple-element.168), channel_id=1, source_target_pairs={{0,3},{1,1},{2,7},{3,5},{4,0},{5,2},{6,4},{7,6},{8,13},{9,15},{10,... | collective-permute-start | bytes 442376 | tf_op jit(solution)/shard_map/ppermute | solution.py:643

commit v8 on v7

--- a/solution.py
+++ b/solution.py
@@ -284,12 +284,12 @@
             acc[7] = acc[7] + w_ref[i + 2] * plane
             acc[8] = acc[8] + oz * plane
 
-    off_diagonal(sh, lambda i: w_ref[i + 2], k, -1, 3, put_ozc)
+    off_diagonal(sh, lambda i: w_ref[i + 2], k, 0, 3, put_ozc)
 
     def put_lastc(i, plane):
         acc[9] = acc[9] + au_ref[i + 2] * plane
 
-    off_diagonal(sh, lambda i: au_ref[i + 2], k, 0, 2, put_lastc)
+    by_elements(sh, lambda i: au_ref[i + 2], k, put_lastc)
     moments_out(acc, red_ref)
 
     hi = [zf_ref[2], ozf_ref[1], ozf_ref[2], oozf_ref[0], oozf_ref[1], oozf_ref[2]]

time: 216 us -> 216 us (level)
  no operation moved by 1% of the time
where the time goes in v8:
time: 216 us; the launch traced here: 215 us
  blocking collectives  107 us (50%)
  starting transfers between devices  69.5 us (32%)
  waiting for transfers between devices  20.8 us (10%)
  Pallas kernels  15.6 us (7%)
    all_to_all x9, blocking collectives, exchanged(): return lax.all_to_all(red, LINE, 0, 0, tiled=True)  107 us
    ppermute x18, starting transfers between devices, trade(): received.append(lax.ppermute(value, LINE, sorted(both)))  28.9 us
    ppermute x8, starting transfers between devices, deal(): received.append(lax.ppermute(value, LINE, sorted(perm)))  23.6 us
    pallas_call x14, Pallas kernels, call(): pl.pallas_call(kernel, name=name, out_shape=[jax.ShapeDtypeStruct(s, f32)...  15.6 us
    ppermute x7, starting transfers between devices, ring(): return lax.ppermute(block, 'tm', [(s, (s - 1) % n_tm) for s in range(n_tm)])  14.4 us
    ppermute x7, waiting for transfers between devices, ring(): return lax.ppermute(block, 'tm', [(s, (s - 1) % n_tm) for s in range(n_tm)])  7.92 us
    ppermute x18, waiting for transfers between devices, trade(): received.append(lax.ppermute(value, LINE, sorted(both)))  6.17 us
  transfers between devices with their start and end apart: 35, of which 6 were waited for; matrix products, arithmetic and copies ran while one was open for 0% of the time, Pallas kernels for 0%

profile of v8, /device:TPU:1, one launch (start us, length us, event | category | flops | bytes accessed | tf_op | source)
XLA Modules:
  0.0 215.1 jit_solution(6542366069070392616)
XLA Ops:
  2.1 6.0 %collective-permute-start = (f32[5,3,16,128]{3,2,1,0:T(8,128)S(1)}, f32[5,3,16,128]{3,2,1,0:T(8,128)S(1)}, u32[]{:S(2)}, u32[]{:S(2)}) collective-permute-start(f32[5,3,16,128]{3,2,1,0:T(8,128)S(1)} %get-tuple-element.88), channel_id=1, source_target_pairs={{0,0},{1,4},{2,1},{3,5},{4,2},{5,6},{6,3},{7,7},{8,11},{9,15},{10,... | collective-permute-start | bytes 368648 | tf_op jit(solution)/shard_map/ppermute | solution.py:643
  8.1 1.9 collective-permute-start.1
  10.0 1.2 collective-permute-start.2
  11.3 4.1 %collective-permute-start.3 = (f32[5,3,16,128]{3,2,1,0:T(8,128)S(1)}, f32[5,3,16,128]{3,2,1,0:T(8,128)S(1)}, u32[]{:S(2)}, u32[]{:S(2)}) collective-permute-start(f32[5,3,16,128]{3,2,1,0:T(8,128)S(1)} %get-tuple-element.91), channel_id=1, source_target_pairs={{0,4},{1,1},{2,5},{3,0},{4,6},{5,3},{6,7},{7,2},{8,15},{9,10},{10,... | collective-permute-start | bytes 368648 | tf_op jit(solution)/shard_map/ppermute | solution.py:643
  15.9 2.4 %collective-permute-done.2.refs_2_ = f32[5,3,16,128]{3,2,1,0:T(8,128)S(1)} collective-permute-done((f32[5,3,16,128]{3,2,1,0:T(8,128)S(1)}, f32[5,3,16,128]{3,2,1,0:T(8,128)S(1)}, u32[]{:S(2)}, u32[]{:S(2)}) %collective-permute-start.2) | collective-permute-done | bytes 122912 | tf_op jit(solution)/shard_map/ppermute | solution.py:643
  18.4 1.9 collective-permute-start.5
  21.2 1.3 collective-permute-start.6
  22.5 3.8 %collective-permute-done.6.far_ref = f32[4,1,1,16,128]{4,3,2,1,0:T(8,128)S(1)} collective-permute-done((f32[4,1,1,16,128]{4,3,2,1,0:T(8,128)S(1)}, f32[4,1,1,16,128]{4,3,2,1,0:T(8,128)S(1)}, u32[]{:S(2)}, u32[]{:S(2)}) %collective-permute-start.6) | collective-permute-done | bytes 32800 | tf_op jit(solution)/shard_map/ppermute | solution.py:656
  26.3 1.6 collective-permute-done.5.odd_ref
  27.9 3.2 %start.1 = (f32[9,64,128]{2,1,0:T(8,128)S(1)}, f32[8,64,128]{2,1,0:T(8,128)S(1)}, f32[8,64,128]{2,1,0:T(8,128)S(1)}, f32[8,64,128]{2,1,0:T(8,128)S(1)}, f32[18,6...) custom-call(f32[4,4,3,16,128]{4,3,2,1,0:T(8,128)S(1)} %get-tuple-ele, ...), custom_call_target="tpu_custom_call" | custom-call | tf_op jit(solution)/shard_map/start/pallas_call | solution.py:602
  31.1 1.1 collective-permute-start.7
  32.2 1.9 collective-permute-start.8
  34.1 1.3 collective-permute-start.9
  35.4 16.2 %all_to_all.45.red_in = f32[32,1,128]{2,1,0:T(1,128)S(1)} all-to-all(f32[32,1,128]{2,1,0:T(1,128)S(1)} %get-tuple-element.93), channel_id=1, replica_groups=mesh['tm'=8,'gx'=8,'gy'=4] {'gx','gy'}, dimensions={0} | all-to-all | bytes 32768 | tf_op jit(solution)/shard_map/all_to_all | solution.py:659
  51.6 1.8 second.1
  53.4 10.7 %all_to_all.46.red_in = f32[32,1,128]{2,1,0:T(1,128)S(1)} all-to-all(f32[32,1,128]{2,1,0:T(1,128)S(1)} %get-tuple-element.107), channel_id=1, replica_groups=mesh['tm'=8,'gx'=8,'gy'=4] {'gx','gy'}, dimensions={0} | all-to-all | bytes 32768 | tf_op jit(solution)/shard_map/all_to_all | solution.py:659
  64.3 5.7 %collective-permute-start.10 = (f32[776,128]{1,0:T(8,128)S(1)}, f32[776,128]{1,0:T(8,128)S(1)}, u32[]{:S(2)}, u32[]{:S(2)}) collective-permute-start(f32[776,128]{1,0:T(8,128)S(1)} %block.1.refs_10_), channel_id=1, source_target_pairs={{0,224},{32,0},{64,32},{96,64},{128,96},{160,128},{192,160},{224,1... | collective-permute-start | bytes 1191944 | tf_op jit(solution)/shard_map/ppermute | solution.py:662
  70.0 7.9 %collective-permute-done.10.blk_ref = f32[776,128]{1,0:T(8,128)S(1)} collective-permute-done((f32[776,128]{1,0:T(8,128)S(1)}, f32[776,128]{1,0:T(8,128)S(1)}, u32[]{:S(2)}, u32[]{:S(2)}) %collective-permute-start.10) | collective-permute-done | bytes 397344 | tf_op jit(solution)/shard_map/ppermute | solution.py:662
  78.0 3.5 %collective-permute-start.13 = (f32[776,128]{1,0:T(8,128)S(1)}, f32[776,128]{1,0:T(8,128)S(1)}, u32[]{:S(2)}, u32[]{:S(2)}) collective-permute-start(f32[776,128]{1,0:T(8,128)S(1)} %collective-permute-done.10.blk_ref), channel_id=1, source_target_pairs={{0,224},{32,0},{64,32},{96,64},{128,96},{160,128},{192,160},{224,1... | collective-permute-start | bytes 1191944 | tf_op jit(solution)/shard_map/ppermute | solution.py:662
  81.4 1.8 collective-permute-start.11
  83.2 2.1 collective-permute-start.12
  85.3 4.5 %collective-permute-done.12.refs_3_ = f32[5,64,128]{2,1,0:T(8,128)S(1)} collective-permute-done((f32[5,64,128]{2,1,0:T(8,128)S(1)}, f32[5,64,128]{2,1,0:T(8,128)S(1)}, u32[]{:S(2)}, u32[]{:S(2)}) %collective-permute-start.12) | collective-permute-done | bytes 163872 | tf_op jit(solution)/shard_map/ppermute | solution.py:651
  89.9 1.2 chain2.1
  91.0 2.2 %collective-permute-start.16 = (f32[776,128]{1,0:T(8,128)S(1)}, f32[776,128]{1,0:T(8,128)S(1)}, u32[]{:S(2)}, u32[]{:S(2)}) collective-permute-start(f32[776,128]{1,0:T(8,128)S(1)} %collective-permute-done.13.refs_7_), channel_id=1, source_target_pairs={{0,224},{32,0},{64,32},{96,64},{128,96},{160,128},{192,160},{224,1... | collective-permute-start | bytes 1191944 | tf_op jit(solution)/shard_map/ppermute | solution.py:662
  93.3 2.7 %collective-permute-start.14 = (f32[8,64,128]{2,1,0:T(8,128)S(1)}, f32[8,64,128]{2,1,0:T(8,128)S(1)}, u32[]{:S(2)}, u32[]{:S(2)}) collective-permute-start(f32[8,64,128]{2,1,0:T(8,128)S(1)} %get-tuple-element.123), channel_id=1, source_target_pairs={{0,4},{1,5},{2,6},{3,7},{4,0},{5,1},{6,2},{7,3},{8,12},{9,13},{10,... | collective-permute-start | bytes 786440 | tf_op jit(solution)/shard_map/ppermute | solution.py:651
  96.0 2.1 collective-permute-start.15
  98.0 11.4 %all_to_all.47.refs_1_ = f32[32,1,128]{2,1,0:T(1,128)S(1)} all-to-all(f32[32,1,128]{2,1,0:T(1,128)S(1)} %get-tuple-element.118), channel_id=1, replica_groups=mesh['tm'=8,'gx'=8,'gy'=4] {'gx','gy'}, dimensions={0} | all-to-all | bytes 32768 | tf_op jit(solution)/shard_map/all_to_all | solution.py:659
  109.5 1.3 chain3.1
  111.6 2.1 collective-permute-start.18
  113.7 11.4 %all_to_all.48.refs_1_ = f32[32,1,128]{2,1,0:T(1,128)S(1)} all-to-all(f32[32,1,128]{2,1,0:T(1,128)S(1)} %get-tuple-element.126), channel_id=1, replica_groups=mesh['tm'=8,'gx'=8,'gy'=4] {'gx','gy'}, dimensions={0} | all-to-all | bytes 32768 | tf_op jit(solution)/shard_map/all_to_all | solution.py:659
  125.1 1.3 chain4.1
  127.3 2.1 collective-permute-start.21
  129.4 11.4 %all_to_all.49.refs_1_ = f32[32,1,128]{2,1,0:T(1,128)S(1)} all-to-all(f32[32,1,128]{2,1,0:T(1,128)S(1)} %get-tuple-element.134), channel_id=1, replica_groups=mesh['tm'=8,'gx'=8,'gy'=4] {'gx','gy'}, dimensions={0} | all-to-all | bytes 32768 | tf_op jit(solution)/shard_map/all_to_all | solution.py:659
  140.8 1.3 chain5.1
  143.2 2.1 collective-permute-start.24
  145.3 11.4 %all_to_all.50.refs_1_ = f32[32,1,128]{2,1,0:T(1,128)S(1)} all-to-all(f32[32,1,128]{2,1,0:T(1,128)S(1)} %get-tuple-element.142), channel_id=1, replica_groups=mesh['tm'=8,'gx'=8,'gy'=4] {'gx','gy'}, dimensions={0} | all-to-all | bytes 32768 | tf_op jit(solution)/shard_map/all_to_all | solution.py:659
  156.7 1.3 chain6.1
  158.0 2.7 %collective-permute-start.28 = (f32[776,128]{1,0:T(8,128)S(1)}, f32[776,128]{1,0:T(8,128)S(1)}, u32[]{:S(2)}, u32[]{:S(2)}) collective-permute-start(f32[776,128]{1,0:T(8,128)S(1)} %collective-permute-done.25.refs_10_), channel_id=1, source_target_pairs={{0,224},{32,0},{64,32},{96,64},{128,96},{160,128},{192,160},{224,1... | collective-permute-start | bytes 1191944 | tf_op jit(solution)/shard_map/ppermute | solution.py:662
  161.7 2.1 collective-permute-start.27
  163.7 11.4 %all_to_all.51.refs_1_ = f32[32,1,128]{2,1,0:T(1,128)S(1)} all-to-all(f32[32,1,128]{2,1,0:T(1,128)S(1)} %get-tuple-element.150), channel_id=1, replica_groups=mesh['tm'=8,'gx'=8,'gy'=4] {'gx','gy'}, dimensions={0} | all-to-all | bytes 32768 | tf_op jit(solution)/shard_map/all_to_all | solution.py:659
  175.2 1.3 chain7.1
  177.2 2.1 collective-permute-start.30
  179.3 11.4 %all_to_all.52.refs_1_ = f32[32,1,128]{2,1,0:T(1,128)S(1)} all-to-all(f32[32,1,128]{2,1,0:T(1,128)S(1)} %get-tuple-element.158), channel_id=1, replica_groups=mesh['tm'=8,'gx'=8,'gy'=4] {'gx','gy'}, dimensions={0} | all-to-all | bytes 32768 | tf_op jit(solution)/shard_map/all_to_all | solution.py:659
  190.7 1.4 chain8.1
  192.1 2.7 %collective-permute-start.31 = (f32[6,3,16,128]{3,2,1,0:T(8,128)S(1)}, f32[6,3,16,128]{3,2,1,0:T(8,128)S(1)}, u32[]{:S(2)}, u32[]{:S(2)}) collective-permute-start(f32[6,3,16,128]{3,2,1,0:T(8,128)S(1)} %get-tuple-element.165), channel_id=1, source_target_pairs={{0,0},{1,2},{2,4},{3,6},{4,1},{5,3},{6,5},{7,7},{8,14},{9,12},{10,... | collective-permute-start | bytes 442376 | tf_op jit(solution)/shard_map/ppermute | solution.py:643
  194.8 4.3 %collective-permute-start.32 = (f32[6,3,16,128]{3,2,1,0:T(8,128)S(1)}, f32[6,3,16,128]{3,2,1,0:T(8,128)S(1)}, u32[]{:S(2)}, u32[]{:S(2)}) collective-permute-start(f32[6,3,16,128]{3,2,1,0:T(8,128)S(1)} %get-tuple-element.166), channel_id=1, source_target_pairs={{0,1},{1,3},{2,5},{3,7},{4,2},{5,0},{6,6},{7,4},{8,15},{9,13},{10,... | collective-permute-start | bytes 442376 | tf_op jit(solution)/shard_map/ppermute | solution.py:643
  199.2 3.1 %collective-permute-start.34 = (f32[6,3,16,128]{3,2,1,0:T(8,128)S(1)}, f32[6,3,16,128]{3,2,1,0:T(8,128)S(1)}, u32[]{:S(2)}, u32[]{:S(2)}) collective-permute-start(f32[6,3,16,128]{3,2,1,0:T(8,128)S(1)} %get-tuple-element.168), channel_id=1, source_target_pairs={{0,3},{1,1},{2,7},{3,5},{4,0},{5,2},{6,4},{7,6},{8,13},{9,15},{10,... | collective-permute-start | bytes 442376 | tf_op jit(solution)/shard_map/ppermute | solution.py:643
  202.4 11.8 %all_to_all.53.red_in = f32[32,1,128]{2,1,0:T(1,128)S(1)} all-to-all(f32[32,1,128]{2,1,0:T(1,128)S(1)} %get-tuple-element.164), channel_id=1, replica_groups=mesh['tm'=8,'gx'=8,'gy'=4] {'gx','gy'}, dimensions={0} | all-to-all | bytes 32768 | tf_op jit(solution)/shard_map/all_to_all | solution.py:659
  (61 shorter events, 9.3 us)
Async XLA Ops:
  0.0 0.9 copy-start.1
  0.1 0.8 copy-start.5
  0.1 0.8 copy-start.6
  0.1 0.8 copy-start.2
  0.1 0.8 copy-start.3
  0.1 0.8 copy-start.4
  0.9 1.0 copy-start
  2.1 13.3 %collective-permute-start = (f32[5,3,16,128]{3,2,1,0:T(8,128)S(1)}, f32[5,3,16,128]{3,2,1,0:T(8,128)S(1)}, u32[]{:S(2)}, u32[]{:S(2)}) collective-permute-start(f32[5,3,16,128]{3,2,1,0:T(8,128)S(1)} %get-tuple-element.88), channel_id=1, source_target_pairs={{0,0},{1,4},{2,1},{3,5},{4,2},{5,6},{6,3},{7,7},{8,11},{9,15},{10,... | collective-permute-start | bytes 368648 | tf_op jit(solution)/shard_map/ppermute | solution.py:643
  8.1 7.8 %collective-permute-start.1 = (f32[5,3,16,128]{3,2,1,0:T(8,128)S(1)}, f32[5,3,16,128]{3,2,1,0:T(8,128)S(1)}, u32[]{:S(2)}, u32[]{:S(2)}) collective-permute-start(f32[5,3,16,128]{3,2,1,0:T(8,128)S(1)} %get-tuple-element.89), channel_id=1, source_target_pairs={{0,5},{1,0},{2,4},{3,1},{4,7},{5,2},{6,6},{7,3},{8,14},{9,11},{10,... | collective-permute-start | bytes 368648 | tf_op jit(solution)/shard_map/ppermute | solution.py:643
  10.0 8.2 %collective-permute-start.2 = (f32[5,3,16,128]{3,2,1,0:T(8,128)S(1)}, f32[5,3,16,128]{3,2,1,0:T(8,128)S(1)}, u32[]{:S(2)}, u32[]{:S(2)}) collective-permute-start(f32[5,3,16,128]{3,2,1,0:T(8,128)S(1)} %get-tuple-element.90), channel_id=1, source_target_pairs={{0,1},{1,5},{2,0},{3,4},{4,3},{5,7},{6,2},{7,6},{8,10},{9,14},{10,... | collective-permute-start | bytes 368648 | tf_op jit(solution)/shard_map/ppermute | solution.py:643
  11.3 7.0 %collective-permute-start.3 = (f32[5,3,16,128]{3,2,1,0:T(8,128)S(1)}, f32[5,3,16,128]{3,2,1,0:T(8,128)S(1)}, u32[]{:S(2)}, u32[]{:S(2)}) collective-permute-start(f32[5,3,16,128]{3,2,1,0:T(8,128)S(1)} %get-tuple-element.91), channel_id=1, source_target_pairs={{0,4},{1,1},{2,5},{3,0},{4,6},{5,3},{6,7},{7,2},{8,15},{9,10},{10,... | collective-permute-start | bytes 368648 | tf_op jit(solution)/shard_map/ppermute | solution.py:643
  18.4 9.4 %collective-permute-start.5 = (f32[4,4,3,16,128]{4,3,2,1,0:T(8,128)S(1)}, f32[4,4,3,16,128]{4,3,2,1,0:T(8,128)S(1)}, u32[]{:S(2)}, u32[]{:S(2)}) collective-permute-start(f32[4,4,3,16,128]{4,3,2,1,0:T(8,128)S(1)} %get-tuple-element.92.own_ref), channel_id=1, source_target_pairs={{1,4},{2,5},{3,6},{4,1},{5,2},{6,3},{7,11},{8,13},{9,14},{10,15},{... | collective-permute-start | bytes 1179656 | tf_op jit(solution)/shard_map/ppermute | solution.py:651
  20.3 7.5 %collective-permute-start.4 = (f32[4,4,3,16,128]{4,3,2,1,0:T(8,128)S(1)}, f32[4,4,3,16,128]{4,3,2,1,0:T(8,128)S(1)}, u32[]{:S(2)}, u32[]{:S(2)}) collective-permute-start(f32[4,4,3,16,128]{4,3,2,1,0:T(8,128)S(1)} %get-tuple-element.92.own_ref), channel_id=1, source_target_pairs={{0,4},{1,5},{2,6},{3,7},{4,0},{5,1},{6,2},{7,3},{8,12},{9,13},{10,... | collective-permute-start | bytes 1179656 | tf_op jit(solution)/shard_map/ppermute | solution.py:651
  21.2 5.1 %collective-permute-start.6 = (f32[4,1,1,16,128]{4,3,2,1,0:T(8,128)S(1)}, f32[4,1,1,16,128]{4,3,2,1,0:T(8,128)S(1)}, u32[]{:S(2)}, u32[]{:S(2)}) collective-permute-start(f32[4,1,1,16,128]{4,3,2,1,0:T(8,128)S(1)} %slice.3), channel_id=1, source_target_pairs={{1,0},{2,1},{3,2},{5,4},{6,5},{7,6},{8,9},{9,10},{10,11},{11,3},{1... | collective-permute-start | bytes 98312 | tf_op jit(solution)/shard_map/ppermute | solution.py:656
  31.1 20.6 %collective-permute-start.7 = (f32[6,64,128]{2,1,0:T(8,128)S(1)}, f32[6,64,128]{2,1,0:T(8,128)S(1)}, u32[]{:S(2)}, u32[]{:S(2)}) collective-permute-start(f32[6,64,128]{2,1,0:T(8,128)S(1)} %get-tuple-element.104), channel_id=1, source_target_pairs={{0,4},{1,5},{2,6},{3,7},{4,0},{5,1},{6,2},{7,3},{8,12},{9,13},{10,... | collective-permute-start | bytes 589832 | tf_op jit(solution)/shard_map/ppermute | solution.py:651
  32.2 19.4 %collective-permute-start.8 = (f32[6,64,128]{2,1,0:T(8,128)S(1)}, f32[6,64,128]{2,1,0:T(8,128)S(1)}, u32[]{:S(2)}, u32[]{:S(2)}) collective-permute-start(f32[6,64,128]{2,1,0:T(8,128)S(1)} %get-tuple-element.105), channel_id=1, source_target_pairs={{1,4},{2,5},{3,6},{4,1},{5,2},{6,3},{7,11},{8,13},{9,14},{10,15},{... | collective-permute-start | bytes 589832 | tf_op jit(solution)/shard_map/ppermute | solution.py:651
  34.1 17.5 %collective-permute-start.9 = (f32[3,64,128]{2,1,0:T(8,128)S(1)}, f32[3,64,128]{2,1,0:T(8,128)S(1)}, u32[]{:S(2)}, u32[]{:S(2)}) collective-permute-start(f32[3,64,128]{2,1,0:T(8,128)S(1)} %get-tuple-element.106), channel_id=1, source_target_pairs={{1,0},{2,1},{3,2},{5,4},{6,5},{7,6},{8,9},{9,10},{10,11},{11,3},{1... | collective-permute-start | bytes 294920 | tf_op jit(solution)/shard_map/ppermute | solution.py:656
  64.3 13.6 %collective-permute-start.10 = (f32[776,128]{1,0:T(8,128)S(1)}, f32[776,128]{1,0:T(8,128)S(1)}, u32[]{:S(2)}, u32[]{:S(2)}) collective-permute-start(f32[776,128]{1,0:T(8,128)S(1)} %block.1.refs_10_), channel_id=1, source_target_pairs={{0,224},{32,0},{64,32},{96,64},{128,96},{160,128},{192,160},{224,1... | collective-permute-start | bytes 1191944 | tf_op jit(solution)/shard_map/ppermute | solution.py:662
  78.0 11.9 %collective-permute-start.13 = (f32[776,128]{1,0:T(8,128)S(1)}, f32[776,128]{1,0:T(8,128)S(1)}, u32[]{:S(2)}, u32[]{:S(2)}) collective-permute-start(f32[776,128]{1,0:T(8,128)S(1)} %collective-permute-done.10.blk_ref), channel_id=1, source_target_pairs={{0,224},{32,0},{64,32},{96,64},{128,96},{160,128},{192,160},{224,1... | collective-permute-start | bytes 1191944 | tf_op jit(solution)/shard_map/ppermute | solution.py:662
  81.4 3.9 %collective-permute-start.11 = (f32[5,64,128]{2,1,0:T(8,128)S(1)}, f32[5,64,128]{2,1,0:T(8,128)S(1)}, u32[]{:S(2)}, u32[]{:S(2)}) collective-permute-start(f32[5,64,128]{2,1,0:T(8,128)S(1)} %get-tuple-element.114), channel_id=1, source_target_pairs={{0,4},{1,5},{2,6},{3,7},{4,0},{5,1},{6,2},{7,3},{8,12},{9,13},{10,... | collective-permute-start | bytes 491528 | tf_op jit(solution)/shard_map/ppermute | solution.py:651
  83.2 6.6 %collective-permute-start.12 = (f32[5,64,128]{2,1,0:T(8,128)S(1)}, f32[5,64,128]{2,1,0:T(8,128)S(1)}, u32[]{:S(2)}, u32[]{:S(2)}) collective-permute-start(f32[5,64,128]{2,1,0:T(8,128)S(1)} %get-tuple-element.115), channel_id=1, source_target_pairs={{1,4},{2,5},{3,6},{4,1},{5,2},{6,3},{7,11},{8,13},{9,14},{10,15},{... | collective-permute-start | bytes 491528 | tf_op jit(solution)/shard_map/ppermute | solution.py:651
  91.0 18.4 %collective-permute-start.16 = (f32[776,128]{1,0:T(8,128)S(1)}, f32[776,128]{1,0:T(8,128)S(1)}, u32[]{:S(2)}, u32[]{:S(2)}) collective-permute-start(f32[776,128]{1,0:T(8,128)S(1)} %collective-permute-done.13.refs_7_), channel_id=1, source_target_pairs={{0,224},{32,0},{64,32},{96,64},{128,96},{160,128},{192,160},{224,1... | collective-permute-start | bytes 1191944 | tf_op jit(solution)/shard_map/ppermute | solution.py:662
  93.3 16.2 %collective-permute-start.14 = (f32[8,64,128]{2,1,0:T(8,128)S(1)}, f32[8,64,128]{2,1,0:T(8,128)S(1)}, u32[]{:S(2)}, u32[]{:S(2)}) collective-permute-start(f32[8,64,128]{2,1,0:T(8,128)S(1)} %get-tuple-element.123), channel_id=1, source_target_pairs={{0,4},{1,5},{2,6},{3,7},{4,0},{5,1},{6,2},{7,3},{8,12},{9,13},{10,... | collective-permute-start | bytes 786440 | tf_op jit(solution)/shard_map/ppermute | solution.py:651
  96.0 13.5 %collective-permute-start.15 = (f32[8,64,128]{2,1,0:T(8,128)S(1)}, f32[8,64,128]{2,1,0:T(8,128)S(1)}, u32[]{:S(2)}, u32[]{:S(2)}) collective-permute-start(f32[8,64,128]{2,1,0:T(8,128)S(1)} %get-tuple-element.124), channel_id=1, source_target_pairs={{1,4},{2,5},{3,6},{4,1},{5,2},{6,3},{7,11},{8,13},{9,14},{10,15},{... | collective-permute-start | bytes 786440 | tf_op jit(solution)/shard_map/ppermute | solution.py:651
  110.8 14.3 %collective-permute-start.19 = (f32[776,128]{1,0:T(8,128)S(1)}, f32[776,128]{1,0:T(8,128)S(1)}, u32[]{:S(2)}, u32[]{:S(2)}) collective-permute-start(f32[776,128]{1,0:T(8,128)S(1)} %collective-permute-done.16.refs_10_), channel_id=1, source_target_pairs={{0,224},{32,0},{64,32},{96,64},{128,96},{160,128},{192,160},{224,1... | collective-permute-start | bytes 1191944 | tf_op jit(solution)/shard_map/ppermute | solution.py:662
  110.9 14.2 %collective-permute-start.17 = (f32[8,64,128]{2,1,0:T(8,128)S(1)}, f32[8,64,128]{2,1,0:T(8,128)S(1)}, u32[]{:S(2)}, u32[]{:S(2)}) collective-permute-start(f32[8,64,128]{2,1,0:T(8,128)S(1)} %get-tuple-element.131), channel_id=1, source_target_pairs={{0,4},{1,5},{2,6},{3,7},{4,0},{5,1},{6,2},{7,3},{8,12},{9,13},{10,... | collective-permute-start | bytes 786440 | tf_op jit(solution)/shard_map/ppermute | solution.py:651
  111.6 13.5 %collective-permute-start.18 = (f32[8,64,128]{2,1,0:T(8,128)S(1)}, f32[8,64,128]{2,1,0:T(8,128)S(1)}, u32[]{:S(2)}, u32[]{:S(2)}) collective-permute-start(f32[8,64,128]{2,1,0:T(8,128)S(1)} %get-tuple-element.132), channel_id=1, source_target_pairs={{1,4},{2,5},{3,6},{4,1},{5,2},{6,3},{7,11},{8,13},{9,14},{10,15},{... | collective-permute-start | bytes 786440 | tf_op jit(solution)/shard_map/ppermute | solution.py:651
  126.4 14.3 %collective-permute-start.22 = (f32[776,128]{1,0:T(8,128)S(1)}, f32[776,128]{1,0:T(8,128)S(1)}, u32[]{:S(2)}, u32[]{:S(2)}) collective-permute-start(f32[776,128]{1,0:T(8,128)S(1)} %collective-permute-done.19.refs_10_), channel_id=1, source_target_pairs={{0,224},{32,0},{64,32},{96,64},{128,96},{160,128},{192,160},{224,1... | collective-permute-start | bytes 1191944 | tf_op jit(solution)/shard_map/ppermute | solution.py:662
  126.5 14.2 %collective-permute-start.20 = (f32[8,64,128]{2,1,0:T(8,128)S(1)}, f32[8,64,128]{2,1,0:T(8,128)S(1)}, u32[]{:S(2)}, u32[]{:S(2)}) collective-permute-start(f32[8,64,128]{2,1,0:T(8,128)S(1)} %get-tuple-element.139), channel_id=1, source_target_pairs={{0,4},{1,5},{2,6},{3,7},{4,0},{5,1},{6,2},{7,3},{8,12},{9,13},{10,... | collective-permute-start | bytes 786440 | tf_op jit(solution)/shard_map/ppermute | solution.py:651
  127.3 13.5 %collective-permute-start.21 = (f32[8,64,128]{2,1,0:T(8,128)S(1)}, f32[8,64,128]{2,1,0:T(8,128)S(1)}, u32[]{:S(2)}, u32[]{:S(2)}) collective-permute-start(f32[8,64,128]{2,1,0:T(8,128)S(1)} %get-tuple-element.140), channel_id=1, source_target_pairs={{1,4},{2,5},{3,6},{4,1},{5,2},{6,3},{7,11},{8,13},{9,14},{10,15},{... | collective-permute-start | bytes 786440 | tf_op jit(solution)/shard_map/ppermute | solution.py:651
  142.1 14.6 %collective-permute-start.25 = (f32[776,128]{1,0:T(8,128)S(1)}, f32[776,128]{1,0:T(8,128)S(1)}, u32[]{:S(2)}, u32[]{:S(2)}) collective-permute-start(f32[776,128]{1,0:T(8,128)S(1)} %collective-permute-done.22.refs_10_), channel_id=1, source_target_pairs={{0,224},{32,0},{64,32},{96,64},{128,96},{160,128},{192,160},{224,1... | collective-permute-start | bytes 1191944 | tf_op jit(solution)/shard_map/ppermute | solution.py:662
  142.3 14.4 %collective-permute-start.23 = (f32[8,64,128]{2,1,0:T(8,128)S(1)}, f32[8,64,128]{2,1,0:T(8,128)S(1)}, u32[]{:S(2)}, u32[]{:S(2)}) collective-permute-start(f32[8,64,128]{2,1,0:T(8,128)S(1)} %get-tuple-element.147), channel_id=1, source_target_pairs={{0,4},{1,5},{2,6},{3,7},{4,0},{5,1},{6,2},{7,3},{8,12},{9,13},{10,... | collective-permute-start | bytes 786440 | tf_op jit(solution)/shard_map/ppermute | solution.py:651
  143.2 13.5 %collective-permute-start.24 = (f32[8,64,128]{2,1,0:T(8,128)S(1)}, f32[8,64,128]{2,1,0:T(8,128)S(1)}, u32[]{:S(2)}, u32[]{:S(2)}) collective-permute-start(f32[8,64,128]{2,1,0:T(8,128)S(1)} %get-tuple-element.148), channel_id=1, source_target_pairs={{1,4},{2,5},{3,6},{4,1},{5,2},{6,3},{7,11},{8,13},{9,14},{10,15},{... | collective-permute-start | bytes 786440 | tf_op jit(solution)/shard_map/ppermute | solution.py:651
  158.0 17.1 %collective-permute-start.28 = (f32[776,128]{1,0:T(8,128)S(1)}, f32[776,128]{1,0:T(8,128)S(1)}, u32[]{:S(2)}, u32[]{:S(2)}) collective-permute-start(f32[776,128]{1,0:T(8,128)S(1)} %collective-permute-done.25.refs_10_), channel_id=1, source_target_pairs={{0,224},{32,0},{64,32},{96,64},{128,96},{160,128},{192,160},{224,1... | collective-permute-start | bytes 1191944 | tf_op jit(solution)/shard_map/ppermute | solution.py:662
  160.7 14.4 %collective-permute-start.26 = (f32[8,64,128]{2,1,0:T(8,128)S(1)}, f32[8,64,128]{2,1,0:T(8,128)S(1)}, u32[]{:S(2)}, u32[]{:S(2)}) collective-permute-start(f32[8,64,128]{2,1,0:T(8,128)S(1)} %get-tuple-element.155), channel_id=1, source_target_pairs={{0,4},{1,5},{2,6},{3,7},{4,0},{5,1},{6,2},{7,3},{8,12},{9,13},{10,... | collective-permute-start | bytes 786440 | tf_op jit(solution)/shard_map/ppermute | solution.py:651
  161.7 13.5 %collective-permute-start.27 = (f32[8,64,128]{2,1,0:T(8,128)S(1)}, f32[8,64,128]{2,1,0:T(8,128)S(1)}, u32[]{:S(2)}, u32[]{:S(2)}) collective-permute-start(f32[8,64,128]{2,1,0:T(8,128)S(1)} %get-tuple-element.156), channel_id=1, source_target_pairs={{1,4},{2,5},{3,6},{4,1},{5,2},{6,3},{7,11},{8,13},{9,14},{10,15},{... | collective-permute-start | bytes 786440 | tf_op jit(solution)/shard_map/ppermute | solution.py:651
  176.5 14.2 %collective-permute-start.29 = (f32[8,64,128]{2,1,0:T(8,128)S(1)}, f32[8,64,128]{2,1,0:T(8,128)S(1)}, u32[]{:S(2)}, u32[]{:S(2)}) collective-permute-start(f32[8,64,128]{2,1,0:T(8,128)S(1)} %get-tuple-element.162), channel_id=1, source_target_pairs={{0,4},{1,5},{2,6},{3,7},{4,0},{5,1},{6,2},{7,3},{8,12},{9,13},{10,... | collective-permute-start | bytes 786440 | tf_op jit(solution)/shard_map/ppermute | solution.py:651
  177.2 13.5 %collective-permute-start.30 = (f32[8,64,128]{2,1,0:T(8,128)S(1)}, f32[8,64,128]{2,1,0:T(8,128)S(1)}, u32[]{:S(2)}, u32[]{:S(2)}) collective-permute-start(f32[8,64,128]{2,1,0:T(8,128)S(1)} %get-tuple-element.163), channel_id=1, source_target_pairs={{1,4},{2,5},{3,6},{4,1},{5,2},{6,3},{7,11},{8,13},{9,14},{10,15},{... | collective-permute-start | bytes 786440 | tf_op jit(solution)/shard_map/ppermute | solution.py:651
  192.1 22.1 %collective-permute-start.31 = (f32[6,3,16,128]{3,2,1,0:T(8,128)S(1)}, f32[6,3,16,128]{3,2,1,0:T(8,128)S(1)}, u32[]{:S(2)}, u32[]{:S(2)}) collective-permute-start(f32[6,3,16,128]{3,2,1,0:T(8,128)S(1)} %get-tuple-element.165), channel_id=1, source_target_pairs={{0,0},{1,2},{2,4},{3,6},{4,1},{5,3},{6,5},{7,7},{8,14},{9,12},{10,... | collective-permute-start | bytes 442376 | tf_op jit(solution)/shard_map/ppermute | solution.py:643
  194.8 19.4 %collective-permute-start.32 = (f32[6,3,16,128]{3,2,1,0:T(8,128)S(1)}, f32[6,3,16,128]{3,2,1,0:T(8,128)S(1)}, u32[]{:S(2)}, u32[]{:S(2)}) collective-permute-start(f32[6,3,16,128]{3,2,1,0:T(8,128)S(1)} %get-tuple-element.166), channel_id=1, source_target_pairs={{0,1},{1,3},{2,5},{3,7},{4,2},{5,0},{6,6},{7,4},{8,15},{9,13},{10,... | collective-permute-start | bytes 442376 | tf_op jit(solution)/shard_map/ppermute | solution.py:643
  199.1 15.0 %collective-permute-start.33 = (f32[6,3,16,128]{3,2,1,0:T(8,128)S(1)}, f32[6,3,16,128]{3,2,1,0:T(8,128)S(1)}, u32[]{:S(2)}, u32[]{:S(2)}) collective-permute-start(f32[6,3,16,128]{3,2,1,0:T(8,128)S(1)} %get-tuple-element.167), channel_id=1, source_target_pairs={{0,2},{1,0},{2,6},{3,4},{4,3},{5,1},{6,7},{7,5},{8,12},{9,14},{10,... | collective-permute-start | bytes 442376 | tf_op jit(solution)/shard_map/ppermute | solution.py:643
  199.2 14.9 %collective-permute-start.34 = (f32[6,3,16,128]{3,2,1,0:T(8,128)S(1)}, f32[6,3,16,128]{3,2,1,0:T(8,128)S(1)}, u32[]{:S(2)}, u32[]{:S(2)}) collective-permute-start(f32[6,3,16,128]{3,2,1,0:T(8,128)S(1)} %get-tuple-element.168), channel_id=1, source_target_pairs={{0,3},{1,1},{2,7},{3,5},{4,0},{5,2},{6,4},{7,6},{8,13},{9,15},{10,... | collective-permute-start | bytes 442376 | tf_op jit(solution)/shard_map/ppermute | solution.py:643
